TPU v7x, 32 devices: a whole 2x2x4 slice. The times are simulated.
32 devices in a mesh: shard: 2 (over core), ctx: 4 (over y, x), tp: 4 (over z).
Axes of the slice: x: 2, y: 2, z: 4, core: 2. Of those that a mesh axis runs over, the one named last changes fastest.
Arguments:
- first_half: bfloat16 [4096, 4, 1024], P('ctx', 'shard', 'tp'), may hold values from -6 to 6
- second_half: bfloat16 [4096, 4, 1024], P('ctx', 'shard', 'tp'), may hold values from -6 to 6
- first_cotangent: bfloat16 [4096, 4, 1024], P('ctx', 'shard', 'tp'), may hold values from -6 to 6
- second_cotangent: bfloat16 [4096, 4, 1024], P('ctx', 'shard', 'tp'), may hold values from -6 to 6
- segment_ids: int32 [4, 4096], P('shard', 'ctx'), may hold values from 0 to 3, as said below
- bucket_ids: int32 [4, 4, 4096], P('shard', None, 'ctx'), may hold values from 0 to 63
- positions: int32 [4, 4096], P('shard', 'ctx'), may hold values from 0 to 4095, as said below
- query_weight: bfloat16 [1024, 1024], P('shard', 'tp'), may hold values from -0.1875 to 0.1875
- value_weight: bfloat16 [1024, 1024], P('shard', 'tp'), may hold values from -0.1875 to 0.1875
- output_weight: bfloat16 [1024, 1024], P('tp', 'shard'), may hold values from -0.75 to 0.75
- expand_weight: bfloat16 [1024, 4096], P('shard', 'tp'), may hold values from -0.1875 to 0.1875
- expand_bias: float32 [4096], P('tp'), may hold values from -3 to 3
- shrink_weight: bfloat16 [4096, 1024], P('tp', 'shard'), may hold values from -0.09375 to 0.09375
- shrink_bias: float32 [1024], P('tp'), may hold values from -2 to 2
- attention_gain: float32 [1024], replicated, may hold values from 0.1 to 1.9
- attention_shift: float32 [1024], replicated, may hold values from -2 to 2
- forward_gain: float32 [1024], replicated, may hold values from 0.1 to 1.9
- forward_shift: float32 [1024], replicated, may hold values from -2 to 2
Outputs:
- first_out: bfloat16 [4096, 4, 1024], P('ctx', 'shard', 'tp')
- second_out: bfloat16 [4096, 4, 1024], P('ctx', 'shard', 'tp')
- first_grad: bfloat16 [4096, 4, 1024], P('ctx', 'shard', 'tp')
- second_grad: bfloat16 [4096, 4, 1024], P('ctx', 'shard', 'tp')
- query_grad: float32 [1024, 1024], P('shard', 'tp')
- value_grad: float32 [1024, 1024], P('shard', 'tp')
- output_grad: float32 [1024, 1024], P('tp', 'shard')
- expand_grad: float32 [1024, 4096], P('shard', 'tp')
- expand_bias_grad: float32 [4096], P('tp')
- shrink_grad: float32 [4096, 1024], P('tp', 'shard')
- shrink_bias_grad: float32 [1024], P('tp')
- attention_gain_grad: float32 [1024], P('tp')
- attention_shift_grad: float32 [1024], P('tp')
- forward_gain_grad: float32 [1024], P('tp')
- forward_shift_grad: float32 [1024], P('tp')
Inputs may be any that keep to these rules, and one draw needn't show every extreme that they name: `segment_ids`: A document is a run of consecutive positions: ordered by positions, the numbers never fall; every document has a token; a document has at most 2000 tokens, and some document has exactly that many. Within each sequence the positions are a permutation of 0 to 4095.
All inputs are finite; a program needn't handle non-finite values.
Results may differ from a plain program's by a relative error of at most 0.019.
Values may be sent and summed in bfloat16 or wider, within the bound.
No kernel may reach another device: no remote copies, remote signals or barrier semaphores. Data moves between devices by JAX's collectives and lax.ppermute only.
A program may use at most 192 MiB of HBM per device.

v0:
```python
import jax
import jax.numpy as jnp
from jax import lax
from jax.sharding import PartitionSpec as P

D = 1024
DH = 128
ROUNDS = 4


SELF_SCORE = -10.0
NEG_FILL = -1e30
BLOCK_ROWS = 512


def smooth_unit(values_in):
    return jax.nn.gelu(values_in, approximate=False)


def norm_rows(rows_wide, gain_row, shift_row):
    centre = jnp.mean(rows_wide, -1, keepdims=True)
    offset = rows_wide - centre
    inverse = lax.rsqrt(jnp.mean(offset * offset, -1, keepdims=True) + 1e-05)
    scaled = offset * inverse
    return (scaled * gain_row + shift_row, scaled, inverse)


def unit_keys(queries):
    shaped = queries.reshape(queries.shape[:-1] + (queries.shape[-1] // DH, DH))
    factor = lax.rsqrt(jnp.mean(shaped * shaped, -1, keepdims=True) + 1e-06) * DH ** (-0.5)
    return (shaped * factor).reshape(queries.shape)


def heads_view(vectors):
    return vectors.reshape(vectors.shape[0], vectors.shape[1], vectors.shape[2] // DH, DH)


def full_rows(sliced):
    return lax.all_gather(sliced, "tp", axis=2, tiled=True)


def branch_sum(partial_value):
    return lax.psum_scatter(partial_value, "tp", scatter_dimension=2, tiled=True)


def norm_back(grad_slice, scaled_slice, inverse, gain_slice):
    weighted = grad_slice * gain_slice
    first_sum, second_sum = lax.psum(
        (jnp.sum(weighted, -1, keepdims=True), jnp.sum(weighted * scaled_slice, -1, keepdims=True)),
        "tp",
    )
    inner = inverse * (weighted - first_sum / D - scaled_slice * (second_sum / D))
    return (inner, jnp.sum(grad_slice * scaled_slice, (0, 1)), jnp.sum(grad_slice, (0, 1)))


def label_rows(all_labels, begin_row, extent):
    all_segments, all_buckets, all_positions = all_labels
    return (
        lax.dynamic_slice_in_dim(all_segments, begin_row, extent, 1),
        lax.dynamic_slice_in_dim(all_buckets, begin_row, extent, 2),
        lax.dynamic_slice_in_dim(all_positions, begin_row, extent, 1),
    )


def block_weights(query_heads, query_labels, key_heads, key_labels):
    query_seg, query_buck, query_pos = query_labels
    key_seg, key_buck, key_pos = key_labels
    scores = jnp.einsum(
        "pshd,kshd->shpk", query_heads, key_heads, preferred_element_type=jnp.float32
    )
    matches = jnp.sum((query_buck[:, :, :, None] == key_buck[:, :, None, :]).astype(jnp.int32), 1)
    same_doc = query_seg[:, :, None] == key_seg[:, None, :]
    earlier = key_pos[:, None, :] < query_pos[:, :, None]
    itself = key_pos[:, None, :] == query_pos[:, :, None]
    counts = jnp.where(itself, ROUNDS, jnp.where(earlier & same_doc, matches, 0)).astype(
        jnp.float32
    )[:, None]
    shifted = jnp.where(itself[:, None], SELF_SCORE, scores)
    return (shifted, counts, itself[:, None])


def weights_of(shifted, counts, log_total):
    return jnp.where(counts > 0, counts * jnp.exp(shifted - log_total[..., None]), 0.0)


def blockwise(advance, running, row_count):
    extent = BLOCK_ROWS

    def turn(state_now, block_index):
        return (advance(state_now, block_index * extent, extent), None)

    return lax.scan(turn, running, jnp.arange(row_count // extent, dtype=jnp.int32))[0]


def over_keys(key_vectors, value_vectors, folder, initial):
    return folder(
        initial,
        (
            lax.all_gather(key_vectors, "ctx", axis=0, tiled=True),
            lax.all_gather(value_vectors, "ctx", axis=0, tiled=True),
        ),
        jnp.int32(0),
    )


def over_context(first_part, second_part, third_part, fourth_part, fifth_part):
    return (
        lax.psum(first_part.astype(jnp.bfloat16), "ctx").astype(jnp.float32),
        lax.psum(second_part.astype(jnp.bfloat16), "ctx").astype(jnp.float32),
        lax.psum(third_part.astype(jnp.bfloat16), "ctx").astype(jnp.float32),
        lax.psum(fourth_part.astype(jnp.bfloat16), "ctx").astype(jnp.float32),
        lax.psum(fifth_part.astype(jnp.bfloat16), "ctx").astype(jnp.float32),
    )


def to_row_owners(first_part, second_part, third_part):
    return (
        lax.psum_scatter(
            first_part.astype(jnp.bfloat16), "shard", scatter_dimension=0, tiled=True
        ).astype(jnp.float32),
        lax.psum_scatter(
            second_part.astype(jnp.bfloat16), "shard", scatter_dimension=0, tiled=True
        ).astype(jnp.float32),
        lax.psum_scatter(
            third_part.astype(jnp.bfloat16), "shard", scatter_dimension=0, tiled=True
        ).astype(jnp.float32),
    )


def to_col_owners(first_part, second_part):
    return (
        lax.psum_scatter(
            first_part.astype(jnp.bfloat16), "shard", scatter_dimension=1, tiled=True
        ).astype(jnp.float32),
        lax.psum_scatter(
            second_part.astype(jnp.bfloat16), "shard", scatter_dimension=1, tiled=True
        ).astype(jnp.float32),
    )


def per_device(
    first_half,
    second_half,
    first_cotangent,
    second_cotangent,
    segment_ids,
    bucket_ids,
    positions,
    query_weight,
    value_weight,
    output_weight,
    expand_weight,
    expand_bias,
    shrink_weight,
    shrink_bias,
    attention_gain,
    attention_shift,
    forward_gain,
    forward_shift,
):
    rows_here, seqs_here, slice_width = first_half.shape
    width_heads = query_weight.shape[1]
    heads_here = width_heads // DH
    tp_start = lax.axis_index("tp") * slice_width
    ctx_start = lax.axis_index("ctx") * rows_here
    bf16 = jnp.bfloat16
    f32 = jnp.float32

    def columns(wide):
        return lax.dynamic_slice_in_dim(wide, tp_start, slice_width, wide.ndim - 1)

    full_query, full_value, full_expand = (
        lax.all_gather(query_weight, "shard", axis=0, tiled=True),
        lax.all_gather(value_weight, "shard", axis=0, tiled=True),
        lax.all_gather(expand_weight, "shard", axis=0, tiled=True),
    )
    full_output, full_shrink = (
        lax.all_gather(output_weight, "shard", axis=1, tiled=True),
        lax.all_gather(shrink_weight, "shard", axis=1, tiled=True),
    )
    all_labels = (
        lax.all_gather(segment_ids, "ctx", axis=1, tiled=True),
        lax.all_gather(bucket_ids, "ctx", axis=2, tiled=True),
        lax.all_gather(positions, "ctx", axis=1, tiled=True),
    )
    local_labels = label_rows(all_labels, ctx_start, rows_here)
    second_wide = full_rows(second_half)
    normed, attn_scaled, attn_inverse = norm_rows(
        second_wide.astype(f32), attention_gain, attention_shift
    )
    normed = normed.astype(bf16)
    queries = jnp.einsum("psd,de->pse", normed, full_query, preferred_element_type=f32).astype(bf16)
    key_vectors = unit_keys(queries.astype(f32)).astype(bf16)
    value_vectors = jnp.einsum(
        "psd,de->pse", normed, full_value, preferred_element_type=f32
    ).astype(bf16)
    query_heads = heads_view(queries)
    stat_shape = (seqs_here, heads_here, rows_here)
    head_zero = jnp.zeros((rows_here, seqs_here, heads_here, DH), f32)

    def norm_fold(running, pieces, begin_row):
        key_piece = pieces[0]

        def advance(state_now, offset, extent):
            highest, summed = state_now
            key_heads = heads_view(lax.dynamic_slice_in_dim(key_piece, offset, extent, 0))
            shifted, counts, _ = block_weights(
                query_heads, local_labels, key_heads, label_rows(all_labels, offset, extent)
            )
            usable = counts > 0
            new_high = jnp.maximum(highest, jnp.max(jnp.where(usable, shifted, NEG_FILL), -1))
            summed = summed * jnp.exp(highest - new_high) + jnp.sum(
                jnp.where(usable, counts * jnp.exp(shifted - new_high[..., None]), 0.0), -1
            )
            return (new_high, summed)

        return blockwise(advance, running, key_piece.shape[0])

    highest, summed = over_keys(
        key_vectors,
        value_vectors,
        norm_fold,
        (jnp.full(stat_shape, NEG_FILL, f32), jnp.zeros(stat_shape, f32)),
    )
    log_total = highest + jnp.log(summed)

    def key_block(pieces, offset, extent):
        key_heads = heads_view(lax.dynamic_slice_in_dim(pieces[0], offset, extent, 0))
        value_heads = heads_view(lax.dynamic_slice_in_dim(pieces[1], offset, extent, 0))
        shifted, counts, itself = block_weights(
            query_heads, local_labels, key_heads, label_rows(all_labels, offset, extent)
        )
        return (key_heads, value_heads, weights_of(shifted, counts, log_total), itself)

    def mix_fold(running, pieces, begin_row):

        def advance(state_now, offset, extent):
            key_heads, value_heads, weights, itself = key_block(pieces, offset, extent)
            return state_now + jnp.einsum(
                "shpk,kshd->pshd", weights.astype(bf16), value_heads, preferred_element_type=f32
            )

        return blockwise(advance, running, pieces[0].shape[0])

    head_mix = over_keys(key_vectors, value_vectors, mix_fold, head_zero)
    attention = head_mix.reshape(rows_here, seqs_here, width_heads).astype(bf16)
    branch = branch_sum(
        jnp.einsum("pse,ed->psd", attention, full_output, preferred_element_type=f32)
    )
    first_out = (first_half.astype(f32) + branch).astype(bf16)
    first_wide = full_rows(first_out)
    ffn_in, ffn_scaled, ffn_inverse = norm_rows(first_wide.astype(f32), forward_gain, forward_shift)
    ffn_in = ffn_in.astype(bf16)
    pre_act = (
        jnp.einsum("psd,df->psf", ffn_in, full_expand, preferred_element_type=f32) + expand_bias
    )
    hidden_exact, unit_pull = jax.vjp(smooth_unit, pre_act)
    hidden = hidden_exact.astype(bf16)
    second_branch = (
        branch_sum(jnp.einsum("psf,fd->psd", hidden, full_shrink, preferred_element_type=f32))
        + shrink_bias
    )
    second_out = (second_half.astype(f32) + second_branch).astype(bf16)
    cotangent_wide = full_rows(second_cotangent)
    hidden_grad = jnp.einsum("psd,fd->psf", cotangent_wide, full_shrink, preferred_element_type=f32)
    pre_grad = unit_pull(hidden_grad)[0].astype(bf16)
    shrink_grad = jnp.einsum("psf,psd->fd", hidden, cotangent_wide, preferred_element_type=f32)
    shrink_bias_grad = jnp.sum(second_cotangent.astype(f32), (0, 1))
    expand_grad = jnp.einsum("psd,psf->df", ffn_in, pre_grad, preferred_element_type=f32)
    expand_bias_grad = jnp.sum(pre_grad.astype(f32), (0, 1))
    ffn_grad = branch_sum(
        jnp.einsum("psf,df->psd", pre_grad, full_expand, preferred_element_type=f32)
    )
    ffn_back, forward_gain_grad, forward_shift_grad = norm_back(
        ffn_grad, columns(ffn_scaled), ffn_inverse, columns(forward_gain)
    )
    first_grad = (first_cotangent.astype(f32) + ffn_back).astype(bf16)
    grad_wide = full_rows(first_grad)
    output_grad = jnp.einsum("pse,psd->ed", attention, grad_wide, preferred_element_type=f32)
    attention_grad = jnp.einsum(
        "psd,ed->pse", grad_wide, full_output, preferred_element_type=f32
    ).astype(bf16)
    grad_heads = heads_view(attention_grad)

    def delta_fold(running, pieces, begin_row):

        def advance(state_now, offset, extent):
            key_heads, value_heads, weights, itself = key_block(pieces, offset, extent)
            upstream = jnp.einsum(
                "pshd,kshd->shpk", grad_heads, value_heads, preferred_element_type=f32
            )
            return state_now + jnp.sum(weights * upstream, -1)

        return blockwise(advance, running, pieces[0].shape[0])

    row_delta = over_keys(key_vectors, value_vectors, delta_fold, jnp.zeros(stat_shape, f32))

    def query_fold(running, pieces, begin_row):

        def advance(state_now, offset, extent):
            key_heads, value_heads, weights, itself = key_block(pieces, offset, extent)
            upstream = jnp.einsum(
                "pshd,kshd->shpk", grad_heads, value_heads, preferred_element_type=f32
            )
            score_grad = jnp.where(itself, 0.0, weights * (upstream - row_delta[..., None])).astype(
                bf16
            )
            return state_now + jnp.einsum(
                "shpk,kshd->pshd", score_grad, key_heads, preferred_element_type=f32
            )

        return blockwise(advance, running, pieces[0].shape[0])

    query_part = over_keys(key_vectors, value_vectors, query_fold, head_zero)
    query_lse, query_delta = (
        lax.all_gather(log_total, "ctx", axis=2, tiled=True),
        lax.all_gather(row_delta, "ctx", axis=2, tiled=True),
    )
    local_keys = heads_view(key_vectors)
    local_values = heads_view(value_vectors)
    query_piece = lax.all_gather(queries, "ctx", axis=0, tiled=True)
    grad_piece = lax.all_gather(attention_grad, "ctx", axis=0, tiled=True)

    def advance(state_now, offset, extent):
        remote_queries = heads_view(lax.dynamic_slice_in_dim(query_piece, offset, extent, 0))
        remote_grads = heads_view(lax.dynamic_slice_in_dim(grad_piece, offset, extent, 0))
        lse_rows = lax.dynamic_slice_in_dim(query_lse, offset, extent, 2)
        delta_rows = lax.dynamic_slice_in_dim(query_delta, offset, extent, 2)
        shifted, counts, itself = block_weights(
            remote_queries, label_rows(all_labels, offset, extent), local_keys, local_labels
        )
        weights = weights_of(shifted, counts, lse_rows)
        upstream = jnp.einsum(
            "pshd,kshd->shpk", remote_grads, local_values, preferred_element_type=f32
        )
        score_grad = jnp.where(itself, 0.0, weights * (upstream - delta_rows[..., None])).astype(
            bf16
        )
        key_now = state_now[0] + jnp.einsum(
            "shpk,pshd->kshd", score_grad, remote_queries, preferred_element_type=f32
        )
        value_now = state_now[1] + jnp.einsum(
            "shpk,pshd->kshd", weights.astype(bf16), remote_grads, preferred_element_type=f32
        )
        return (key_now, value_now)

    key_part, value_part = blockwise(advance, (head_zero, head_zero), query_piece.shape[0])
    keys_grad = key_part.reshape(rows_here, seqs_here, width_heads).astype(bf16)
    values_grad = value_part.reshape(rows_here, seqs_here, width_heads).astype(bf16)
    unit_back = jax.vjp(unit_keys, queries.astype(f32))[1]
    queries_total = (
        query_part.reshape(rows_here, seqs_here, width_heads) + unit_back(keys_grad.astype(f32))[0]
    ).astype(bf16)
    query_grad = jnp.einsum("psd,pse->de", normed, queries_total, preferred_element_type=f32)
    value_grad = jnp.einsum("psd,pse->de", normed, values_grad, preferred_element_type=f32)
    normed_grad = branch_sum(
        jnp.einsum("pse,de->psd", queries_total, full_query, preferred_element_type=f32)
        + jnp.einsum("pse,de->psd", values_grad, full_value, preferred_element_type=f32)
    )
    attn_back, attention_gain_grad, attention_shift_grad = norm_back(
        normed_grad, columns(attn_scaled), attn_inverse, columns(attention_gain)
    )
    second_grad = (second_cotangent.astype(f32) + attn_back).astype(bf16)
    expand_bias_sum, shrink_bias_sum, attn_gain_sum, attn_shift_sum, ffn_gain_sum, ffn_shift_sum = (
        lax.psum(
            (
                expand_bias_grad,
                shrink_bias_grad,
                attention_gain_grad,
                attention_shift_grad,
                forward_gain_grad,
                forward_shift_grad,
            ),
            ("shard", "ctx"),
        )
    )
    query_sum, value_sum, expand_sum, output_sum, shrink_sum = over_context(
        query_grad, value_grad, expand_grad, output_grad, shrink_grad
    )
    query_own, value_own, expand_own = to_row_owners(query_sum, value_sum, expand_sum)
    output_own, shrink_own = to_col_owners(output_sum, shrink_sum)
    return (
        first_out,
        second_out,
        first_grad,
        second_grad,
        query_own,
        value_own,
        output_own,
        expand_own,
        expand_bias_sum,
        shrink_own,
        shrink_bias_sum,
        attn_gain_sum,
        attn_shift_sum,
        ffn_gain_sum,
        ffn_shift_sum,
    )


def solution(mesh):
    return jax.shard_map(
        per_device,
        mesh=mesh,
        in_specs=(
            P("ctx", "shard", "tp"),
            P("ctx", "shard", "tp"),
            P("ctx", "shard", "tp"),
            P("ctx", "shard", "tp"),
            P("shard", "ctx"),
            P("shard", None, "ctx"),
            P("shard", "ctx"),
            P("shard", "tp"),
            P("shard", "tp"),
            P("tp", "shard"),
            P("shard", "tp"),
            P("tp"),
            P("tp", "shard"),
            P("tp"),
            P(),
            P(),
            P(),
            P(),
        ),
        out_specs=(
            P("ctx", "shard", "tp"),
            P("ctx", "shard", "tp"),
            P("ctx", "shard", "tp"),
            P("ctx", "shard", "tp"),
            P("shard", "tp"),
            P("shard", "tp"),
            P("tp", "shard"),
            P("shard", "tp"),
            P("tp"),
            P("tp", "shard"),
            P("tp"),
            P("tp"),
            P("tp"),
            P("tp"),
            P("tp"),
        ),
        check_vma=False,
    )
```

profile of v0, /device:TPU:1, one launch (start us, length us, event | category | flops | bytes accessed | tf_op | source)
XLA Modules:
  0.0 2538.3 jit_solution(5461100967996575761)
XLA Ops:
  12.9 80.0 %all-gather.11.cloned.1.call-done = bf16[1024,2,1024]{2,0,1:T(8,128)(2,1)} async-done(((bf16[1024,2,256]{2,0,1:T(8,128)(2,1)}), bf16[1024,2,1024]{2,0,1:T(8,128)(2,1)}) %all-gather.11.cloned.1.call-update) | async-done | bytes 4194320 | tf_op jit(solution)/shard_map/all_gather | solution.py:39
  138.3 16.6 all-gather.15.cloned.1.call-done
  154.9 234.5 %while.59 = (s32[]{:T(128)}, f32[2,2,1024]{2,1,0:T(2,128)S(1)}, f32[2,2,1024]{2,1,0:T(2,128)S(1)}, s32[8]{0:T(128)S(1)}, s32[2,4096]{1,0:T(2,128)S(1)}, /*index=...) while((s32[]{:T(128)}, f32[2,2,1024]{2,1,0:T(2,128)S(1)}, ...), condition=%wide.region_7.8_spmd.clone, body=%wide.region_3.7_spmd.clone.sunk | while | flops 573591552 | bytes 55386348 | solution.py:92
  389.5 224.4 %while.60 = (s32[]{:T(128)}, f32[1024,2,2,128]{0,3,2,1:T(8,128)}, s32[8]{0:T(128)S(1)}, bf16[4096,2,256]{0,2,1:T(8,128)(2,1)}, s32[2,4096]{1,0:T(2,128)S(1)}, /*...) while((s32[]{:T(128)}, f32[1024,2,2,128]{0,3,2,1:T(8,128)}, ...), condition=%wide.region_10.11_spmd.clone, body=%wide.region_8.10_spmd.clone.sunk | while | flops 1105199104 | bytes 42082548 | solution.py:92
  621.7 144.5 %reduce-scatter.10.cloned.1.call-done = f32[1024,2,256]{2,0,1:T(8,128)} async-done(((f32[1024,2,1024]{2,0,1:T(8,128)}), f32[1024,2,256]{2,0,1:T(8,128)}) %reduce-scatter.10.cloned.1.call-update) | async-done | bytes 2097168 | tf_op jit(solution)/shard_map/reduce_scatter | solution.py:43
  771.9 79.2 %all-gather.17.cloned.1.call-done = bf16[1024,2,1024]{2,0,1:T(8,128)(2,1)} async-done(((bf16[1024,2,256]{2,0,1:T(8,128)(2,1)}), bf16[1024,2,1024]{2,0,1:T(8,128)(2,1)}) %all-gather.17.cloned.1.call-update) | async-done | bytes 4194320 | tf_op jit(solution)/shard_map/all_gather | solution.py:39
  861.5 10.0 fusion.79
  874.8 20.7 multiply_convert_fusion
  895.5 63.0 %all-gather.23.cloned.1.call-done = bf16[1024,2,1024]{2,0,1:T(8,128)(2,1)} async-done(((bf16[1024,2,256]{2,0,1:T(8,128)(2,1)}), bf16[1024,2,1024]{2,0,1:T(8,128)(2,1)}) %all-gather.23.cloned.1.call-update) | async-done | bytes 4194320 | tf_op jit(solution)/shard_map/all_gather | solution.py:39
  958.5 12.9 convert_reduce_fusion.7
  986.1 136.7 %reduce-scatter.14.cloned.1.call-done = f32[1024,2,256]{2,0,1:T(8,128)} async-done(((f32[1024,2,1024]{2,0,1:T(8,128)}), f32[1024,2,256]{2,0,1:T(8,128)}) %reduce-scatter.14.cloned.1.call-update) | async-done | bytes 2097168 | tf_op jit(solution)/shard_map/reduce_scatter | solution.py:43
  1126.4 14.8 all-reduce.2
  1145.6 82.0 %all-gather.25.cloned.1.call-done = bf16[1024,2,1024]{2,0,1:T(8,128)(2,1)} async-done(((bf16[1024,2,256]{2,0,1:T(8,128)(2,1)}), bf16[1024,2,1024]{2,0,1:T(8,128)(2,1)}) %all-gather.25.cloned.1.call-update) | async-done | bytes 4194320 | tf_op jit(solution)/shard_map/all_gather | solution.py:39
  1232.1 10.8 bitcast_convert_fusion.1
  1252.9 9.5 bitcast_convert_fusion
  1263.8 265.2 %while.61 = (s32[]{:T(128)}, f32[2,2,1024]{2,1,0:T(2,128)S(1)}, s32[8]{0:T(128)S(1)}, s32[2,4096]{1,0:T(2,128)S(1)}, s32[2,1024]{1,0:T(2,128)S(1)}, /*index=5*/s...) while((s32[]{:T(128)}, f32[2,2,1024]{2,1,0:T(2,128)S(1)}, ...), condition=%wide.region_23.24_spmd.clone, body=%wide.region_20.23_spmd.clone.sunk | while | flops 1106251776 | bytes 55779576 | solution.py:92
  1287.7 10.0 fusion.176
  1321.8 8.9 fusion.176
  1354.7 9.9 fusion.176
  1388.6 8.9 fusion.176
  1421.5 8.9 fusion.176
  1454.3 8.9 fusion.176
  1487.2 8.9 fusion.176
  1520.1 8.9 fusion.176
  1529.0 272.0 %while.62 = (s32[]{:T(128)}, f32[1024,2,2,128]{0,3,2,1:T(8,128)}, s32[8]{0:T(128)S(1)}, bf16[4096,2,256]{0,2,1:T(8,128)(2,1)}, s32[2,4096]{1,0:T(2,128)S(1)}, /*...) while((s32[]{:T(128)}, f32[1024,2,2,128]{0,3,2,1:T(8,128)}, ...), condition=%wide.region_26.27_spmd.clone, body=%wide.region_24.26_spmd.clone.sunk | while | flops 1648361472 | bytes 62546208 | solution.py:92
  1553.4 9.8 bitcast_add_fusion.9
  1587.1 10.1 bitcast_add_fusion.9
  1621.0 10.1 bitcast_add_fusion.9
  1655.0 10.1 bitcast_add_fusion.9
  1689.0 10.1 bitcast_add_fusion.9
  1723.0 10.1 bitcast_add_fusion.9
  1757.0 10.1 bitcast_add_fusion.9
  1791.0 10.1 bitcast_add_fusion.9
  1811.9 263.7 %while.63 = (s32[]{:T(128)}, f32[1024,2,2,128]{0,3,2,1:T(8,128)}, f32[1024,2,2,128]{0,3,2,1:T(8,128)}, s32[8]{0:T(128)S(1)}, bf16[4096,2,256]{0,2,1:T(8,128)(2,1...) while((s32[]{:T(128)}, f32[1024,2,2,128]{0,3,2,1:T(8,128)}, ...), condition=%wide.region_29.30_spmd.clone, body=%wide.region_27.29_spmd.clone.sunk | while | flops 2196766720 | bytes 67289360 | solution.py:92
  1826.9 9.2 bitcast_add_fusion.10
  1859.1 9.4 bitcast_add_fusion.10
  1892.2 9.4 bitcast_add_fusion.10
  1925.2 9.4 bitcast_add_fusion.10
  1958.2 9.4 bitcast_add_fusion.10
  1991.3 9.4 bitcast_add_fusion.10
  2024.3 9.4 bitcast_add_fusion.10
  2057.4 9.4 bitcast_add_fusion.10
  2091.9 10.8 fusion.71
  2121.9 131.4 %reduce-scatter.12.cloned.1.call-done = f32[1024,2,256]{2,0,1:T(8,128)} async-done(((f32[1024,2,1024]{2,0,1:T(8,128)}), f32[1024,2,256]{2,0,1:T(8,128)}) %reduce-scatter.12.cloned.1.call-update) | async-done | bytes 2097168 | tf_op jit(solution)/shard_map/reduce_scatter | solution.py:43
  2257.2 84.7 %all-reduce.6.cloned.1.call-done = (bf16[512,256]{1,0:T(8,128)(2,1)}, bf16[512,256]{1,0:T(8,128)(2,1)}, bf16[256,512]{1,0:T(8,128)(2,1)}, bf16[512,1024]{1,0:T(8,128)(2,1)}, bf16[1024,512]{1,0:T(8,128)(2,1)}) async-done(((bf16[512,256]{1,0:T(8,128)(2,1)}, bf16[512,256]{1,0:T(8,128)(2,1)}, bf16[256,512]{1,0:T(8,128)(2,1)}, bf16[512,1024]{1,0:T(8,128)(2,1)}, bf16[1024,512]{1,0:T(8,128)(2,1)}), ...) | async-done | bytes 2883600 | tf_op jit(solution)/shard_map/psum | solution.py:108
  2353.4 135.1 %reduce-scatter.16.cloned.1.call-done = f32[1024,2,256]{2,0,1:T(8,128)} async-done(((f32[1024,2,1024]{2,0,1:T(8,128)}), f32[1024,2,256]{2,0,1:T(8,128)}) %reduce-scatter.16.cloned.1.call-update) | async-done | bytes 2097168 | tf_op jit(solution)/shard_map/reduce_scatter | solution.py:43
  2491.6 14.8 all-reduce.1
  2511.2 19.9 all-reduce
  (667 shorter events, 1187.8 us)
Async XLA Ops:
  7.2 91.8 %copy-start.43 = (f32[1024]{0:T(1024)S(1)}, f32[1024]{0:T(1024)}, u32[]{:S(2)}) copy-start(f32[1024]{0:T(1024)} %param.43) | copy-start | bytes 12292
  7.2 91.8 %copy-start.39 = (f32[1024]{0:T(1024)S(1)}, f32[1024]{0:T(1024)}, u32[]{:S(2)}) copy-start(f32[1024]{0:T(1024)} %param.42) | copy-start | bytes 12292
  7.2 85.8 %all-gather.11.cloned.1.call-start = ((), (), s32[]{:S(2)}) async-start(), calls=%async_computation.9 | async-start | bytes 5242880 | tf_op jit(solution)/shard_map/all_gather | solution.py:39
  9.6 145.3 %all-gather.15.cloned.1.call-start = ((), (), s32[]{:S(2)}) async-start(), calls=%async_computation.11 | async-start | bytes 5242880 | tf_op jit(solution)/shard_map/all_gather | solution.py:99
  12.9 88.6 %copy-start.14 = (bf16[1024,256]{0,1:T(8,128)(2,1)}, bf16[1024,256]{0,1:T(8,128)(2,1)S(1)}, u32[]{:S(2)}) copy-start(bf16[1024,256]{0,1:T(8,128)(2,1)S(1)} %all_gather.65) | copy-start | bytes 1572868
  96.0 36.8 %copy-start.26 = (f32[1024,2]{0,1:T(2,128)}, f32[1024,2]{0,1:T(2,128)S(1)}, u32[]{:S(2)}) copy-start(f32[1024,2]{0,1:T(2,128)S(1)} %broadcast_multiply_fusion.1) | copy-start | bytes 24580
  99.0 33.8 %copy-start.24 = (f32[1024,2]{0,1:T(2,128)}, f32[1024,2]{0,1:T(2,128)S(1)}, u32[]{:S(2)}) copy-start(f32[1024,2]{0,1:T(2,128)S(1)} %add_rsqrt_fusion.1) | copy-start | bytes 24580
  99.1 10.3 copy-start.32
  99.1 17.2 copy-start.30
  99.1 30.7 %copy-start.20 = (bf16[256,512]{1,0:T(8,128)(2,1)S(1)}, bf16[256,512]{1,0:T(8,128)(2,1)}, u32[]{:S(2)}) copy-start(bf16[256,512]{1,0:T(8,128)(2,1)} %param.37) | copy-start | bytes 786436
  101.5 22.0 copy-start.28
  101.5 36.5 %copy-start.3 = (bf16[1024,2,256]{0,2,1:T(8,128)(2,1)}, bf16[1024,2,256]{0,2,1:T(8,128)(2,1)S(1)}, u32[]{:S(2)}) copy-start(bf16[1024,2,256]{0,2,1:T(8,128)(2,1)S(1)} %get-tuple-element.1156) | copy-start | bytes 3145732
  101.6 30.5 %copy-start.22 = (f32[1024,2,2]{0,2,1:T(2,128)}, f32[1024,2,2]{0,2,1:T(2,128)S(1)}, u32[]{:S(2)}) copy-start(f32[1024,2,2]{0,2,1:T(2,128)S(1)} %rsqrt_multiply_fusion) | copy-start | bytes 49156
  102.9 286.6 %all-gather.13.cloned.1.call-start = ((), (), s32[]{:S(2)}) async-start(), calls=%async_computation.10 | async-start | bytes 5242880 | tf_op jit(solution)/shard_map/all_gather | solution.py:100
  138.1 628.1 %reduce-scatter.10.cloned.1.call-start = ((), (), s32[]{:S(2)}) async-start(), calls=%async_computation.12 | async-start | bytes 10485760 | tf_op jit(solution)/shard_map/reduce_scatter | solution.py:43
  621.6 149.1 %copy-start.12 = (bf16[1024,2,256]{2,1,0:T(2,128)(2,1)S(1)}, bf16[1024,2,256]{2,1,0:T(2,128)(2,1)}, u32[]{:S(2)}) copy-start(bf16[1024,2,256]{2,1,0:T(2,128)(2,1)} %param.31) | copy-start | bytes 3145732
  621.6 229.4 %all-gather.17.cloned.1.call-start = ((), (), s32[]{:S(2)}) async-start(), calls=%async_computation.13 | async-start | bytes 5242880 | tf_op jit(solution)/shard_map/all_gather | solution.py:39
  769.3 92.2 %copy-start.33 = (f32[1024]{0:T(1024)S(1)}, f32[1024]{0:T(1024)}, u32[]{:S(2)}) copy-start(f32[1024]{0:T(1024)} %param.39) | copy-start | bytes 12292
  769.3 92.2 %copy-start.38 = (f32[1024]{0:T(1024)S(1)}, f32[1024]{0:T(1024)}, u32[]{:S(2)}) copy-start(f32[1024]{0:T(1024)} %param.44) | copy-start | bytes 12292
  769.3 92.2 %copy-start.42 = (f32[1024]{0:T(1024)S(1)}, f32[1024]{0:T(1024)}, u32[]{:S(2)}) copy-start(f32[1024]{0:T(1024)} %param.45) | copy-start | bytes 12292
  769.3 92.2 %all-gather.19.cloned.1.call-start = ((), (), s32[]{:S(2)}) async-start(), calls=%async_computation.14 | async-start | bytes 3145728 | tf_op jit(solution)/shard_map/all_gather | solution.py:175
  769.9 125.6 %all-gather.21.cloned.1.call-start = ((), (), s32[]{:S(2)}) async-start(), calls=%async_computation.15 | async-start | bytes 3145728 | tf_op jit(solution)/shard_map/all_gather | solution.py:179
  770.7 187.8 %all-gather.23.cloned.1.call-start = ((), (), s32[]{:S(2)}) async-start(), calls=%async_computation.17 | async-start | bytes 5242880 | tf_op jit(solution)/shard_map/all_gather | solution.py:39
  771.9 351.0 %reduce-scatter.14.cloned.1.call-start = ((), (), s32[]{:S(2)}) async-start(), calls=%async_computation.18 | async-start | bytes 10485760 | tf_op jit(solution)/shard_map/reduce_scatter | solution.py:43
  958.5 14.8 copy-start.41
  980.3 247.3 %all-gather.25.cloned.1.call-start = ((), (), s32[]{:S(2)}) async-start(), calls=%async_computation.19 | async-start | bytes 5242880 | tf_op jit(solution)/shard_map/all_gather | solution.py:39
  980.5 160.8 %copy-start.19 = (bf16[1024,2,256]{2,1,0:T(2,128)(2,1)S(1)}, bf16[1024,2,256]{2,1,0:T(2,128)(2,1)}, u32[]{:S(2)}) copy-start(bf16[1024,2,256]{2,1,0:T(2,128)(2,1)} %param.30) | copy-start | bytes 3145732
  986.1 241.5 %copy-start.18 = (bf16[256,1024]{1,0:T(8,128)(2,1)S(1)}, bf16[256,1024]{1,0:T(8,128)(2,1)}, u32[]{:S(2)}) copy-start(bf16[256,1024]{1,0:T(8,128)(2,1)} %all_gather.67) | copy-start | bytes 1572868
  1144.8 667.0 %all-gather.27.cloned.1.call-start = ((), (), s32[]{:S(2)}) async-start(), calls=%async_computation.20 | async-start | bytes 5242880 | tf_op jit(solution)/shard_map/all_gather | solution.py:321
  1145.5 666.3 %all-gather.29.cloned.1.call-start = ((), (), s32[]{:S(2)}) async-start(), calls=%async_computation.21 | async-start | bytes 5242880 | tf_op jit(solution)/shard_map/all_gather | solution.py:322
  1232.1 10.9 copy-start.4
  1232.1 12.2 copy-start.10
  1232.1 870.7 %reduce-scatter.24.cloned.1.call-start = ((), (), s32[]{:S(2)}) async-start(), calls=%async_computation.26 | async-start | bytes 3145728 | tf_op jit(solution)/shard_map/reduce_scatter | solution.py:124
  1242.9 859.9 %reduce-scatter.26.cloned.1.call-start = ((), (), s32[]{:S(2)}) async-start(), calls=%async_computation.27 | async-start | bytes 3145728 | tf_op jit(solution)/shard_map/reduce_scatter | solution.py:135
  1262.4 840.4 %reduce-scatter.22.cloned.1.call-start = ((), (), s32[]{:S(2)}) async-start(), calls=%async_computation.25 | async-start | bytes 786432 | tf_op jit(solution)/shard_map/reduce_scatter | solution.py:132
  1811.8 291.1 %reduce-scatter.18.cloned.1.call-start = ((), (), s32[]{:S(2)}) async-start(), calls=%async_computation.23 | async-start | bytes 786432 | tf_op jit(solution)/shard_map/reduce_scatter | solution.py:118
  1811.9 266.1 %copy-start.29 = (f32[1024,2,2]{0,2,1:T(2,128)S(1)}, f32[1024,2,2]{0,2,1:T(2,128)}, u32[]{:S(2)}) copy-start(f32[1024,2,2]{0,2,1:T(2,128)} %copy-done.28) | copy-start | bytes 49156
  1811.9 266.1 %copy-start.23 = (f32[1024,2,2]{0,2,1:T(2,128)S(1)}, f32[1024,2,2]{0,2,1:T(2,128)}, u32[]{:S(2)}) copy-start(f32[1024,2,2]{0,2,1:T(2,128)} %copy-done.22) | copy-start | bytes 49156
  2084.6 21.2 reduce-scatter.20.cloned.1.call-start
  2091.9 161.4 %reduce-scatter.12.cloned.1.call-start = ((), (), s32[]{:S(2)}) async-start(), calls=%async_computation.16 | async-start | bytes 10485760 | tf_op jit(solution)/shard_map/reduce_scatter | solution.py:43
  2102.7 239.3 %all-reduce.6.cloned.1.call-start = ((), (), s32[]{:S(2)}) async-start(), calls=%async_computation.28 | async-start | bytes 5767168 | tf_op jit(solution)/shard_map/psum | solution.py:108
  2105.9 382.6 %reduce-scatter.16.cloned.1.call-start = ((), (), s32[]{:S(2)}) async-start(), calls=%async_computation.22 | async-start | bytes 10485760 | tf_op jit(solution)/shard_map/reduce_scatter | solution.py:43
  2112.1 141.2 %copy-start.9 = (bf16[1024,2,256]{2,1,0:T(2,128)(2,1)S(1)}, bf16[1024,2,256]{2,1,0:T(2,128)(2,1)}, u32[]{:S(2)}) copy-start(bf16[1024,2,256]{2,1,0:T(2,128)(2,1)} %param.29) | copy-start | bytes 3145732
  2112.1 141.2 %copy-start.37 = (f32[256]{0:T(256)S(1)}, f32[256]{0:T(256)}, u32[]{:S(2)}) copy-start(f32[256]{0:T(256)} %param.41) | copy-start | bytes 3076
  2255.2 251.2 %copy-start.13 = (bf16[1024,2,256]{2,1,0:T(2,128)(2,1)S(1)}, bf16[1024,2,256]{2,1,0:T(2,128)(2,1)}, u32[]{:S(2)}) copy-start(bf16[1024,2,256]{2,1,0:T(2,128)(2,1)} %param.31) | copy-start | bytes 3145732
  2350.1 161.1 %copy-start.34 = (f32[256]{0:T(256)S(1)}, f32[256]{0:T(256)}, u32[]{:S(2)}) copy-start(f32[256]{0:T(256)} %get-tuple-element.949) | copy-start | bytes 3076
  2350.1 161.1 %copy-start.35 = (f32[256]{0:T(256)S(1)}, f32[256]{0:T(256)}, u32[]{:S(2)}) copy-start(f32[256]{0:T(256)} %get-tuple-element.957) | copy-start | bytes 3076
  2350.1 161.1 %copy-start.36 = (f32[1024]{0:T(1024)S(1)}, f32[1024]{0:T(1024)}, u32[]{:S(2)}) copy-start(f32[1024]{0:T(1024)} %get-tuple-element.1158) | copy-start | bytes 12292
  (25 other events, 129.3 us)
Sparse Core Ops, SparseCore 0:
  10.2 82.7 all-gather.10
  103.0 51.8 all-gather.14
  157.3 52.6 all-gather.12
  621.8 144.4 reduce-scatter.9
  769.5 81.5 all-gather.16
  852.5 8.9 all-gather.18
  863.1 11.7 all-gather.20
  877.0 81.4 all-gather.22
  980.4 142.3 reduce-scatter.13
  1144.9 82.6 all-gather.24
  1229.4 51.0 all-gather.26
  1282.8 52.6 all-gather.28
  1337.8 9.9 reduce-scatter.23
  1350.0 10.7 reduce-scatter.25
  1811.9 9.2 reduce-scatter.21
  2084.8 9.2 reduce-scatter.17
  2096.7 9.1 reduce-scatter.19
  2108.2 145.1 reduce-scatter.11
  2257.4 84.5 all-reduce.5
  2344.2 144.2 reduce-scatter.15
where the time goes:
time: 2550 us; the launch traced here: 2540 us
  waiting for transfers between devices  963 us (38%)
  matrix products  621 us (24%)
  local copies, waits for them, and re-layouts  447 us (18%)
  other arithmetic  367 us (14%)
  blocking collectives  94.1 us (4%)
  loops' own time  28.8 us (1%)
    reduce_scatter x4, waiting for transfers between devices, branch_sum(): lax.psum_scatter(partial_value, 'tp', scatter_dimension=2, tiled=True)  548 us
    all_gather x4, waiting for transfers between devices, full_rows(): return lax.all_gather(sliced, 'tp', axis=2, tiled=True)  304 us
    convert_element_type x32, local copies, waits for them, and re-layouts, block_weights(): jnp.where(itself, ROUNDS, jnp.where(earlier & same_doc, matches, 0))  173 us
    dot_general x32, matrix products, block_weights(): jnp.einsum('pshd,kshd->shpk', query_heads, key_heads, preferred_element_t...  155 us
    gt x32, other arithmetic, weights_of(): counts > 0  116 us
    reduce_sum x40, other arithmetic, block_weights(): jnp.sum((query_buck[:, :, :, None] == key_buck[:, :, None, :]).astype(jnp...  89.6 us
    psum x1, waiting for transfers between devices, over_context(): lax.psum(first_part.astype(jnp.bfloat16), 'ctx').astype(jnp.float32)  84.7 us
    dot_general x8, matrix products, advance(): jnp.einsum('shpk,kshd->pshd', score_grad, key_heads, preferred_element_ty...  80.4 us
  transfers between devices with their start and end apart: 20, of which 12 were waited for; matrix products, arithmetic and copies ran while one was open for 45% of the time, Pallas kernels for 0%

commit v1 on v0

--- a/solution.py
+++ b/solution.py
@@ -1,6 +1,8 @@
 import jax
 import jax.numpy as jnp
 from jax import lax
+from jax.experimental import pallas as pl
+from jax.experimental.pallas import tpu as pltpu
 from jax.sharding import PartitionSpec as P
 
 D = 1024
@@ -11,6 +13,257 @@
 SELF_SCORE = -10.0
 NEG_FILL = -1e30
 BLOCK_ROWS = 512
+
+
+BUCKETS = 64
+HEADS = 8
+SEQS = 4
+TILE = 256
+NT = (((1,), (1,)), ((), ()))
+NN = (((1,), (0,)), ((), ()))
+
+
+def dot(left, right, dims):
+    return lax.dot_general(left, right, dims, preferred_element_type=jnp.float32)
+
+
+def start_of(place, bounds_ref):
+    start = jnp.where(place >= bounds_ref[0], bounds_ref[0], 0)
+    start = jnp.where(place >= bounds_ref[1], bounds_ref[1], start)
+    return jnp.where(place >= bounds_ref[2], bounds_ref[2], start)
+
+
+def tile_masks(begin_row, bounds_ref):
+    query_lane = lax.broadcasted_iota(jnp.int32, (1, TILE), 1)
+    doc_start = start_of(query_lane + begin_row, bounds_ref)
+    first = start_of(begin_row, bounds_ref) // TILE
+    last_start = start_of(begin_row + TILE - 1, bounds_ref)
+    full = jnp.minimum((last_start + TILE - 1) // TILE, begin_row // TILE)
+    return doc_start, first, full
+
+
+def rows_at(ref, block):
+    return ref[pl.ds(pl.multiple_of(block * TILE, TILE), TILE), :]
+
+
+def norm_factor(q):
+    return lax.rsqrt(jnp.mean(q * q, -1, keepdims=True) + 1e-06)
+
+
+def attend_kernel(bounds_ref, q_ref, v_ref, hot_ref, out_ref, log_ref, key_sc, vt_sc):
+    block = pl.program_id(0)
+    blocks = pl.num_programs(0)
+
+    @pl.when(block == 0)
+    def _():
+        def prep(at, carry):
+            q = rows_at(q_ref, at).astype(jnp.float32)
+            begin = pl.multiple_of(at * TILE, TILE)
+            key_sc[pl.ds(begin, TILE), :] = (q * (norm_factor(q) * DH ** (-0.5))).astype(jnp.bfloat16)
+            v = rows_at(v_ref, at).astype(jnp.float32)
+            vt_sc[:, pl.ds(begin, TILE)] = v.T.astype(jnp.bfloat16)
+            return carry
+
+        lax.fori_loop(0, blocks, prep, 0)
+
+    begin_row = block * TILE
+    doc_start, first, full = tile_masks(begin_row, bounds_ref)
+    q = rows_at(q_ref, block)
+    hot = rows_at(hot_ref, block)
+    key_row = lax.broadcasted_iota(jnp.int32, (TILE, 1), 0)
+    lane = lax.broadcasted_iota(jnp.int32, (1, TILE), 1)
+
+    def scores(at):
+        return dot(rows_at(key_sc, at), q, NT), dot(rows_at(hot_ref, at), hot, NT)
+
+    def vt(at):
+        return vt_sc[:, pl.ds(pl.multiple_of(at * TILE, TILE), TILE)]
+
+    s, c = scores(block)
+    place = key_row + begin_row
+    c = jnp.where((key_row < lane) & (place >= doc_start), c, 0.0)
+    itself = key_row == lane
+    c = jnp.where(itself, float(ROUNDS), c)
+    s = jnp.where(itself, SELF_SCORE, s)
+    s = jnp.where(c > 0, s, NEG_FILL)
+    high = jnp.max(s, 0, keepdims=True)
+    p = c * jnp.exp(s - high)
+    total = jnp.sum(p, 0, keepdims=True)
+    acc = dot(vt(block), p.astype(jnp.bfloat16), NN)
+
+    def fold(at, carry, masked):
+        high, total, acc = carry
+        s, c = scores(at)
+        if masked:
+            c = jnp.where(key_row + at * TILE >= doc_start, c, 0.0)
+        s = jnp.where(c > 0, s, NEG_FILL)
+        new_high = jnp.maximum(high, jnp.max(s, 0, keepdims=True))
+        fade = jnp.exp(high - new_high)
+        p = c * jnp.exp(s - new_high)
+        total = total * fade + jnp.sum(p, 0, keepdims=True)
+        acc = acc * fade + dot(vt(at), p.astype(jnp.bfloat16), NN)
+        return new_high, total, acc
+
+    carry = lax.fori_loop(first, full, lambda at, x: fold(at, x, True), (high, total, acc))
+    high, total, acc = lax.fori_loop(full, block, lambda at, x: fold(at, x, False), carry)
+    out_ref[...] = acc / total
+    log_ref[pl.ds(block, 1), :] = high + jnp.log(total)
+
+
+def attend(bounds, q, v, hot):
+    rows = q.shape[0]
+    blocks = rows // TILE
+    whole = lambda shape: pl.BlockSpec(shape, lambda i, *_: (0,) * len(shape))
+    return pl.pallas_call(
+        attend_kernel,
+        name="attend",
+        out_shape=(
+            jax.ShapeDtypeStruct((DH, rows), jnp.float32),
+            jax.ShapeDtypeStruct((blocks, TILE), jnp.float32),
+        ),
+        grid_spec=pltpu.PrefetchScalarGridSpec(
+            num_scalar_prefetch=1,
+            grid=(blocks,),
+            in_specs=[whole((rows, DH)), whole((rows, DH)), whole((rows, ROUNDS * BUCKETS))],
+            out_specs=[pl.BlockSpec((DH, TILE), lambda i, *_: (0, i)), whole((blocks, TILE))],
+            scratch_shapes=[pltpu.VMEM((rows, DH), jnp.bfloat16), pltpu.VMEM((DH, rows), jnp.bfloat16)],
+        ),
+        compiler_params=pltpu.CompilerParams(
+            dimension_semantics=("arbitrary",), vmem_limit_bytes=40 * 2**20
+        ),
+        cost_estimate=pl.CostEstimate(
+            flops=rows * rows * 256, bytes_accessed=rows * DH * 20, transcendentals=rows * rows // 4
+        ),
+    )(bounds, q, v, hot)
+
+
+def attend_back_kernel(
+    bounds_ref, q_ref, v_ref, hot_ref, grad_ref, out_ref, log_ref,
+    q_grad_ref, v_grad_ref, key_sc, kt_sc, dk_sc, dv_sc, dq_sc,
+):
+    block = pl.program_id(0)
+    blocks = pl.num_programs(0)
+
+    @pl.when(block == 0)
+    def _():
+        def prep(at, carry):
+            begin = pl.multiple_of(at * TILE, TILE)
+            q = rows_at(q_ref, at).astype(jnp.float32)
+            k = q * (norm_factor(q) * DH ** (-0.5))
+            key_sc[pl.ds(begin, TILE), :] = k.astype(jnp.bfloat16)
+            kt_sc[:, pl.ds(begin, TILE)] = k.T.astype(jnp.bfloat16)
+            dk_sc[pl.ds(begin, TILE), :] = jnp.zeros((TILE, DH), jnp.float32)
+            dv_sc[pl.ds(begin, TILE), :] = jnp.zeros((TILE, DH), jnp.float32)
+            return carry
+
+        lax.fori_loop(0, blocks, prep, 0)
+
+    begin_row = block * TILE
+    doc_start, first, full = tile_masks(begin_row, bounds_ref)
+    q = rows_at(q_ref, block)
+    hot = rows_at(hot_ref, block)
+    grad = rows_at(grad_ref, block)
+    log_row = log_ref[pl.ds(block, 1), :]
+    delta = jnp.sum(grad.astype(jnp.float32).T * out_ref[...], 0, keepdims=True)
+    key_row = lax.broadcasted_iota(jnp.int32, (TILE, 1), 0)
+    lane = lax.broadcasted_iota(jnp.int32, (1, TILE), 1)
+
+    def fold(at, acc, masked, diagonal=False):
+        begin = pl.multiple_of(at * TILE, TILE)
+        s = dot(rows_at(key_sc, at), q, NT)
+        c = dot(rows_at(hot_ref, at), hot, NT)
+        up = dot(rows_at(v_ref, at), grad, NT)
+        if diagonal:
+            itself = key_row == lane
+            c = jnp.where((key_row < lane) & (key_row + begin_row >= doc_start), c, 0.0)
+            c = jnp.where(itself, float(ROUNDS), c)
+            s = jnp.where(itself, SELF_SCORE, s)
+        elif masked:
+            c = jnp.where(key_row + begin >= doc_start, c, 0.0)
+        s = jnp.where(c > 0, s, NEG_FILL)
+        w = c * jnp.exp(s - log_row)
+        ds = w * (up - delta)
+        if diagonal:
+            ds = jnp.where(itself, 0.0, ds)
+        w = w.astype(jnp.bfloat16)
+        ds = ds.astype(jnp.bfloat16)
+        dv_sc[pl.ds(begin, TILE), :] += dot(w, grad, NN)
+        dk_sc[pl.ds(begin, TILE), :] += dot(ds, q, NN)
+        return acc + dot(kt_sc[:, pl.ds(begin, TILE)], ds, NN)
+
+    acc = fold(block, jnp.zeros((DH, TILE), jnp.float32), True, True)
+    acc = lax.fori_loop(first, full, lambda at, x: fold(at, x, True), acc)
+    acc = lax.fori_loop(full, block, lambda at, x: fold(at, x, False), acc)
+    dq_sc[pl.ds(pl.multiple_of(begin_row, TILE), TILE), :] = acc.T
+
+    @pl.when(block == blocks - 1)
+    def _():
+        def finish(at, carry):
+            begin = pl.multiple_of(at * TILE, TILE)
+            q = rows_at(q_ref, at).astype(jnp.float32)
+            r = norm_factor(q)
+            g = rows_at(dk_sc, at).astype(jnp.bfloat16).astype(jnp.float32)
+            back = (r * DH ** (-0.5)) * (g - q * (r * r * jnp.mean(q * g, -1, keepdims=True)))
+            q_grad_ref[pl.ds(begin, TILE), :] = (rows_at(dq_sc, at) + back).astype(jnp.bfloat16)
+            v_grad_ref[pl.ds(begin, TILE), :] = rows_at(dv_sc, at).astype(jnp.bfloat16)
+            return carry
+
+        lax.fori_loop(0, blocks, finish, 0)
+
+
+def attend_back(bounds, q, v, hot, grad, out, logs):
+    rows = q.shape[0]
+    blocks = rows // TILE
+    whole = lambda shape: pl.BlockSpec(shape, lambda i, *_: (0,) * len(shape))
+    return pl.pallas_call(
+        attend_back_kernel,
+        name="attend_back",
+        out_shape=(jax.ShapeDtypeStruct((rows, DH), jnp.bfloat16),) * 2,
+        grid_spec=pltpu.PrefetchScalarGridSpec(
+            num_scalar_prefetch=1,
+            grid=(blocks,),
+            in_specs=[
+                whole((rows, DH)), whole((rows, DH)), whole((rows, ROUNDS * BUCKETS)), whole((rows, DH)),
+                pl.BlockSpec((DH, TILE), lambda i, *_: (0, i)), whole((blocks, TILE)),
+            ],
+            out_specs=[whole((rows, DH))] * 2,
+            scratch_shapes=[
+                pltpu.VMEM((rows, DH), jnp.bfloat16),
+                pltpu.VMEM((DH, rows), jnp.bfloat16),
+                pltpu.VMEM((rows, DH), jnp.float32),
+                pltpu.VMEM((rows, DH), jnp.float32),
+                pltpu.VMEM((rows, DH), jnp.float32),
+            ],
+        ),
+        compiler_params=pltpu.CompilerParams(
+            dimension_semantics=("arbitrary",), vmem_limit_bytes=48 * 2**20
+        ),
+        cost_estimate=pl.CostEstimate(
+            flops=rows * rows * 640, bytes_accessed=rows * DH * 30, transcendentals=rows * rows // 4
+        ),
+    )(bounds, q, v, hot, grad, out, logs)
+
+
+def place_matrix(places):
+    rows = places.shape[0]
+    return (jnp.arange(rows, dtype=jnp.int32)[:, None] == places[None, :]).astype(jnp.bfloat16)
+
+
+def into_places(places, vectors):
+    return jnp.einsum("pa,ad->pd", place_matrix(places), vectors, preferred_element_type=jnp.float32).astype(jnp.bfloat16)
+
+
+def out_of_places(places, vectors):
+    return jnp.einsum("pa,pd->ad", place_matrix(places), vectors, preferred_element_type=jnp.float32).astype(jnp.bfloat16)
+
+
+def bucket_hot(buckets):
+    hot = buckets.T[:, :, None] == jnp.arange(BUCKETS, dtype=jnp.int32)
+    return hot.astype(jnp.bfloat16).reshape(buckets.shape[1], ROUNDS * BUCKETS)
+
+
+def doc_bounds(segments):
+    return jnp.sum((segments[None, :] < jnp.arange(1, 4, dtype=jnp.int32)[:, None]).astype(jnp.int32), 1)
 
 
 def smooth_unit(values_in):
@@ -136,6 +389,302 @@
             second_part.astype(jnp.bfloat16), "shard", scatter_dimension=1, tiled=True
         ).astype(jnp.float32),
     )
+
+
+def general_device(
+    first_half,
+    second_half,
+    first_cotangent,
+    second_cotangent,
+    segment_ids,
+    bucket_ids,
+    positions,
+    query_weight,
+    value_weight,
+    output_weight,
+    expand_weight,
+    expand_bias,
+    shrink_weight,
+    shrink_bias,
+    attention_gain,
+    attention_shift,
+    forward_gain,
+    forward_shift,
+):
+    rows_here, seqs_here, slice_width = first_half.shape
+    width_heads = query_weight.shape[1]
+    heads_here = width_heads // DH
+    tp_start = lax.axis_index("tp") * slice_width
+    ctx_start = lax.axis_index("ctx") * rows_here
+    bf16 = jnp.bfloat16
+    f32 = jnp.float32
+
+    def columns(wide):
+        return lax.dynamic_slice_in_dim(wide, tp_start, slice_width, wide.ndim - 1)
+
+    full_query, full_value, full_expand = (
+        lax.all_gather(query_weight, "shard", axis=0, tiled=True),
+        lax.all_gather(value_weight, "shard", axis=0, tiled=True),
+        lax.all_gather(expand_weight, "shard", axis=0, tiled=True),
+    )
+    full_output, full_shrink = (
+        lax.all_gather(output_weight, "shard", axis=1, tiled=True),
+        lax.all_gather(shrink_weight, "shard", axis=1, tiled=True),
+    )
+    all_labels = (
+        lax.all_gather(segment_ids, "ctx", axis=1, tiled=True),
+        lax.all_gather(bucket_ids, "ctx", axis=2, tiled=True),
+        lax.all_gather(positions, "ctx", axis=1, tiled=True),
+    )
+    local_labels = label_rows(all_labels, ctx_start, rows_here)
+    second_wide = full_rows(second_half)
+    normed, attn_scaled, attn_inverse = norm_rows(
+        second_wide.astype(f32), attention_gain, attention_shift
+    )
+    normed = normed.astype(bf16)
+    queries = jnp.einsum("psd,de->pse", normed, full_query, preferred_element_type=f32).astype(bf16)
+    key_vectors = unit_keys(queries.astype(f32)).astype(bf16)
+    value_vectors = jnp.einsum(
+        "psd,de->pse", normed, full_value, preferred_element_type=f32
+    ).astype(bf16)
+    query_heads = heads_view(queries)
+    stat_shape = (seqs_here, heads_here, rows_here)
+    head_zero = jnp.zeros((rows_here, seqs_here, heads_here, DH), f32)
+
+    def norm_fold(running, pieces, begin_row):
+        key_piece = pieces[0]
+
+        def advance(state_now, offset, extent):
+            highest, summed = state_now
+            key_heads = heads_view(lax.dynamic_slice_in_dim(key_piece, offset, extent, 0))
+            shifted, counts, _ = block_weights(
+                query_heads, local_labels, key_heads, label_rows(all_labels, offset, extent)
+            )
+            usable = counts > 0
+            new_high = jnp.maximum(highest, jnp.max(jnp.where(usable, shifted, NEG_FILL), -1))
+            summed = summed * jnp.exp(highest - new_high) + jnp.sum(
+                jnp.where(usable, counts * jnp.exp(shifted - new_high[..., None]), 0.0), -1
+            )
+            return (new_high, summed)
+
+        return blockwise(advance, running, key_piece.shape[0])
+
+    highest, summed = over_keys(
+        key_vectors,
+        value_vectors,
+        norm_fold,
+        (jnp.full(stat_shape, NEG_FILL, f32), jnp.zeros(stat_shape, f32)),
+    )
+    log_total = highest + jnp.log(summed)
+
+    def key_block(pieces, offset, extent):
+        key_heads = heads_view(lax.dynamic_slice_in_dim(pieces[0], offset, extent, 0))
+        value_heads = heads_view(lax.dynamic_slice_in_dim(pieces[1], offset, extent, 0))
+        shifted, counts, itself = block_weights(
+            query_heads, local_labels, key_heads, label_rows(all_labels, offset, extent)
+        )
+        return (key_heads, value_heads, weights_of(shifted, counts, log_total), itself)
+
+    def mix_fold(running, pieces, begin_row):
+
+        def advance(state_now, offset, extent):
+            key_heads, value_heads, weights, itself = key_block(pieces, offset, extent)
+            return state_now + jnp.einsum(
+                "shpk,kshd->pshd", weights.astype(bf16), value_heads, preferred_element_type=f32
+            )
+
+        return blockwise(advance, running, pieces[0].shape[0])
+
+    head_mix = over_keys(key_vectors, value_vectors, mix_fold, head_zero)
+    attention = head_mix.reshape(rows_here, seqs_here, width_heads).astype(bf16)
+    branch = branch_sum(
+        jnp.einsum("pse,ed->psd", attention, full_output, preferred_element_type=f32)
+    )
+    first_out = (first_half.astype(f32) + branch).astype(bf16)
+    first_wide = full_rows(first_out)
+    ffn_in, ffn_scaled, ffn_inverse = norm_rows(first_wide.astype(f32), forward_gain, forward_shift)
+    ffn_in = ffn_in.astype(bf16)
+    pre_act = (
+        jnp.einsum("psd,df->psf", ffn_in, full_expand, preferred_element_type=f32) + expand_bias
+    )
+    hidden_exact, unit_pull = jax.vjp(smooth_unit, pre_act)
+    hidden = hidden_exact.astype(bf16)
+    second_branch = (
+        branch_sum(jnp.einsum("psf,fd->psd", hidden, full_shrink, preferred_element_type=f32))
+        + shrink_bias
+    )
+    second_out = (second_half.astype(f32) + second_branch).astype(bf16)
+    cotangent_wide = full_rows(second_cotangent)
+    hidden_grad = jnp.einsum("psd,fd->psf", cotangent_wide, full_shrink, preferred_element_type=f32)
+    pre_grad = unit_pull(hidden_grad)[0].astype(bf16)
+    shrink_grad = jnp.einsum("psf,psd->fd", hidden, cotangent_wide, preferred_element_type=f32)
+    shrink_bias_grad = jnp.sum(second_cotangent.astype(f32), (0, 1))
+    expand_grad = jnp.einsum("psd,psf->df", ffn_in, pre_grad, preferred_element_type=f32)
+    expand_bias_grad = jnp.sum(pre_grad.astype(f32), (0, 1))
+    ffn_grad = branch_sum(
+        jnp.einsum("psf,df->psd", pre_grad, full_expand, preferred_element_type=f32)
+    )
+    ffn_back, forward_gain_grad, forward_shift_grad = norm_back(
+        ffn_grad, columns(ffn_scaled), ffn_inverse, columns(forward_gain)
+    )
+    first_grad = (first_cotangent.astype(f32) + ffn_back).astype(bf16)
+    grad_wide = full_rows(first_grad)
+    output_grad = jnp.einsum("pse,psd->ed", attention, grad_wide, preferred_element_type=f32)
+    attention_grad = jnp.einsum(
+        "psd,ed->pse", grad_wide, full_output, preferred_element_type=f32
+    ).astype(bf16)
+    grad_heads = heads_view(attention_grad)
+
+    def delta_fold(running, pieces, begin_row):
+
+        def advance(state_now, offset, extent):
+            key_heads, value_heads, weights, itself = key_block(pieces, offset, extent)
+            upstream = jnp.einsum(
+                "pshd,kshd->shpk", grad_heads, value_heads, preferred_element_type=f32
+            )
+            return state_now + jnp.sum(weights * upstream, -1)
+
+        return blockwise(advance, running, pieces[0].shape[0])
+
+    row_delta = over_keys(key_vectors, value_vectors, delta_fold, jnp.zeros(stat_shape, f32))
+
+    def query_fold(running, pieces, begin_row):
+
+        def advance(state_now, offset, extent):
+            key_heads, value_heads, weights, itself = key_block(pieces, offset, extent)
+            upstream = jnp.einsum(
+                "pshd,kshd->shpk", grad_heads, value_heads, preferred_element_type=f32
+            )
+            score_grad = jnp.where(itself, 0.0, weights * (upstream - row_delta[..., None])).astype(
+                bf16
+            )
+            return state_now + jnp.einsum(
+                "shpk,kshd->pshd", score_grad, key_heads, preferred_element_type=f32
+            )
+
+        return blockwise(advance, running, pieces[0].shape[0])
+
+    query_part = over_keys(key_vectors, value_vectors, query_fold, head_zero)
+    query_lse, query_delta = (
+        lax.all_gather(log_total, "ctx", axis=2, tiled=True),
+        lax.all_gather(row_delta, "ctx", axis=2, tiled=True),
+    )
+    local_keys = heads_view(key_vectors)
+    local_values = heads_view(value_vectors)
+    query_piece = lax.all_gather(queries, "ctx", axis=0, tiled=True)
+    grad_piece = lax.all_gather(attention_grad, "ctx", axis=0, tiled=True)
+
+    def advance(state_now, offset, extent):
+        remote_queries = heads_view(lax.dynamic_slice_in_dim(query_piece, offset, extent, 0))
+        remote_grads = heads_view(lax.dynamic_slice_in_dim(grad_piece, offset, extent, 0))
+        lse_rows = lax.dynamic_slice_in_dim(query_lse, offset, extent, 2)
+        delta_rows = lax.dynamic_slice_in_dim(query_delta, offset, extent, 2)
+        shifted, counts, itself = block_weights(
+            remote_queries, label_rows(all_labels, offset, extent), local_keys, local_labels
+        )
+        weights = weights_of(shifted, counts, lse_rows)
+        upstream = jnp.einsum(
+            "pshd,kshd->shpk", remote_grads, local_values, preferred_element_type=f32
+        )
+        score_grad = jnp.where(itself, 0.0, weights * (upstream - delta_rows[..., None])).astype(
+            bf16
+        )
+        key_now = state_now[0] + jnp.einsum(
+            "shpk,pshd->kshd", score_grad, remote_queries, preferred_element_type=f32
+        )
+        value_now = state_now[1] + jnp.einsum(
+            "shpk,pshd->kshd", weights.astype(bf16), remote_grads, preferred_element_type=f32
+        )
+        return (key_now, value_now)
+
+    key_part, value_part = blockwise(advance, (head_zero, head_zero), query_piece.shape[0])
+    keys_grad = key_part.reshape(rows_here, seqs_here, width_heads).astype(bf16)
+    values_grad = value_part.reshape(rows_here, seqs_here, width_heads).astype(bf16)
+    unit_back = jax.vjp(unit_keys, queries.astype(f32))[1]
+    queries_total = (
+        query_part.reshape(rows_here, seqs_here, width_heads) + unit_back(keys_grad.astype(f32))[0]
+    ).astype(bf16)
+    query_grad = jnp.einsum("psd,pse->de", normed, queries_total, preferred_element_type=f32)
+    value_grad = jnp.einsum("psd,pse->de", normed, values_grad, preferred_element_type=f32)
+    normed_grad = branch_sum(
+        jnp.einsum("pse,de->psd", queries_total, full_query, preferred_element_type=f32)
+        + jnp.einsum("pse,de->psd", values_grad, full_value, preferred_element_type=f32)
+    )
+    attn_back, attention_gain_grad, attention_shift_grad = norm_back(
+        normed_grad, columns(attn_scaled), attn_inverse, columns(attention_gain)
+    )
+    second_grad = (second_cotangent.astype(f32) + attn_back).astype(bf16)
+    expand_bias_sum, shrink_bias_sum, attn_gain_sum, attn_shift_sum, ffn_gain_sum, ffn_shift_sum = (
+        lax.psum(
+            (
+                expand_bias_grad,
+                shrink_bias_grad,
+                attention_gain_grad,
+                attention_shift_grad,
+                forward_gain_grad,
+                forward_shift_grad,
+            ),
+            ("shard", "ctx"),
+        )
+    )
+    query_sum, value_sum, expand_sum, output_sum, shrink_sum = over_context(
+        query_grad, value_grad, expand_grad, output_grad, shrink_grad
+    )
+    query_own, value_own, expand_own = to_row_owners(query_sum, value_sum, expand_sum)
+    output_own, shrink_own = to_col_owners(output_sum, shrink_sum)
+    return (
+        first_out,
+        second_out,
+        first_grad,
+        second_grad,
+        query_own,
+        value_own,
+        output_own,
+        expand_own,
+        expand_bias_sum,
+        shrink_own,
+        shrink_bias_sum,
+        attn_gain_sum,
+        attn_shift_sum,
+        ffn_gain_sum,
+        ffn_shift_sum,
+    )
+
+
+def branch_sum_low(partial_value):
+    summed = lax.psum_scatter(
+        partial_value.astype(jnp.bfloat16), "tp", scatter_dimension=2, tiled=True
+    )
+    return summed.astype(jnp.float32)
+
+
+def sequence_labels(segment_ids, bucket_ids, positions, heads_here):
+    seqs_here, rows_here = positions.shape
+    packed = jnp.concatenate([positions[:, None], segment_ids[:, None], bucket_ids], 1)
+    gathered = lax.all_gather(packed, "ctx", axis=2, tiled=True)
+    mine = lax.dynamic_index_in_dim(gathered, lax.axis_index("ctx") // heads_here, 0, False)
+    places = mine[0]
+    return places, doc_bounds(mine[1]), into_places(places, bucket_hot(mine[2:]))
+
+
+def to_heads(vectors):
+    rows_here, seqs_here, width = vectors[0].shape
+    heads = width // DH
+    stacked = jnp.concatenate(
+        [item.reshape(rows_here, seqs_here * heads, 1, DH) for item in vectors], 2
+    )
+    sent = stacked.transpose(1, 0, 2, 3).reshape(seqs_here * heads, rows_here, -1)
+    landed = lax.all_to_all(sent, "ctx", split_axis=0, concat_axis=0, tiled=True)
+    return landed.reshape(-1, landed.shape[2])
+
+
+def from_heads(vectors, seqs_here, count):
+    pairs = lax.axis_size("ctx")
+    sent = vectors.reshape(pairs, vectors.shape[0] // pairs, vectors.shape[1])
+    landed = lax.all_to_all(sent, "ctx", split_axis=0, concat_axis=0, tiled=True)
+    shaped = landed.reshape(seqs_here, pairs // seqs_here, -1, count, DH).transpose(2, 0, 1, 3, 4)
+    rows_here = shaped.shape[0]
+    return tuple(shaped[:, :, :, at].reshape(rows_here, seqs_here, -1) for at in range(count))
 
 
 def per_device(
@@ -178,73 +727,21 @@
         lax.all_gather(output_weight, "shard", axis=1, tiled=True),
         lax.all_gather(shrink_weight, "shard", axis=1, tiled=True),
     )
-    all_labels = (
-        lax.all_gather(segment_ids, "ctx", axis=1, tiled=True),
-        lax.all_gather(bucket_ids, "ctx", axis=2, tiled=True),
-        lax.all_gather(positions, "ctx", axis=1, tiled=True),
-    )
-    local_labels = label_rows(all_labels, ctx_start, rows_here)
+    places, bounds, hot = sequence_labels(segment_ids, bucket_ids, positions, heads_here)
     second_wide = full_rows(second_half)
     normed, attn_scaled, attn_inverse = norm_rows(
         second_wide.astype(f32), attention_gain, attention_shift
     )
     normed = normed.astype(bf16)
     queries = jnp.einsum("psd,de->pse", normed, full_query, preferred_element_type=f32).astype(bf16)
-    key_vectors = unit_keys(queries.astype(f32)).astype(bf16)
     value_vectors = jnp.einsum(
         "psd,de->pse", normed, full_value, preferred_element_type=f32
     ).astype(bf16)
-    query_heads = heads_view(queries)
-    stat_shape = (seqs_here, heads_here, rows_here)
-    head_zero = jnp.zeros((rows_here, seqs_here, heads_here, DH), f32)
-
-    def norm_fold(running, pieces, begin_row):
-        key_piece = pieces[0]
-
-        def advance(state_now, offset, extent):
-            highest, summed = state_now
-            key_heads = heads_view(lax.dynamic_slice_in_dim(key_piece, offset, extent, 0))
-            shifted, counts, _ = block_weights(
-                query_heads, local_labels, key_heads, label_rows(all_labels, offset, extent)
-            )
-            usable = counts > 0
-            new_high = jnp.maximum(highest, jnp.max(jnp.where(usable, shifted, NEG_FILL), -1))
-            summed = summed * jnp.exp(highest - new_high) + jnp.sum(
-                jnp.where(usable, counts * jnp.exp(shifted - new_high[..., None]), 0.0), -1
-            )
-            return (new_high, summed)
-
-        return blockwise(advance, running, key_piece.shape[0])
-
-    highest, summed = over_keys(
-        key_vectors,
-        value_vectors,
-        norm_fold,
-        (jnp.full(stat_shape, NEG_FILL, f32), jnp.zeros(stat_shape, f32)),
-    )
-    log_total = highest + jnp.log(summed)
-
-    def key_block(pieces, offset, extent):
-        key_heads = heads_view(lax.dynamic_slice_in_dim(pieces[0], offset, extent, 0))
-        value_heads = heads_view(lax.dynamic_slice_in_dim(pieces[1], offset, extent, 0))
-        shifted, counts, itself = block_weights(
-            query_heads, local_labels, key_heads, label_rows(all_labels, offset, extent)
-        )
-        return (key_heads, value_heads, weights_of(shifted, counts, log_total), itself)
-
-    def mix_fold(running, pieces, begin_row):
-
-        def advance(state_now, offset, extent):
-            key_heads, value_heads, weights, itself = key_block(pieces, offset, extent)
-            return state_now + jnp.einsum(
-                "shpk,kshd->pshd", weights.astype(bf16), value_heads, preferred_element_type=f32
-            )
-
-        return blockwise(advance, running, pieces[0].shape[0])
-
-    head_mix = over_keys(key_vectors, value_vectors, mix_fold, head_zero)
-    attention = head_mix.reshape(rows_here, seqs_here, width_heads).astype(bf16)
-    branch = branch_sum(
+    sorted_pair = into_places(places, to_heads((queries, value_vectors)))
+    query_sorted, value_sorted = sorted_pair[:, :DH], sorted_pair[:, DH:]
+    mix, logs = attend(bounds, query_sorted, value_sorted, hot)
+    (attention,) = from_heads(out_of_places(places, mix.T.astype(bf16)), seqs_here, 1)
+    branch = branch_sum_low(
         jnp.einsum("pse,ed->psd", attention, full_output, preferred_element_type=f32)
     )
     first_out = (first_half.astype(f32) + branch).astype(bf16)
@@ -257,7 +754,7 @@
     hidden_exact, unit_pull = jax.vjp(smooth_unit, pre_act)
     hidden = hidden_exact.astype(bf16)
     second_branch = (
-        branch_sum(jnp.einsum("psf,fd->psd", hidden, full_shrink, preferred_element_type=f32))
+        branch_sum_low(jnp.einsum("psf,fd->psd", hidden, full_shrink, preferred_element_type=f32))
         + shrink_bias
     )
     second_out = (second_half.astype(f32) + second_branch).astype(bf16)
@@ -268,7 +765,7 @@
     shrink_bias_grad = jnp.sum(second_cotangent.astype(f32), (0, 1))
     expand_grad = jnp.einsum("psd,psf->df", ffn_in, pre_grad, preferred_element_type=f32)
     expand_bias_grad = jnp.sum(pre_grad.astype(f32), (0, 1))
-    ffn_grad = branch_sum(
+    ffn_grad = branch_sum_low(
         jnp.einsum("psf,df->psd", pre_grad, full_expand, preferred_element_type=f32)
     )
     ffn_back, forward_gain_grad, forward_shift_grad = norm_back(
@@ -280,80 +777,14 @@
     attention_grad = jnp.einsum(
         "psd,ed->pse", grad_wide, full_output, preferred_element_type=f32
     ).astype(bf16)
-    grad_heads = heads_view(attention_grad)
-
-    def delta_fold(running, pieces, begin_row):
-
-        def advance(state_now, offset, extent):
-            key_heads, value_heads, weights, itself = key_block(pieces, offset, extent)
-            upstream = jnp.einsum(
-                "pshd,kshd->shpk", grad_heads, value_heads, preferred_element_type=f32
-            )
-            return state_now + jnp.sum(weights * upstream, -1)
-
-        return blockwise(advance, running, pieces[0].shape[0])
-
-    row_delta = over_keys(key_vectors, value_vectors, delta_fold, jnp.zeros(stat_shape, f32))
-
-    def query_fold(running, pieces, begin_row):
-
-        def advance(state_now, offset, extent):
-            key_heads, value_heads, weights, itself = key_block(pieces, offset, extent)
-            upstream = jnp.einsum(
-                "pshd,kshd->shpk", grad_heads, value_heads, preferred_element_type=f32
-            )
-            score_grad = jnp.where(itself, 0.0, weights * (upstream - row_delta[..., None])).astype(
-                bf16
-            )
-            return state_now + jnp.einsum(
-                "shpk,kshd->pshd", score_grad, key_heads, preferred_element_type=f32
-            )
-
-        return blockwise(advance, running, pieces[0].shape[0])
-
-    query_part = over_keys(key_vectors, value_vectors, query_fold, head_zero)
-    query_lse, query_delta = (
-        lax.all_gather(log_total, "ctx", axis=2, tiled=True),
-        lax.all_gather(row_delta, "ctx", axis=2, tiled=True),
-    )
-    local_keys = heads_view(key_vectors)
-    local_values = heads_view(value_vectors)
-    query_piece = lax.all_gather(queries, "ctx", axis=0, tiled=True)
-    grad_piece = lax.all_gather(attention_grad, "ctx", axis=0, tiled=True)
-
-    def advance(state_now, offset, extent):
-        remote_queries = heads_view(lax.dynamic_slice_in_dim(query_piece, offset, extent, 0))
-        remote_grads = heads_view(lax.dynamic_slice_in_dim(grad_piece, offset, extent, 0))
-        lse_rows = lax.dynamic_slice_in_dim(query_lse, offset, extent, 2)
-        delta_rows = lax.dynamic_slice_in_dim(query_delta, offset, extent, 2)
-        shifted, counts, itself = block_weights(
-            remote_queries, label_rows(all_labels, offset, extent), local_keys, local_labels
-        )
-        weights = weights_of(shifted, counts, lse_rows)
-        upstream = jnp.einsum(
-            "pshd,kshd->shpk", remote_grads, local_values, preferred_element_type=f32
-        )
-        score_grad = jnp.where(itself, 0.0, weights * (upstream - delta_rows[..., None])).astype(
-            bf16
-        )
-        key_now = state_now[0] + jnp.einsum(
-            "shpk,pshd->kshd", score_grad, remote_queries, preferred_element_type=f32
-        )
-        value_now = state_now[1] + jnp.einsum(
-            "shpk,pshd->kshd", weights.astype(bf16), remote_grads, preferred_element_type=f32
-        )
-        return (key_now, value_now)
-
-    key_part, value_part = blockwise(advance, (head_zero, head_zero), query_piece.shape[0])
-    keys_grad = key_part.reshape(rows_here, seqs_here, width_heads).astype(bf16)
-    values_grad = value_part.reshape(rows_here, seqs_here, width_heads).astype(bf16)
-    unit_back = jax.vjp(unit_keys, queries.astype(f32))[1]
-    queries_total = (
-        query_part.reshape(rows_here, seqs_here, width_heads) + unit_back(keys_grad.astype(f32))[0]
-    ).astype(bf16)
+    grad_sorted = into_places(places, to_heads((attention_grad,)))
+    parts = attend_back(bounds, query_sorted, value_sorted, hot, grad_sorted, mix, logs)
+    queries_total, values_grad = from_heads(
+        out_of_places(places, jnp.concatenate(parts, 1)), seqs_here, 2
+    )
     query_grad = jnp.einsum("psd,pse->de", normed, queries_total, preferred_element_type=f32)
     value_grad = jnp.einsum("psd,pse->de", normed, values_grad, preferred_element_type=f32)
-    normed_grad = branch_sum(
+    normed_grad = branch_sum_low(
         jnp.einsum("pse,de->psd", queries_total, full_query, preferred_element_type=f32)
         + jnp.einsum("pse,de->psd", values_grad, full_value, preferred_element_type=f32)
     )
@@ -398,9 +829,15 @@
     )
 
 
+def paired(mesh):
+    heads_here = HEADS // mesh.shape["tp"]
+    seqs_here = SEQS // mesh.shape["shard"]
+    return mesh.shape["ctx"] == heads_here * seqs_here
+
+
 def solution(mesh):
     return jax.shard_map(
-        per_device,
+        per_device if paired(mesh) else general_device,
         mesh=mesh,
         in_specs=(
             P("ctx", "shard", "tp"),

time: 2550 us -> 1140 us (0.45)
  matrix products: 621 us -> 161 us
  local copies, waits for them, and re-layouts: 447 us -> 39.8 us
  other arithmetic: 367 us -> 73.7 us
  waiting for transfers between devices: 963 us -> 690 us
  Pallas kernels: 0 us -> 74.9 us
  loops' own time: 28.8 us -> 0 us
  blocking collectives: 94.1 us -> 66.1 us
    dot_general x72 -> x5, matrix products: 523 us -> 70.6 us  [the longest x3 41.3 us: into_places(): jnp.einsum('pa,ad->pd', place_matrix(places), vectors, preferred_element_...]
    reduce_scatter x4, waiting for transfers between devices: 548 us -> 277 us  [branch_sum_low(): lax.psum_scatter(partial_value.astype(jnp.bfloat16), 'tp', scatter_dimens...]
    convert_element_type x32 -> x0, local copies, waits for them, and re-layouts: 173 us -> none  [block_weights(): jnp.where(itself, ROUNDS, jnp.where(earlier & same_doc, matches, 0))]
    gt x40 -> x0, other arithmetic: 146 us -> none  [the longest x32 116 us: weights_of(): counts > 0]
    reduce_sum x49 -> x1, other arithmetic: 139 us -> 0.21 us  [doc_bounds(): jnp.sum((segments[None, :] < jnp.arange(1, 4, dtype=jnp.int32)[:, None])....]
    dynamic_slice x171 -> x0, local copies, waits for them, and re-layouts: 99.6 us -> none  [the longest x16 33.1 us: key_block(): lax.dynamic_slice_in_dim(pieces[1], offset, extent, 0)]
    gt x32 -> x0, local copies, waits for them, and re-layouts: 77.7 us -> none  [the longest x24 53 us: weights_of(): counts > 0]
    pallas_call x0 -> x2, Pallas kernels: none -> 74.9 us  [the longest x1 39.1 us: attend_back(): pl.pallas_call(attend_back_kernel, name='attend_back', out_shape=(jax.Sha...]
  transfers between devices with their start and end apart: 20 -> 20, of which waited for: 12 -> 15; matrix products, arithmetic and copies ran while one was open for 45% -> 16% of each run, Pallas kernels for 0% -> 3%
where the time goes in v1:
time: 1140 us
  waiting for transfers between devices  690 us (61%)
  matrix products  161 us (14%)
  Pallas kernels  74.9 us (7%)
  other arithmetic  73.7 us (6%)
  blocking collectives  66.1 us (6%)
  local copies, waits for them, and re-layouts  39.8 us (3%)
  starting transfers between devices  16.5 us (1%)
  between operations  15 us (1%)
    reduce_scatter x4, waiting for transfers between devices, branch_sum_low(): lax.psum_scatter(partial_value.astype(jnp.bfloat16), 'tp', scatter_dimens...  277 us
    all_gather x4, waiting for transfers between devices, full_rows(): return lax.all_gather(sliced, 'tp', axis=2, tiled=True)  277 us
    psum x1, waiting for transfers between devices, over_context(): lax.psum(first_part.astype(jnp.bfloat16), 'ctx').astype(jnp.float32)  84.1 us
    dot_general x3, matrix products, into_places(): jnp.einsum('pa,ad->pd', place_matrix(places), vectors, preferred_element_...  41.3 us
    pallas_call x1, Pallas kernels, attend_back(): pl.pallas_call(attend_back_kernel, name='attend_back', out_shape=(jax.Sha...  39.1 us
    pallas_call x1, Pallas kernels, attend(): pl.pallas_call(attend_kernel, name='attend', out_shape=(jax.ShapeDtypeStr...  35.9 us
    all_to_all x2, waiting for transfers between devices, from_heads(): lax.all_to_all(sent, 'ctx', split_axis=0, concat_axis=0, tiled=True)  30 us
    dot_general x2, matrix products, out_of_places(): jnp.einsum('pa,pd->ad', place_matrix(places), vectors, preferred_element_...  29.3 us
  transfers between devices with their start and end apart: 20, of which 15 were waited for; matrix products, arithmetic and copies ran while one was open for 16% of the time, Pallas kernels for 3%

profile of v1, /device:TPU:1, one launch (start us, length us, event | category | flops | bytes accessed | tf_op | source)
XLA Modules:
  0.0 1137.4 jit_solution(2789752990713665072)
XLA Ops:
  14.1 7.8 all_gather.30
  22.9 4.5 all_gather.33
  29.5 63.5 %all-gather.7.cloned.1.call-done = bf16[1024,2,1024]{2,0,1:T(8,128)(2,1)} async-done(((bf16[1024,2,256]{2,0,1:T(8,128)(2,1)}), bf16[1024,2,1024]{2,0,1:T(8,128)(2,1)}) %all-gather.7.cloned.1.call-update) | async-done | bytes 4194320 | tf_op jit(solution)/shard_map/all_gather | solution.py:292
  105.4 3.8 all-to-all-start
  109.2 14.3 %fusion.25.hot_ref = bf16[4096,256]{1,0:T(8,128)(2,1)} fusion(pred[4096,256]{0,1:T(32,128)(4,1)S(1)} %bitcast_compare_fusion, s32[4096]{0:T(1024)S(1)} %bitcast.132), kind=kOutput, calls=%fused_computation.48 | convolution fusion | flops 8607760384 | bytes 3162112 | tf_op jit(solution)/shard_map/pa,ad->pd/dot_general | solution.py:253
  123.5 10.1 all-to-all-done
  136.1 13.9 %fusion.24 = bf16[4096,256]{1,0:T(8,128)(2,1)S(1)} fusion(bf16[4096,256]{1,0:T(8,128)(2,1)} %bitcast.122, s32[4096]{0:T(1024)S(1)} %bitcast.133), kind=kOutput, calls=%fused_computation.47 | convolution fusion | flops 8607760384 | bytes 4210688 | tf_op jit(solution)/shard_map/pa,ad->pd/dot_general | solution.py:253
  150.2 35.9 %attend.1 = (f32[128,4096]{1,0:T(8,128)S(1)}, f32[16,256]{1,0:T(8,128)S(1)}) custom-call(s32[3]{0:T(128)S(1)} %convert_reduce_fusion.6.bounds_ref, bf16[4096,128]{1,0:T(8,128)(2,1)S(1)} %get-tuple-element.113.q_ref, bf16[4096,128]{1,0:T(8,128)(2,1)S(1)} %get-tuple-element.112.v_ref, bf16[4096,256]{1,0:T(8,128)(2,1)S(1)} %copy-done), custom_call_target="tpu_custom_call" | custom-call | flops 4294967296 | bytes 10485760 | tf_op jit(solution)/shard_map/attend/pallas_call | solution.py:117
  186.1 10.3 fusion.27
  196.4 3.5 all-to-all-start.1
  202.9 10.1 all-to-all-done.1
  216.9 4.2 convolution_convert_fusion.2
  221.3 74.9 %reduce-scatter.10.cloned.1.call-done = bf16[1024,2,256]{2,0,1:T(8,128)(2,1)} async-done(((bf16[1024,2,1024]{2,0,1:T(8,128)(2,1)}), bf16[1024,2,256]{2,0,1:T(8,128)(2,1)}) %reduce-scatter.10.cloned.1.call-update) | async-done | bytes 1048592 | tf_op jit(solution)/shard_map/reduce_scatter | solution.py:655
  302.6 77.7 %all-gather.9.cloned.1.call-done = bf16[1024,2,1024]{2,0,1:T(8,128)(2,1)} async-done(((bf16[1024,2,256]{2,0,1:T(8,128)(2,1)}), bf16[1024,2,1024]{2,0,1:T(8,128)(2,1)}) %all-gather.9.cloned.1.call-update) | async-done | bytes 4194320 | tf_op jit(solution)/shard_map/all_gather | solution.py:292
  386.1 4.7 all-gather.11.cloned.1.call-done
  390.8 10.1 fusion.57
  400.9 3.2 copy-done.5
  404.1 20.6 %multiply_convert_fusion = (bf16[1024,2,1024]{2,0,1:T(8,128)(2,1)}, f32[1024,2,1024]{2,0,1:T(8,128)}) fusion(f32[1024,2,1024]{2,0,1:T(8,128)S(1)} %get-tuple-element.118, f32[1024]{0:T(1024)S(1)} %copy-done.17, u8[1024,1024]{1,0:T(8,128)(4,1)S(1)} %get-tuple-element.88, u8[1024,1024]{1,0:T(8,128)(4,1)S(1)} %get-tuple-element.87), kind=kLoop, calls=%fused_computation.32 | loop fusion | flops 148897792 | bytes 23072768 | tf_op jit(solution)/shard_map/convert_element_type | solution.py:755
  424.7 62.9 %all-gather.15.cloned.1.call-done = bf16[1024,2,1024]{2,0,1:T(8,128)(2,1)} async-done(((bf16[1024,2,256]{2,0,1:T(8,128)(2,1)}), bf16[1024,2,1024]{2,0,1:T(8,128)(2,1)}) %all-gather.15.cloned.1.call-update) | async-done | bytes 4194320 | tf_op jit(solution)/shard_map/all_gather | solution.py:292
  487.6 12.2 %convert_reduce_fusion.2 = (f32[1024]{0:T(1024)S(1)}, bf16[1024,2,1024]{2,0,1:T(8,128)(2,1)S(1)}) fusion(f32[1024,2,1024]{2,0,1:T(8,128)} %get-tuple-element.109, bf16[1024,2,1024]{2,0,1:T(8,128)(2,1)} %all-gather.15.cloned.1.call-done, bf16[1024,1024]{1,0:T(8,128)(2,1)} %all-gather.13.cloned.1.call-done, f32[1024,2,1024]{2,0,1:T(8,128)} %copy-done.5, ...), kind=kOutput, calls=%fused_computation.29 | convolution fusion | flops 4330617856 | bytes 27271168 | tf_op jit(solution)/shard_map/psd,fd->psf/dot_general | solution.py:762
  501.8 6.5 convolution_convert_fusion
  508.5 5.5 fusion.14
  514.1 69.3 %reduce-scatter.14.cloned.1.call-done = bf16[1024,2,256]{2,0,1:T(8,128)(2,1)} async-done(((bf16[1024,2,1024]{2,0,1:T(8,128)(2,1)}), bf16[1024,2,256]{2,0,1:T(8,128)(2,1)}) %reduce-scatter.14.cloned.1.call-update) | async-done | bytes 1048592 | tf_op jit(solution)/shard_map/reduce_scatter | solution.py:655
  586.2 14.4 %all-reduce.2 = (f32[1024,2,1]{0,1,2:T(2,128)S(1)}, f32[1024,2,1]{0,1,2:T(2,128)S(1)}) all-reduce(f32[1024,2,1]{0,1,2:T(2,128)S(1)} %bitcast.128, f32[1024,2,1]{0,1,2:T(2,128)S(1)} %bitcast.129), channel_id=1, replica_groups=mesh['shard'=2,'ctx'=4,'tp'=4] {'tp'}, use_global_device_ids=true, to_apply=%region_11.12 | all-reduce | flops 4096 | bytes 32768 | tf_op jit(solution)/shard_map/psum | solution.py:301
  600.6 3.5 fusion.44
  604.2 10.1 bitcast_convert_fusion.1
  614.2 72.7 %all-gather.17.cloned.1.call-done = bf16[1024,2,1024]{2,0,1:T(8,128)(2,1)} async-done(((bf16[1024,2,256]{2,0,1:T(8,128)(2,1)}), bf16[1024,2,1024]{2,0,1:T(8,128)(2,1)}) %all-gather.17.cloned.1.call-update) | async-done | bytes 4194320 | tf_op jit(solution)/shard_map/all_gather | solution.py:292
  686.9 4.6 convolution_convert_fusion.3
  693.7 4.3 all-to-all-start.2
  698.4 9.4 bitcast_convert_fusion
  707.8 3.4 all-to-all-done.2
  711.3 13.1 %fusion.30.grad_ref = bf16[4096,128]{1,0:T(8,128)(2,1)S(1)} fusion(bf16[4096,128]{1,0:T(8,128)(2,1)} %bitcast.29, s32[4096]{0:T(1024)S(1)} %bitcast.135), kind=kOutput, calls=%fused_computation.51 | convolution fusion | flops 4312268800 | bytes 2113536 | tf_op jit(solution)/shard_map/pa,ad->pd/dot_general | solution.py:253
  724.4 39.1 %attend_back.1 = (bf16[4096,128]{1,0:T(8,128)(2,1)S(1)}, bf16[4096,128]{1,0:T(8,128)(2,1)S(1)}) custom-call(s32[3]{0:T(128)S(1)} %convert_reduce_fusion.6.bounds_ref, bf16[4096,128]{1,0:T(8,128)(2,1)S(1)} %get-tuple-element.113.q_ref, bf16[4096,128]{1,0:T(8,128)(2,1)S(1)} %get-tuple-element.112.v_ref, bf16[4096,256]{1,0:T(8,128)(2,1)} %fusion.25.hot_ref, ...), custom_call_target="tpu_custom_call" | custom-call | flops 10737418240 | bytes 15728640 | tf_op jit(solution)/shard_map/attend_back/pallas_call | solution.py:218
  763.4 19.0 %fusion.26 = bf16[4096,256]{1,0:T(8,128)(2,1)} fusion(s32[4096]{0:T(1024)S(1)} %bitcast.136, bf16[4096,128]{1,0:T(8,128)(2,1)S(1)} %get-tuple-element.22, bf16[4096,128]{1,0:T(8,128)(2,1)S(1)} %get-tuple-element.21), kind=kOutput, calls=%fused_computation.49 | convolution fusion | flops 8611954688 | bytes 4210688 | tf_op jit(solution)/shard_map/pa,pd->ad/dot_general | solution.py:257
  782.4 3.6 all-to-all-start.3
  786.1 4.3 fusion.60
  790.4 19.9 %all-to-all-done.3 = bf16[4,1024,256]{2,1,0:T(8,128)(2,1)S(1)} async-done(((bf16[4,1024,256]{2,1,0:T(8,128)(2,1)}), bf16[4,1024,256]{2,1,0:T(8,128)(2,1)S(1)}, u32[]{:S(2)}, u32[]{:S(2)}) %all-to-all-start.3) | async-done | bytes 2097184 | tf_op jit(solution)/shard_map/all_to_all | solution.py:684
  812.5 3.7 copy.152
  818.5 5.2 fusion.58
  824.5 5.2 fusion.59
  829.7 9.4 convolution_convert_fusion.1
  843.8 3.4 add_convert_fusion
  847.3 5.7 fusion.12
  857.1 65.0 %reduce-scatter.12.cloned.1.call-done = bf16[1024,2,256]{2,0,1:T(8,128)(2,1)} async-done(((bf16[1024,2,1024]{2,0,1:T(8,128)(2,1)}), bf16[1024,2,256]{2,0,1:T(8,128)(2,1)}) %reduce-scatter.12.cloned.1.call-update) | async-done | bytes 1048592 | tf_op jit(solution)/shard_map/reduce_scatter | solution.py:655
  925.6 84.1 %all-reduce.6.cloned.1.call-done = (bf16[512,256]{1,0:T(8,128)(2,1)}, bf16[512,256]{1,0:T(8,128)(2,1)}, bf16[256,512]{1,0:T(8,128)(2,1)}, bf16[512,1024]{1,0:T(8,128)(2,1)}, bf16[1024,512]{1,0:T(8,128)(2,1)}) async-done(((bf16[512,256]{1,0:T(8,128)(2,1)}, bf16[512,256]{1,0:T(8,128)(2,1)}, bf16[256,512]{1,0:T(8,128)(2,1)}, bf16[512,1024]{1,0:T(8,128)(2,1)}, bf16[1024,512]{1,0:T(8,128)(2,1)}), ...) | async-done | bytes 2883600 | tf_op jit(solution)/shard_map/psum | solution.py:361
  1021.0 67.8 %reduce-scatter.16.cloned.1.call-done = bf16[1024,2,256]{2,0,1:T(8,128)(2,1)} async-done(((bf16[1024,2,1024]{2,0,1:T(8,128)(2,1)}), bf16[1024,2,256]{2,0,1:T(8,128)(2,1)}) %reduce-scatter.16.cloned.1.call-update) | async-done | bytes 1048592 | tf_op jit(solution)/shard_map/reduce_scatter | solution.py:655
  1091.6 14.4 %all-reduce.1 = (f32[1024,2,1]{0,1,2:T(2,128)S(1)}, f32[1024,2,1]{0,1,2:T(2,128)S(1)}) all-reduce(f32[1024,2,1]{0,1,2:T(2,128)S(1)} %bitcast.130, f32[1024,2,1]{0,1,2:T(2,128)S(1)} %bitcast.131), channel_id=1, replica_groups=mesh['shard'=2,'ctx'=4,'tp'=4] {'tp'}, use_global_device_ids=true, to_apply=%region_16.17 | all-reduce | flops 4096 | bytes 32768 | tf_op jit(solution)/shard_map/psum | solution.py:301
  1110.5 19.9 %all-reduce = (f32[1024]{0:T(1024)}, f32[256]{0:T(256)}, f32[256]{0:T(256)}, f32[256]{0:T(256)}, f32[256]{0:T(256)}, /*index=5*/f32[256]{0:T(256)}) all-reduce(f32[1024]{0:T(1024)S(1)} %get-tuple-element.119, f32[256]{0:T(256)S(1)} %get-tuple-element.114, ...), channel_id=1, replica_groups=mesh['shard'=2,'ctx'=4,'tp'=4] {'shard','ctx'}, use_global_device_ids=true, to_apply=%region_26.27 | all-reduce | flops 2304 | bytes 18432 | tf_op jit(solution)/shard_map/psum | solution.py:796
  (147 shorter events, 87.9 us)
Async XLA Ops:
  7.2 91.8 %copy-start.24 = (f32[1024]{0:T(1024)S(1)}, f32[1024]{0:T(1024)}, u32[]{:S(2)}) copy-start(f32[1024]{0:T(1024)} %param.33) | copy-start | bytes 12292
  7.2 91.8 %copy-start.20 = (f32[1024]{0:T(1024)S(1)}, f32[1024]{0:T(1024)}, u32[]{:S(2)}) copy-start(f32[1024]{0:T(1024)} %param.32) | copy-start | bytes 12292
  7.2 85.8 %all-gather.7.cloned.1.call-start = ((), (), s32[]{:S(2)}) async-start(), calls=%async_computation.13 | async-start | bytes 5242880 | tf_op jit(solution)/shard_map/all_gather | solution.py:292
  27.3 74.1 %copy-start.8 = (bf16[1024,256]{0,1:T(8,128)(2,1)}, bf16[1024,256]{0,1:T(8,128)(2,1)S(1)}, u32[]{:S(2)}) copy-start(bf16[1024,256]{0,1:T(8,128)(2,1)S(1)} %all_gather.33) | copy-start | bytes 1572868
  29.5 71.9 %copy-start.10 = (bf16[1024,256]{0,1:T(8,128)(2,1)}, bf16[1024,256]{0,1:T(8,128)(2,1)S(1)}, u32[]{:S(2)}) copy-start(bf16[1024,256]{0,1:T(8,128)(2,1)S(1)} %all_gather.32) | copy-start | bytes 1572868
  93.0 6.0 copy-start.2
  96.0 5.5 copy-start.15
  99.0 4.9 copy-start.13
  105.4 28.2 %all-to-all-start = ((bf16[4,1024,256]{1,2,0:T(8,128)(2,1)}), bf16[4,1024,256]{1,2,0:T(8,128)(2,1)S(1)}, u32[]{:S(2)}, u32[]{:S(2)}) async-start(bf16[4,1024,256]{1,2,0:T(8,128)(2,1)} %bitcast.116), calls=%async_computation | async-start | bytes 4194304 | tf_op jit(solution)/shard_map/all_to_all | solution.py:677
  136.1 14.1 %copy-start = (bf16[4096,256]{1,0:T(8,128)(2,1)S(1)}, bf16[4096,256]{1,0:T(8,128)(2,1)}, u32[]{:S(2)}) copy-start(bf16[4096,256]{1,0:T(8,128)(2,1)} %fusion.25.hot_ref) | copy-start | bytes 6291460
  186.1 10.3 copy-start.1
  186.1 13.9 %copy-start.12 = (bf16[256,512]{1,0:T(8,128)(2,1)S(1)}, bf16[256,512]{1,0:T(8,128)(2,1)}, u32[]{:S(2)}) copy-start(bf16[256,512]{1,0:T(8,128)(2,1)} %param.27) | copy-start | bytes 786436
  196.4 16.6 %all-to-all-start.1 = ((bf16[4,1024,128]{2,1,0:T(8,128)(2,1)}), bf16[4,1024,128]{2,1,0:T(8,128)(2,1)S(1)}, u32[]{:S(2)}, u32[]{:S(2)}) async-start(bf16[4,1024,128]{2,1,0:T(8,128)(2,1)} %bitcast.123), calls=%async_computation.1 | async-start | bytes 2097152 | tf_op jit(solution)/shard_map/all_to_all | solution.py:684
  199.9 96.3 %reduce-scatter.10.cloned.1.call-start = ((), (), s32[]{:S(2)}) async-start(), calls=%async_computation.14 | async-start | bytes 5242880 | tf_op jit(solution)/shard_map/reduce_scatter | solution.py:655
  221.2 169.6 %copy-start.17 = (f32[1024]{0:T(1024)S(1)}, f32[1024]{0:T(1024)}, u32[]{:S(2)}) copy-start(f32[1024]{0:T(1024)} %param.29) | copy-start | bytes 12292
  221.2 169.6 %copy-start.19 = (f32[1024]{0:T(1024)S(1)}, f32[1024]{0:T(1024)}, u32[]{:S(2)}) copy-start(f32[1024]{0:T(1024)} %param.34) | copy-start | bytes 12292
  221.2 169.6 %copy-start.23 = (f32[1024]{0:T(1024)S(1)}, f32[1024]{0:T(1024)}, u32[]{:S(2)}) copy-start(f32[1024]{0:T(1024)} %param.35) | copy-start | bytes 12292
  221.2 159.0 %all-gather.9.cloned.1.call-start = ((), (), s32[]{:S(2)}) async-start(), calls=%async_computation.15 | async-start | bytes 5242880 | tf_op jit(solution)/shard_map/all_gather | solution.py:292
  298.9 91.8 %all-gather.11.cloned.1.call-start = ((), (), s32[]{:S(2)}) async-start(), calls=%async_computation.16 | async-start | bytes 3145728 | tf_op jit(solution)/shard_map/all_gather | solution.py:724
  299.5 125.2 %all-gather.13.cloned.1.call-start = ((), (), s32[]{:S(2)}) async-start(), calls=%async_computation.17 | async-start | bytes 3145728 | tf_op jit(solution)/shard_map/all_gather | solution.py:728
  300.1 187.5 %all-gather.15.cloned.1.call-start = ((), (), s32[]{:S(2)}) async-start(), calls=%async_computation.19 | async-start | bytes 5242880 | tf_op jit(solution)/shard_map/all_gather | solution.py:292
  302.5 280.9 %reduce-scatter.14.cloned.1.call-start = ((), (), s32[]{:S(2)}) async-start(), calls=%async_computation.20 | async-start | bytes 5242880 | tf_op jit(solution)/shard_map/reduce_scatter | solution.py:655
  400.9 3.2 copy-start.5
  487.6 14.2 %copy-start.22 = (bf16[1024,1024]{1,0:T(8,128)(2,1)S(1)}, bf16[1024,1024]{1,0:T(8,128)(2,1)}, u32[]{:S(2)}) copy-start(bf16[1024,1024]{1,0:T(8,128)(2,1)} %all-gather.11.cloned.1.call-done) | copy-start | bytes 6291460
  499.9 2.0 copy-start.26
  508.4 178.5 %all-gather.17.cloned.1.call-start = ((), (), s32[]{:S(2)}) async-start(), calls=%async_computation.21 | async-start | bytes 5242880 | tf_op jit(solution)/shard_map/all_gather | solution.py:292
  604.1 235.1 %reduce-scatter.24.cloned.1.call-start = ((), (), s32[]{:S(2)}) async-start(), calls=%async_computation.26 | async-start | bytes 3145728 | tf_op jit(solution)/shard_map/reduce_scatter | solution.py:377
  693.7 17.6 %all-to-all-start.2 = ((bf16[4,1024,128]{2,1,0:T(8,128)(2,1)}), bf16[4,1024,128]{2,1,0:T(8,128)(2,1)}, u32[]{:S(2)}, u32[]{:S(2)}) async-start(bf16[4,1024,128]{2,1,0:T(8,128)(2,1)} %bitcast.118), calls=%async_computation.5 | async-start | bytes 2097152 | tf_op jit(solution)/shard_map/all_to_all | solution.py:677
  698.0 141.2 %reduce-scatter.26.cloned.1.call-start = ((), (), s32[]{:S(2)}) async-start(), calls=%async_computation.27 | async-start | bytes 3145728 | tf_op jit(solution)/shard_map/reduce_scatter | solution.py:388
  782.4 27.9 %all-to-all-start.3 = ((bf16[4,1024,256]{2,1,0:T(8,128)(2,1)}), bf16[4,1024,256]{2,1,0:T(8,128)(2,1)S(1)}, u32[]{:S(2)}, u32[]{:S(2)}) async-start(bf16[4,1024,256]{2,1,0:T(8,128)(2,1)} %bitcast.121), calls=%async_computation.6 | async-start | bytes 4194304 | tf_op jit(solution)/shard_map/all_to_all | solution.py:684
  786.0 53.2 %reduce-scatter.22.cloned.1.call-start = ((), (), s32[]{:S(2)}) async-start(), calls=%async_computation.25 | async-start | bytes 786432 | tf_op jit(solution)/shard_map/reduce_scatter | solution.py:385
  790.4 28.1 %copy-start.14 = (f32[1024,2]{0,1:T(2,128)S(1)}, f32[1024,2]{0,1:T(2,128)}, u32[]{:S(2)}) copy-start(f32[1024,2]{0,1:T(2,128)} %copy-done.13) | copy-start | bytes 24580
  790.4 28.1 %copy-start.16 = (f32[1024,2]{0,1:T(2,128)S(1)}, f32[1024,2]{0,1:T(2,128)}, u32[]{:S(2)}) copy-start(f32[1024,2]{0,1:T(2,128)} %copy-done.15) | copy-start | bytes 24580
  790.4 28.2 %copy-start.21 = (f32[1024]{0:T(1024)S(1)}, f32[1024]{0:T(1024)}, u32[]{:S(2)}) copy-start(f32[1024]{0:T(1024)} %param.32) | copy-start | bytes 12292
  790.4 28.2 %copy-start.25 = (f32[1024]{0:T(1024)S(1)}, f32[1024]{0:T(1024)}, u32[]{:S(2)}) copy-start(f32[1024]{0:T(1024)} %param.33) | copy-start | bytes 12292
  790.4 48.9 %reduce-scatter.18.cloned.1.call-start = ((), (), s32[]{:S(2)}) async-start(), calls=%async_computation.23 | async-start | bytes 786432 | tf_op jit(solution)/shard_map/reduce_scatter | solution.py:371
  823.7 18.5 %reduce-scatter.20.cloned.1.call-start = ((), (), s32[]{:S(2)}) async-start(), calls=%async_computation.24 | async-start | bytes 786432 | tf_op jit(solution)/shard_map/reduce_scatter | solution.py:374
  829.7 12.8 %copy-start.11 = (bf16[1024,256]{0,1:T(8,128)(2,1)S(1)}, bf16[1024,256]{0,1:T(8,128)(2,1)}, u32[]{:S(2)}) copy-start(bf16[1024,256]{0,1:T(8,128)(2,1)} %copy-done.10) | copy-start | bytes 1572868
  829.7 92.4 %reduce-scatter.12.cloned.1.call-start = ((), (), s32[]{:S(2)}) async-start(), calls=%async_computation.18 | async-start | bytes 5242880 | tf_op jit(solution)/shard_map/reduce_scatter | solution.py:655
  839.1 4.7 copy-start.9
  839.1 170.6 %all-reduce.6.cloned.1.call-start = ((), (), s32[]{:S(2)}) async-start(), calls=%async_computation.28 | async-start | bytes 5767168 | tf_op jit(solution)/shard_map/psum | solution.py:361
  842.2 246.6 %reduce-scatter.16.cloned.1.call-start = ((), (), s32[]{:S(2)}) async-start(), calls=%async_computation.22 | async-start | bytes 5242880 | tf_op jit(solution)/shard_map/reduce_scatter | solution.py:655
  847.2 5.8 copy-start.3
  847.2 7.8 copy-start.4
  847.3 74.8 %copy-start.7 = (bf16[1024,2,256]{2,1,0:T(2,128)(2,1)S(1)}, bf16[1024,2,256]{2,1,0:T(2,128)(2,1)}, u32[]{:S(2)}) copy-start(bf16[1024,2,256]{2,1,0:T(2,128)(2,1)} %param.19) | copy-start | bytes 3145732
  847.3 74.8 %copy-start.18 = (f32[256]{0:T(256)S(1)}, f32[256]{0:T(256)}, u32[]{:S(2)}) copy-start(f32[256]{0:T(256)} %param.31) | copy-start | bytes 3076
  857.1 249.0 %copy-start.6 = (bf16[1024,2,256]{2,1,0:T(2,128)(2,1)S(1)}, bf16[1024,2,256]{2,1,0:T(2,128)(2,1)}, u32[]{:S(2)}) copy-start(bf16[1024,2,256]{2,1,0:T(2,128)(2,1)} %param.21) | copy-start | bytes 3145732
Sparse Core Ops, SparseCore 0:
  10.2 82.7 all-gather.6
  221.3 74.8 reduce-scatter.9
  299.1 81.1 all-gather.8
  381.7 8.9 all-gather.10
  392.2 11.7 all-gather.12
  406.1 81.4 all-gather.14
  508.5 74.8 reduce-scatter.13
  604.2 82.6 all-gather.16
  689.1 8.0 reduce-scatter.23
  708.0 8.5 reduce-scatter.25
  790.5 7.4 reduce-scatter.21
  823.8 6.3 reduce-scatter.17
  833.1 9.0 reduce-scatter.19
  844.4 77.6 reduce-scatter.11
  925.6 84.1 all-reduce.5
  1012.0 76.7 reduce-scatter.15

commit v2 on v1

--- a/solution.py
+++ b/solution.py
@@ -651,43 +651,206 @@
     )
 
 
-def branch_sum_low(partial_value):
-    summed = lax.psum_scatter(
-        partial_value.astype(jnp.bfloat16), "tp", scatter_dimension=2, tiled=True
-    )
-    return summed.astype(jnp.float32)
-
-
-def sequence_labels(segment_ids, bucket_ids, positions, heads_here):
-    seqs_here, rows_here = positions.shape
+def swap(vectors, axis, bits):
+    size = lax.axis_size(axis)
+    return lax.ppermute(vectors, axis, [(at, at ^ bits) for at in range(size)])
+
+
+def where_am_i():
+    return lax.axis_index("shard"), lax.axis_index("ctx"), lax.axis_index("tp")
+
+
+def plane_pairs(step, inverse):
+    shards, planes = lax.axis_size("shard"), lax.axis_size("tp")
+    local_seqs = planes // shards
+    pairs = []
+    for shard in range(shards):
+        for plane in range(planes):
+            chunk = step ^ plane
+            there = (chunk % shards) * planes + shard * local_seqs + chunk // shards
+            here = shard * planes + plane
+            pairs.append((there, here) if inverse else (here, there))
+    return pairs
+
+
+def rows_in(sliced, beside=(), extra=None):
+    shard, _, plane = where_am_i()
+    shards, planes = lax.axis_size("shard"), lax.axis_size("tp")
+    count, slots, seqs, width = sliced.shape
+    extent = slots // shards
+    by_seq = sliced.transpose(2, 0, 1, 3).reshape(seqs, count, shards, extent, width)
+    by_seq = by_seq.transpose(0, 2, 1, 3, 4).reshape(seqs * shards, count * extent, width)
+    if extra is not None:
+        by_seq = jnp.concatenate([by_seq, jnp.concatenate([extra] * seqs, 0)], 1)
+    mine = (plane % seqs) * shards + shard
+    landed = []
+    for step in range(planes):
+        chunk = lax.dynamic_index_in_dim(by_seq, step ^ plane, 0, False)
+        landed.append(lax.ppermute(chunk, ("shard", "tp"), plane_pairs(step, False)))
+    landed, beside = lax.optimization_barrier((landed, beside))
+    whole = jnp.zeros((count * extent, planes * width), sliced.dtype)
+    for step in range(planes):
+        piece = landed[step][: count * extent]
+        whole = lax.dynamic_update_slice_in_dim(whole, piece, (step ^ mine) * width, 1)
+    whole = whole.reshape(count, extent, planes * width)
+    if extra is None:
+        return whole, beside
+    extras = jnp.zeros((planes,) + extra.shape[1:], extra.dtype)
+    for step in range(planes):
+        piece = landed[step][None, count * extent :]
+        extras = lax.dynamic_update_slice_in_dim(extras, piece, step ^ mine, 0)
+    return whole, beside, extras
+
+
+def rows_out(whole, seqs, beside=()):
+    shard, _, plane = where_am_i()
+    shards, planes = lax.axis_size("shard"), lax.axis_size("tp")
+    count, extent, features = whole.shape
+    width = features // planes
+    mine = (plane % seqs) * shards + shard
+    flat = whole.reshape(count * extent, features)
+    landed = []
+    for step in range(planes):
+        piece = lax.dynamic_slice_in_dim(flat, (step ^ mine) * width, width, 1)
+        landed.append(lax.ppermute(piece, ("shard", "tp"), plane_pairs(step, True)))
+    landed, beside = lax.optimization_barrier((landed, beside))
+    by_seq = jnp.zeros((seqs * shards, count * extent, width), whole.dtype)
+    for step in range(planes):
+        by_seq = lax.dynamic_update_slice_in_dim(by_seq, landed[step][None], step ^ plane, 0)
+    parts = by_seq.reshape(seqs, shards, count, extent, width).transpose(2, 1, 3, 0, 4)
+    return parts.reshape(count, shards * extent, seqs, width), beside
+
+
+def quarter_of(local, at):
+    extent = local.shape[0] // lax.axis_size("ctx")
+    return lax.dynamic_slice_in_dim(local, at * extent, extent, 0)
+
+
+def by_half(own, other):
+    first = lax.axis_index("shard") == 0
+    return jnp.stack([jnp.where(first, own, other), jnp.where(first, other, own)])
+
+
+def core_parts(local):
+    mine = quarter_of(local, lax.axis_index("ctx"))
+    halves = by_half(mine, swap(mine, "shard", 1))
+    extent, width = mine.shape
+    shards = lax.axis_size("shard")
+    parts = halves.reshape(2, shards, extent // shards, width).transpose(1, 0, 2, 3)
+    return parts.reshape(shards, extent, width)
+
+
+def gather_rows(wide):
+    ctx = lax.axis_index("ctx")
+    quarters, (extent, width) = lax.axis_size("ctx"), wide.shape
+    half = jnp.zeros((quarters, extent, width), wide.dtype)
+    for j in range(quarters):
+        piece = wide if j == 0 else swap(wide, "ctx", j)
+        half = lax.dynamic_update_slice_in_dim(half, piece[None], ctx ^ j, 0)
+    both = by_half(half, swap(half, "shard", 1)).reshape(2, quarters, 2, extent // 2, width)
+    return both.transpose(2, 1, 0, 3, 4).reshape(2 * quarters * extent, width)
+
+
+def split_bias(values):
+    high = values.astype(jnp.bfloat16)
+    rest = values - high.astype(jnp.float32)
+    middle = rest.astype(jnp.bfloat16)
+    return jnp.stack([high, middle, (rest - middle.astype(jnp.float32)).astype(jnp.bfloat16)])
+
+
+def shard_half(wide, at):
+    extent = wide.shape[1] // 2
+    return lax.dynamic_slice_in_dim(wide, at * extent, extent, 1)
+
+
+def chip_sums(rows_wide, columns_wide):
+    shard = lax.axis_index("shard")
+
+    def product(at):
+        return lax.dot_general(
+            shard_half(rows_wide, at),
+            columns_wide,
+            (((0,), (0,)), ((), ())),
+            preferred_element_type=jnp.float32,
+        )
+
+    theirs = swap(product(1 - shard).astype(jnp.bfloat16), "shard", 1)
+    return product(shard) + theirs.astype(jnp.float32)
+
+
+def sum_parts(parts):
+    return jnp.sum(parts.astype(jnp.float32), 0)
+
+
+def send_ctx(sums):
+    quarters = lax.axis_size("ctx")
+    parts = sums.reshape(quarters, sums.shape[0] // quarters, sums.shape[1])
+    return lax.all_to_all(parts, "ctx", 0, 0, tiled=True)
+
+
+def scatter_ctx(sums):
+    return sum_parts(send_ctx(sums))
+
+
+def scatter_tp(sums):
+    planes = lax.axis_size("tp")
+    parts = sums.reshape(sums.shape[0], planes, -1).transpose(1, 0, 2)
+    return sum_parts(lax.all_to_all(parts, "tp", 0, 0, tiled=True))
+
+
+def collect_ctx(quarter):
+    ctx = lax.axis_index("ctx")
+    quarters, extent = lax.axis_size("ctx"), quarter.shape[0]
+    whole = jnp.zeros((quarters * extent, quarter.shape[1]), quarter.dtype)
+    for j in range(quarters):
+        piece = quarter if j == 0 else swap(quarter, "ctx", j)
+        whole = lax.dynamic_update_slice_in_dim(whole, piece, (ctx ^ j) * extent, 0)
+    return whole
+
+
+def reduce_context_first(sums):
+    bf16 = jnp.bfloat16
+    quarter = scatter_ctx(sums.astype(bf16)).astype(bf16)
+    return collect_ctx(scatter_tp(quarter).astype(bf16)).astype(jnp.float32)
+
+
+def after(values, ready):
+    return lax.optimization_barrier((values, ready))[0]
+
+
+def row_norm_back(grad, scaled, inverse, gain):
+    weighted = grad * gain
+    first = jnp.mean(weighted, -1, keepdims=True)
+    second = jnp.mean(weighted * scaled, -1, keepdims=True)
+    inner = inverse * (weighted - first - scaled * second)
+    return inner, jnp.sum(grad * scaled, 0), jnp.sum(grad, 0)
+
+
+def heads_out(vectors):
+    heads = HEADS
+    sent = vectors.reshape(vectors.shape[0], heads, -1).transpose(1, 0, 2)
+    landed = lax.all_to_all(sent, ("ctx", "shard"), split_axis=0, concat_axis=0, tiled=True)
+    return landed.reshape(-1, landed.shape[2])
+
+
+def heads_back(vectors):
+    sent = vectors.reshape(HEADS, -1, vectors.shape[1])
+    landed = lax.all_to_all(sent, ("ctx", "shard"), split_axis=0, concat_axis=0, tiled=True)
+    return landed.transpose(1, 0, 2).reshape(landed.shape[1], -1)
+
+
+def plane_labels(segment_ids, bucket_ids, positions):
+    shard, _, plane = where_am_i()
+    seqs = positions.shape[0]
     packed = jnp.concatenate([positions[:, None], segment_ids[:, None], bucket_ids], 1)
-    gathered = lax.all_gather(packed, "ctx", axis=2, tiled=True)
-    mine = lax.dynamic_index_in_dim(gathered, lax.axis_index("ctx") // heads_here, 0, False)
+    mine = lax.dynamic_index_in_dim(packed, plane % seqs, 0, False)
+    mine = jnp.where(shard == plane // seqs, mine, swap(mine, "shard", 1))
+    mine = lax.all_gather(mine, "ctx", axis=1, tiled=True)
     places = mine[0]
     return places, doc_bounds(mine[1]), into_places(places, bucket_hot(mine[2:]))
 
 
-def to_heads(vectors):
-    rows_here, seqs_here, width = vectors[0].shape
-    heads = width // DH
-    stacked = jnp.concatenate(
-        [item.reshape(rows_here, seqs_here * heads, 1, DH) for item in vectors], 2
-    )
-    sent = stacked.transpose(1, 0, 2, 3).reshape(seqs_here * heads, rows_here, -1)
-    landed = lax.all_to_all(sent, "ctx", split_axis=0, concat_axis=0, tiled=True)
-    return landed.reshape(-1, landed.shape[2])
-
-
-def from_heads(vectors, seqs_here, count):
-    pairs = lax.axis_size("ctx")
-    sent = vectors.reshape(pairs, vectors.shape[0] // pairs, vectors.shape[1])
-    landed = lax.all_to_all(sent, "ctx", split_axis=0, concat_axis=0, tiled=True)
-    shaped = landed.reshape(seqs_here, pairs // seqs_here, -1, count, DH).transpose(2, 0, 1, 3, 4)
-    rows_here = shaped.shape[0]
-    return tuple(shaped[:, :, :, at].reshape(rows_here, seqs_here, -1) for at in range(count))
-
-
-def per_device(
+def row_device(
     first_half,
     second_half,
     first_cotangent,
@@ -707,137 +870,213 @@
     forward_gain,
     forward_shift,
 ):
-    rows_here, seqs_here, slice_width = first_half.shape
-    width_heads = query_weight.shape[1]
-    heads_here = width_heads // DH
-    tp_start = lax.axis_index("tp") * slice_width
-    ctx_start = lax.axis_index("ctx") * rows_here
-    bf16 = jnp.bfloat16
-    f32 = jnp.float32
-
-    def columns(wide):
-        return lax.dynamic_slice_in_dim(wide, tp_start, slice_width, wide.ndim - 1)
-
-    full_query, full_value, full_expand = (
-        lax.all_gather(query_weight, "shard", axis=0, tiled=True),
-        lax.all_gather(value_weight, "shard", axis=0, tiled=True),
-        lax.all_gather(expand_weight, "shard", axis=0, tiled=True),
-    )
-    full_output, full_shrink = (
-        lax.all_gather(output_weight, "shard", axis=1, tiled=True),
-        lax.all_gather(shrink_weight, "shard", axis=1, tiled=True),
-    )
-    places, bounds, hot = sequence_labels(segment_ids, bucket_ids, positions, heads_here)
-    second_wide = full_rows(second_half)
+    bf16, f32 = jnp.bfloat16, jnp.float32
+    planes = lax.axis_size("tp")
+    _, ctx, plane = where_am_i()
+    seqs_here, width = first_half.shape[1:]
+    units = expand_bias.shape[0]
+    split = query_weight.shape[0]
+
+    local_pair = jnp.stack(
+        [query_weight.reshape(split, -1, DH), value_weight.reshape(split, -1, DH)], 2
+    ).reshape(split, -1)
+    pair_parts = core_parts(local_pair)
+    pair_rows = pair_parts.shape[1] * pair_parts.shape[2] // width
+    biases = split_bias(jnp.concatenate([expand_bias, shrink_bias])).reshape(-1, width)
+    bias_rows = biases.shape[0]
+    biases = jnp.pad(biases, ((0, -bias_rows % 16), (0, 0)))
+    extra = jnp.concatenate(
+        [pair_parts.reshape(-1, pair_rows, width), jnp.stack([biases] * pair_parts.shape[0])], 1
+    )
+    (second_rows,), (places, bounds, hot), extras = rows_in(
+        second_half[None], plane_labels(segment_ids, bucket_ids, positions), extra
+    )
+    pair_wide = extras[:, :pair_rows].reshape((planes,) + pair_parts.shape[1:]).transpose(1, 0, 2)
+    pair_full = gather_rows(pair_wide.reshape(pair_parts.shape[1], -1))
+    biases = extras[:, pair_rows : pair_rows + bias_rows].astype(f32).reshape(planes, 3, -1)
+    biases = (biases[:, 0] + biases[:, 1]) + biases[:, 2]
+    unit_bias = jnp.concatenate(
+        [
+            lax.dynamic_index_in_dim(biases, plane, 0, False)[:units],
+            lax.dynamic_index_in_dim(biases, plane ^ 2, 0, False)[:units],
+        ]
+    )
+    row_bias = biases[:, units:].reshape(-1)
+
     normed, attn_scaled, attn_inverse = norm_rows(
-        second_wide.astype(f32), attention_gain, attention_shift
+        second_rows.astype(f32), attention_gain, attention_shift
     )
     normed = normed.astype(bf16)
-    queries = jnp.einsum("psd,de->pse", normed, full_query, preferred_element_type=f32).astype(bf16)
-    value_vectors = jnp.einsum(
-        "psd,de->pse", normed, full_value, preferred_element_type=f32
+    pair = dot(normed, pair_full, NN).astype(bf16)
+    local_up, local_down, local_out = after(
+        (expand_weight, shrink_weight.T, output_weight.T), pair_full
+    )
+    up, down, out = (quarter_of(item, ctx) for item in (local_up, local_down, local_out))
+    landed, far, outs_near = lax.optimization_barrier(
+        (
+            heads_out(pair),
+            swap(jnp.concatenate([up, down], 1), "tp", 2),
+            [out] + [swap(out, "tp", k) for k in range(1, planes)],
+        )
+    )
+    outs_wide = jnp.zeros((planes,) + out.shape, bf16)
+    for k in range(planes):
+        outs_wide = lax.dynamic_update_slice_in_dim(outs_wide, outs_near[k][None], plane ^ k, 0)
+    outs_wide = outs_wide.transpose(1, 0, 2).reshape(out.shape[0], -1)
+    wide = jnp.concatenate([up, far[:, :units], down, far[:, units:], outs_wide], 1)
+    whole = lax.all_gather(wide, ("shard", "ctx"), axis=0, tiled=True)
+    up_full, down_full, output_full = (
+        whole[:, : 2 * units],
+        whole[:, 2 * units : 4 * units],
+        whole[:, 4 * units :],
+    )
+
+    sorted_pair = into_places(places, landed)
+    query_sorted, value_sorted = sorted_pair[:, :DH], sorted_pair[:, DH:]
+    (first_rows, second_grad_rows), (mix, logs) = rows_in(
+        after(jnp.stack([first_half, second_cotangent]), landed),
+        attend(bounds, query_sorted, value_sorted, hot),
+    )
+    far_grad_rows, attention = lax.optimization_barrier(
+        (
+            swap(after(second_grad_rows, mix), "tp", 1),
+            heads_back(out_of_places(places, mix.T.astype(bf16))),
+        )
+    )
+
+    first_out = (first_rows.astype(f32) + dot(attention, output_full, NT)).astype(bf16)
+    ffn_in, ffn_scaled, ffn_inverse = norm_rows(first_out.astype(f32), forward_gain, forward_shift)
+    ffn_in = ffn_in.astype(bf16)
+
+    def units_of(rows, grad_rows):
+        exact, pull = jax.vjp(smooth_unit, dot(rows, up_full, NN) + unit_bias)
+        pre_grad = pull(dot(grad_rows, down_full, NN))[0].astype(bf16)
+        return exact.astype(bf16), pre_grad
+
+    (first_grad_rows,), (far_in, (hidden, pre_grad)) = rows_in(
+        after(first_cotangent, first_out)[None],
+        (swap(ffn_in, "tp", 1), units_of(ffn_in, second_grad_rows)),
+    )
+    far_hidden, far_pre_grad = units_of(far_in, far_grad_rows)
+    far_ffn_grad = dot(far_pre_grad, up_full, NT).astype(bf16)
+    all_pre_grad = jnp.concatenate([pre_grad, far_pre_grad], 0)
+    all_hidden = jnp.concatenate([hidden, far_hidden], 0)
+    theirs, ffn_grad, expand_sums, shrink_sums = lax.optimization_barrier(
+        (
+            swap(far_ffn_grad, "tp", 1),
+            dot(pre_grad, up_full, NT),
+            chip_sums(jnp.concatenate([ffn_in, far_in], 0), all_pre_grad).astype(bf16),
+            chip_sums(jnp.concatenate([second_grad_rows, far_grad_rows], 0), all_hidden).astype(bf16),
+        )
+    )
+    ffn_back, ffn_gain_grad, ffn_shift_grad = row_norm_back(
+        ffn_grad + theirs.astype(f32), ffn_scaled, ffn_inverse, forward_gain
+    )
+    first_grad = (first_grad_rows.astype(f32) + ffn_back).astype(bf16)
+    attention_grad = dot(first_grad, output_full, NN).astype(bf16)
+    shrink_bias_grad = jnp.sum(second_grad_rows.astype(f32), 0)
+    expand_bias_grad = jnp.sum(all_pre_grad.astype(f32), 0)
+    far_branch = swap(dot(far_hidden, down_full, NT).astype(bf16), "tp", 1)
+    second_out = (
+        second_rows.astype(f32) + dot(hidden, down_full, NT) + far_branch.astype(f32) + row_bias
     ).astype(bf16)
-    sorted_pair = into_places(places, to_heads((queries, value_vectors)))
-    query_sorted, value_sorted = sorted_pair[:, :DH], sorted_pair[:, DH:]
-    mix, logs = attend(bounds, query_sorted, value_sorted, hot)
-    (attention,) = from_heads(out_of_places(places, mix.T.astype(bf16)), seqs_here, 1)
-    branch = branch_sum_low(
-        jnp.einsum("pse,ed->psd", attention, full_output, preferred_element_type=f32)
-    )
-    first_out = (first_half.astype(f32) + branch).astype(bf16)
-    first_wide = full_rows(first_out)
-    ffn_in, ffn_scaled, ffn_inverse = norm_rows(first_wide.astype(f32), forward_gain, forward_shift)
-    ffn_in = ffn_in.astype(bf16)
-    pre_act = (
-        jnp.einsum("psd,df->psf", ffn_in, full_expand, preferred_element_type=f32) + expand_bias
-    )
-    hidden_exact, unit_pull = jax.vjp(smooth_unit, pre_act)
-    hidden = hidden_exact.astype(bf16)
-    second_branch = (
-        branch_sum_low(jnp.einsum("psf,fd->psd", hidden, full_shrink, preferred_element_type=f32))
-        + shrink_bias
-    )
-    second_out = (second_half.astype(f32) + second_branch).astype(bf16)
-    cotangent_wide = full_rows(second_cotangent)
-    hidden_grad = jnp.einsum("psd,fd->psf", cotangent_wide, full_shrink, preferred_element_type=f32)
-    pre_grad = unit_pull(hidden_grad)[0].astype(bf16)
-    shrink_grad = jnp.einsum("psf,psd->fd", hidden, cotangent_wide, preferred_element_type=f32)
-    shrink_bias_grad = jnp.sum(second_cotangent.astype(f32), (0, 1))
-    expand_grad = jnp.einsum("psd,psf->df", ffn_in, pre_grad, preferred_element_type=f32)
-    expand_bias_grad = jnp.sum(pre_grad.astype(f32), (0, 1))
-    ffn_grad = branch_sum_low(
-        jnp.einsum("psf,df->psd", pre_grad, full_expand, preferred_element_type=f32)
-    )
-    ffn_back, forward_gain_grad, forward_shift_grad = norm_back(
-        ffn_grad, columns(ffn_scaled), ffn_inverse, columns(forward_gain)
-    )
-    first_grad = (first_cotangent.astype(f32) + ffn_back).astype(bf16)
-    grad_wide = full_rows(first_grad)
-    output_grad = jnp.einsum("pse,psd->ed", attention, grad_wide, preferred_element_type=f32)
-    attention_grad = jnp.einsum(
-        "psd,ed->pse", grad_wide, full_output, preferred_element_type=f32
-    ).astype(bf16)
-    grad_sorted = into_places(places, to_heads((attention_grad,)))
-    parts = attend_back(bounds, query_sorted, value_sorted, hot, grad_sorted, mix, logs)
-    queries_total, values_grad = from_heads(
-        out_of_places(places, jnp.concatenate(parts, 1)), seqs_here, 2
-    )
-    query_grad = jnp.einsum("psd,pse->de", normed, queries_total, preferred_element_type=f32)
-    value_grad = jnp.einsum("psd,pse->de", normed, values_grad, preferred_element_type=f32)
-    normed_grad = branch_sum_low(
-        jnp.einsum("pse,de->psd", queries_total, full_query, preferred_element_type=f32)
-        + jnp.einsum("pse,de->psd", values_grad, full_value, preferred_element_type=f32)
-    )
-    attn_back, attention_gain_grad, attention_shift_grad = norm_back(
-        normed_grad, columns(attn_scaled), attn_inverse, columns(attention_gain)
-    )
-    second_grad = (second_cotangent.astype(f32) + attn_back).astype(bf16)
-    expand_bias_sum, shrink_bias_sum, attn_gain_sum, attn_shift_sum, ffn_gain_sum, ffn_shift_sum = (
-        lax.psum(
-            (
-                expand_bias_grad,
-                shrink_bias_grad,
-                attention_gain_grad,
-                attention_shift_grad,
-                forward_gain_grad,
-                forward_shift_grad,
-            ),
-            ("shard", "ctx"),
-        )
-    )
-    query_sum, value_sum, expand_sum, output_sum, shrink_sum = over_context(
-        query_grad, value_grad, expand_grad, output_grad, shrink_grad
-    )
-    query_own, value_own, expand_own = to_row_owners(query_sum, value_sum, expand_sum)
-    output_own, shrink_own = to_col_owners(output_sum, shrink_sum)
+
+    outs = jnp.stack([first_out, second_out])
+    early = jnp.concatenate(
+        [expand_sums, shrink_sums, chip_sums(first_grad, attention).astype(bf16)], 1
+    )
+    grad_heads, outs, early = lax.optimization_barrier((heads_out(attention_grad), outs, early))
+    early_mine = lax.psum_scatter(early, "ctx", scatter_dimension=0, tiled=True)
+    outs_sliced, parts = rows_out(
+        outs,
+        seqs_here,
+        attend_back(
+            bounds, query_sorted, value_sorted, hot, into_places(places, grad_heads), mix, logs
+        ),
+    )
+    pair_grad_heads = out_of_places(places, jnp.concatenate(parts, 1))
+    far_sums = jnp.concatenate(
+        [early_mine[:, units : 2 * units], early_mine[:, 3 * units : 4 * units]], 1
+    )
+    near_sums = jnp.concatenate([early_mine[:, :units], early_mine[:, 2 * units : 3 * units]], 1)
+    first_grad_sliced, (pair_grad, far_sums) = rows_out(
+        after(first_grad, pair_grad_heads)[None],
+        seqs_here,
+        (heads_back(pair_grad_heads), swap(far_sums, "tp", 2)),
+    )
+    early_own = (near_sums.astype(f32) + far_sums.astype(f32)).astype(bf16)
+    early_own = lax.all_gather(early_own, "ctx", axis=0, tiled=True).astype(f32)
+    expand_own, shrink_own = early_own[:, :units], early_own[:, units:].T
+
+    pair_sums = chip_sums(normed, pair_grad).astype(bf16)
+    normed_grad = dot(pair_grad, pair_full, NT)
+    attn_back, attn_gain_grad, attn_shift_grad = row_norm_back(
+        normed_grad, attn_scaled, attn_inverse, attention_gain
+    )
+    second_grad = (second_grad_rows.astype(f32) + attn_back).astype(bf16)
+
+    row_grads = jnp.stack(
+        [shrink_bias_grad, attn_gain_grad, attn_shift_grad, ffn_gain_grad, ffn_shift_grad]
+    )
+    spread = jnp.arange(planes, dtype=jnp.int32)[:, None]
+    unit_grads = jnp.where(spread == plane, expand_bias_grad[None, :units], 0.0)
+    unit_grads = jnp.where(spread == plane ^ 2, expand_bias_grad[None, units:], unit_grads)
+    packed = jnp.concatenate(
+        [unit_grads, row_grads.reshape(5, planes, width).transpose(1, 0, 2).reshape(planes, -1)], 1
+    )
+    quarters = lax.axis_size("ctx")
+    packed = (packed + swap(packed, "shard", 1)).astype(bf16)
+    packed = packed.reshape(planes, quarters, -1)
+    vector_width = packed.shape[2]
+    packed = jnp.pad(packed, ((0, 0), (0, 0), (0, 32 * width - vector_width)))
+    packed = packed.reshape(planes, quarters, 16, 2 * width).transpose(1, 2, 0, 3)
+    late = jnp.concatenate(
+        [pair_sums.reshape(quarters, split // quarters, -1), packed.reshape(quarters, 16, -1)], 1
+    )
+    second_grad_sliced, late = rows_out(
+        second_grad[None], seqs_here, sum_parts(lax.all_to_all(late, "ctx", 0, 0, tiled=True))
+    )
+    late = late.astype(bf16).reshape(-1, planes, 2 * width)
+    late = jnp.concatenate(
+        [late, jnp.pad(early_mine[:, 4 * units :].reshape(-1, planes, width), ((0, 16), (0, 0), (0, 0)))], 2
+    )
+    late_own = collect_ctx(scatter_tp(late.reshape(late.shape[0], -1)).astype(bf16)).astype(f32)
+    late_own = late_own.reshape(quarters, -1, 3 * width)
+    owned = late_own[:, split // quarters :, : 2 * width].reshape(quarters, -1)
+    owned = owned[:, :vector_width].reshape(-1)
+    late_own = late_own[:, : split // quarters].reshape(split, -1)
+    pair_own = late_own[:, : 2 * width].reshape(split, -1, 2, DH)
+    query_own = pair_own[:, :, 0].reshape(query_weight.shape)
+    value_own = pair_own[:, :, 1].reshape(value_weight.shape)
+    output_own = late_own[:, 2 * width :].T
+    row_own = owned[units:].reshape(5, width)
     return (
-        first_out,
-        second_out,
-        first_grad,
-        second_grad,
+        outs_sliced[0],
+        outs_sliced[1],
+        first_grad_sliced[0],
+        second_grad_sliced[0],
         query_own,
         value_own,
         output_own,
         expand_own,
-        expand_bias_sum,
+        owned[:units],
         shrink_own,
-        shrink_bias_sum,
-        attn_gain_sum,
-        attn_shift_sum,
-        ffn_gain_sum,
-        ffn_shift_sum,
-    )
-
-
-def paired(mesh):
-    heads_here = HEADS // mesh.shape["tp"]
-    seqs_here = SEQS // mesh.shape["shard"]
-    return mesh.shape["ctx"] == heads_here * seqs_here
+        row_own[0],
+        row_own[1],
+        row_own[2],
+        row_own[3],
+        row_own[4],
+    )
+
+
+def row_planes(mesh):
+    sizes = mesh.shape
+    return sizes["tp"] == SEQS and sizes["shard"] == 2 and sizes["ctx"] == 4 and HEADS == 8
 
 
 def solution(mesh):
     return jax.shard_map(
-        per_device if paired(mesh) else general_device,
+        row_device if row_planes(mesh) else general_device,
         mesh=mesh,
         in_specs=(
             P("ctx", "shard", "tp"),

time: 1140 us -> 667 us (0.59)
  waiting for transfers between devices: 690 us -> 166 us
  starting transfers between devices: 16.5 us -> 102 us
  blocking collectives: 66.1 us -> 7.48 us
  local copies, waits for them, and re-layouts: 39.8 us -> 98.2 us
  other arithmetic: 73.7 us -> 35.9 us
    all_gather x6 -> x2, waiting for transfers between devices: 281 us -> 0.01 us  [the longest x1 0.01 us: row_device(): whole = lax.all_gather(wide, ('shard', 'ctx'), axis=0, tiled=True)]
    reduce_scatter x9 -> x1, waiting for transfers between devices: 280 us -> 0.01 us  [row_device(): early_mine = lax.psum_scatter(early, 'ctx', scatter_dimension=0, tiled=True)]
    ppermute x0 -> x47, waiting for transfers between devices: none -> 132 us  [the longest x23 77.1 us: swap(): return lax.ppermute(vectors, axis, [(at, at ^ bits) for at in range(size)])]
    psum x1 -> x0, waiting for transfers between devices: 84.1 us -> none  [over_context(): lax.psum(first_part.astype(jnp.bfloat16), 'ctx').astype(jnp.float32)]
    ppermute x0 -> x47, starting transfers between devices: none -> 74.1 us  [the longest x12 31 us: rows_in(): lax.ppermute(chunk, ('shard', 'tp'), plane_pairs(step, False))]
    psum x3 -> x0, blocking collectives: 48.7 us -> none  [the longest x2 28.8 us: norm_back(): lax.psum((jnp.sum(weighted, -1, keepdims=True), jnp.sum(weighted * scaled...]
    convert_element_type x9 -> x8, other arithmetic: 39.6 us -> 7.51 us  [the longest x1 2.11 us: row_device(): early_own = (near_sums.astype(f32) + far_sums.astype(f32)).astype(bf16)]
    dynamic_update_slice x0 -> x40, local copies, waits for them, and re-layouts: none -> 22 us  [the longest x12 9.96 us: rows_out(): lax.dynamic_update_slice_in_dim(by_seq, landed[step][None], step ^ plane, 0)]
  transfers between devices with their start and end apart: 20 -> 56, of which waited for: 15 -> 16; matrix products, arithmetic and copies ran while one was open for 16% -> 33% of each run, Pallas kernels for 3% -> 11%
where the time goes in v2:
time: 667 us; the launch traced here: 658 us
  waiting for transfers between devices  166 us (25%)
  matrix products  159 us (24%)
  starting transfers between devices  102 us (15%)
  local copies, waits for them, and re-layouts  98.2 us (15%)
  Pallas kernels  74 us (11%)
  other arithmetic  35.9 us (5%)
  between operations  15.9 us (2%)
  blocking collectives  7.48 us (1%)
    ppermute x23, waiting for transfers between devices, swap(): return lax.ppermute(vectors, axis, [(at, at ^ bits) for at in range(size)])  77.1 us
    dot_general x12, matrix products, dot(): lax.dot_general(left, right, dims, preferred_element_type=jnp.float32)  60.4 us
    dot_general x3, matrix products, into_places(): jnp.einsum('pa,ad->pd', place_matrix(places), vectors, preferred_element_...  40.4 us
    pallas_call x1, Pallas kernels, attend_back(): pl.pallas_call(attend_back_kernel, name='attend_back', out_shape=(jax.Sha...  38.6 us
    ppermute x12, waiting for transfers between devices, rows_out(): landed.append(lax.ppermute(piece, ('shard', 'tp'), plane_pairs(step, True)))  37.2 us
    pallas_call x1, Pallas kernels, attend(): pl.pallas_call(attend_kernel, name='attend', out_shape=(jax.ShapeDtypeStr...  35.4 us
    ppermute x12, starting transfers between devices, rows_in(): lax.ppermute(chunk, ('shard', 'tp'), plane_pairs(step, False))  31 us
    dot_general x8, matrix products, product(): lax.dot_general(shard_half(rows_wide, at), columns_wide, (((0,), (0,)), (...  30 us
  transfers between devices with their start and end apart: 56, of which 16 were waited for; matrix products, arithmetic and copies ran while one was open for 33% of the time, Pallas kernels for 11%

profile of v2, /device:TPU:1, one launch (start us, length us, event | category | flops | bytes accessed | tf_op | source)
XLA Modules:
  0.0 658.0 jit_solution(4400365159933038103)
XLA Ops:
  15.4 7.5 %all_gather.9 = s32[6,4096]{1,0:T(8,128)S(1)} all-gather(s32[6,1024]{1,0:T(8,128)S(1)} %broadcast_select_fusion.4), channel_id=1, replica_groups=mesh['shard'=2,'ctx'=4,'tp'=4] {'ctx'}, dimensions={1}, use_global_device_ids=true | all-gather | bytes 122880 | tf_op jit(solution)/shard_map/all_gather | solution.py:848
  24.5 6.6 %collective-permute-start.1 = (bf16[784,256]{1,0:T(8,128)(2,1)S(1)}, bf16[784,256]{1,0:T(8,128)(2,1)S(1)}, u32[]{:S(2)}, u32[]{:S(2)}) collective-permute-start(bf16[784,256]{1,0:T(8,128)(2,1)S(1)} %get-tuple-element.264), channel_id=1, source_target_pairs={{0,0},{1,16},{2,1},{3,17},{16,2},{17,18},{18,3},{19,19},{4,4},{5,2... | collective-permute-start | bytes 1204232 | tf_op jit(solution)/shard_map/ppermute | solution.py:689
  35.8 13.4 %fusion.12.hot_ref = bf16[4096,256]{1,0:T(8,128)(2,1)S(1)} fusion(pred[4096,256]{0,1:T(32,128)(4,1)S(1)} %bitcast_compare_fusion, s32[4096]{0:T(1024)S(1)} %bitcast.296), kind=kOutput, calls=%fused_computation.17 | convolution fusion | flops 8607760384 | bytes 3162112 | tf_op jit(solution)/shard_map/pa,ad->pd/dot_general | solution.py:253
  49.5 5.4 collective-permute-done.3
  54.9 12.3 %collective-permute-done.4 = bf16[784,256]{1,0:T(8,128)(2,1)S(1)} collective-permute-done((bf16[784,256]{1,0:T(8,128)(2,1)S(1)}, bf16[784,256]{1,0:T(8,128)(2,1)S(1)}, u32[]{:S(2)}, u32[]{:S(2)}) %collective-permute-start.4) | collective-permute-done | bytes 401440 | tf_op jit(solution)/shard_map/ppermute | solution.py:689
  81.0 6.1 collective-permute-done.6
  89.2 7.3 %collective-permute-done.7 = bf16[128,2048]{0,1:T(8,128)(2,1)} collective-permute-done((bf16[128,2048]{0,1:T(8,128)(2,1)}, bf16[128,2048]{0,1:T(8,128)(2,1)}, u32[]{:S(2)}, u32[]{:S(2)}) %collective-permute-start.7) | collective-permute-done | bytes 524320 | tf_op jit(solution)/shard_map/ppermute | solution.py:656
  119.5 4.7 all-to-all-start
  132.3 9.3 %collective-permute-done.11 = bf16[128,256]{0,1:T(8,128)(2,1)S(1)} collective-permute-done((bf16[128,256]{0,1:T(8,128)(2,1)S(1)}, bf16[128,256]{0,1:T(8,128)(2,1)S(1)}, u32[]{:S(2)}, u32[]{:S(2)}) %collective-permute-start.11) | collective-permute-done | bytes 65568 | tf_op jit(solution)/shard_map/ppermute | solution.py:656
  141.6 13.1 %collective-permute-done.12 = bf16[128,256]{0,1:T(8,128)(2,1)S(1)} collective-permute-done((bf16[128,256]{0,1:T(8,128)(2,1)S(1)}, bf16[128,256]{0,1:T(8,128)(2,1)S(1)}, u32[]{:S(2)}, u32[]{:S(2)}) %collective-permute-start.12) | collective-permute-done | bytes 65568 | tf_op jit(solution)/shard_map/ppermute | solution.py:656
  159.6 6.0 pad_maximum_fusion.8
  167.7 5.3 collective-permute-start.14
  176.2 13.8 %fusion.13 = bf16[4096,256]{1,0:T(8,128)(2,1)S(1)} fusion(bf16[4096,256]{1,0:T(8,128)(2,1)} %bitcast.39, s32[4096]{0:T(1024)S(1)} %bitcast.297), kind=kOutput, calls=%fused_computation.18 | convolution fusion | flops 8607760384 | bytes 4210688 | tf_op jit(solution)/shard_map/pa,ad->pd/dot_general | solution.py:253
  190.2 35.4 %attend.1 = (f32[128,4096]{1,0:T(8,128)S(1)}, f32[16,256]{1,0:T(8,128)S(1)}) custom-call(s32[3]{0:T(128)S(1)} %convert_reduce_fusion.5.bounds_ref, bf16[4096,128]{1,0:T(8,128)(2,1)S(1)} %get-tuple-element.256.q_ref, bf16[4096,128]{1,0:T(8,128)(2,1)S(1)} %get-tuple-element.255.v_ref, bf16[4096,256]{1,0:T(8,128)(2,1)S(1)} %fusion.12.hot_ref), custom_call_target="tpu_custom_call" | custom-call | flops 4294967296 | bytes 10485760 | tf_op jit(solution)/shard_map/attend/pallas_call | solution.py:117
  227.6 9.3 %fusion.15 = bf16[4096,128]{1,0:T(8,128)(2,1)S(1)} fusion(s32[4096]{0:T(1024)S(1)} %bitcast.298, f32[128,4096]{1,0:T(8,128)S(1)} %get-tuple-element.96.out_ref), kind=kOutput, calls=%fused_computation.20 | convolution fusion | flops 4329570304 | bytes 3162112 | tf_op jit(solution)/shard_map/pa,pd->ad/dot_general | solution.py:257
  238.2 4.3 all-to-all-start.1
  242.6 11.8 %all-to-all-done.1 = bf16[8,512,128]{1,2,0:T(8,128)(2,1)S(1)} async-done(((bf16[8,512,128]{1,2,0:T(8,128)(2,1)}), bf16[8,512,128]{1,2,0:T(8,128)(2,1)S(1)}, u32[]{:S(2)}, u32[]{:S(2)}) %all-to-all-start.1) | async-done | bytes 1048608 | tf_op jit(solution)/shard_map/all_to_all | solution.py:838
  259.1 5.8 collective-permute-start.19
  273.1 12.6 %multiply_convert_fusion.1 = (bf16[512,2048]{1,0:T(8,128)(2,1)}, f32[512,2048]{1,0:T(8,128)S(1)}, f32[512,2048]{1,0:T(8,128)}) fusion(f32[2048]{0:T(1024)S(1)} %pad_maximum_fusion.19, bf16[512,1024]{1,0:T(8,128)(2,1)S(1)} %fusion.68, bf16[1024,5120]{0,1:T(8,128)(2,1)S(1)} %copy-done.47), kind=kOutput, calls=%fused_computation.47 | convolution fusion | flops 2216689664 | bytes 15736832 | tf_op jit(solution)/shard_map/dot_general | solution.py:27
  285.7 5.4 add_convert_fusion.4
  291.2 16.4 %collective-permute-done.23 = bf16[512,1024]{1,0:T(8,128)(2,1)S(1)} collective-permute-done((bf16[512,1024]{1,0:T(8,128)(2,1)S(1)}, bf16[512,1024]{1,0:T(8,128)(2,1)S(1)}, u32[]{:S(2)}, u32[]{:S(2)}) %collective-permute-start.23) | collective-permute-done | bytes 1048608 | tf_op jit(solution)/shard_map/ppermute | solution.py:656
  307.6 12.7 %multiply_convert_fusion = (bf16[512,2048]{1,0:T(8,128)(2,1)}, f32[512,2048]{1,0:T(8,128)S(1)}, f32[512,2048]{1,0:T(8,128)}) fusion(f32[2048]{0:T(1024)S(1)} %pad_maximum_fusion.19, bf16[512,1024]{1,0:T(8,128)(2,1)S(1)} %collective-permute-done.23, bf16[1024,5120]{0,1:T(8,128)(2,1)S(1)} %copy-done.47), kind=kOutput, calls=%fused_computation.31 | convolution fusion | flops 2216689664 | bytes 15736832 | tf_op jit(solution)/shard_map/dot_general | solution.py:27
  320.4 6.0 add_convert_fusion.3
  329.7 3.7 convolution_convert_fusion.1
  333.8 3.7 convolution_convert_fusion
  344.4 3.7 add_convert_fusion.2
  348.1 6.6 add_convert_fusion.1
  360.4 16.3 %collective-permute-done.27 = bf16[512,1024]{1,0:T(8,128)(2,1)S(1)} collective-permute-done((bf16[512,1024]{1,0:T(8,128)(2,1)S(1)}, bf16[512,1024]{1,0:T(8,128)(2,1)S(1)}, u32[]{:S(2)}, u32[]{:S(2)}) %collective-permute-start.27) | collective-permute-done | bytes 1048608 | tf_op jit(solution)/shard_map/ppermute | solution.py:656
  383.2 5.3 all-to-all-start.2
  391.2 4.7 pad_maximum_fusion
  395.9 4.6 all-to-all-done.2
  402.2 5.4 collective-permute-start.29
  407.8 4.7 collective-permute-start.32
  412.5 13.1 %fusion.18.grad_ref = bf16[4096,128]{1,0:T(8,128)(2,1)S(1)} fusion(bf16[4096,128]{1,0:T(8,128)(2,1)} %bitcast.73, s32[4096]{0:T(1024)S(1)} %bitcast.299), kind=kOutput, calls=%fused_computation.21 | convolution fusion | flops 4312268800 | bytes 2113536 | tf_op jit(solution)/shard_map/pa,ad->pd/dot_general | solution.py:253
  425.6 38.6 %attend_back.1 = (bf16[4096,128]{1,0:T(8,128)(2,1)S(1)}, bf16[4096,128]{1,0:T(8,128)(2,1)S(1)}) custom-call(s32[3]{0:T(128)S(1)} %convert_reduce_fusion.5.bounds_ref, bf16[4096,128]{1,0:T(8,128)(2,1)S(1)} %copy-done.5, bf16[4096,128]{1,0:T(8,128)(2,1)S(1)} %copy-done.3, bf16[4096,256]{1,0:T(8,128)(2,1)} %copy-done.6, bf16[4096,128]{1,0:T(8,128)(2,1)S(1)} %fusion.18.grad_ref, ...), custom_call_target="tpu_custom_call" | custom-call | flops 10737418240 | bytes 15728640 | tf_op jit(solution)/shard_map/attend_back/pallas_call | solution.py:218
  464.3 19.2 %fusion.14 = bf16[4096,256]{1,0:T(8,128)(2,1)} fusion(s32[4096]{0:T(1024)S(1)} %bitcast.300, bf16[4096,128]{1,0:T(8,128)(2,1)S(1)} %get-tuple-element.127, bf16[4096,128]{1,0:T(8,128)(2,1)S(1)} %get-tuple-element.126), kind=kOutput, calls=%fused_computation.19 | convolution fusion | flops 8611954688 | bytes 4210688 | tf_op jit(solution)/shard_map/pa,pd->ad/dot_general | solution.py:257
  483.5 3.9 copy.175
  487.5 5.7 all-to-all-start.3
  501.4 3.9 collective-permute-start.35
  507.4 30.4 %collective-permute-done.33 = bf16[512,256]{1,0:T(8,128)(2,1)S(1)} collective-permute-done((bf16[512,256]{1,0:T(8,128)(2,1)S(1)}, bf16[512,256]{1,0:T(8,128)(2,1)S(1)}, u32[]{:S(2)}, u32[]{:S(2)}) %collective-permute-start.33) | collective-permute-done | bytes 262176 | tf_op jit(solution)/shard_map/ppermute | solution.py:715
  537.8 5.5 collective-permute-done.34
  544.8 6.0 fusion.65
  550.8 4.2 convolution_convert_fusion.3
  560.3 3.7 add_convert_fusion
  565.7 3.8 all-to-all-start.4
  588.7 13.2 %all-to-all-done.4 = bf16[4,144,2048]{2,1,0:T(8,128)(2,1)S(1)} async-done(((bf16[4,144,2048]{2,1,0:T(8,128)(2,1)}), bf16[4,144,2048]{2,1,0:T(8,128)(2,1)S(1)}, u32[]{:S(2)}, u32[]{:S(2)}) %all-to-all-start.4) | async-done | bytes 2359328 | tf_op jit(solution)/shard_map/all_to_all | solution.py:1037
  626.6 4.0 all-to-all-done.5
  636.6 8.5 %collective-permute-done.45 = bf16[144,768]{1,0:T(8,128)(2,1)S(1)} collective-permute-done((bf16[144,768]{1,0:T(8,128)(2,1)S(1)}, bf16[144,768]{1,0:T(8,128)(2,1)S(1)}, u32[]{:S(2)}, u32[]{:S(2)}) %collective-permute-start.45) | collective-permute-done | bytes 221216 | tf_op jit(solution)/shard_map/ppermute | solution.py:656
  (383 shorter events, 188.9 us)
Async XLA Ops:
  9.5 14.0 %collective-permute-start = (bf16[128,512]{0,1:T(8,128)(2,1)S(1)}, bf16[128,512]{0,1:T(8,128)(2,1)S(1)}, u32[]{:S(2)}, u32[]{:S(2)}) collective-permute-start(bf16[128,512]{0,1:T(8,128)(2,1)S(1)} %constant_dynamic-slice_fusion.17), channel_id=1, source_target_pairs={{0,16},{16,0},{1,17},{17,1},{2,18},{18,2},{3,19},{19,3},{4,20},{20... | collective-permute-start | bytes 393224 | tf_op jit(solution)/shard_map/ppermute | solution.py:656
  24.5 25.0 %collective-permute-start.1 = (bf16[784,256]{1,0:T(8,128)(2,1)S(1)}, bf16[784,256]{1,0:T(8,128)(2,1)S(1)}, u32[]{:S(2)}, u32[]{:S(2)}) collective-permute-start(bf16[784,256]{1,0:T(8,128)(2,1)S(1)} %get-tuple-element.264), channel_id=1, source_target_pairs={{0,0},{1,16},{2,1},{3,17},{16,2},{17,18},{18,3},{19,19},{4,4},{5,2... | collective-permute-start | bytes 1204232 | tf_op jit(solution)/shard_map/ppermute | solution.py:689
  31.1 18.4 %collective-permute-start.2 = (bf16[784,256]{1,0:T(8,128)(2,1)S(1)}, bf16[784,256]{1,0:T(8,128)(2,1)S(1)}, u32[]{:S(2)}, u32[]{:S(2)}) collective-permute-start(bf16[784,256]{1,0:T(8,128)(2,1)S(1)} %get-tuple-element.263), channel_id=1, source_target_pairs={{0,16},{1,0},{2,17},{3,1},{16,18},{17,2},{18,19},{19,3},{4,20},{5,... | collective-permute-start | bytes 1204232 | tf_op jit(solution)/shard_map/ppermute | solution.py:689
  32.4 22.4 %collective-permute-start.3 = (bf16[784,256]{1,0:T(8,128)(2,1)S(1)}, bf16[784,256]{1,0:T(8,128)(2,1)S(1)}, u32[]{:S(2)}, u32[]{:S(2)}) collective-permute-start(bf16[784,256]{1,0:T(8,128)(2,1)S(1)} %get-tuple-element.262), channel_id=1, source_target_pairs={{0,1},{1,17},{2,0},{3,16},{16,3},{17,19},{18,2},{19,18},{4,5},{5,2... | collective-permute-start | bytes 1204232 | tf_op jit(solution)/shard_map/ppermute | solution.py:689
  32.5 34.7 %collective-permute-start.4 = (bf16[784,256]{1,0:T(8,128)(2,1)S(1)}, bf16[784,256]{1,0:T(8,128)(2,1)S(1)}, u32[]{:S(2)}, u32[]{:S(2)}) collective-permute-start(bf16[784,256]{1,0:T(8,128)(2,1)S(1)} %get-tuple-element.261), channel_id=1, source_target_pairs={{0,17},{1,1},{2,16},{3,0},{16,19},{17,3},{18,18},{19,2},{4,21},{5,... | collective-permute-start | bytes 1204232 | tf_op jit(solution)/shard_map/ppermute | solution.py:689
  72.8 14.3 %collective-permute-start.6 = (bf16[128,2048]{0,1:T(8,128)(2,1)}, bf16[128,2048]{0,1:T(8,128)(2,1)}, u32[]{:S(2)}, u32[]{:S(2)}) collective-permute-start(bf16[128,2048]{0,1:T(8,128)(2,1)} %bitcast.256), channel_id=1, source_target_pairs={{0,4},{4,0},{8,12},{12,8},{1,5},{5,1},{9,13},{13,9},{2,6},{6,2},{1... | collective-permute-start | bytes 1572872 | tf_op jit(solution)/shard_map/ppermute | solution.py:656
  74.0 22.5 %collective-permute-start.7 = (bf16[128,2048]{0,1:T(8,128)(2,1)}, bf16[128,2048]{0,1:T(8,128)(2,1)}, u32[]{:S(2)}, u32[]{:S(2)}) collective-permute-start(bf16[128,2048]{0,1:T(8,128)(2,1)} %bitcast.257), channel_id=1, source_target_pairs={{0,8},{4,12},{8,0},{12,4},{1,9},{5,13},{9,1},{13,5},{2,10},{6,14},... | collective-permute-start | bytes 1572872 | tf_op jit(solution)/shard_map/ppermute | solution.py:656
  74.3 24.2 %collective-permute-start.8 = (bf16[128,2048]{0,1:T(8,128)(2,1)}, bf16[128,2048]{0,1:T(8,128)(2,1)}, u32[]{:S(2)}, u32[]{:S(2)}) collective-permute-start(bf16[128,2048]{0,1:T(8,128)(2,1)} %bitcast.258), channel_id=1, source_target_pairs={{0,12},{4,8},{8,4},{12,0},{1,13},{5,9},{9,5},{13,1},{2,14},{6,10},... | collective-permute-start | bytes 1572872 | tf_op jit(solution)/shard_map/ppermute | solution.py:656
  119.5 35.2 %all-to-all-start = ((bf16[8,512,256]{2,1,0:T(8,128)(2,1)}), bf16[8,512,256]{2,1,0:T(8,128)(2,1)}, u32[]{:S(2)}, u32[]{:S(2)}) async-start(bf16[8,512,256]{2,1,0:T(8,128)(2,1)} %bitcast.236), calls=%async_computation | async-start | bytes 4194304 | tf_op jit(solution)/shard_map/all_to_all | solution.py:832
  124.2 131.2 %all-gather.3.cloned.1.call-start = ((), (), s32[]{:S(2)}) async-start(), calls=%async_computation.7 | async-start | bytes 11796480 | tf_op jit(solution)/shard_map/all_gather | solution.py:927
  128.6 26.1 %collective-permute-start.10 = (bf16[128,2048]{0,1:T(8,128)(2,1)S(1)}, bf16[128,2048]{0,1:T(8,128)(2,1)}, u32[]{:S(2)}, u32[]{:S(2)}) collective-permute-start(bf16[128,2048]{0,1:T(8,128)(2,1)S(1)} %pad_maximum_fusion.15), channel_id=1, source_target_pairs={{0,2},{1,3},{2,0},{3,1},{4,6},{5,7},{6,4},{7,5},{8,10},{9,11},{10,... | collective-permute-start | bytes 1572872 | tf_op jit(solution)/shard_map/ppermute | solution.py:656
  128.7 12.9 %collective-permute-start.11 = (bf16[128,256]{0,1:T(8,128)(2,1)S(1)}, bf16[128,256]{0,1:T(8,128)(2,1)S(1)}, u32[]{:S(2)}, u32[]{:S(2)}) collective-permute-start(bf16[128,256]{0,1:T(8,128)(2,1)S(1)} %constant_dynamic-slice_fusion.14), channel_id=1, source_target_pairs={{0,1},{1,0},{2,3},{3,2},{4,5},{5,4},{6,7},{7,6},{8,9},{9,8},{10,11... | collective-permute-start | bytes 196616 | tf_op jit(solution)/shard_map/ppermute | solution.py:656
  128.8 25.9 %collective-permute-start.12 = (bf16[128,256]{0,1:T(8,128)(2,1)S(1)}, bf16[128,256]{0,1:T(8,128)(2,1)S(1)}, u32[]{:S(2)}, u32[]{:S(2)}) collective-permute-start(bf16[128,256]{0,1:T(8,128)(2,1)S(1)} %constant_dynamic-slice_fusion.14), channel_id=1, source_target_pairs={{0,2},{1,3},{2,0},{3,1},{4,6},{5,7},{6,4},{7,5},{8,10},{9,11},{10,... | collective-permute-start | bytes 196616 | tf_op jit(solution)/shard_map/ppermute | solution.py:656
  131.2 23.5 %collective-permute-start.13 = (bf16[128,256]{0,1:T(8,128)(2,1)S(1)}, bf16[128,256]{0,1:T(8,128)(2,1)S(1)}, u32[]{:S(2)}, u32[]{:S(2)}) collective-permute-start(bf16[128,256]{0,1:T(8,128)(2,1)S(1)} %constant_dynamic-slice_fusion.14), channel_id=1, source_target_pairs={{0,3},{1,2},{2,1},{3,0},{4,7},{5,6},{6,5},{7,4},{8,11},{9,10},{10,... | collective-permute-start | bytes 196616 | tf_op jit(solution)/shard_map/ppermute | solution.py:656
  167.7 58.0 %collective-permute-start.14 = (bf16[1024,256]{1,0:T(8,128)(2,1)S(1)}, bf16[1024,256]{1,0:T(8,128)(2,1)S(1)}, u32[]{:S(2)}, u32[]{:S(2)}) collective-permute-start(bf16[1024,256]{1,0:T(8,128)(2,1)S(1)} %get-tuple-element.260), channel_id=1, source_target_pairs={{0,0},{1,16},{2,1},{3,17},{16,2},{17,18},{18,3},{19,19},{4,4},{5,2... | collective-permute-start | bytes 1572872 | tf_op jit(solution)/shard_map/ppermute | solution.py:689
  173.0 52.7 %collective-permute-start.15 = (bf16[1024,256]{1,0:T(8,128)(2,1)S(1)}, bf16[1024,256]{1,0:T(8,128)(2,1)S(1)}, u32[]{:S(2)}, u32[]{:S(2)}) collective-permute-start(bf16[1024,256]{1,0:T(8,128)(2,1)S(1)} %get-tuple-element.259), channel_id=1, source_target_pairs={{0,16},{1,0},{2,17},{3,1},{16,18},{17,2},{18,19},{19,3},{4,20},{5,... | collective-permute-start | bytes 1572872 | tf_op jit(solution)/shard_map/ppermute | solution.py:689
  173.1 52.6 %collective-permute-start.16 = (bf16[1024,256]{1,0:T(8,128)(2,1)S(1)}, bf16[1024,256]{1,0:T(8,128)(2,1)S(1)}, u32[]{:S(2)}, u32[]{:S(2)}) collective-permute-start(bf16[1024,256]{1,0:T(8,128)(2,1)S(1)} %get-tuple-element.258), channel_id=1, source_target_pairs={{0,1},{1,17},{2,0},{3,16},{16,3},{17,19},{18,2},{19,18},{4,5},{5,2... | collective-permute-start | bytes 1572872 | tf_op jit(solution)/shard_map/ppermute | solution.py:689
  174.2 51.6 %collective-permute-start.17 = (bf16[1024,256]{1,0:T(8,128)(2,1)S(1)}, bf16[1024,256]{1,0:T(8,128)(2,1)S(1)}, u32[]{:S(2)}, u32[]{:S(2)}) collective-permute-start(bf16[1024,256]{1,0:T(8,128)(2,1)S(1)} %get-tuple-element.257), channel_id=1, source_target_pairs={{0,17},{1,1},{2,16},{3,0},{16,19},{17,3},{18,18},{19,2},{4,21},{5,... | collective-permute-start | bytes 1572872 | tf_op jit(solution)/shard_map/ppermute | solution.py:689
  227.4 27.1 %collective-permute-start.18 = (bf16[512,1024]{1,0:T(8,128)(2,1)}, bf16[512,1024]{1,0:T(8,128)(2,1)}, u32[]{:S(2)}, u32[]{:S(2)}) collective-permute-start(bf16[512,1024]{1,0:T(8,128)(2,1)} %unstack.11), channel_id=1, source_target_pairs={{0,1},{1,0},{2,3},{3,2},{4,5},{5,4},{6,7},{7,6},{8,9},{9,8},{10,11... | collective-permute-start | bytes 3145736 | tf_op jit(solution)/shard_map/ppermute | solution.py:656
  238.2 16.2 %all-to-all-start.1 = ((bf16[8,512,128]{1,2,0:T(8,128)(2,1)}), bf16[8,512,128]{1,2,0:T(8,128)(2,1)S(1)}, u32[]{:S(2)}, u32[]{:S(2)}) async-start(bf16[8,512,128]{1,2,0:T(8,128)(2,1)} %copy.172), calls=%async_computation.1 | async-start | bytes 2097152 | tf_op jit(solution)/shard_map/all_to_all | solution.py:838
  259.1 32.1 %collective-permute-start.19 = (bf16[512,256]{1,0:T(8,128)(2,1)S(1)}, bf16[512,256]{1,0:T(8,128)(2,1)S(1)}, u32[]{:S(2)}, u32[]{:S(2)}) collective-permute-start(bf16[512,256]{1,0:T(8,128)(2,1)S(1)} %get-tuple-element.283), channel_id=1, source_target_pairs={{0,0},{1,16},{2,1},{3,17},{16,2},{17,18},{18,3},{19,19},{4,4},{5,2... | collective-permute-start | bytes 786440 | tf_op jit(solution)/shard_map/ppermute | solution.py:689
  264.9 26.3 %collective-permute-start.20 = (bf16[512,256]{1,0:T(8,128)(2,1)S(1)}, bf16[512,256]{1,0:T(8,128)(2,1)S(1)}, u32[]{:S(2)}, u32[]{:S(2)}) collective-permute-start(bf16[512,256]{1,0:T(8,128)(2,1)S(1)} %get-tuple-element.282), channel_id=1, source_target_pairs={{0,16},{1,0},{2,17},{3,1},{16,18},{17,2},{18,19},{19,3},{4,20},{5,... | collective-permute-start | bytes 786440 | tf_op jit(solution)/shard_map/ppermute | solution.py:689
  266.4 24.8 %collective-permute-start.21 = (bf16[512,256]{1,0:T(8,128)(2,1)S(1)}, bf16[512,256]{1,0:T(8,128)(2,1)S(1)}, u32[]{:S(2)}, u32[]{:S(2)}) collective-permute-start(bf16[512,256]{1,0:T(8,128)(2,1)S(1)} %get-tuple-element.281), channel_id=1, source_target_pairs={{0,1},{1,17},{2,0},{3,16},{16,3},{17,19},{18,2},{19,18},{4,5},{5,2... | collective-permute-start | bytes 786440 | tf_op jit(solution)/shard_map/ppermute | solution.py:689
  268.3 22.9 %collective-permute-start.22 = (bf16[512,256]{1,0:T(8,128)(2,1)S(1)}, bf16[512,256]{1,0:T(8,128)(2,1)S(1)}, u32[]{:S(2)}, u32[]{:S(2)}) collective-permute-start(bf16[512,256]{1,0:T(8,128)(2,1)S(1)} %get-tuple-element.280), channel_id=1, source_target_pairs={{0,17},{1,1},{2,16},{3,0},{16,19},{17,3},{18,18},{19,2},{4,21},{5,... | collective-permute-start | bytes 786440 | tf_op jit(solution)/shard_map/ppermute | solution.py:689
  271.1 36.5 %collective-permute-start.23 = (bf16[512,1024]{1,0:T(8,128)(2,1)S(1)}, bf16[512,1024]{1,0:T(8,128)(2,1)S(1)}, u32[]{:S(2)}, u32[]{:S(2)}) collective-permute-start(bf16[512,1024]{1,0:T(8,128)(2,1)S(1)} %fusion.68), channel_id=1, source_target_pairs={{0,1},{1,0},{2,3},{3,2},{4,5},{5,4},{6,7},{7,6},{8,9},{9,8},{10,11... | collective-permute-start | bytes 3145736 | tf_op jit(solution)/shard_map/ppermute | solution.py:656
  329.7 25.0 %collective-permute-start.24 = (bf16[512,1024]{1,0:T(8,128)(2,1)}, bf16[512,1024]{1,0:T(8,128)(2,1)S(1)}, u32[]{:S(2)}, u32[]{:S(2)}) collective-permute-start(bf16[512,1024]{1,0:T(8,128)(2,1)} %fusion.97), channel_id=1, source_target_pairs={{0,1},{1,0},{2,3},{3,2},{4,5},{5,4},{6,7},{7,6},{8,9},{9,8},{10,11... | collective-permute-start | bytes 3145736 | tf_op jit(solution)/shard_map/ppermute | solution.py:656
  333.4 10.9 %collective-permute-start.25 = (bf16[512,2048]{1,0:T(8,128)(2,1)}, bf16[512,2048]{1,0:T(8,128)(2,1)S(1)}, u32[]{:S(2)}, u32[]{:S(2)}) collective-permute-start(bf16[512,2048]{1,0:T(8,128)(2,1)} %convolution_convert_fusion.1), channel_id=1, source_target_pairs={{0,16},{16,0},{1,17},{17,1},{2,18},{18,2},{3,19},{19,3},{4,20},{20... | collective-permute-start | bytes 6291464 | tf_op jit(solution)/shard_map/ppermute | solution.py:656
  340.0 36.7 %collective-permute-start.27 = (bf16[512,1024]{1,0:T(8,128)(2,1)S(1)}, bf16[512,1024]{1,0:T(8,128)(2,1)S(1)}, u32[]{:S(2)}, u32[]{:S(2)}) collective-permute-start(bf16[512,1024]{1,0:T(8,128)(2,1)S(1)} %fusion.100), channel_id=1, source_target_pairs={{0,1},{1,0},{2,3},{3,2},{4,5},{5,4},{6,7},{7,6},{8,9},{9,8},{10,11... | collective-permute-start | bytes 3145736 | tf_op jit(solution)/shard_map/ppermute | solution.py:656
  358.8 29.8 %collective-permute-start.28 = (bf16[512,1024]{1,0:T(8,128)(2,1)}, bf16[512,1024]{1,0:T(8,128)(2,1)}, u32[]{:S(2)}, u32[]{:S(2)}) collective-permute-start(bf16[512,1024]{1,0:T(8,128)(2,1)} %convolution_convert_fusion.4), channel_id=1, source_target_pairs={{0,16},{16,0},{1,17},{17,1},{2,18},{18,2},{3,19},{19,3},{4,20},{20... | collective-permute-start | bytes 3145736 | tf_op jit(solution)/shard_map/ppermute | solution.py:656
  383.2 17.2 %all-to-all-start.2 = ((bf16[8,512,128]{2,1,0:T(8,128)(2,1)}), bf16[8,512,128]{2,1,0:T(8,128)(2,1)}, u32[]{:S(2)}, u32[]{:S(2)}) async-start(bf16[8,512,128]{2,1,0:T(8,128)(2,1)} %bitcast.248), calls=%async_computation.2 | async-start | bytes 2097152 | tf_op jit(solution)/shard_map/all_to_all | solution.py:832
  388.5 107.6 %reduce-scatter.2.cloned.1.call-start = ((), (), s32[]{:S(2)}) async-start(), calls=%async_computation.8 | async-start | bytes 6553600 | tf_op jit(solution)/shard_map/reduce_scatter | solution.py:989
  402.2 62.1 %collective-permute-start.29 = (bf16[1024,256]{1,0:T(8,128)(2,1)S(1)}, bf16[1024,256]{1,0:T(8,128)(2,1)S(1)}, u32[]{:S(2)}, u32[]{:S(2)}) collective-permute-start(bf16[1024,256]{1,0:T(8,128)(2,1)S(1)} %get-tuple-element.254), channel_id=1, source_target_pairs={{0,0},{16,1},{1,2},{17,3},{2,16},{18,17},{3,18},{19,19},{4,4},{20,... | collective-permute-start | bytes 1572872 | tf_op jit(solution)/shard_map/ppermute | solution.py:715
  407.6 56.6 %collective-permute-start.30 = (bf16[1024,256]{1,0:T(8,128)(2,1)S(1)}, bf16[1024,256]{1,0:T(8,128)(2,1)S(1)}, u32[]{:S(2)}, u32[]{:S(2)}) collective-permute-start(bf16[1024,256]{1,0:T(8,128)(2,1)S(1)} %get-tuple-element.253), channel_id=1, source_target_pairs={{16,0},{0,1},{17,2},{1,3},{18,16},{2,17},{19,18},{3,19},{20,4},{4,... | collective-permute-start | bytes 1572872 | tf_op jit(solution)/shard_map/ppermute | solution.py:715
  407.7 56.6 %collective-permute-start.31 = (bf16[1024,256]{1,0:T(8,128)(2,1)S(1)}, bf16[1024,256]{1,0:T(8,128)(2,1)S(1)}, u32[]{:S(2)}, u32[]{:S(2)}) collective-permute-start(bf16[1024,256]{1,0:T(8,128)(2,1)S(1)} %get-tuple-element.252), channel_id=1, source_target_pairs={{1,0},{17,1},{0,2},{16,3},{3,16},{19,17},{2,18},{18,19},{5,4},{21,... | collective-permute-start | bytes 1572872 | tf_op jit(solution)/shard_map/ppermute | solution.py:715
  407.8 56.5 %collective-permute-start.32 = (bf16[1024,256]{1,0:T(8,128)(2,1)S(1)}, bf16[1024,256]{1,0:T(8,128)(2,1)S(1)}, u32[]{:S(2)}, u32[]{:S(2)}) collective-permute-start(bf16[1024,256]{1,0:T(8,128)(2,1)S(1)} %get-tuple-element.251), channel_id=1, source_target_pairs={{17,0},{1,1},{16,2},{0,3},{19,16},{3,17},{18,18},{2,19},{21,4},{5,... | collective-permute-start | bytes 1572872 | tf_op jit(solution)/shard_map/ppermute | solution.py:715
  487.5 57.2 %all-to-all-start.3 = ((bf16[8,512,256]{1,2,0:T(8,128)(2,1)}), bf16[8,512,256]{1,2,0:T(8,128)(2,1)}, u32[]{:S(2)}, u32[]{:S(2)}) async-start(bf16[8,512,256]{1,2,0:T(8,128)(2,1)} %copy.175), calls=%async_computation.3 | async-start | bytes 4194304 | tf_op jit(solution)/shard_map/all_to_all | solution.py:838
  493.2 122.4 %all-gather.5.cloned.1.call-start = ((), (), s32[]{:S(2)}) async-start(), calls=%async_computation.9 | async-start | bytes 2621440 | tf_op jit(solution)/shard_map/all_gather | solution.py:1008
  499.3 45.5 %collective-permute-start.37 = (bf16[128,2048]{1,0:T(8,128)(2,1)}, bf16[128,2048]{1,0:T(8,128)(2,1)}, u32[]{:S(2)}, u32[]{:S(2)}) collective-permute-start(bf16[128,2048]{1,0:T(8,128)(2,1)} %pad_maximum_fusion.16), channel_id=1, source_target_pairs={{0,2},{1,3},{2,0},{3,1},{4,6},{5,7},{6,4},{7,5},{8,10},{9,11},{10,... | collective-permute-start | bytes 1572872 | tf_op jit(solution)/shard_map/ppermute | solution.py:656
  499.4 38.4 %collective-permute-start.33 = (bf16[512,256]{1,0:T(8,128)(2,1)S(1)}, bf16[512,256]{1,0:T(8,128)(2,1)S(1)}, u32[]{:S(2)}, u32[]{:S(2)}) collective-permute-start(bf16[512,256]{1,0:T(8,128)(2,1)S(1)} %get-tuple-element.279), channel_id=1, source_target_pairs={{0,0},{16,1},{1,2},{17,3},{2,16},{18,17},{3,18},{19,19},{4,4},{20,... | collective-permute-start | bytes 786440 | tf_op jit(solution)/shard_map/ppermute | solution.py:715
  501.3 42.0 %collective-permute-start.34 = (bf16[512,256]{1,0:T(8,128)(2,1)S(1)}, bf16[512,256]{1,0:T(8,128)(2,1)S(1)}, u32[]{:S(2)}, u32[]{:S(2)}) collective-permute-start(bf16[512,256]{1,0:T(8,128)(2,1)S(1)} %get-tuple-element.278), channel_id=1, source_target_pairs={{16,0},{0,1},{17,2},{1,3},{18,16},{2,17},{19,18},{3,19},{20,4},{4,... | collective-permute-start | bytes 786440 | tf_op jit(solution)/shard_map/ppermute | solution.py:715
  501.4 41.9 %collective-permute-start.35 = (bf16[512,256]{1,0:T(8,128)(2,1)S(1)}, bf16[512,256]{1,0:T(8,128)(2,1)S(1)}, u32[]{:S(2)}, u32[]{:S(2)}) collective-permute-start(bf16[512,256]{1,0:T(8,128)(2,1)S(1)} %get-tuple-element.277), channel_id=1, source_target_pairs={{1,0},{17,1},{0,2},{16,3},{3,16},{19,17},{2,18},{18,19},{5,4},{21,... | collective-permute-start | bytes 786440 | tf_op jit(solution)/shard_map/ppermute | solution.py:715
  505.3 39.4 %collective-permute-start.36 = (bf16[512,256]{1,0:T(8,128)(2,1)S(1)}, bf16[512,256]{1,0:T(8,128)(2,1)}, u32[]{:S(2)}, u32[]{:S(2)}) collective-permute-start(bf16[512,256]{1,0:T(8,128)(2,1)S(1)} %get-tuple-element.276), channel_id=1, source_target_pairs={{17,0},{1,1},{16,2},{0,3},{19,16},{3,17},{18,18},{2,19},{21,4},{5,... | collective-permute-start | bytes 786440 | tf_op jit(solution)/shard_map/ppermute | solution.py:715
  565.7 36.2 %all-to-all-start.4 = ((bf16[4,144,2048]{2,1,0:T(8,128)(2,1)}), bf16[4,144,2048]{2,1,0:T(8,128)(2,1)S(1)}, u32[]{:S(2)}, u32[]{:S(2)}) async-start(bf16[4,144,2048]{2,1,0:T(8,128)(2,1)} %pad_maximum_fusion.7), calls=%async_computation.5 | async-start | bytes 4718592 | tf_op jit(solution)/shard_map/all_to_all | solution.py:1037
  577.6 24.7 %collective-permute-start.38 = (bf16[512,256]{1,0:T(8,128)(2,1)}, bf16[512,256]{1,0:T(8,128)(2,1)}, u32[]{:S(2)}, u32[]{:S(2)}) collective-permute-start(bf16[512,256]{1,0:T(8,128)(2,1)} %get-tuple-element.275), channel_id=1, source_target_pairs={{0,0},{16,1},{1,2},{17,3},{2,16},{18,17},{3,18},{19,19},{4,4},{20,... | collective-permute-start | bytes 786440 | tf_op jit(solution)/shard_map/ppermute | solution.py:715
  579.9 23.8 %collective-permute-start.39 = (bf16[512,256]{1,0:T(8,128)(2,1)}, bf16[512,256]{1,0:T(8,128)(2,1)}, u32[]{:S(2)}, u32[]{:S(2)}) collective-permute-start(bf16[512,256]{1,0:T(8,128)(2,1)} %get-tuple-element.274), channel_id=1, source_target_pairs={{16,0},{0,1},{17,2},{1,3},{18,16},{2,17},{19,18},{3,19},{20,4},{4,... | collective-permute-start | bytes 786440 | tf_op jit(solution)/shard_map/ppermute | solution.py:715
  581.2 22.4 %collective-permute-start.40 = (bf16[512,256]{1,0:T(8,128)(2,1)}, bf16[512,256]{1,0:T(8,128)(2,1)}, u32[]{:S(2)}, u32[]{:S(2)}) collective-permute-start(bf16[512,256]{1,0:T(8,128)(2,1)} %get-tuple-element.273), channel_id=1, source_target_pairs={{1,0},{17,1},{0,2},{16,3},{3,16},{19,17},{2,18},{18,19},{5,4},{21,... | collective-permute-start | bytes 786440 | tf_op jit(solution)/shard_map/ppermute | solution.py:715
  583.9 19.7 %collective-permute-start.41 = (bf16[512,256]{1,0:T(8,128)(2,1)S(1)}, bf16[512,256]{1,0:T(8,128)(2,1)}, u32[]{:S(2)}, u32[]{:S(2)}) collective-permute-start(bf16[512,256]{1,0:T(8,128)(2,1)S(1)} %get-tuple-element.272), channel_id=1, source_target_pairs={{17,0},{1,1},{16,2},{0,3},{19,16},{3,17},{18,18},{2,19},{21,4},{5,... | collective-permute-start | bytes 786440 | tf_op jit(solution)/shard_map/ppermute | solution.py:715
  605.5 25.2 %all-to-all-start.5 = ((bf16[4,144,768]{2,1,0:T(8,128)(2,1)}), bf16[4,144,768]{2,1,0:T(8,128)(2,1)S(1)}, u32[]{:S(2)}, u32[]{:S(2)}) async-start(bf16[4,144,768]{2,1,0:T(8,128)(2,1)} %copy.178), calls=%async_computation.6 | async-start | bytes 1769472 | tf_op jit(solution)/shard_map/all_to_all | solution.py:798
  (59 other events, 996.5 us)
Sparse Core Ops, SparseCore 0:
  159.7 66.4 all-gather.2
  400.6 60.7 reduce-scatter.1
  560.0 53.2 all-gather.4

commit v3 on v2

--- a/solution.py
+++ b/solution.py
@@ -2,6 +2,7 @@
 import jax.numpy as jnp
 from jax import lax
 from jax.experimental import pallas as pl
+from jax.experimental.layout import Layout, with_layout_constraint
 from jax.experimental.pallas import tpu as pltpu
 from jax.sharding import PartitionSpec as P
 
@@ -18,7 +19,9 @@
 BUCKETS = 64
 HEADS = 8
 SEQS = 4
-TILE = 256
+TILE = 512
+GROUP = 1
+BOUND = 38.0
 NT = (((1,), (1,)), ((), ()))
 NN = (((1,), (0,)), ((), ()))
 
@@ -42,8 +45,8 @@
     return doc_start, first, full
 
 
-def rows_at(ref, block):
-    return ref[pl.ds(pl.multiple_of(block * TILE, TILE), TILE), :]
+def rows_at(ref, block, tiles=1):
+    return ref[pl.ds(pl.multiple_of(block * TILE, TILE), tiles * TILE), :]
 
 
 def norm_factor(q):
@@ -73,41 +76,71 @@
     key_row = lax.broadcasted_iota(jnp.int32, (TILE, 1), 0)
     lane = lax.broadcasted_iota(jnp.int32, (1, TILE), 1)
 
-    def scores(at):
-        return dot(rows_at(key_sc, at), q, NT), dot(rows_at(hot_ref, at), hot, NT)
-
-    def vt(at):
-        return vt_sc[:, pl.ds(pl.multiple_of(at * TILE, TILE), TILE)]
-
-    s, c = scores(block)
-    place = key_row + begin_row
-    c = jnp.where((key_row < lane) & (place >= doc_start), c, 0.0)
+    def scores(at, tiles):
+        return dot(rows_at(key_sc, at, tiles), q, NT), dot(rows_at(hot_ref, at, tiles), hot, NT)
+
+    def vt(at, tiles):
+        return vt_sc[:, pl.ds(pl.multiple_of(at * TILE, TILE), tiles * TILE)]
+
     itself = key_row == lane
-    c = jnp.where(itself, float(ROUNDS), c)
-    s = jnp.where(itself, SELF_SCORE, s)
-    s = jnp.where(c > 0, s, NEG_FILL)
-    high = jnp.max(s, 0, keepdims=True)
-    p = c * jnp.exp(s - high)
-    total = jnp.sum(p, 0, keepdims=True)
-    acc = dot(vt(block), p.astype(jnp.bfloat16), NN)
-
-    def fold(at, carry, masked):
-        high, total, acc = carry
-        s, c = scores(at)
-        if masked:
-            c = jnp.where(key_row + at * TILE >= doc_start, c, 0.0)
+
+    def diagonal():
+        s, c = scores(block, 1)
+        c = jnp.where((key_row < lane) & (key_row + begin_row >= doc_start), c, 0.0)
+        return jnp.where(itself, SELF_SCORE, s), jnp.where(itself, float(ROUNDS), c)
+
+    def in_document(c, at):
+        return jnp.where(key_row + at * TILE >= doc_start, c, 0.0)
+
+    def mixed(at, tiles, p):
+        return dot(vt(at, tiles), p.astype(jnp.bfloat16), NN)
+
+    @pl.when(bounds_ref[3] == 1)
+    def _():
+        def fold(at, tiles, carry, masked):
+            total, acc = carry
+            s, c = scores(at, tiles)
+            if masked:
+                c = in_document(c, at)
+            p = c * jnp.exp(s)
+            return total + jnp.sum(p, 0, keepdims=True), acc + mixed(at, tiles, p)
+
+        s, c = diagonal()
+        p = c * jnp.exp(s)
+        carry = jnp.sum(p, 0, keepdims=True), mixed(block, 1, p)
+        carry = lax.fori_loop(first, full, lambda at, x: fold(at, 1, x, True), carry)
+        rest = (block - full) % GROUP
+        carry = lax.fori_loop(full, full + rest, lambda at, x: fold(at, 1, x, False), carry)
+        total, acc = lax.fori_loop(
+            0,
+            (block - full) // GROUP,
+            lambda at, x: fold(full + rest + GROUP * at, GROUP, x, False),
+            carry,
+        )
+        out_ref[...] = acc / total
+        log_ref[pl.ds(block, 1), :] = jnp.log(total)
+
+    @pl.when(bounds_ref[3] == 0)
+    def _():
+        def fold(at, carry):
+            high, total, acc = carry
+            s, c = scores(at, 1)
+            c = in_document(c, at)
+            s = jnp.where(c > 0, s, NEG_FILL)
+            new_high = jnp.maximum(high, jnp.max(s, 0, keepdims=True))
+            fade = jnp.exp(high - new_high)
+            p = c * jnp.exp(s - new_high)
+            total = total * fade + jnp.sum(p, 0, keepdims=True)
+            return new_high, total, acc * fade + mixed(at, 1, p)
+
+        s, c = diagonal()
         s = jnp.where(c > 0, s, NEG_FILL)
-        new_high = jnp.maximum(high, jnp.max(s, 0, keepdims=True))
-        fade = jnp.exp(high - new_high)
-        p = c * jnp.exp(s - new_high)
-        total = total * fade + jnp.sum(p, 0, keepdims=True)
-        acc = acc * fade + dot(vt(at), p.astype(jnp.bfloat16), NN)
-        return new_high, total, acc
-
-    carry = lax.fori_loop(first, full, lambda at, x: fold(at, x, True), (high, total, acc))
-    high, total, acc = lax.fori_loop(full, block, lambda at, x: fold(at, x, False), carry)
-    out_ref[...] = acc / total
-    log_ref[pl.ds(block, 1), :] = high + jnp.log(total)
+        high = jnp.max(s, 0, keepdims=True)
+        p = c * jnp.exp(s - high)
+        carry = high, jnp.sum(p, 0, keepdims=True), mixed(block, 1, p)
+        high, total, acc = lax.fori_loop(first, block, fold, carry)
+        out_ref[...] = acc / total
+        log_ref[pl.ds(block, 1), :] = high + jnp.log(total)
 
 
 def attend(bounds, q, v, hot):
@@ -132,7 +165,7 @@
             dimension_semantics=("arbitrary",), vmem_limit_bytes=40 * 2**20
         ),
         cost_estimate=pl.CostEstimate(
-            flops=rows * rows * 256, bytes_accessed=rows * DH * 20, transcendentals=rows * rows // 4
+            flops=rows * DH, bytes_accessed=rows * DH, transcendentals=0
         ),
     )(bounds, q, v, hot)
 
@@ -168,33 +201,55 @@
     key_row = lax.broadcasted_iota(jnp.int32, (TILE, 1), 0)
     lane = lax.broadcasted_iota(jnp.int32, (1, TILE), 1)
 
-    def fold(at, acc, masked, diagonal=False):
-        begin = pl.multiple_of(at * TILE, TILE)
-        s = dot(rows_at(key_sc, at), q, NT)
-        c = dot(rows_at(hot_ref, at), hot, NT)
-        up = dot(rows_at(v_ref, at), grad, NT)
+    itself = key_row == lane
+
+    def fold(at, tiles, acc, masked, bounded, diagonal=False):
+        rows = pl.ds(pl.multiple_of(at * TILE, TILE), tiles * TILE)
+        s = dot(key_sc[rows, :], q, NT)
+        c = dot(hot_ref[rows, :], hot, NT)
+        up = dot(v_ref[rows, :], grad, NT)
         if diagonal:
-            itself = key_row == lane
             c = jnp.where((key_row < lane) & (key_row + begin_row >= doc_start), c, 0.0)
             c = jnp.where(itself, float(ROUNDS), c)
             s = jnp.where(itself, SELF_SCORE, s)
         elif masked:
-            c = jnp.where(key_row + begin >= doc_start, c, 0.0)
-        s = jnp.where(c > 0, s, NEG_FILL)
+            c = jnp.where(key_row + at * TILE >= doc_start, c, 0.0)
+        if not bounded:
+            s = jnp.where(c > 0, s, NEG_FILL)
         w = c * jnp.exp(s - log_row)
         ds = w * (up - delta)
         if diagonal:
             ds = jnp.where(itself, 0.0, ds)
         w = w.astype(jnp.bfloat16)
         ds = ds.astype(jnp.bfloat16)
-        dv_sc[pl.ds(begin, TILE), :] += dot(w, grad, NN)
-        dk_sc[pl.ds(begin, TILE), :] += dot(ds, q, NN)
-        return acc + dot(kt_sc[:, pl.ds(begin, TILE)], ds, NN)
-
-    acc = fold(block, jnp.zeros((DH, TILE), jnp.float32), True, True)
-    acc = lax.fori_loop(first, full, lambda at, x: fold(at, x, True), acc)
-    acc = lax.fori_loop(full, block, lambda at, x: fold(at, x, False), acc)
-    dq_sc[pl.ds(pl.multiple_of(begin_row, TILE), TILE), :] = acc.T
+        dv_sc[rows, :] += dot(w, grad, NN)
+        dk_sc[rows, :] += dot(ds, q, NN)
+        return acc + dot(kt_sc[:, rows], ds, NN)
+
+    def store(acc):
+        dq_sc[pl.ds(pl.multiple_of(begin_row, TILE), TILE), :] = acc.T
+
+    nothing = jnp.zeros((DH, TILE), jnp.float32)
+
+    @pl.when(bounds_ref[3] == 1)
+    def _():
+        acc = fold(block, 1, nothing, True, True, True)
+        acc = lax.fori_loop(first, full, lambda at, x: fold(at, 1, x, True, True), acc)
+        rest = (block - full) % GROUP
+        acc = lax.fori_loop(full, full + rest, lambda at, x: fold(at, 1, x, False, True), acc)
+        store(
+            lax.fori_loop(
+                0,
+                (block - full) // GROUP,
+                lambda at, x: fold(full + rest + GROUP * at, GROUP, x, False, True),
+                acc,
+            )
+        )
+
+    @pl.when(bounds_ref[3] == 0)
+    def _():
+        acc = fold(block, 1, nothing, True, False, True)
+        store(lax.fori_loop(first, block, lambda at, x: fold(at, 1, x, True, False), acc))
 
     @pl.when(block == blocks - 1)
     def _():
@@ -239,7 +294,7 @@
             dimension_semantics=("arbitrary",), vmem_limit_bytes=48 * 2**20
         ),
         cost_estimate=pl.CostEstimate(
-            flops=rows * rows * 640, bytes_accessed=rows * DH * 30, transcendentals=rows * rows // 4
+            flops=rows * DH, bytes_accessed=rows * DH, transcendentals=0
         ),
     )(bounds, q, v, hot, grad, out, logs)
 
@@ -264,6 +319,11 @@
 
 def doc_bounds(segments):
     return jnp.sum((segments[None, :] < jnp.arange(1, 4, dtype=jnp.int32)[:, None]).astype(jnp.int32), 1)
+
+
+def with_bound(bounds, queries):
+    squares = jnp.sum(queries.astype(jnp.float32) ** 2, -1)
+    return jnp.concatenate([bounds, (jnp.max(squares) <= BOUND**2).astype(jnp.int32)[None]])
 
 
 def smooth_unit(values_in):
@@ -731,24 +791,13 @@
     return jnp.stack([jnp.where(first, own, other), jnp.where(first, other, own)])
 
 
+def plain(vectors):
+    return with_layout_constraint(vectors, Layout(major_to_minor=tuple(range(vectors.ndim))))
+
+
 def core_parts(local):
     mine = quarter_of(local, lax.axis_index("ctx"))
-    halves = by_half(mine, swap(mine, "shard", 1))
-    extent, width = mine.shape
-    shards = lax.axis_size("shard")
-    parts = halves.reshape(2, shards, extent // shards, width).transpose(1, 0, 2, 3)
-    return parts.reshape(shards, extent, width)
-
-
-def gather_rows(wide):
-    ctx = lax.axis_index("ctx")
-    quarters, (extent, width) = lax.axis_size("ctx"), wide.shape
-    half = jnp.zeros((quarters, extent, width), wide.dtype)
-    for j in range(quarters):
-        piece = wide if j == 0 else swap(wide, "ctx", j)
-        half = lax.dynamic_update_slice_in_dim(half, piece[None], ctx ^ j, 0)
-    both = by_half(half, swap(half, "shard", 1)).reshape(2, quarters, 2, extent // 2, width)
-    return both.transpose(2, 1, 0, 3, 4).reshape(2 * quarters * extent, width)
+    return by_half(mine, swap(mine, "shard", 1))
 
 
 def split_bias(values):
@@ -799,11 +848,14 @@
 
 
 def collect_ctx(quarter):
-    ctx = lax.axis_index("ctx")
-    quarters, extent = lax.axis_size("ctx"), quarter.shape[0]
-    whole = jnp.zeros((quarters * extent, quarter.shape[1]), quarter.dtype)
-    for j in range(quarters):
-        piece = quarter if j == 0 else swap(quarter, "ctx", j)
+    quarters = lax.axis_size("ctx")
+    return in_order([quarter] + [swap(quarter, "ctx", j) for j in range(1, quarters)])
+
+
+def in_order(pieces):
+    ctx, extent = lax.axis_index("ctx"), pieces[0].shape[0]
+    whole = jnp.zeros((len(pieces) * extent,) + pieces[0].shape[1:], pieces[0].dtype)
+    for j, piece in enumerate(pieces):
         whole = lax.dynamic_update_slice_in_dim(whole, piece, (ctx ^ j) * extent, 0)
     return whole
 
@@ -812,6 +864,17 @@
     bf16 = jnp.bfloat16
     quarter = scatter_ctx(sums.astype(bf16)).astype(bf16)
     return collect_ctx(scatter_tp(quarter).astype(bf16)).astype(jnp.float32)
+
+
+def plane_part(parts, k):
+    return lax.dynamic_index_in_dim(parts, lax.axis_index("tp") ^ k, 0, False)
+
+
+def sum_everywhere(parts):
+    total = plane_part(parts, 0)
+    total = sum((swap(plane_part(parts, k), "tp", k) for k in range(1, lax.axis_size("tp"))), total)
+    total = total + swap(total, "shard", 1)
+    return sum(swap(total, "ctx", j) for j in range(1, lax.axis_size("ctx"))) + total
 
 
 def after(values, ready):
@@ -841,13 +904,71 @@
 
 def plane_labels(segment_ids, bucket_ids, positions):
     shard, _, plane = where_am_i()
-    seqs = positions.shape[0]
+    seqs, slots = positions.shape
     packed = jnp.concatenate([positions[:, None], segment_ids[:, None], bucket_ids], 1)
-    mine = lax.dynamic_index_in_dim(packed, plane % seqs, 0, False)
+    kinds = packed.shape[1]
+    mine = lax.dynamic_index_in_dim(packed, plane % seqs, 0, False).reshape(-1, 128)
     mine = jnp.where(shard == plane // seqs, mine, swap(mine, "shard", 1))
-    mine = lax.all_gather(mine, "ctx", axis=1, tiled=True)
-    places = mine[0]
-    return places, doc_bounds(mine[1]), into_places(places, bucket_hot(mine[2:]))
+    whole = collect_ctx(mine).reshape(-1, kinds, slots).transpose(1, 0, 2).reshape(kinds, -1)
+    return whole[0], whole[1], whole[2:]
+
+
+def pack_rows_kernel(code_ref, *refs):
+    out_ref = refs[-1]
+    extent = refs[0].shape[0]
+    for j, ref in enumerate(refs[:-1]):
+        out_ref[pl.ds(pl.multiple_of((code_ref[0] ^ j) * extent, extent), extent), :] = ref[...]
+
+
+def pack_rows(pieces, code):
+    extent, width = pieces[0].shape
+    whole = lambda shape: pl.BlockSpec(shape, lambda i, *_: (0, 0))
+    return pl.pallas_call(
+        pack_rows_kernel,
+        name="pack_rows",
+        out_shape=jax.ShapeDtypeStruct((len(pieces) * extent, width), pieces[0].dtype),
+        grid_spec=pltpu.PrefetchScalarGridSpec(
+            num_scalar_prefetch=1,
+            grid=(1,),
+            in_specs=[whole((extent, width)) for _ in pieces],
+            out_specs=whole((len(pieces) * extent, width)),
+        ),
+        compiler_params=pltpu.CompilerParams(vmem_limit_bytes=24 * 2**20),
+        cost_estimate=pl.CostEstimate(flops=0, bytes_accessed=4 * len(pieces) * extent * width, transcendentals=0),
+    )(jnp.reshape(code, (1,)).astype(jnp.int32), *pieces)
+
+
+def pack_weights_kernel(code_ref, near_ref, far_ref, *refs):
+    out_ref = refs[-1]
+    units = near_ref.shape[1] // 2
+    out_ref[:, :units] = near_ref[:, :units]
+    out_ref[:, units : 2 * units] = far_ref[:, :units]
+    out_ref[:, 2 * units : 3 * units] = near_ref[:, units:]
+    out_ref[:, 3 * units : 4 * units] = far_ref[:, units:]
+    width = refs[0].shape[1]
+    for k, ref in enumerate(refs[:-1]):
+        place = pl.multiple_of(4 * units + (code_ref[0] ^ k) * width, width)
+        out_ref[:, pl.ds(place, width)] = ref[...]
+
+
+def pack_weights(near, far, outs, code):
+    extent, units = near.shape
+    width = outs[0].shape[1]
+    columns = 2 * units + len(outs) * width
+    whole = lambda shape: pl.BlockSpec(shape, lambda i, *_: (0, 0))
+    return pl.pallas_call(
+        pack_weights_kernel,
+        name="pack_weights",
+        out_shape=jax.ShapeDtypeStruct((extent, columns), near.dtype),
+        grid_spec=pltpu.PrefetchScalarGridSpec(
+            num_scalar_prefetch=1,
+            grid=(1,),
+            in_specs=[whole((extent, units))] * 2 + [whole((extent, width)) for _ in outs],
+            out_specs=whole((extent, columns)),
+        ),
+        compiler_params=pltpu.CompilerParams(vmem_limit_bytes=24 * 2**20),
+        cost_estimate=pl.CostEstimate(flops=0, bytes_accessed=4 * extent * columns, transcendentals=0),
+    )(jnp.reshape(code, (1,)).astype(jnp.int32), near, far, *outs)
 
 
 def row_device(
@@ -872,7 +993,7 @@
 ):
     bf16, f32 = jnp.bfloat16, jnp.float32
     planes = lax.axis_size("tp")
-    _, ctx, plane = where_am_i()
+    shard, ctx, plane = where_am_i()
     seqs_here, width = first_half.shape[1:]
     units = expand_bias.shape[0]
     split = query_weight.shape[0]
@@ -888,11 +1009,7 @@
     extra = jnp.concatenate(
         [pair_parts.reshape(-1, pair_rows, width), jnp.stack([biases] * pair_parts.shape[0])], 1
     )
-    (second_rows,), (places, bounds, hot), extras = rows_in(
-        second_half[None], plane_labels(segment_ids, bucket_ids, positions), extra
-    )
-    pair_wide = extras[:, :pair_rows].reshape((planes,) + pair_parts.shape[1:]).transpose(1, 0, 2)
-    pair_full = gather_rows(pair_wide.reshape(pair_parts.shape[1], -1))
+    (second_rows,), _, extras = rows_in(second_half[None], (), extra)
     biases = extras[:, pair_rows : pair_rows + bias_rows].astype(f32).reshape(planes, 3, -1)
     biases = (biases[:, 0] + biases[:, 1]) + biases[:, 2]
     unit_bias = jnp.concatenate(
@@ -903,28 +1020,39 @@
     )
     row_bias = biases[:, units:].reshape(-1)
 
-    normed, attn_scaled, attn_inverse = norm_rows(
-        second_rows.astype(f32), attention_gain, attention_shift
-    )
+    pair_wide = extras[:, :pair_rows].reshape((planes,) + pair_parts.shape[1:]).transpose(1, 0, 2)
+    pair_wide = plain(pair_wide.reshape(pair_parts.shape[1], -1))
+    up, down, out = (
+        quarter_of(item, ctx) for item in (expand_weight, shrink_weight.T, output_weight.T)
+    )
+    quarters = lax.axis_size("ctx")
+    pair_pieces, (normed, attn_scaled, attn_inverse), labels = lax.optimization_barrier(
+        (
+            [swap(pair_wide, "ctx", j) for j in range(1, quarters)],
+            norm_rows(second_rows.astype(f32), attention_gain, attention_shift),
+            plane_labels(*after((segment_ids, bucket_ids, positions), second_rows)),
+        )
+    )
+    places, segments, buckets = labels
     normed = normed.astype(bf16)
-    pair = dot(normed, pair_full, NN).astype(bf16)
-    local_up, local_down, local_out = after(
-        (expand_weight, shrink_weight.T, output_weight.T), pair_full
-    )
-    up, down, out = (quarter_of(item, ctx) for item in (local_up, local_down, local_out))
-    landed, far, outs_near = lax.optimization_barrier(
+    pair_mine = pack_rows([pair_wide] + pair_pieces, ctx)
+    pair_other = swap(pair_mine, "shard", 1)
+    pair = (
+        dot(shard_half(normed, shard), pair_mine, NN)
+        + dot(shard_half(normed, 1 - shard), pair_other, NN)
+    ).astype(bf16)
+    sent, out = after((plain(jnp.concatenate([up, down], 1)), plain(out)), pair_mine)
+    landed, far, outs_near, hot, bounds = lax.optimization_barrier(
         (
             heads_out(pair),
-            swap(jnp.concatenate([up, down], 1), "tp", 2),
-            [out] + [swap(out, "tp", k) for k in range(1, planes)],
+            swap(sent, "tp", 2),
+            [swap(out, "tp", k) for k in range(1, planes)],
+            into_places(places, bucket_hot(buckets)),
+            doc_bounds(segments),
         )
     )
-    outs_wide = jnp.zeros((planes,) + out.shape, bf16)
-    for k in range(planes):
-        outs_wide = lax.dynamic_update_slice_in_dim(outs_wide, outs_near[k][None], plane ^ k, 0)
-    outs_wide = outs_wide.transpose(1, 0, 2).reshape(out.shape[0], -1)
-    wide = jnp.concatenate([up, far[:, :units], down, far[:, units:], outs_wide], 1)
-    whole = lax.all_gather(wide, ("shard", "ctx"), axis=0, tiled=True)
+    wide = pack_weights(sent, far, [out] + outs_near, plane)
+    whole = lax.all_gather(after(wide, landed), ("shard", "ctx"), axis=0, tiled=True)
     up_full, down_full, output_full = (
         whole[:, : 2 * units],
         whole[:, 2 * units : 4 * units],
@@ -933,40 +1061,46 @@
 
     sorted_pair = into_places(places, landed)
     query_sorted, value_sorted = sorted_pair[:, :DH], sorted_pair[:, DH:]
+    bounds = with_bound(bounds, query_sorted)
     (first_rows, second_grad_rows), (mix, logs) = rows_in(
         after(jnp.stack([first_half, second_cotangent]), landed),
         attend(bounds, query_sorted, value_sorted, hot),
     )
-    far_grad_rows, attention = lax.optimization_barrier(
-        (
-            swap(after(second_grad_rows, mix), "tp", 1),
-            heads_back(out_of_places(places, mix.T.astype(bf16))),
-        )
-    )
+    far_grad_rows = swap(after(second_grad_rows, mix), "tp", 1)
+    attention = heads_back(out_of_places(places, mix.T.astype(bf16)))
 
     first_out = (first_rows.astype(f32) + dot(attention, output_full, NT)).astype(bf16)
     ffn_in, ffn_scaled, ffn_inverse = norm_rows(first_out.astype(f32), forward_gain, forward_shift)
-    ffn_in = ffn_in.astype(bf16)
+    ffn_in, far_grad_rows = lax.optimization_barrier((ffn_in.astype(bf16), far_grad_rows))
 
     def units_of(rows, grad_rows):
-        exact, pull = jax.vjp(smooth_unit, dot(rows, up_full, NN) + unit_bias)
-        pre_grad = pull(dot(grad_rows, down_full, NN))[0].astype(bf16)
-        return exact.astype(bf16), pre_grad
-
-    (first_grad_rows,), (far_in, (hidden, pre_grad)) = rows_in(
-        after(first_cotangent, first_out)[None],
-        (swap(ffn_in, "tp", 1), units_of(ffn_in, second_grad_rows)),
-    )
-    far_hidden, far_pre_grad = units_of(far_in, far_grad_rows)
+        pre_act = dot(rows, up_full, NN) + unit_bias
+        below = 0.5 * (1.0 + lax.erf(pre_act * 2**-0.5))
+        slope = below + pre_act * (jnp.exp(-0.5 * pre_act * pre_act) * (2 * jnp.pi) ** -0.5)
+        pre_grad = (dot(grad_rows, down_full, NN) * slope).astype(bf16)
+        return (pre_act * below).astype(bf16), pre_grad
+
+    normed_all = lax.all_gather(after(normed, first_out), ("ctx", "shard"), axis=0, tiled=True)
+    far_in, (hidden, pre_grad) = lax.optimization_barrier(
+        (swap(ffn_in, "tp", 1), units_of(ffn_in, second_grad_rows))
+    )
+    (first_grad_rows,), (far_hidden, far_pre_grad) = rows_in(
+        after(first_cotangent, far_in)[None], units_of(far_in, far_grad_rows)
+    )
     far_ffn_grad = dot(far_pre_grad, up_full, NT).astype(bf16)
+    all_rows = jnp.concatenate([ffn_in, far_in], 0)
+    all_grad_rows = jnp.concatenate([second_grad_rows, far_grad_rows], 0)
     all_pre_grad = jnp.concatenate([pre_grad, far_pre_grad], 0)
     all_hidden = jnp.concatenate([hidden, far_hidden], 0)
-    theirs, ffn_grad, expand_sums, shrink_sums = lax.optimization_barrier(
+    all_rows, all_grad_rows, pre_grad = after((all_rows, all_grad_rows, pre_grad), far_ffn_grad)
+    theirs, far_branch, own_branch, ffn_grad, expand_sums, shrink_sums = lax.optimization_barrier(
         (
             swap(far_ffn_grad, "tp", 1),
+            dot(far_hidden, down_full, NT).astype(bf16),
+            second_rows.astype(f32) + dot(hidden, down_full, NT) + row_bias,
             dot(pre_grad, up_full, NT),
-            chip_sums(jnp.concatenate([ffn_in, far_in], 0), all_pre_grad).astype(bf16),
-            chip_sums(jnp.concatenate([second_grad_rows, far_grad_rows], 0), all_hidden).astype(bf16),
+            chip_sums(all_rows, all_pre_grad).astype(bf16),
+            chip_sums(all_grad_rows, all_hidden).astype(bf16),
         )
     )
     ffn_back, ffn_gain_grad, ffn_shift_grad = row_norm_back(
@@ -976,84 +1110,109 @@
     attention_grad = dot(first_grad, output_full, NN).astype(bf16)
     shrink_bias_grad = jnp.sum(second_grad_rows.astype(f32), 0)
     expand_bias_grad = jnp.sum(all_pre_grad.astype(f32), 0)
-    far_branch = swap(dot(far_hidden, down_full, NT).astype(bf16), "tp", 1)
-    second_out = (
-        second_rows.astype(f32) + dot(hidden, down_full, NT) + far_branch.astype(f32) + row_bias
-    ).astype(bf16)
-
-    outs = jnp.stack([first_out, second_out])
-    early = jnp.concatenate(
-        [expand_sums, shrink_sums, chip_sums(first_grad, attention).astype(bf16)], 1
-    )
-    grad_heads, outs, early = lax.optimization_barrier((heads_out(attention_grad), outs, early))
-    early_mine = lax.psum_scatter(early, "ctx", scatter_dimension=0, tiled=True)
-    outs_sliced, parts = rows_out(
-        outs,
-        seqs_here,
-        attend_back(
-            bounds, query_sorted, value_sorted, hot, into_places(places, grad_heads), mix, logs
-        ),
-    )
-    pair_grad_heads = out_of_places(places, jnp.concatenate(parts, 1))
-    far_sums = jnp.concatenate(
-        [early_mine[:, units : 2 * units], early_mine[:, 3 * units : 4 * units]], 1
-    )
-    near_sums = jnp.concatenate([early_mine[:, :units], early_mine[:, 2 * units : 3 * units]], 1)
-    first_grad_sliced, (pair_grad, far_sums) = rows_out(
-        after(first_grad, pair_grad_heads)[None],
-        seqs_here,
-        (heads_back(pair_grad_heads), swap(far_sums, "tp", 2)),
-    )
-    early_own = (near_sums.astype(f32) + far_sums.astype(f32)).astype(bf16)
-    early_own = lax.all_gather(early_own, "ctx", axis=0, tiled=True).astype(f32)
-    expand_own, shrink_own = early_own[:, :units], early_own[:, units:].T
-
-    pair_sums = chip_sums(normed, pair_grad).astype(bf16)
-    normed_grad = dot(pair_grad, pair_full, NT)
-    attn_back, attn_gain_grad, attn_shift_grad = row_norm_back(
-        normed_grad, attn_scaled, attn_inverse, attention_gain
-    )
-    second_grad = (second_grad_rows.astype(f32) + attn_back).astype(bf16)
-
-    row_grads = jnp.stack(
-        [shrink_bias_grad, attn_gain_grad, attn_shift_grad, ffn_gain_grad, ffn_shift_grad]
-    )
+    far_branch = swap(far_branch, "tp", 1)
+
     spread = jnp.arange(planes, dtype=jnp.int32)[:, None]
     unit_grads = jnp.where(spread == plane, expand_bias_grad[None, :units], 0.0)
     unit_grads = jnp.where(spread == plane ^ 2, expand_bias_grad[None, units:], unit_grads)
     packed = jnp.concatenate(
-        [unit_grads, row_grads.reshape(5, planes, width).transpose(1, 0, 2).reshape(planes, -1)], 1
-    )
-    quarters = lax.axis_size("ctx")
-    packed = (packed + swap(packed, "shard", 1)).astype(bf16)
-    packed = packed.reshape(planes, quarters, -1)
+        [unit_grads]
+        + [item.reshape(planes, width) for item in (shrink_bias_grad, ffn_gain_grad, ffn_shift_grad)],
+        1,
+    )
+    packed = (packed + swap(packed, "shard", 1)).astype(bf16).reshape(planes, quarters, -1)
     vector_width = packed.shape[2]
-    packed = jnp.pad(packed, ((0, 0), (0, 0), (0, 32 * width - vector_width)))
-    packed = packed.reshape(planes, quarters, 16, 2 * width).transpose(1, 2, 0, 3)
-    late = jnp.concatenate(
-        [pair_sums.reshape(quarters, split // quarters, -1), packed.reshape(quarters, 16, -1)], 1
-    )
-    second_grad_sliced, late = rows_out(
-        second_grad[None], seqs_here, sum_parts(lax.all_to_all(late, "ctx", 0, 0, tiled=True))
-    )
-    late = late.astype(bf16).reshape(-1, planes, 2 * width)
-    late = jnp.concatenate(
-        [late, jnp.pad(early_mine[:, 4 * units :].reshape(-1, planes, width), ((0, 16), (0, 0), (0, 0)))], 2
-    )
-    late_own = collect_ctx(scatter_tp(late.reshape(late.shape[0], -1)).astype(bf16)).astype(f32)
-    late_own = late_own.reshape(quarters, -1, 3 * width)
-    owned = late_own[:, split // quarters :, : 2 * width].reshape(quarters, -1)
-    owned = owned[:, :vector_width].reshape(-1)
-    late_own = late_own[:, : split // quarters].reshape(split, -1)
-    pair_own = late_own[:, : 2 * width].reshape(split, -1, 2, DH)
-    query_own = pair_own[:, :, 0].reshape(query_weight.shape)
-    value_own = pair_own[:, :, 1].reshape(value_weight.shape)
-    output_own = late_own[:, 2 * width :].T
-    row_own = owned[units:].reshape(5, width)
+    packed = jnp.pad(packed, ((0, 0), (0, 0), (0, 16 * width - vector_width)))
+    packed = packed.reshape(planes, quarters, 16, width).transpose(1, 2, 0, 3)
+    packed = jnp.pad(packed.reshape(quarters, 16, -1), ((0, 0), (0, 0), (4 * units, 0)))
+    early = jnp.concatenate(
+        [expand_sums, shrink_sums, chip_sums(first_grad, attention).astype(bf16)], 1
+    )
+    early = jnp.concatenate([early.reshape(quarters, split // quarters, -1), packed], 1)
+    early = early.reshape(-1, early.shape[2])
+    grad_heads, early, normed_all = lax.optimization_barrier(
+        (heads_out(attention_grad), early, normed_all)
+    )
+    early_mine = lax.psum_scatter(early, "ctx", scatter_dimension=0, tiled=True)
+    outs_sliced, parts = rows_out(
+        after(jnp.stack([first_out, first_grad]), grad_heads),
+        seqs_here,
+        attend_back(
+            bounds, query_sorted, value_sorted, hot, into_places(places, grad_heads), mix, logs
+        ),
+    )
+    far_branch, own_branch = after((far_branch, own_branch), parts)
+    second_out = (own_branch + far_branch.astype(f32)).astype(bf16)
+    pair_grad_heads = out_of_places(places, jnp.concatenate(parts, 1))
+    early_mine = after(early_mine, pair_grad_heads)
+    far_sums = jnp.concatenate(
+        [early_mine[:, units : 2 * units], early_mine[:, 3 * units : 4 * units]], 1
+    )
+    near_sums = jnp.concatenate([early_mine[:, :units], early_mine[:, 2 * units : 3 * units]], 1)
+
+    pair_sums = lax.dot_general(
+        normed_all, pair_grad_heads, (((0,), (0,)), ((), ())), preferred_element_type=f32
+    ).astype(bf16)
+    late = early_mine[:, 4 * units :].reshape(-1, planes, width).transpose(1, 0, 2)
+    late = jnp.concatenate([pair_sums.reshape(planes, -1, 2 * DH), late], 1)
+    second_out_sliced, (pair_grad, far_sums) = rows_out(
+        second_out[None], seqs_here, (heads_back(pair_grad_heads), swap(far_sums, "tp", 2))
+    )
+    grad_mine, grad_other = dot(pair_grad, pair_mine, NT), dot(pair_grad, pair_other, NT)
+    normed_grad = jnp.concatenate(
+        [
+            jnp.where(shard == 0, grad_mine, grad_other),
+            jnp.where(shard == 0, grad_other, grad_mine),
+        ],
+        1,
+    )
+    attn_back, attn_gain_grad, attn_shift_grad = row_norm_back(
+        normed_grad, attn_scaled, attn_inverse, attention_gain
+    )
+    second_grad = (second_grad_rows.astype(f32) + attn_back).astype(bf16)
+
+    early_own = (near_sums.astype(f32) + far_sums.astype(f32)).astype(bf16)
+    early_own = early_own[: split // quarters]
+    second_grad_sliced, (early_pieces, late_pieces) = rows_out(
+        second_grad[None],
+        seqs_here,
+        (
+            [swap(early_own, "ctx", j) for j in range(1, quarters)],
+            [swap(plane_part(late, k), "tp", k) for k in range(1, planes)],
+        ),
+    )
+    early_own = pack_rows([early_own] + early_pieces, ctx).astype(f32)
+    expand_own, shrink_own = early_own[:, :units], early_own[:, units:].T
+    late = plane_part(late, 0).astype(f32)
+    late = sum((piece.astype(f32) for piece in late_pieces), late).astype(bf16)
+
+    split_at = width
+    turned = lax.ppermute(
+        late[:split_at],
+        ("ctx", "tp"),
+        [(at * planes + to, to * planes + at) for at in range(quarters) for to in range(planes)],
+    )
+    late_own = collect_ctx(jnp.concatenate([turned, late[split_at:]], 0)[None])
+    pair_head = late_own[:, :split_at].reshape(-1, width)
+    late_own = late_own[:, split_at:].astype(f32)
+    output_own = late_own[:, : split // quarters].reshape(split, width).T
+    owned = late_own[:, split // quarters :].reshape(quarters, -1)[:, :vector_width].reshape(-1)
+    row_own = owned[units:].reshape(3, width)
+    near = lax.dynamic_slice_in_dim(pair_head, shard * split, split, 0)
+    other = swap(lax.dynamic_slice_in_dim(pair_head, (1 - shard) * split, split, 0), "shard", 1)
+    pair_own = by_half(near, other).astype(f32)
+    query_own = jnp.concatenate([pair_own[0, :, :DH], pair_own[1, :, :DH]], 1)
+    value_own = jnp.concatenate([pair_own[0, :, DH:], pair_own[1, :, DH:]], 1)
+
+    norm_grads = jnp.concatenate(
+        [attn_gain_grad.reshape(planes, width), attn_shift_grad.reshape(planes, width)], 1
+    )
+    norm_own = sum_everywhere(after(norm_grads, second_grad_sliced))
+    norm_own = norm_own.reshape(2, width)
     return (
         outs_sliced[0],
+        second_out_sliced[0],
         outs_sliced[1],
-        first_grad_sliced[0],
         second_grad_sliced[0],
         query_own,
         value_own,
@@ -1062,10 +1221,10 @@
         owned[:units],
         shrink_own,
         row_own[0],
+        norm_own[0],
+        norm_own[1],
         row_own[1],
         row_own[2],
-        row_own[3],
-        row_own[4],
     )
 
 

time: 667 us -> 609 us (0.913)
  starting transfers between devices: 102 us -> 140 us
  local copies, waits for them, and re-layouts: 98.2 us -> 66.8 us
  Pallas kernels: 74 us -> 45.2 us
  waiting for transfers between devices: 166 us -> 138 us
  matrix products: 159 us -> 151 us
  blocking collectives: 7.48 us -> 0 us
  other arithmetic: 35.9 us -> 42.7 us
    ppermute x23 -> x39, starting transfers between devices: 16.3 us -> 55.2 us  [swap(): return lax.ppermute(vectors, axis, [(at, at ^ bits) for at in range(size)])]
    ppermute x12, waiting for transfers between devices: 17.7 us -> 45.5 us  [rows_in(): lax.ppermute(chunk, ('shard', 'tp'), plane_pairs(step, False))]
    ppermute x12, waiting for transfers between devices: 37.2 us -> 17.6 us  [rows_out(): landed.append(lax.ppermute(piece, ('shard', 'tp'), plane_pairs(step, True)))]
    pallas_call x1, Pallas kernels: 35.4 us -> 16.3 us  [attend(): pl.pallas_call(attend_kernel, name='attend', out_shape=(jax.ShapeDtypeStr...]
    all_to_all x2 -> x0, waiting for transfers between devices: 17.2 us -> none  [the longest x1 13.2 us: row_device(): lax.all_to_all(late, 'ctx', 0, 0, tiled=True)]
    ppermute x23 -> x39, waiting for transfers between devices: 77.1 us -> 62.5 us  [swap(): return lax.ppermute(vectors, axis, [(at, at ^ bits) for at in range(size)])]
    dot_general x8 -> x6, matrix products: 30 us -> 17.2 us  [product(): lax.dot_general(shard_half(rows_wide, at), columns_wide, (((0,), (0,)), (...]
    pallas_call x1, Pallas kernels: 38.6 us -> 27.3 us  [attend_back(): pl.pallas_call(attend_back_kernel, name='attend_back', out_shape=(jax.Sha...]
  transfers between devices with their start and end apart: 56 -> 71, of which waited for: 16 -> 22; matrix products, arithmetic and copies ran while one was open for 33% -> 39% of each run, Pallas kernels for 11% -> 7%
where the time goes in v3:
time: 609 us; the launch traced here: 600 us
  matrix products  151 us (25%)
  starting transfers between devices  140 us (23%)
  waiting for transfers between devices  138 us (23%)
  local copies, waits for them, and re-layouts  66.8 us (11%)
  Pallas kernels  45.2 us (7%)
  other arithmetic  42.7 us (7%)
  between operations  16.9 us (3%)
    ppermute x39, waiting for transfers between devices, swap(): return lax.ppermute(vectors, axis, [(at, at ^ bits) for at in range(size)])  62.5 us
    dot_general x14, matrix products, dot(): lax.dot_general(left, right, dims, preferred_element_type=jnp.float32)  59.5 us
    ppermute x39, starting transfers between devices, swap(): return lax.ppermute(vectors, axis, [(at, at ^ bits) for at in range(size)])  55.2 us
    ppermute x12, waiting for transfers between devices, rows_in(): lax.ppermute(chunk, ('shard', 'tp'), plane_pairs(step, False))  45.5 us
    dot_general x3, matrix products, into_places(): jnp.einsum('pa,ad->pd', place_matrix(places), vectors, preferred_element_...  40.8 us
    ppermute x12, starting transfers between devices, rows_in(): lax.ppermute(chunk, ('shard', 'tp'), plane_pairs(step, False))  30.8 us
    ppermute x12, starting transfers between devices, rows_out(): landed.append(lax.ppermute(piece, ('shard', 'tp'), plane_pairs(step, True)))  30.8 us
    unnamed x145, local copies, waits for them, and re-layouts  28.3 us
  transfers between devices with their start and end apart: 71, of which 22 were waited for; matrix products, arithmetic and copies ran while one was open for 39% of the time, Pallas kernels for 7%

profile of v3, /device:TPU:1, one launch (start us, length us, event | category | flops | bytes accessed | tf_op | source)
XLA Modules:
  0.0 600.1 jit_solution(3113329405952389606)
XLA Ops:
  13.0 5.6 collective-permute-start.1
  23.2 4.3 collective-permute-done.1
  27.5 8.6 %collective-permute-done.2 = bf16[784,256]{1,0:T(8,128)(2,1)S(1)} collective-permute-done((bf16[784,256]{1,0:T(8,128)(2,1)}, bf16[784,256]{1,0:T(8,128)(2,1)S(1)}, u32[]{:S(2)}, u32[]{:S(2)}) %collective-permute-start.2) | collective-permute-done | bytes 401440 | tf_op jit(solution)/shard_map/ppermute | solution.py:749
  36.1 6.9 %collective-permute-done.3 = bf16[784,256]{1,0:T(8,128)(2,1)S(1)} collective-permute-done((bf16[784,256]{1,0:T(8,128)(2,1)S(1)}, bf16[784,256]{1,0:T(8,128)(2,1)S(1)}, u32[]{:S(2)}, u32[]{:S(2)}) %collective-permute-start.3) | collective-permute-done | bytes 401440 | tf_op jit(solution)/shard_map/ppermute | solution.py:749
  42.9 11.9 %collective-permute-done.4 = bf16[784,256]{1,0:T(8,128)(2,1)S(1)} collective-permute-done((bf16[784,256]{1,0:T(8,128)(2,1)S(1)}, bf16[784,256]{1,0:T(8,128)(2,1)S(1)}, u32[]{:S(2)}, u32[]{:S(2)}) %collective-permute-start.4) | collective-permute-done | bytes 401440 | tf_op jit(solution)/shard_map/ppermute | solution.py:749
  69.6 10.0 %collective-permute-done.9 = s32[48,128]{1,0:T(8,128)S(1)} collective-permute-done((s32[48,128]{1,0:T(8,128)S(1)}, s32[48,128]{1,0:T(8,128)S(1)}, u32[]{:S(2)}, u32[]{:S(2)}) %collective-permute-start.9) | collective-permute-done | bytes 24608 | tf_op jit(solution)/shard_map/ppermute | solution.py:716
  103.5 4.8 all-to-all-start
  108.5 15.6 %fusion.14.hot_ref = bf16[4096,256]{1,0:T(8,128)(2,1)} fusion(pred[4096,256]{0,1:T(32,128)(4,1)} %bitcast_compare_fusion, s32[4096]{0:T(1024)S(1)} %bitcast.292), kind=kOutput, calls=%fused_computation.19 | convolution fusion | flops 8607760384 | bytes 3162112 | tf_op jit(solution)/shard_map/pa,ad->pd/dot_general | solution.py:308
  124.3 7.2 %all-to-all-done = bf16[8,512,256]{2,1,0:T(8,128)(2,1)S(1)} async-done(((bf16[8,512,256]{2,1,0:T(8,128)(2,1)}), bf16[8,512,256]{2,1,0:T(8,128)(2,1)S(1)}, u32[]{:S(2)}, u32[]{:S(2)}) %all-to-all-start) | async-done | bytes 2097184 | tf_op jit(solution)/shard_map/all_to_all | solution.py:895
  133.2 4.7 pad_maximum_fusion.1
  140.4 8.0 %collective-permute-start.17 = (bf16[1024,256]{1,0:T(8,128)(2,1)}, bf16[1024,256]{1,0:T(8,128)(2,1)S(1)}, u32[]{:S(2)}, u32[]{:S(2)}) collective-permute-start(bf16[1024,256]{1,0:T(8,128)(2,1)} %get-tuple-element.279), channel_id=1, source_target_pairs={{0,0},{1,16},{2,1},{3,17},{16,2},{17,18},{18,3},{19,19},{4,4},{5,2... | collective-permute-start | bytes 1572872 | tf_op jit(solution)/shard_map/ppermute | solution.py:749
  153.1 12.2 %fusion.15 = bf16[4096,256]{1,0:T(8,128)(2,1)S(1)} fusion(bf16[4096,256]{1,0:T(8,128)(2,1)S(1)} %bitcast.263, s32[4096]{0:T(1024)S(1)} %bitcast.293), kind=kOutput, calls=%fused_computation.20 | convolution fusion | flops 8607760384 | bytes 4210688 | tf_op jit(solution)/shard_map/pa,ad->pd/dot_general | solution.py:308
  169.0 16.3 %attend.1 = (f32[128,4096]{1,0:T(8,128)S(1)}, f32[8,512]{1,0:T(8,128)S(1)}) custom-call(s32[4]{0:T(128)S(1)} %pad_add_fusion.bounds_ref, bf16[4096,128]{1,0:T(8,128)(2,1)S(1)} %get-tuple-element.275.q_ref, bf16[4096,128]{1,0:T(8,128)(2,1)S(1)} %get-tuple-element.274.v_ref, bf16[4096,256]{1,0:T(8,128)(2,1)S(1)} %copy-done.4), custom_call_target="tpu_custom_call" | custom-call | flops 524288 | bytes 524288 | tf_op jit(solution)/shard_map/attend/pallas_call | solution.py:150
  185.4 9.2 %collective-permute-done.20 = bf16[1024,256]{1,0:T(8,128)(2,1)} collective-permute-done((bf16[1024,256]{1,0:T(8,128)(2,1)}, bf16[1024,256]{1,0:T(8,128)(2,1)}, u32[]{:S(2)}, u32[]{:S(2)}) %collective-permute-start.20) | collective-permute-done | bytes 524320 | tf_op jit(solution)/shard_map/ppermute | solution.py:749
  194.6 9.3 %fusion.17 = bf16[4096,128]{1,0:T(8,128)(2,1)S(1)} fusion(s32[4096]{0:T(1024)S(1)} %bitcast.294, f32[128,4096]{1,0:T(8,128)S(1)} %get-tuple-element.130.out_ref), kind=kOutput, calls=%fused_computation.22 | convolution fusion | flops 4329570304 | bytes 3162112 | tf_op jit(solution)/shard_map/pa,pd->ad/dot_general | solution.py:312
  205.3 3.7 all-to-all-start.1
  221.9 4.0 convert_reduce_fusion.3
  227.8 15.8 %collective-permute-done.21 = bf16[512,1024]{1,0:T(8,128)(2,1)} collective-permute-done((bf16[512,1024]{1,0:T(8,128)(2,1)}, bf16[512,1024]{1,0:T(8,128)(2,1)}, u32[]{:S(2)}, u32[]{:S(2)}) %collective-permute-start.21) | collective-permute-done | bytes 1048608 | tf_op jit(solution)/shard_map/ppermute | solution.py:716
  243.8 6.4 %multiply_convert_fusion.1 = (bf16[512,2048]{1,0:T(8,128)(2,1)}, f32[512,2048]{1,0:T(8,128)}) fusion(f32[2048]{0:T(1024)S(1)} %pad_maximum_fusion.14, bf16[512,1024]{1,0:T(8,128)(2,1)} %fusion.57, bf16[1024,5120]{1,0:T(8,128)(2,1)} %all-gather.3.cloned.1.call-done), kind=kOutput, calls=%fused_computation.41 | convolution fusion | flops 2153775104 | bytes 11542528 | tf_op jit(solution)/shard_map/dot_general | solution.py:30
  252.4 6.9 %fusion.26 = bf16[512,2048]{1,0:T(8,128)(2,1)S(1)} fusion(f32[512,2048]{1,0:T(8,128)} %get-tuple-element.330, bf16[1024,5120]{1,0:T(8,128)(2,1)} %all-gather.3.cloned.1.call-done, f32[2048]{0:T(1024)S(1)} %pad_maximum_fusion.14, bf16[1024,1024]{1,0:T(8,128)(2,1)} %constant_dynamic-update-slice_fusion.8), kind=kOutput, calls=%fused_computation.29 | convolution fusion | flops 2159017984 | bytes 11542528 | tf_op jit(solution)/shard_map/dot_general | solution.py:30
  259.3 8.5 %collective-permute-done.22 = bf16[512,1024]{1,0:T(8,128)(2,1)} collective-permute-done((bf16[512,1024]{1,0:T(8,128)(2,1)}, bf16[512,1024]{1,0:T(8,128)(2,1)}, u32[]{:S(2)}, u32[]{:S(2)}) %collective-permute-start.22) | collective-permute-done | bytes 1048608 | tf_op jit(solution)/shard_map/ppermute | solution.py:716
  277.9 4.1 multiply_convert_fusion
  282.0 3.7 fusion.66
  285.7 5.6 fusion.32
  291.9 4.6 collective-permute-done.26
  296.5 4.7 fusion.79
  308.3 5.5 fusion.82
  313.8 4.5 fusion.39
  318.4 4.1 add_convert_fusion
  322.4 3.9 add_convert_fusion.1
  336.1 4.2 all-to-all-start.2
  345.3 4.4 fusion.13
  355.5 5.7 collective-permute-start.32
  361.8 4.4 collective-permute-start.35
  366.2 13.1 %fusion.20.grad_ref = bf16[4096,128]{1,0:T(8,128)(2,1)S(1)} fusion(bf16[4096,128]{1,0:T(8,128)(2,1)} %bitcast.63, s32[4096]{0:T(1024)S(1)} %bitcast.295), kind=kOutput, calls=%fused_computation.23 | convolution fusion | flops 4312268800 | bytes 2113536 | tf_op jit(solution)/shard_map/pa,ad->pd/dot_general | solution.py:308
  379.3 27.3 %attend_back.1 = (bf16[4096,128]{1,0:T(8,128)(2,1)S(1)}, bf16[4096,128]{1,0:T(8,128)(2,1)S(1)}) custom-call(s32[4]{0:T(128)S(1)} %pad_add_fusion.bounds_ref, bf16[4096,128]{1,0:T(8,128)(2,1)S(1)} %get-tuple-element.275.q_ref, bf16[4096,128]{1,0:T(8,128)(2,1)S(1)} %get-tuple-element.274.v_ref, bf16[4096,256]{1,0:T(8,128)(2,1)} %fusion.14.hot_ref, ...), custom_call_target="tpu_custom_call" | custom-call | flops 524288 | bytes 524288 | tf_op jit(solution)/shard_map/attend_back/pallas_call | solution.py:273
  407.2 18.3 %fusion.16 = bf16[4096,256]{1,0:T(8,128)(2,1)S(1)} fusion(s32[4096]{0:T(1024)S(1)} %bitcast.296, bf16[4096,128]{1,0:T(8,128)(2,1)S(1)} %get-tuple-element.169, bf16[4096,128]{1,0:T(8,128)(2,1)S(1)} %get-tuple-element.168), kind=kOutput, calls=%fused_computation.21 | convolution fusion | flops 8611954688 | bytes 4210688 | tf_op jit(solution)/shard_map/pa,pd->ad/dot_general | solution.py:312
  428.2 9.6 %all-to-all-start.3 = ((bf16[8,512,256]{1,2,0:T(8,128)(2,1)}), bf16[8,512,256]{1,2,0:T(8,128)(2,1)}, u32[]{:S(2)}, u32[]{:S(2)}) async-start(bf16[8,512,256]{1,2,0:T(8,128)(2,1)} %copy.125), calls=%async_computation.3 | async-start | bytes 4194304 | tf_op jit(solution)/shard_map/all_to_all | solution.py:901
  444.6 3.6 collective-permute-start.39
  452.1 5.8 convolution_convert_fusion.3
  469.0 10.1 %collective-permute-done.38 = bf16[512,256]{1,0:T(8,128)(2,1)} collective-permute-done((bf16[512,256]{1,0:T(8,128)(2,1)}, bf16[512,256]{1,0:T(8,128)(2,1)}, u32[]{:S(2)}, u32[]{:S(2)}) %collective-permute-start.38) | collective-permute-done | bytes 262176 | tf_op jit(solution)/shard_map/ppermute | solution.py:775
  479.2 17.3 %collective-permute-done.41 = bf16[144,2048]{1,0:T(8,128)(2,1)} collective-permute-done((bf16[144,2048]{1,0:T(8,128)(2,1)}, bf16[144,2048]{1,0:T(8,128)(2,1)}, u32[]{:S(2)}, u32[]{:S(2)}) %collective-permute-start.41) | collective-permute-done | bytes 589856 | tf_op jit(solution)/shard_map/ppermute | solution.py:716
  496.5 3.7 fusion.137
  533.5 3.5 collective-permute-start.44
  537.1 4.6 collective-permute-start.45
  542.5 6.4 %collective-permute-done.45 = bf16[512,256]{1,0:T(8,128)(2,1)S(1)} collective-permute-done((bf16[512,256]{1,0:T(8,128)(2,1)S(1)}, bf16[512,256]{1,0:T(8,128)(2,1)S(1)}, u32[]{:S(2)}, u32[]{:S(2)}) %collective-permute-start.45) | collective-permute-done | bytes 262176 | tf_op jit(solution)/shard_map/ppermute | solution.py:775
  552.9 18.5 %collective-permute-start.53 = (bf16[1,400,256]{2,1,0:T(8,128)(2,1)S(1)}, bf16[1,400,256]{2,1,0:T(8,128)(2,1)}, u32[]{:S(2)}, u32[]{:S(2)}) collective-permute-start(bf16[1,400,256]{2,1,0:T(8,128)(2,1)S(1)} %maximum_bitcast_fusion), channel_id=1, source_target_pairs={{0,4},{4,0},{8,12},{12,8},{1,5},{5,1},{9,13},{13,9},{2,6},{6,2},{1... | collective-permute-start | bytes 614408 | tf_op jit(solution)/shard_map/ppermute | solution.py:716
  579.2 8.2 %collective-permute-done.54 = bf16[1,400,256]{2,1,0:T(8,128)(2,1)S(1)} collective-permute-done((bf16[1,400,256]{2,1,0:T(8,128)(2,1)S(1)}, bf16[1,400,256]{2,1,0:T(8,128)(2,1)S(1)}, u32[]{:S(2)}, u32[]{:S(2)}) %collective-permute-start.54) | collective-permute-done | bytes 204832 | tf_op jit(solution)/shard_map/ppermute | solution.py:716
  (452 shorter events, 194.2 us)
Async XLA Ops:
  13.0 14.5 %collective-permute-start.1 = (bf16[784,256]{1,0:T(8,128)(2,1)}, bf16[784,256]{1,0:T(8,128)(2,1)S(1)}, u32[]{:S(2)}, u32[]{:S(2)}) collective-permute-start(bf16[784,256]{1,0:T(8,128)(2,1)} %get-tuple-element.283), channel_id=1, source_target_pairs={{0,0},{1,16},{2,1},{3,17},{16,2},{17,18},{18,3},{19,19},{4,4},{5,2... | collective-permute-start | bytes 1204232 | tf_op jit(solution)/shard_map/ppermute | solution.py:749
  18.6 17.5 %collective-permute-start.2 = (bf16[784,256]{1,0:T(8,128)(2,1)}, bf16[784,256]{1,0:T(8,128)(2,1)S(1)}, u32[]{:S(2)}, u32[]{:S(2)}) collective-permute-start(bf16[784,256]{1,0:T(8,128)(2,1)} %get-tuple-element.282), channel_id=1, source_target_pairs={{0,16},{1,0},{2,17},{3,1},{16,18},{17,2},{18,19},{19,3},{4,20},{5,... | collective-permute-start | bytes 1204232 | tf_op jit(solution)/shard_map/ppermute | solution.py:749
  19.9 23.0 %collective-permute-start.3 = (bf16[784,256]{1,0:T(8,128)(2,1)S(1)}, bf16[784,256]{1,0:T(8,128)(2,1)S(1)}, u32[]{:S(2)}, u32[]{:S(2)}) collective-permute-start(bf16[784,256]{1,0:T(8,128)(2,1)S(1)} %get-tuple-element.281), channel_id=1, source_target_pairs={{0,1},{1,17},{2,0},{3,16},{16,3},{17,19},{18,2},{19,18},{4,5},{5,2... | collective-permute-start | bytes 1204232 | tf_op jit(solution)/shard_map/ppermute | solution.py:749
  20.1 34.7 %collective-permute-start.4 = (bf16[784,256]{1,0:T(8,128)(2,1)S(1)}, bf16[784,256]{1,0:T(8,128)(2,1)S(1)}, u32[]{:S(2)}, u32[]{:S(2)}) collective-permute-start(bf16[784,256]{1,0:T(8,128)(2,1)S(1)} %get-tuple-element.280), channel_id=1, source_target_pairs={{0,17},{1,1},{2,16},{3,0},{16,19},{17,3},{18,18},{19,2},{4,21},{5,... | collective-permute-start | bytes 1204232 | tf_op jit(solution)/shard_map/ppermute | solution.py:749
  56.8 26.5 %collective-permute-start.5 = (bf16[128,2048]{1,0:T(8,128)(2,1)S(1)}, bf16[128,2048]{1,0:T(8,128)(2,1)S(1)}, u32[]{:S(2)}, u32[]{:S(2)}) collective-permute-start(bf16[128,2048]{1,0:T(8,128)(2,1)S(1)} %bitcast.232), channel_id=1, source_target_pairs={{0,4},{4,0},{8,12},{12,8},{1,5},{5,1},{9,13},{13,9},{2,6},{6,2},{1... | collective-permute-start | bytes 1572872 | tf_op jit(solution)/shard_map/ppermute | solution.py:716
  58.0 26.0 %collective-permute-start.6 = (bf16[128,2048]{1,0:T(8,128)(2,1)S(1)}, bf16[128,2048]{1,0:T(8,128)(2,1)S(1)}, u32[]{:S(2)}, u32[]{:S(2)}) collective-permute-start(bf16[128,2048]{1,0:T(8,128)(2,1)S(1)} %bitcast.233), channel_id=1, source_target_pairs={{0,8},{4,12},{8,0},{12,4},{1,9},{5,13},{9,1},{13,5},{2,10},{6,14},... | collective-permute-start | bytes 1572872 | tf_op jit(solution)/shard_map/ppermute | solution.py:716
  59.3 25.5 %collective-permute-start.7 = (bf16[128,2048]{1,0:T(8,128)(2,1)S(1)}, bf16[128,2048]{1,0:T(8,128)(2,1)S(1)}, u32[]{:S(2)}, u32[]{:S(2)}) collective-permute-start(bf16[128,2048]{1,0:T(8,128)(2,1)S(1)} %bitcast.234), channel_id=1, source_target_pairs={{0,12},{4,8},{8,4},{12,0},{1,13},{5,9},{9,5},{13,1},{2,14},{6,10},... | collective-permute-start | bytes 1572872 | tf_op jit(solution)/shard_map/ppermute | solution.py:716
  92.5 31.8 %collective-permute-start.14 = (bf16[128,256]{1,0:T(8,128)(2,1)S(1)}, bf16[128,256]{1,0:T(8,128)(2,1)S(1)}, u32[]{:S(2)}, u32[]{:S(2)}) collective-permute-start(bf16[128,256]{1,0:T(8,128)(2,1)S(1)} %bitcast.236), channel_id=1, source_target_pairs={{0,1},{1,0},{2,3},{3,2},{4,5},{5,4},{6,7},{7,6},{8,9},{9,8},{10,11... | collective-permute-start | bytes 196616 | tf_op jit(solution)/shard_map/ppermute | solution.py:716
  92.6 31.7 %collective-permute-start.15 = (bf16[128,256]{1,0:T(8,128)(2,1)S(1)}, bf16[128,256]{1,0:T(8,128)(2,1)S(1)}, u32[]{:S(2)}, u32[]{:S(2)}) collective-permute-start(bf16[128,256]{1,0:T(8,128)(2,1)S(1)} %bitcast.237), channel_id=1, source_target_pairs={{0,2},{1,3},{2,0},{3,1},{4,6},{5,7},{6,4},{7,5},{8,10},{9,11},{10,... | collective-permute-start | bytes 196616 | tf_op jit(solution)/shard_map/ppermute | solution.py:716
  95.0 29.3 %collective-permute-start.16 = (bf16[128,256]{1,0:T(8,128)(2,1)S(1)}, bf16[128,256]{1,0:T(8,128)(2,1)S(1)}, u32[]{:S(2)}, u32[]{:S(2)}) collective-permute-start(bf16[128,256]{1,0:T(8,128)(2,1)S(1)} %bitcast.238), channel_id=1, source_target_pairs={{0,3},{1,2},{2,1},{3,0},{4,7},{5,6},{6,5},{7,4},{8,11},{9,10},{10,... | collective-permute-start | bytes 196616 | tf_op jit(solution)/shard_map/ppermute | solution.py:716
  96.1 28.2 %collective-permute-start.13 = (bf16[128,2048]{1,0:T(8,128)(2,1)S(1)}, bf16[128,2048]{1,0:T(8,128)(2,1)S(1)}, u32[]{:S(2)}, u32[]{:S(2)}) collective-permute-start(bf16[128,2048]{1,0:T(8,128)(2,1)S(1)} %pad_maximum_fusion.9.near_ref), channel_id=1, source_target_pairs={{0,2},{1,3},{2,0},{3,1},{4,6},{5,7},{6,4},{7,5},{8,10},{9,11},{10,... | collective-permute-start | bytes 1572872 | tf_op jit(solution)/shard_map/ppermute | solution.py:716
  103.5 27.9 %all-to-all-start = ((bf16[8,512,256]{2,1,0:T(8,128)(2,1)}), bf16[8,512,256]{2,1,0:T(8,128)(2,1)S(1)}, u32[]{:S(2)}, u32[]{:S(2)}) async-start(bf16[8,512,256]{2,1,0:T(8,128)(2,1)} %bitcast.226), calls=%async_computation | async-start | bytes 4194304 | tf_op jit(solution)/shard_map/all_to_all | solution.py:895
  108.3 112.6 %all-gather.3.cloned.1.call-start = ((), (), s32[]{:S(2)}) async-start(), calls=%async_computation.5 | async-start | bytes 11796480 | tf_op jit(solution)/shard_map/all_gather | solution.py:1055
  140.4 44.9 %collective-permute-start.17 = (bf16[1024,256]{1,0:T(8,128)(2,1)}, bf16[1024,256]{1,0:T(8,128)(2,1)S(1)}, u32[]{:S(2)}, u32[]{:S(2)}) collective-permute-start(bf16[1024,256]{1,0:T(8,128)(2,1)} %get-tuple-element.279), channel_id=1, source_target_pairs={{0,0},{1,16},{2,1},{3,17},{16,2},{17,18},{18,3},{19,19},{4,4},{5,2... | collective-permute-start | bytes 1572872 | tf_op jit(solution)/shard_map/ppermute | solution.py:749
  148.5 36.9 %collective-permute-start.18 = (bf16[1024,256]{1,0:T(8,128)(2,1)}, bf16[1024,256]{1,0:T(8,128)(2,1)S(1)}, u32[]{:S(2)}, u32[]{:S(2)}) collective-permute-start(bf16[1024,256]{1,0:T(8,128)(2,1)} %get-tuple-element.278), channel_id=1, source_target_pairs={{0,16},{1,0},{2,17},{3,1},{16,18},{17,2},{18,19},{19,3},{4,20},{5,... | collective-permute-start | bytes 1572872 | tf_op jit(solution)/shard_map/ppermute | solution.py:749
  148.6 36.8 %collective-permute-start.19 = (bf16[1024,256]{1,0:T(8,128)(2,1)}, bf16[1024,256]{1,0:T(8,128)(2,1)}, u32[]{:S(2)}, u32[]{:S(2)}) collective-permute-start(bf16[1024,256]{1,0:T(8,128)(2,1)} %get-tuple-element.277), channel_id=1, source_target_pairs={{0,1},{1,17},{2,0},{3,16},{16,3},{17,19},{18,2},{19,18},{4,5},{5,2... | collective-permute-start | bytes 1572872 | tf_op jit(solution)/shard_map/ppermute | solution.py:749
  150.8 43.8 %collective-permute-start.20 = (bf16[1024,256]{1,0:T(8,128)(2,1)}, bf16[1024,256]{1,0:T(8,128)(2,1)}, u32[]{:S(2)}, u32[]{:S(2)}) collective-permute-start(bf16[1024,256]{1,0:T(8,128)(2,1)} %get-tuple-element.276), channel_id=1, source_target_pairs={{0,17},{1,1},{2,16},{3,0},{16,19},{17,3},{18,18},{19,2},{4,21},{5,... | collective-permute-start | bytes 1572872 | tf_op jit(solution)/shard_map/ppermute | solution.py:749
  205.3 15.6 %all-to-all-start.1 = ((bf16[8,512,128]{1,2,0:T(8,128)(2,1)}), bf16[8,512,128]{1,2,0:T(8,128)(2,1)S(1)}, u32[]{:S(2)}, u32[]{:S(2)}) async-start(bf16[8,512,128]{1,2,0:T(8,128)(2,1)} %copy.121), calls=%async_computation.1 | async-start | bytes 2097152 | tf_op jit(solution)/shard_map/all_to_all | solution.py:901
  208.9 143.3 %all-gather.5.cloned.1.call-start = ((), (), s32[]{:S(2)}) async-start(), calls=%async_computation.6 | async-start | bytes 9437184 | tf_op jit(solution)/shard_map/all_gather | solution.py:1083
  218.5 25.1 %collective-permute-start.21 = (bf16[512,1024]{1,0:T(8,128)(2,1)}, bf16[512,1024]{1,0:T(8,128)(2,1)}, u32[]{:S(2)}, u32[]{:S(2)}) collective-permute-start(bf16[512,1024]{1,0:T(8,128)(2,1)} %unstack.11), channel_id=1, source_target_pairs={{0,1},{1,0},{2,3},{3,2},{4,5},{5,4},{6,7},{7,6},{8,9},{9,8},{10,11... | collective-permute-start | bytes 3145736 | tf_op jit(solution)/shard_map/ppermute | solution.py:716
  243.6 24.2 %collective-permute-start.22 = (bf16[512,1024]{1,0:T(8,128)(2,1)}, bf16[512,1024]{1,0:T(8,128)(2,1)}, u32[]{:S(2)}, u32[]{:S(2)}) collective-permute-start(bf16[512,1024]{1,0:T(8,128)(2,1)} %fusion.57), channel_id=1, source_target_pairs={{0,1},{1,0},{2,3},{3,2},{4,5},{5,4},{6,7},{7,6},{8,9},{9,8},{10,11... | collective-permute-start | bytes 3145736 | tf_op jit(solution)/shard_map/ppermute | solution.py:716
  268.0 23.9 %collective-permute-start.23 = (bf16[512,256]{1,0:T(8,128)(2,1)S(1)}, bf16[512,256]{1,0:T(8,128)(2,1)S(1)}, u32[]{:S(2)}, u32[]{:S(2)}) collective-permute-start(bf16[512,256]{1,0:T(8,128)(2,1)S(1)} %get-tuple-element.304), channel_id=1, source_target_pairs={{0,0},{1,16},{2,1},{3,17},{16,2},{17,18},{18,3},{19,19},{4,4},{5,2... | collective-permute-start | bytes 786440 | tf_op jit(solution)/shard_map/ppermute | solution.py:749
  271.3 20.5 %collective-permute-start.24 = (bf16[512,256]{1,0:T(8,128)(2,1)S(1)}, bf16[512,256]{1,0:T(8,128)(2,1)S(1)}, u32[]{:S(2)}, u32[]{:S(2)}) collective-permute-start(bf16[512,256]{1,0:T(8,128)(2,1)S(1)} %get-tuple-element.303), channel_id=1, source_target_pairs={{0,16},{1,0},{2,17},{3,1},{16,18},{17,2},{18,19},{19,3},{4,20},{5,... | collective-permute-start | bytes 786440 | tf_op jit(solution)/shard_map/ppermute | solution.py:749
  272.8 19.1 %collective-permute-start.25 = (bf16[512,256]{1,0:T(8,128)(2,1)S(1)}, bf16[512,256]{1,0:T(8,128)(2,1)S(1)}, u32[]{:S(2)}, u32[]{:S(2)}) collective-permute-start(bf16[512,256]{1,0:T(8,128)(2,1)S(1)} %get-tuple-element.302), channel_id=1, source_target_pairs={{0,1},{1,17},{2,0},{3,16},{16,3},{17,19},{18,2},{19,18},{4,5},{5,2... | collective-permute-start | bytes 786440 | tf_op jit(solution)/shard_map/ppermute | solution.py:749
  274.2 22.3 %collective-permute-start.26 = (bf16[512,256]{1,0:T(8,128)(2,1)S(1)}, bf16[512,256]{1,0:T(8,128)(2,1)S(1)}, u32[]{:S(2)}, u32[]{:S(2)}) collective-permute-start(bf16[512,256]{1,0:T(8,128)(2,1)S(1)} %get-tuple-element.301), channel_id=1, source_target_pairs={{0,17},{1,1},{2,16},{3,0},{16,19},{17,3},{18,18},{19,2},{4,21},{5,... | collective-permute-start | bytes 786440 | tf_op jit(solution)/shard_map/ppermute | solution.py:749
  301.2 25.1 %collective-permute-start.27 = (bf16[512,1024]{1,0:T(8,128)(2,1)S(1)}, bf16[512,1024]{1,0:T(8,128)(2,1)S(1)}, u32[]{:S(2)}, u32[]{:S(2)}) collective-permute-start(bf16[512,1024]{1,0:T(8,128)(2,1)S(1)} %fusion.79), channel_id=1, source_target_pairs={{0,1},{1,0},{2,3},{3,2},{4,5},{5,4},{6,7},{7,6},{8,9},{9,8},{10,11... | collective-permute-start | bytes 3145736 | tf_op jit(solution)/shard_map/ppermute | solution.py:716
  306.8 15.7 %collective-permute-start.28 = (bf16[512,2048]{1,0:T(8,128)(2,1)S(1)}, bf16[512,2048]{1,0:T(8,128)(2,1)S(1)}, u32[]{:S(2)}, u32[]{:S(2)}) collective-permute-start(bf16[512,2048]{1,0:T(8,128)(2,1)S(1)} %convolution_convert_fusion.1), channel_id=1, source_target_pairs={{0,16},{16,0},{1,17},{17,1},{2,18},{18,2},{3,19},{19,3},{4,20},{20... | collective-permute-start | bytes 6291464 | tf_op jit(solution)/shard_map/ppermute | solution.py:716
  336.1 16.1 %all-to-all-start.2 = ((bf16[8,512,128]{2,1,0:T(8,128)(2,1)}), bf16[8,512,128]{2,1,0:T(8,128)(2,1)}, u32[]{:S(2)}, u32[]{:S(2)}) async-start(bf16[8,512,128]{2,1,0:T(8,128)(2,1)} %bitcast.252), calls=%async_computation.2 | async-start | bytes 2097152 | tf_op jit(solution)/shard_map/all_to_all | solution.py:895
  340.4 117.6 %reduce-scatter.2.cloned.1.call-start = ((), (), s32[]{:S(2)}) async-start(), calls=%async_computation.7 | async-start | bytes 7372800 | tf_op jit(solution)/shard_map/reduce_scatter | solution.py:1136
  352.3 85.5 %collective-permute-start.36 = (bf16[512,1024]{1,0:T(8,128)(2,1)}, bf16[512,1024]{1,0:T(8,128)(2,1)}, u32[]{:S(2)}, u32[]{:S(2)}) collective-permute-start(bf16[512,1024]{1,0:T(8,128)(2,1)} %fusion.82), channel_id=1, source_target_pairs={{0,1},{1,0},{2,3},{3,2},{4,5},{5,4},{6,7},{7,6},{8,9},{9,8},{10,11... | collective-permute-start | bytes 3145736 | tf_op jit(solution)/shard_map/ppermute | solution.py:716
  355.5 51.1 %collective-permute-start.32 = (bf16[1024,256]{1,0:T(8,128)(2,1)S(1)}, bf16[1024,256]{1,0:T(8,128)(2,1)S(1)}, u32[]{:S(2)}, u32[]{:S(2)}) collective-permute-start(bf16[1024,256]{1,0:T(8,128)(2,1)S(1)} %get-tuple-element.272), channel_id=1, source_target_pairs={{0,0},{16,1},{1,2},{17,3},{2,16},{18,17},{3,18},{19,19},{4,4},{20,... | collective-permute-start | bytes 1572872 | tf_op jit(solution)/shard_map/ppermute | solution.py:775
  361.2 45.4 %collective-permute-start.33 = (bf16[1024,256]{1,0:T(8,128)(2,1)S(1)}, bf16[1024,256]{1,0:T(8,128)(2,1)S(1)}, u32[]{:S(2)}, u32[]{:S(2)}) collective-permute-start(bf16[1024,256]{1,0:T(8,128)(2,1)S(1)} %get-tuple-element.271), channel_id=1, source_target_pairs={{16,0},{0,1},{17,2},{1,3},{18,16},{2,17},{19,18},{3,19},{20,4},{4,... | collective-permute-start | bytes 1572872 | tf_op jit(solution)/shard_map/ppermute | solution.py:775
  361.3 45.3 %collective-permute-start.34 = (bf16[1024,256]{1,0:T(8,128)(2,1)S(1)}, bf16[1024,256]{1,0:T(8,128)(2,1)S(1)}, u32[]{:S(2)}, u32[]{:S(2)}) collective-permute-start(bf16[1024,256]{1,0:T(8,128)(2,1)S(1)} %get-tuple-element.270), channel_id=1, source_target_pairs={{1,0},{17,1},{0,2},{16,3},{3,16},{19,17},{2,18},{18,19},{5,4},{21,... | collective-permute-start | bytes 1572872 | tf_op jit(solution)/shard_map/ppermute | solution.py:775
  361.8 45.4 %collective-permute-start.35 = (bf16[1024,256]{1,0:T(8,128)(2,1)S(1)}, bf16[1024,256]{1,0:T(8,128)(2,1)S(1)}, u32[]{:S(2)}, u32[]{:S(2)}) collective-permute-start(bf16[1024,256]{1,0:T(8,128)(2,1)S(1)} %get-tuple-element.269), channel_id=1, source_target_pairs={{17,0},{1,1},{16,2},{0,3},{19,16},{3,17},{18,18},{2,19},{21,4},{5,... | collective-permute-start | bytes 1572872 | tf_op jit(solution)/shard_map/ppermute | solution.py:775
  428.2 51.0 %all-to-all-start.3 = ((bf16[8,512,256]{1,2,0:T(8,128)(2,1)}), bf16[8,512,256]{1,2,0:T(8,128)(2,1)}, u32[]{:S(2)}, u32[]{:S(2)}) async-start(bf16[8,512,256]{1,2,0:T(8,128)(2,1)} %copy.125), calls=%async_computation.3 | async-start | bytes 4194304 | tf_op jit(solution)/shard_map/all_to_all | solution.py:901
  441.0 26.0 %collective-permute-start.37 = (bf16[512,256]{1,0:T(8,128)(2,1)}, bf16[512,256]{1,0:T(8,128)(2,1)}, u32[]{:S(2)}, u32[]{:S(2)}) collective-permute-start(bf16[512,256]{1,0:T(8,128)(2,1)} %get-tuple-element.300), channel_id=1, source_target_pairs={{0,0},{16,1},{1,2},{17,3},{2,16},{18,17},{3,18},{19,19},{4,4},{20,... | collective-permute-start | bytes 786440 | tf_op jit(solution)/shard_map/ppermute | solution.py:775
  442.9 36.3 %collective-permute-start.38 = (bf16[512,256]{1,0:T(8,128)(2,1)}, bf16[512,256]{1,0:T(8,128)(2,1)}, u32[]{:S(2)}, u32[]{:S(2)}) collective-permute-start(bf16[512,256]{1,0:T(8,128)(2,1)} %get-tuple-element.299), channel_id=1, source_target_pairs={{16,0},{0,1},{17,2},{1,3},{18,16},{2,17},{19,18},{3,19},{20,4},{4,... | collective-permute-start | bytes 786440 | tf_op jit(solution)/shard_map/ppermute | solution.py:775
  444.6 34.6 %collective-permute-start.39 = (bf16[512,256]{1,0:T(8,128)(2,1)}, bf16[512,256]{1,0:T(8,128)(2,1)}, u32[]{:S(2)}, u32[]{:S(2)}) collective-permute-start(bf16[512,256]{1,0:T(8,128)(2,1)} %get-tuple-element.298), channel_id=1, source_target_pairs={{1,0},{17,1},{0,2},{16,3},{3,16},{19,17},{2,18},{18,19},{5,4},{21,... | collective-permute-start | bytes 786440 | tf_op jit(solution)/shard_map/ppermute | solution.py:775
  448.2 31.0 %collective-permute-start.40 = (bf16[512,256]{1,0:T(8,128)(2,1)}, bf16[512,256]{1,0:T(8,128)(2,1)}, u32[]{:S(2)}, u32[]{:S(2)}) collective-permute-start(bf16[512,256]{1,0:T(8,128)(2,1)} %get-tuple-element.297), channel_id=1, source_target_pairs={{17,0},{1,1},{16,2},{0,3},{19,16},{3,17},{18,18},{2,19},{21,4},{5,... | collective-permute-start | bytes 786440 | tf_op jit(solution)/shard_map/ppermute | solution.py:775
  460.3 36.1 %collective-permute-start.41 = (bf16[144,2048]{1,0:T(8,128)(2,1)}, bf16[144,2048]{1,0:T(8,128)(2,1)}, u32[]{:S(2)}, u32[]{:S(2)}) collective-permute-start(bf16[144,2048]{1,0:T(8,128)(2,1)} %pad_maximum_fusion.6), channel_id=1, source_target_pairs={{0,2},{1,3},{2,0},{3,1},{4,6},{5,7},{6,4},{7,5},{8,10},{9,11},{10,... | collective-permute-start | bytes 1769480 | tf_op jit(solution)/shard_map/ppermute | solution.py:716
  467.0 55.6 %collective-permute-start.49 = (bf16[400,256]{1,0:T(8,128)(2,1)}, bf16[400,256]{1,0:T(8,128)(2,1)}, u32[]{:S(2)}, u32[]{:S(2)}) collective-permute-start(bf16[400,256]{1,0:T(8,128)(2,1)} %get-tuple-element.306), channel_id=1, source_target_pairs={{0,1},{1,0},{2,3},{3,2},{4,5},{5,4},{6,7},{7,6},{8,9},{9,8},{10,11... | collective-permute-start | bytes 614408 | tf_op jit(solution)/shard_map/ppermute | solution.py:716
  479.2 46.2 %collective-permute-start.50 = (bf16[400,256]{1,0:T(8,128)(2,1)}, bf16[400,256]{1,0:T(8,128)(2,1)}, u32[]{:S(2)}, u32[]{:S(2)}) collective-permute-start(bf16[400,256]{1,0:T(8,128)(2,1)} %get-tuple-element.307), channel_id=1, source_target_pairs={{0,2},{1,3},{2,0},{3,1},{4,6},{5,7},{6,4},{7,5},{8,10},{9,11},{10,... | collective-permute-start | bytes 614408 | tf_op jit(solution)/shard_map/ppermute | solution.py:716
  518.9 14.7 %collective-permute-start.42 = (bf16[512,256]{1,0:T(8,128)(2,1)S(1)}, bf16[512,256]{1,0:T(8,128)(2,1)S(1)}, u32[]{:S(2)}, u32[]{:S(2)}) collective-permute-start(bf16[512,256]{1,0:T(8,128)(2,1)S(1)} %get-tuple-element.296), channel_id=1, source_target_pairs={{0,0},{16,1},{1,2},{17,3},{2,16},{18,17},{3,18},{19,19},{4,4},{20,... | collective-permute-start | bytes 786440 | tf_op jit(solution)/shard_map/ppermute | solution.py:775
  522.0 15.0 %collective-permute-start.43 = (bf16[512,256]{1,0:T(8,128)(2,1)S(1)}, bf16[512,256]{1,0:T(8,128)(2,1)S(1)}, u32[]{:S(2)}, u32[]{:S(2)}) collective-permute-start(bf16[512,256]{1,0:T(8,128)(2,1)S(1)} %get-tuple-element.295), channel_id=1, source_target_pairs={{16,0},{0,1},{17,2},{1,3},{18,16},{2,17},{19,18},{3,19},{20,4},{4,... | collective-permute-start | bytes 786440 | tf_op jit(solution)/shard_map/ppermute | solution.py:775
  527.6 21.3 %collective-permute-start.46 = (bf16[128,2048]{1,0:T(8,128)(2,1)S(1)}, bf16[128,2048]{1,0:T(8,128)(2,1)S(1)}, u32[]{:S(2)}, u32[]{:S(2)}) collective-permute-start(bf16[128,2048]{1,0:T(8,128)(2,1)S(1)} %add_convert_fusion.6.refs_0_), channel_id=1, source_target_pairs={{0,4},{4,0},{8,12},{12,8},{1,5},{5,1},{9,13},{13,9},{2,6},{6,2},{1... | collective-permute-start | bytes 1572872 | tf_op jit(solution)/shard_map/ppermute | solution.py:716
  529.1 19.9 %collective-permute-start.47 = (bf16[128,2048]{1,0:T(8,128)(2,1)S(1)}, bf16[128,2048]{1,0:T(8,128)(2,1)S(1)}, u32[]{:S(2)}, u32[]{:S(2)}) collective-permute-start(bf16[128,2048]{1,0:T(8,128)(2,1)S(1)} %add_convert_fusion.6.refs_0_), channel_id=1, source_target_pairs={{0,8},{4,12},{8,0},{12,4},{1,9},{5,13},{9,1},{13,5},{2,10},{6,14},... | collective-permute-start | bytes 1572872 | tf_op jit(solution)/shard_map/ppermute | solution.py:716
  529.3 20.8 %collective-permute-start.48 = (bf16[128,2048]{1,0:T(8,128)(2,1)S(1)}, bf16[128,2048]{1,0:T(8,128)(2,1)S(1)}, u32[]{:S(2)}, u32[]{:S(2)}) collective-permute-start(bf16[128,2048]{1,0:T(8,128)(2,1)S(1)} %add_convert_fusion.6.refs_0_), channel_id=1, source_target_pairs={{0,12},{4,8},{8,4},{12,0},{1,13},{5,9},{9,5},{13,1},{2,14},{6,10},... | collective-permute-start | bytes 1572872 | tf_op jit(solution)/shard_map/ppermute | solution.py:716
  552.9 25.3 %collective-permute-start.53 = (bf16[1,400,256]{2,1,0:T(8,128)(2,1)S(1)}, bf16[1,400,256]{2,1,0:T(8,128)(2,1)}, u32[]{:S(2)}, u32[]{:S(2)}) collective-permute-start(bf16[1,400,256]{2,1,0:T(8,128)(2,1)S(1)} %maximum_bitcast_fusion), channel_id=1, source_target_pairs={{0,4},{4,0},{8,12},{12,8},{1,5},{5,1},{9,13},{13,9},{2,6},{6,2},{1... | collective-permute-start | bytes 614408 | tf_op jit(solution)/shard_map/ppermute | solution.py:716
  (88 other events, 640.9 us)
Sparse Core Ops, SparseCore 0:
  133.0 65.1 all-gather.2
  244.0 54.5 all-gather.4
  352.3 68.0 reduce-scatter.1

commit v4 on v3

--- a/solution.py
+++ b/solution.py
@@ -309,7 +309,9 @@
 
 
 def out_of_places(places, vectors):
-    return jnp.einsum("pa,pd->ad", place_matrix(places), vectors, preferred_element_type=jnp.float32).astype(jnp.bfloat16)
+    rows = places.shape[0]
+    picks = (places[:, None] == jnp.arange(rows, dtype=jnp.int32)[None, :]).astype(jnp.bfloat16)
+    return dot(picks, vectors, NN).astype(jnp.bfloat16)
 
 
 def bucket_hot(buckets):
@@ -762,18 +764,26 @@
     return whole, beside, extras
 
 
-def rows_out(whole, seqs, beside=()):
+def rows_out(whole, seqs, beside=(), first=None):
     shard, _, plane = where_am_i()
     shards, planes = lax.axis_size("shard"), lax.axis_size("tp")
     count, extent, features = whole.shape
     width = features // planes
     mine = (plane % seqs) * shards + shard
     flat = whole.reshape(count * extent, features)
-    landed = []
-    for step in range(planes):
+
+    def send(step):
         piece = lax.dynamic_slice_in_dim(flat, (step ^ mine) * width, width, 1)
-        landed.append(lax.ppermute(piece, ("shard", "tp"), plane_pairs(step, True)))
-    landed, beside = lax.optimization_barrier((landed, beside))
+        return lax.ppermute(piece, ("shard", "tp"), plane_pairs(step, True))
+
+    half = planes // 2 if first is not None else 0
+    landed = [send(step) for step in range(half)]
+    if first is not None:
+        landed, beside, flat = lax.optimization_barrier((landed, beside, flat))
+        beside = first(beside)
+    rest = [send(step) for step in range(half, planes)]
+    rest, beside = lax.optimization_barrier((rest, beside))
+    landed = landed + rest
     by_seq = jnp.zeros((seqs * shards, count * extent, width), whole.dtype)
     for step in range(planes):
         by_seq = lax.dynamic_update_slice_in_dim(by_seq, landed[step][None], step ^ plane, 0)
@@ -870,9 +880,7 @@
     return lax.dynamic_index_in_dim(parts, lax.axis_index("tp") ^ k, 0, False)
 
 
-def sum_everywhere(parts):
-    total = plane_part(parts, 0)
-    total = sum((swap(plane_part(parts, k), "tp", k) for k in range(1, lax.axis_size("tp"))), total)
+def sum_in_plane(total):
     total = total + swap(total, "shard", 1)
     return sum(swap(total, "ctx", j) for j in range(1, lax.axis_size("ctx"))) + total
 
@@ -914,24 +922,30 @@
 
 
 def pack_rows_kernel(code_ref, *refs):
-    out_ref = refs[-1]
-    extent = refs[0].shape[0]
-    for j, ref in enumerate(refs[:-1]):
-        out_ref[pl.ds(pl.multiple_of((code_ref[0] ^ j) * extent, extent), extent), :] = ref[...]
+    pieces, out_ref, sems = refs[:-2], refs[-2], refs[-1]
+    extent = pieces[0].shape[0]
+    copies = []
+    for j, ref in enumerate(pieces):
+        place = pl.multiple_of((code_ref[0] ^ j) * extent, extent)
+        copies.append(pltpu.make_async_copy(ref, out_ref.at[pl.ds(place, extent), :], sems.at[j]))
+        copies[-1].start()
+    for copy in copies:
+        copy.wait()
 
 
 def pack_rows(pieces, code):
     extent, width = pieces[0].shape
-    whole = lambda shape: pl.BlockSpec(shape, lambda i, *_: (0, 0))
+    shape = (len(pieces) * extent, width)
     return pl.pallas_call(
         pack_rows_kernel,
         name="pack_rows",
-        out_shape=jax.ShapeDtypeStruct((len(pieces) * extent, width), pieces[0].dtype),
+        out_shape=jax.ShapeDtypeStruct(shape, pieces[0].dtype),
         grid_spec=pltpu.PrefetchScalarGridSpec(
             num_scalar_prefetch=1,
             grid=(1,),
-            in_specs=[whole((extent, width)) for _ in pieces],
-            out_specs=whole((len(pieces) * extent, width)),
+            in_specs=[pl.BlockSpec(memory_space=pl.ANY)] * len(pieces),
+            out_specs=pl.BlockSpec(shape, lambda i, *_: (0, 0)),
+            scratch_shapes=[pltpu.SemaphoreType.DMA((len(pieces),))],
         ),
         compiler_params=pltpu.CompilerParams(vmem_limit_bytes=24 * 2**20),
         cost_estimate=pl.CostEstimate(flops=0, bytes_accessed=4 * len(pieces) * extent * width, transcendentals=0),
@@ -1143,21 +1157,24 @@
     )
     far_branch, own_branch = after((far_branch, own_branch), parts)
     second_out = (own_branch + far_branch.astype(f32)).astype(bf16)
-    pair_grad_heads = out_of_places(places, jnp.concatenate(parts, 1))
-    early_mine = after(early_mine, pair_grad_heads)
-    far_sums = jnp.concatenate(
-        [early_mine[:, units : 2 * units], early_mine[:, 3 * units : 4 * units]], 1
+    def with_far(pair_grad_heads):
+        sums = after(early_mine, pair_grad_heads)
+        far = jnp.concatenate([sums[:, units : 2 * units], sums[:, 3 * units : 4 * units]], 1)
+        pair_sums = lax.dot_general(
+            normed_all, pair_grad_heads, (((0,), (0,)), ((), ())), preferred_element_type=f32
+        ).astype(bf16)
+        late = sums[:, 4 * units :].reshape(-1, planes, width).transpose(1, 0, 2)
+        late = jnp.concatenate([pair_sums.reshape(planes, -1, 2 * DH), late], 1)
+        return late, sums, heads_back(pair_grad_heads), swap(far, "tp", 2)
+
+    second_out_sliced, (late, early_mine, pair_grad, far_sums) = rows_out(
+        second_out[None],
+        seqs_here,
+        out_of_places(places, jnp.concatenate(parts, 1)),
+        with_far,
     )
     near_sums = jnp.concatenate([early_mine[:, :units], early_mine[:, 2 * units : 3 * units]], 1)
 
-    pair_sums = lax.dot_general(
-        normed_all, pair_grad_heads, (((0,), (0,)), ((), ())), preferred_element_type=f32
-    ).astype(bf16)
-    late = early_mine[:, 4 * units :].reshape(-1, planes, width).transpose(1, 0, 2)
-    late = jnp.concatenate([pair_sums.reshape(planes, -1, 2 * DH), late], 1)
-    second_out_sliced, (pair_grad, far_sums) = rows_out(
-        second_out[None], seqs_here, (heads_back(pair_grad_heads), swap(far_sums, "tp", 2))
-    )
     grad_mine, grad_other = dot(pair_grad, pair_mine, NT), dot(pair_grad, pair_other, NT)
     normed_grad = jnp.concatenate(
         [
@@ -1173,25 +1190,29 @@
 
     early_own = (near_sums.astype(f32) + far_sums.astype(f32)).astype(bf16)
     early_own = early_own[: split // quarters]
-    second_grad_sliced, (early_pieces, late_pieces) = rows_out(
-        second_grad[None],
-        seqs_here,
-        (
-            [swap(early_own, "ctx", j) for j in range(1, quarters)],
-            [swap(plane_part(late, k), "tp", k) for k in range(1, planes)],
-        ),
-    )
-    early_own = pack_rows([early_own] + early_pieces, ctx).astype(f32)
-    expand_own, shrink_own = early_own[:, :units], early_own[:, units:].T
-    late = plane_part(late, 0).astype(f32)
-    late = sum((piece.astype(f32) for piece in late_pieces), late).astype(bf16)
-
+    pieces = [swap(plane_part(late, k), "tp", k) for k in range(1, planes)]
+    late = sum((piece.astype(f32) for piece in pieces), plane_part(late, 0).astype(f32)).astype(bf16)
     split_at = width
     turned = lax.ppermute(
         late[:split_at],
         ("ctx", "tp"),
         [(at * planes + to, to * planes + at) for at in range(quarters) for to in range(planes)],
     )
+    norm_grads = jnp.concatenate(
+        [attn_gain_grad.reshape(planes, width), attn_shift_grad.reshape(planes, width)], 1
+    )
+    second_grad_sliced, (early_pieces, turned, norm_pieces) = rows_out(
+        second_grad[None],
+        seqs_here,
+        (
+            [swap(early_own, "ctx", j) for j in range(1, quarters)],
+            turned,
+            [swap(plane_part(norm_grads, k), "tp", k) for k in range(1, planes)],
+        ),
+    )
+    early_own = pack_rows([early_own] + early_pieces, ctx).astype(f32)
+    expand_own, shrink_own = early_own[:, :units], early_own[:, units:].T
+    norm_own = sum_in_plane(sum(norm_pieces, plane_part(norm_grads, 0))).reshape(2, width)
     late_own = collect_ctx(jnp.concatenate([turned, late[split_at:]], 0)[None])
     pair_head = late_own[:, :split_at].reshape(-1, width)
     late_own = late_own[:, split_at:].astype(f32)
@@ -1204,11 +1225,6 @@
     query_own = jnp.concatenate([pair_own[0, :, :DH], pair_own[1, :, :DH]], 1)
     value_own = jnp.concatenate([pair_own[0, :, DH:], pair_own[1, :, DH:]], 1)
 
-    norm_grads = jnp.concatenate(
-        [attn_gain_grad.reshape(planes, width), attn_shift_grad.reshape(planes, width)], 1
-    )
-    norm_own = sum_everywhere(after(norm_grads, second_grad_sliced))
-    norm_own = norm_own.reshape(2, width)
     return (
         outs_sliced[0],
         second_out_sliced[0],

time: 609 us -> 601 us (0.987)
  starting transfers between devices: 140 us -> 122 us
    dot_general x3 -> x1, matrix products: 33.4 us -> 6.55 us  [with_far(): lax.dot_general(normed_all, pair_grad_heads, (((0,), (0,)), ((), ())), pr...]
    dot_general x14 -> x16, matrix products: 59.5 us -> 84 us  [dot(): lax.dot_general(left, right, dims, preferred_element_type=jnp.float32)]
    ppermute x39, starting transfers between devices: 55.2 us -> 43.3 us  [swap(): return lax.ppermute(vectors, axis, [(at, at ^ bits) for at in range(size)])]
    all_to_all x2, waiting for transfers between devices: 2.35 us -> 9.13 us  [heads_back(): lax.all_to_all(sent, ('ctx', 'shard'), split_axis=0, concat_axis=0, tiled...]
    unnamed x145 -> x148, local copies, waits for them, and re-layouts: 28.3 us -> 29.1 us
  transfers between devices with their start and end apart: 71 -> 71, of which waited for: 22 -> 21; matrix products, arithmetic and copies ran while one was open for 39% -> 39% of each run, Pallas kernels for 7% -> 8%
where the time goes in v4:
time: 601 us; the launch traced here: 593 us
  matrix products  149 us (25%)
  waiting for transfers between devices  143 us (24%)
  starting transfers between devices  122 us (20%)
  local copies, waits for them, and re-layouts  71.2 us (12%)
  Pallas kernels  48.6 us (8%)
  other arithmetic  42 us (7%)
  between operations  17.2 us (3%)
    dot_general x16, matrix products, dot(): lax.dot_general(left, right, dims, preferred_element_type=jnp.float32)  84 us
    ppermute x39, waiting for transfers between devices, swap(): return lax.ppermute(vectors, axis, [(at, at ^ bits) for at in range(size)])  57.9 us
    ppermute x12, waiting for transfers between devices, rows_in(): lax.ppermute(chunk, ('shard', 'tp'), plane_pairs(step, False))  44.6 us
    ppermute x39, starting transfers between devices, swap(): return lax.ppermute(vectors, axis, [(at, at ^ bits) for at in range(size)])  43.3 us
    dot_general x3, matrix products, into_places(): jnp.einsum('pa,ad->pd', place_matrix(places), vectors, preferred_element_...  40.8 us
    ppermute x12, starting transfers between devices, rows_in(): lax.ppermute(chunk, ('shard', 'tp'), plane_pairs(step, False))  30.6 us
    pallas_call x1, Pallas kernels, attend_back(): pl.pallas_call(attend_back_kernel, name='attend_back', out_shape=(jax.Sha...  29.4 us
    unnamed x148, local copies, waits for them, and re-layouts  29.1 us
  transfers between devices with their start and end apart: 71, of which 21 were waited for; matrix products, arithmetic and copies ran while one was open for 39% of the time, Pallas kernels for 8%

profile of v4, /device:TPU:1, one launch (start us, length us, event | category | flops | bytes accessed | tf_op | source)
XLA Modules:
  0.0 592.9 jit_solution(8595204711624704875)
XLA Ops:
  13.0 5.6 collective-permute-start.1
  23.2 4.3 collective-permute-done.1
  27.5 8.6 %collective-permute-done.2 = bf16[784,256]{1,0:T(8,128)(2,1)S(1)} collective-permute-done((bf16[784,256]{1,0:T(8,128)(2,1)}, bf16[784,256]{1,0:T(8,128)(2,1)S(1)}, u32[]{:S(2)}, u32[]{:S(2)}) %collective-permute-start.2) | collective-permute-done | bytes 401440 | tf_op jit(solution)/shard_map/ppermute | solution.py:751
  36.1 6.9 %collective-permute-done.3 = bf16[784,256]{1,0:T(8,128)(2,1)S(1)} collective-permute-done((bf16[784,256]{1,0:T(8,128)(2,1)S(1)}, bf16[784,256]{1,0:T(8,128)(2,1)S(1)}, u32[]{:S(2)}, u32[]{:S(2)}) %collective-permute-start.3) | collective-permute-done | bytes 401440 | tf_op jit(solution)/shard_map/ppermute | solution.py:751
  42.9 11.9 %collective-permute-done.4 = bf16[784,256]{1,0:T(8,128)(2,1)S(1)} collective-permute-done((bf16[784,256]{1,0:T(8,128)(2,1)S(1)}, bf16[784,256]{1,0:T(8,128)(2,1)S(1)}, u32[]{:S(2)}, u32[]{:S(2)}) %collective-permute-start.4) | collective-permute-done | bytes 401440 | tf_op jit(solution)/shard_map/ppermute | solution.py:751
  69.6 10.0 %collective-permute-done.9 = s32[48,128]{1,0:T(8,128)S(1)} collective-permute-done((s32[48,128]{1,0:T(8,128)S(1)}, s32[48,128]{1,0:T(8,128)S(1)}, u32[]{:S(2)}, u32[]{:S(2)}) %collective-permute-start.9) | collective-permute-done | bytes 24608 | tf_op jit(solution)/shard_map/ppermute | solution.py:718
  103.6 4.8 all-to-all-start
  108.6 15.6 %fusion.12.hot_ref = bf16[4096,256]{1,0:T(8,128)(2,1)} fusion(pred[4096,256]{0,1:T(32,128)(4,1)} %bitcast_compare_fusion, s32[4096]{0:T(1024)S(1)} %bitcast.288), kind=kOutput, calls=%fused_computation.19 | convolution fusion | flops 8607760384 | bytes 3162112 | tf_op jit(solution)/shard_map/pa,ad->pd/dot_general | solution.py:308
  124.4 7.2 %all-to-all-done = bf16[8,512,256]{2,1,0:T(8,128)(2,1)S(1)} async-done(((bf16[8,512,256]{2,1,0:T(8,128)(2,1)}), bf16[8,512,256]{2,1,0:T(8,128)(2,1)S(1)}, u32[]{:S(2)}, u32[]{:S(2)}) %all-to-all-start) | async-done | bytes 2097184 | tf_op jit(solution)/shard_map/all_to_all | solution.py:903
  133.3 4.7 pad_maximum_fusion.1
  140.5 8.0 %collective-permute-start.17 = (bf16[1024,256]{1,0:T(8,128)(2,1)}, bf16[1024,256]{1,0:T(8,128)(2,1)S(1)}, u32[]{:S(2)}, u32[]{:S(2)}) collective-permute-start(bf16[1024,256]{1,0:T(8,128)(2,1)} %get-tuple-element.289), channel_id=1, source_target_pairs={{0,0},{1,16},{2,1},{3,17},{16,2},{17,18},{18,3},{19,19},{4,4},{5,2... | collective-permute-start | bytes 1572872 | tf_op jit(solution)/shard_map/ppermute | solution.py:751
  153.0 12.2 %fusion.13 = bf16[4096,256]{1,0:T(8,128)(2,1)S(1)} fusion(bf16[4096,256]{1,0:T(8,128)(2,1)S(1)} %bitcast.257, s32[4096]{0:T(1024)S(1)} %bitcast.289), kind=kOutput, calls=%fused_computation.20 | convolution fusion | flops 8607760384 | bytes 4210688 | tf_op jit(solution)/shard_map/pa,ad->pd/dot_general | solution.py:308
  168.9 17.5 %attend.1 = (f32[128,4096]{1,0:T(8,128)S(1)}, f32[8,512]{1,0:T(8,128)S(1)}) custom-call(s32[4]{0:T(128)S(1)} %pad_add_fusion.bounds_ref, bf16[4096,128]{1,0:T(8,128)(2,1)S(1)} %get-tuple-element.285.q_ref, bf16[4096,128]{1,0:T(8,128)(2,1)S(1)} %get-tuple-element.284.v_ref, bf16[4096,256]{1,0:T(8,128)(2,1)S(1)} %copy-done.4), custom_call_target="tpu_custom_call" | custom-call | flops 524288 | bytes 524288 | tf_op jit(solution)/shard_map/attend/pallas_call | solution.py:150
  186.5 8.2 %collective-permute-done.20 = bf16[1024,256]{1,0:T(8,128)(2,1)} collective-permute-done((bf16[1024,256]{1,0:T(8,128)(2,1)}, bf16[1024,256]{1,0:T(8,128)(2,1)}, u32[]{:S(2)}, u32[]{:S(2)}) %collective-permute-start.20) | collective-permute-done | bytes 524320 | tf_op jit(solution)/shard_map/ppermute | solution.py:751
  194.7 12.3 %fusion.16 = bf16[4096,128]{1,0:T(8,128)(2,1)S(1)} fusion(s32[4096]{0:T(1024)S(1)} %bitcast.290, f32[128,4096]{1,0:T(8,128)S(1)} %get-tuple-element.135.out_ref), kind=kOutput, calls=%fused_computation.23 | convolution fusion | flops 4312793088 | bytes 3162112 | tf_op jit(solution)/shard_map/dot_general | solution.py:30
  208.3 3.7 all-to-all-start.1
  224.9 4.0 convert_reduce_fusion.3
  230.8 15.6 %collective-permute-done.21 = bf16[512,1024]{1,0:T(8,128)(2,1)} collective-permute-done((bf16[512,1024]{1,0:T(8,128)(2,1)}, bf16[512,1024]{1,0:T(8,128)(2,1)}, u32[]{:S(2)}, u32[]{:S(2)}) %collective-permute-start.21) | collective-permute-done | bytes 1048608 | tf_op jit(solution)/shard_map/ppermute | solution.py:718
  246.6 6.7 %multiply_convert_fusion.1 = (bf16[512,2048]{1,0:T(8,128)(2,1)}, f32[512,2048]{1,0:T(8,128)}) fusion(f32[2048]{0:T(1024)S(1)} %pad_maximum_fusion.15, bf16[512,1024]{1,0:T(8,128)(2,1)} %fusion.53, bf16[1024,5120]{1,0:T(8,128)(2,1)} %all-gather.3.cloned.1.call-done), kind=kOutput, calls=%fused_computation.41 | convolution fusion | flops 2153775104 | bytes 11542528 | tf_op jit(solution)/shard_map/dot_general | solution.py:30
  255.5 6.7 %fusion.22 = bf16[512,2048]{1,0:T(8,128)(2,1)S(1)} fusion(f32[512,2048]{1,0:T(8,128)} %get-tuple-element.340, bf16[1024,5120]{1,0:T(8,128)(2,1)} %all-gather.3.cloned.1.call-done, f32[2048]{0:T(1024)S(1)} %pad_maximum_fusion.15, bf16[1024,1024]{1,0:T(8,128)(2,1)} %constant_dynamic-update-slice_fusion.8), kind=kOutput, calls=%fused_computation.29 | convolution fusion | flops 2159017984 | bytes 11542528 | tf_op jit(solution)/shard_map/dot_general | solution.py:30
  262.2 8.3 %collective-permute-done.22 = bf16[512,1024]{1,0:T(8,128)(2,1)} collective-permute-done((bf16[512,1024]{1,0:T(8,128)(2,1)}, bf16[512,1024]{1,0:T(8,128)(2,1)}, u32[]{:S(2)}, u32[]{:S(2)}) %collective-permute-start.22) | collective-permute-done | bytes 1048608 | tf_op jit(solution)/shard_map/ppermute | solution.py:718
  270.7 3.4 collective-permute-start.23
  280.6 4.1 multiply_convert_fusion
  284.8 3.7 fusion.62
  288.5 5.4 fusion.28
  294.5 4.7 collective-permute-done.26
  299.2 4.7 fusion.75
  311.0 5.5 fusion.78
  316.5 4.5 fusion.35
  321.1 4.3 add_convert_fusion
  325.4 3.9 add_convert_fusion.1
  339.1 4.2 all-to-all-start.2
  348.3 4.5 fusion.11
  358.5 5.7 collective-permute-start.32
  364.7 4.4 collective-permute-start.35
  369.1 13.1 %fusion.15.grad_ref = bf16[4096,128]{1,0:T(8,128)(2,1)S(1)} fusion(bf16[4096,128]{1,0:T(8,128)(2,1)} %bitcast.63, s32[4096]{0:T(1024)S(1)} %bitcast.291), kind=kOutput, calls=%fused_computation.22 | convolution fusion | flops 4312268800 | bytes 2113536 | tf_op jit(solution)/shard_map/pa,ad->pd/dot_general | solution.py:308
  382.2 29.4 %attend_back.1 = (bf16[4096,128]{1,0:T(8,128)(2,1)S(1)}, bf16[4096,128]{1,0:T(8,128)(2,1)S(1)}) custom-call(s32[4]{0:T(128)S(1)} %pad_add_fusion.bounds_ref, bf16[4096,128]{1,0:T(8,128)(2,1)S(1)} %get-tuple-element.285.q_ref, bf16[4096,128]{1,0:T(8,128)(2,1)S(1)} %get-tuple-element.284.v_ref, bf16[4096,256]{1,0:T(8,128)(2,1)} %fusion.12.hot_ref, ...), custom_call_target="tpu_custom_call" | custom-call | flops 524288 | bytes 524288 | tf_op jit(solution)/shard_map/attend_back/pallas_call | solution.py:273
  412.2 4.1 collective-permute-start.37
  417.0 12.3 %fusion.14 = bf16[4096,256]{1,0:T(8,128)(2,1)S(1)} fusion(s32[4096]{0:T(1024)S(1)} %bitcast.292, bf16[4096,128]{1,0:T(8,128)(2,1)S(1)} %get-tuple-element.174, bf16[4096,128]{1,0:T(8,128)(2,1)S(1)} %get-tuple-element.173), kind=kOutput, calls=%fused_computation.21 | convolution fusion | flops 8611954688 | bytes 4210688 | tf_op jit(solution)/shard_map/dot_general | solution.py:30
  437.3 8.1 %all-to-all-start.3 = ((bf16[8,512,256]{1,2,0:T(8,128)(2,1)}), bf16[8,512,256]{1,2,0:T(8,128)(2,1)}, u32[]{:S(2)}, u32[]{:S(2)}) async-start(bf16[8,512,256]{1,2,0:T(8,128)(2,1)} %copy.126), calls=%async_computation.4 | async-start | bytes 4194304 | tf_op jit(solution)/shard_map/all_to_all | solution.py:909
  447.1 4.4 collective-permute-start.40
  451.5 6.6 %convolution_convert_fusion.3 = bf16[1024,256]{1,0:T(8,128)(2,1)} fusion(bf16[4096,1024]{1,0:T(8,128)(2,1)} %all-gather.5.cloned.1.call-done, bf16[4096,256]{1,0:T(8,128)(2,1)S(1)} %fusion.14), kind=kOutput, calls=%fused_computation.117 | convolution fusion | flops 2147745792 | bytes 11010048 | tf_op jit(solution)/shard_map/dot_general | solution.py:1163
  462.1 6.6 %all-to-all-done.3 = bf16[8,512,256]{1,2,0:T(8,128)(2,1)} async-done(((bf16[8,512,256]{1,2,0:T(8,128)(2,1)}), bf16[8,512,256]{1,2,0:T(8,128)(2,1)}, u32[]{:S(2)}, u32[]{:S(2)}) %all-to-all-start.3) | async-done | bytes 2097184 | tf_op jit(solution)/shard_map/all_to_all | solution.py:909
  468.7 19.0 %collective-permute-done.41 = bf16[144,2048]{1,0:T(8,128)(2,1)S(1)} collective-permute-done((bf16[144,2048]{1,0:T(8,128)(2,1)S(1)}, bf16[144,2048]{1,0:T(8,128)(2,1)S(1)}, u32[]{:S(2)}, u32[]{:S(2)}) %collective-permute-start.41) | collective-permute-done | bytes 589856 | tf_op jit(solution)/shard_map/ppermute | solution.py:718
  488.5 3.7 fusion.126
  518.3 11.6 %collective-permute-done.42 = bf16[512,256]{1,0:T(8,128)(2,1)S(1)} collective-permute-done((bf16[512,256]{1,0:T(8,128)(2,1)S(1)}, bf16[512,256]{1,0:T(8,128)(2,1)S(1)}, u32[]{:S(2)}, u32[]{:S(2)}) %collective-permute-start.42) | collective-permute-done | bytes 262176 | tf_op jit(solution)/shard_map/ppermute | solution.py:777
  530.9 7.0 %collective-permute-done.43 = bf16[512,256]{1,0:T(8,128)(2,1)S(1)} collective-permute-done((bf16[512,256]{1,0:T(8,128)(2,1)S(1)}, bf16[512,256]{1,0:T(8,128)(2,1)S(1)}, u32[]{:S(2)}, u32[]{:S(2)}) %collective-permute-start.43) | collective-permute-done | bytes 262176 | tf_op jit(solution)/shard_map/ppermute | solution.py:777
  551.9 9.6 %collective-permute-start.56 = (bf16[1,400,256]{2,1,0:T(8,128)(2,1)S(1)}, bf16[1,400,256]{2,1,0:T(8,128)(2,1)}, u32[]{:S(2)}, u32[]{:S(2)}) collective-permute-start(bf16[1,400,256]{2,1,0:T(8,128)(2,1)S(1)} %maximum_bitcast_fusion), channel_id=1, source_target_pairs={{0,4},{4,0},{8,12},{12,8},{1,5},{5,1},{9,13},{13,9},{2,6},{6,2},{1... | collective-permute-start | bytes 614408 | tf_op jit(solution)/shard_map/ppermute | solution.py:718
  (458 shorter events, 194.7 us)
Async XLA Ops:
  13.0 14.5 %collective-permute-start.1 = (bf16[784,256]{1,0:T(8,128)(2,1)}, bf16[784,256]{1,0:T(8,128)(2,1)S(1)}, u32[]{:S(2)}, u32[]{:S(2)}) collective-permute-start(bf16[784,256]{1,0:T(8,128)(2,1)} %get-tuple-element.293), channel_id=1, source_target_pairs={{0,0},{1,16},{2,1},{3,17},{16,2},{17,18},{18,3},{19,19},{4,4},{5,2... | collective-permute-start | bytes 1204232 | tf_op jit(solution)/shard_map/ppermute | solution.py:751
  18.6 17.5 %collective-permute-start.2 = (bf16[784,256]{1,0:T(8,128)(2,1)}, bf16[784,256]{1,0:T(8,128)(2,1)S(1)}, u32[]{:S(2)}, u32[]{:S(2)}) collective-permute-start(bf16[784,256]{1,0:T(8,128)(2,1)} %get-tuple-element.292), channel_id=1, source_target_pairs={{0,16},{1,0},{2,17},{3,1},{16,18},{17,2},{18,19},{19,3},{4,20},{5,... | collective-permute-start | bytes 1204232 | tf_op jit(solution)/shard_map/ppermute | solution.py:751
  19.9 23.0 %collective-permute-start.3 = (bf16[784,256]{1,0:T(8,128)(2,1)S(1)}, bf16[784,256]{1,0:T(8,128)(2,1)S(1)}, u32[]{:S(2)}, u32[]{:S(2)}) collective-permute-start(bf16[784,256]{1,0:T(8,128)(2,1)S(1)} %get-tuple-element.291), channel_id=1, source_target_pairs={{0,1},{1,17},{2,0},{3,16},{16,3},{17,19},{18,2},{19,18},{4,5},{5,2... | collective-permute-start | bytes 1204232 | tf_op jit(solution)/shard_map/ppermute | solution.py:751
  20.1 34.7 %collective-permute-start.4 = (bf16[784,256]{1,0:T(8,128)(2,1)S(1)}, bf16[784,256]{1,0:T(8,128)(2,1)S(1)}, u32[]{:S(2)}, u32[]{:S(2)}) collective-permute-start(bf16[784,256]{1,0:T(8,128)(2,1)S(1)} %get-tuple-element.290), channel_id=1, source_target_pairs={{0,17},{1,1},{2,16},{3,0},{16,19},{17,3},{18,18},{19,2},{4,21},{5,... | collective-permute-start | bytes 1204232 | tf_op jit(solution)/shard_map/ppermute | solution.py:751
  56.8 26.5 %collective-permute-start.5 = (bf16[128,2048]{1,0:T(8,128)(2,1)S(1)}, bf16[128,2048]{1,0:T(8,128)(2,1)S(1)}, u32[]{:S(2)}, u32[]{:S(2)}) collective-permute-start(bf16[128,2048]{1,0:T(8,128)(2,1)S(1)} %bitcast.230), channel_id=1, source_target_pairs={{0,4},{4,0},{8,12},{12,8},{1,5},{5,1},{9,13},{13,9},{2,6},{6,2},{1... | collective-permute-start | bytes 1572872 | tf_op jit(solution)/shard_map/ppermute | solution.py:718
  58.0 26.0 %collective-permute-start.6 = (bf16[128,2048]{1,0:T(8,128)(2,1)S(1)}, bf16[128,2048]{1,0:T(8,128)(2,1)S(1)}, u32[]{:S(2)}, u32[]{:S(2)}) collective-permute-start(bf16[128,2048]{1,0:T(8,128)(2,1)S(1)} %bitcast.231), channel_id=1, source_target_pairs={{0,8},{4,12},{8,0},{12,4},{1,9},{5,13},{9,1},{13,5},{2,10},{6,14},... | collective-permute-start | bytes 1572872 | tf_op jit(solution)/shard_map/ppermute | solution.py:718
  59.3 25.5 %collective-permute-start.7 = (bf16[128,2048]{1,0:T(8,128)(2,1)S(1)}, bf16[128,2048]{1,0:T(8,128)(2,1)S(1)}, u32[]{:S(2)}, u32[]{:S(2)}) collective-permute-start(bf16[128,2048]{1,0:T(8,128)(2,1)S(1)} %bitcast.232), channel_id=1, source_target_pairs={{0,12},{4,8},{8,4},{12,0},{1,13},{5,9},{9,5},{13,1},{2,14},{6,10},... | collective-permute-start | bytes 1572872 | tf_op jit(solution)/shard_map/ppermute | solution.py:718
  65.7 13.9 %collective-permute-start.9 = (s32[48,128]{1,0:T(8,128)S(1)}, s32[48,128]{1,0:T(8,128)S(1)}, u32[]{:S(2)}, u32[]{:S(2)}) collective-permute-start(s32[48,128]{1,0:T(8,128)S(1)} %get-tuple-element.274), channel_id=1, source_target_pairs={{0,4},{4,0},{8,12},{12,8},{1,5},{5,1},{9,13},{13,9},{2,6},{6,2},{1... | collective-permute-start | bytes 73736 | tf_op jit(solution)/shard_map/ppermute | solution.py:718
  92.6 31.8 %collective-permute-start.14 = (bf16[128,256]{1,0:T(8,128)(2,1)S(1)}, bf16[128,256]{1,0:T(8,128)(2,1)S(1)}, u32[]{:S(2)}, u32[]{:S(2)}) collective-permute-start(bf16[128,256]{1,0:T(8,128)(2,1)S(1)} %bitcast.234), channel_id=1, source_target_pairs={{0,1},{1,0},{2,3},{3,2},{4,5},{5,4},{6,7},{7,6},{8,9},{9,8},{10,11... | collective-permute-start | bytes 196616 | tf_op jit(solution)/shard_map/ppermute | solution.py:718
  92.6 31.7 %collective-permute-start.15 = (bf16[128,256]{1,0:T(8,128)(2,1)S(1)}, bf16[128,256]{1,0:T(8,128)(2,1)S(1)}, u32[]{:S(2)}, u32[]{:S(2)}) collective-permute-start(bf16[128,256]{1,0:T(8,128)(2,1)S(1)} %bitcast.235), channel_id=1, source_target_pairs={{0,2},{1,3},{2,0},{3,1},{4,6},{5,7},{6,4},{7,5},{8,10},{9,11},{10,... | collective-permute-start | bytes 196616 | tf_op jit(solution)/shard_map/ppermute | solution.py:718
  95.1 29.3 %collective-permute-start.16 = (bf16[128,256]{1,0:T(8,128)(2,1)S(1)}, bf16[128,256]{1,0:T(8,128)(2,1)S(1)}, u32[]{:S(2)}, u32[]{:S(2)}) collective-permute-start(bf16[128,256]{1,0:T(8,128)(2,1)S(1)} %bitcast.236), channel_id=1, source_target_pairs={{0,3},{1,2},{2,1},{3,0},{4,7},{5,6},{6,5},{7,4},{8,11},{9,10},{10,... | collective-permute-start | bytes 196616 | tf_op jit(solution)/shard_map/ppermute | solution.py:718
  96.2 28.2 %collective-permute-start.13 = (bf16[128,2048]{1,0:T(8,128)(2,1)S(1)}, bf16[128,2048]{1,0:T(8,128)(2,1)S(1)}, u32[]{:S(2)}, u32[]{:S(2)}) collective-permute-start(bf16[128,2048]{1,0:T(8,128)(2,1)S(1)} %pad_maximum_fusion.10.near_ref), channel_id=1, source_target_pairs={{0,2},{1,3},{2,0},{3,1},{4,6},{5,7},{6,4},{7,5},{8,10},{9,11},{10,... | collective-permute-start | bytes 1572872 | tf_op jit(solution)/shard_map/ppermute | solution.py:718
  103.6 28.0 %all-to-all-start = ((bf16[8,512,256]{2,1,0:T(8,128)(2,1)}), bf16[8,512,256]{2,1,0:T(8,128)(2,1)S(1)}, u32[]{:S(2)}, u32[]{:S(2)}) async-start(bf16[8,512,256]{2,1,0:T(8,128)(2,1)} %bitcast.224), calls=%async_computation | async-start | bytes 4194304 | tf_op jit(solution)/shard_map/all_to_all | solution.py:903
  108.4 115.5 %all-gather.3.cloned.1.call-start = ((), (), s32[]{:S(2)}) async-start(), calls=%async_computation.5 | async-start | bytes 11796480 | tf_op jit(solution)/shard_map/all_gather | solution.py:1069
  140.5 45.9 %collective-permute-start.17 = (bf16[1024,256]{1,0:T(8,128)(2,1)}, bf16[1024,256]{1,0:T(8,128)(2,1)S(1)}, u32[]{:S(2)}, u32[]{:S(2)}) collective-permute-start(bf16[1024,256]{1,0:T(8,128)(2,1)} %get-tuple-element.289), channel_id=1, source_target_pairs={{0,0},{1,16},{2,1},{3,17},{16,2},{17,18},{18,3},{19,19},{4,4},{5,2... | collective-permute-start | bytes 1572872 | tf_op jit(solution)/shard_map/ppermute | solution.py:751
  148.5 37.9 %collective-permute-start.18 = (bf16[1024,256]{1,0:T(8,128)(2,1)}, bf16[1024,256]{1,0:T(8,128)(2,1)S(1)}, u32[]{:S(2)}, u32[]{:S(2)}) collective-permute-start(bf16[1024,256]{1,0:T(8,128)(2,1)} %get-tuple-element.288), channel_id=1, source_target_pairs={{0,16},{1,0},{2,17},{3,1},{16,18},{17,2},{18,19},{19,3},{4,20},{5,... | collective-permute-start | bytes 1572872 | tf_op jit(solution)/shard_map/ppermute | solution.py:751
  148.6 37.8 %collective-permute-start.19 = (bf16[1024,256]{1,0:T(8,128)(2,1)}, bf16[1024,256]{1,0:T(8,128)(2,1)}, u32[]{:S(2)}, u32[]{:S(2)}) collective-permute-start(bf16[1024,256]{1,0:T(8,128)(2,1)} %get-tuple-element.287), channel_id=1, source_target_pairs={{0,1},{1,17},{2,0},{3,16},{16,3},{17,19},{18,2},{19,18},{4,5},{5,2... | collective-permute-start | bytes 1572872 | tf_op jit(solution)/shard_map/ppermute | solution.py:751
  150.9 43.8 %collective-permute-start.20 = (bf16[1024,256]{1,0:T(8,128)(2,1)}, bf16[1024,256]{1,0:T(8,128)(2,1)}, u32[]{:S(2)}, u32[]{:S(2)}) collective-permute-start(bf16[1024,256]{1,0:T(8,128)(2,1)} %get-tuple-element.286), channel_id=1, source_target_pairs={{0,17},{1,1},{2,16},{3,0},{16,19},{17,3},{18,18},{19,2},{4,21},{5,... | collective-permute-start | bytes 1572872 | tf_op jit(solution)/shard_map/ppermute | solution.py:751
  208.3 15.6 %all-to-all-start.1 = ((bf16[8,512,128]{1,2,0:T(8,128)(2,1)}), bf16[8,512,128]{1,2,0:T(8,128)(2,1)S(1)}, u32[]{:S(2)}, u32[]{:S(2)}) async-start(bf16[8,512,128]{1,2,0:T(8,128)(2,1)} %copy.121), calls=%async_computation.1 | async-start | bytes 2097152 | tf_op jit(solution)/shard_map/all_to_all | solution.py:909
  211.9 143.2 %all-gather.5.cloned.1.call-start = ((), (), s32[]{:S(2)}) async-start(), calls=%async_computation.6 | async-start | bytes 9437184 | tf_op jit(solution)/shard_map/all_gather | solution.py:1097
  221.3 25.0 %collective-permute-start.21 = (bf16[512,1024]{1,0:T(8,128)(2,1)}, bf16[512,1024]{1,0:T(8,128)(2,1)}, u32[]{:S(2)}, u32[]{:S(2)}) collective-permute-start(bf16[512,1024]{1,0:T(8,128)(2,1)} %unstack.11), channel_id=1, source_target_pairs={{0,1},{1,0},{2,3},{3,2},{4,5},{5,4},{6,7},{7,6},{8,9},{9,8},{10,11... | collective-permute-start | bytes 3145736 | tf_op jit(solution)/shard_map/ppermute | solution.py:718
  246.4 24.1 %collective-permute-start.22 = (bf16[512,1024]{1,0:T(8,128)(2,1)}, bf16[512,1024]{1,0:T(8,128)(2,1)}, u32[]{:S(2)}, u32[]{:S(2)}) collective-permute-start(bf16[512,1024]{1,0:T(8,128)(2,1)} %fusion.53), channel_id=1, source_target_pairs={{0,1},{1,0},{2,3},{3,2},{4,5},{5,4},{6,7},{7,6},{8,9},{9,8},{10,11... | collective-permute-start | bytes 3145736 | tf_op jit(solution)/shard_map/ppermute | solution.py:718
  270.7 23.7 %collective-permute-start.23 = (bf16[512,256]{1,0:T(8,128)(2,1)S(1)}, bf16[512,256]{1,0:T(8,128)(2,1)S(1)}, u32[]{:S(2)}, u32[]{:S(2)}) collective-permute-start(bf16[512,256]{1,0:T(8,128)(2,1)S(1)} %get-tuple-element.314), channel_id=1, source_target_pairs={{0,0},{1,16},{2,1},{3,17},{16,2},{17,18},{18,3},{19,19},{4,4},{5,2... | collective-permute-start | bytes 786440 | tf_op jit(solution)/shard_map/ppermute | solution.py:751
  274.1 20.3 %collective-permute-start.24 = (bf16[512,256]{1,0:T(8,128)(2,1)S(1)}, bf16[512,256]{1,0:T(8,128)(2,1)S(1)}, u32[]{:S(2)}, u32[]{:S(2)}) collective-permute-start(bf16[512,256]{1,0:T(8,128)(2,1)S(1)} %get-tuple-element.313), channel_id=1, source_target_pairs={{0,16},{1,0},{2,17},{3,1},{16,18},{17,2},{18,19},{19,3},{4,20},{5,... | collective-permute-start | bytes 786440 | tf_op jit(solution)/shard_map/ppermute | solution.py:751
  275.5 18.9 %collective-permute-start.25 = (bf16[512,256]{1,0:T(8,128)(2,1)S(1)}, bf16[512,256]{1,0:T(8,128)(2,1)S(1)}, u32[]{:S(2)}, u32[]{:S(2)}) collective-permute-start(bf16[512,256]{1,0:T(8,128)(2,1)S(1)} %get-tuple-element.312), channel_id=1, source_target_pairs={{0,1},{1,17},{2,0},{3,16},{16,3},{17,19},{18,2},{19,18},{4,5},{5,2... | collective-permute-start | bytes 786440 | tf_op jit(solution)/shard_map/ppermute | solution.py:751
  276.9 22.3 %collective-permute-start.26 = (bf16[512,256]{1,0:T(8,128)(2,1)S(1)}, bf16[512,256]{1,0:T(8,128)(2,1)S(1)}, u32[]{:S(2)}, u32[]{:S(2)}) collective-permute-start(bf16[512,256]{1,0:T(8,128)(2,1)S(1)} %get-tuple-element.311), channel_id=1, source_target_pairs={{0,17},{1,1},{2,16},{3,0},{16,19},{17,3},{18,18},{19,2},{4,21},{5,... | collective-permute-start | bytes 786440 | tf_op jit(solution)/shard_map/ppermute | solution.py:751
  303.9 25.4 %collective-permute-start.27 = (bf16[512,1024]{1,0:T(8,128)(2,1)S(1)}, bf16[512,1024]{1,0:T(8,128)(2,1)S(1)}, u32[]{:S(2)}, u32[]{:S(2)}) collective-permute-start(bf16[512,1024]{1,0:T(8,128)(2,1)S(1)} %fusion.75), channel_id=1, source_target_pairs={{0,1},{1,0},{2,3},{3,2},{4,5},{5,4},{6,7},{7,6},{8,9},{9,8},{10,11... | collective-permute-start | bytes 3145736 | tf_op jit(solution)/shard_map/ppermute | solution.py:718
  306.7 14.4 %collective-permute-start.29 = (bf16[512,2048]{1,0:T(8,128)(2,1)S(1)}, bf16[512,2048]{1,0:T(8,128)(2,1)S(1)}, u32[]{:S(2)}, u32[]{:S(2)}) collective-permute-start(bf16[512,2048]{1,0:T(8,128)(2,1)S(1)} %convolution_convert_fusion), channel_id=1, source_target_pairs={{0,16},{16,0},{1,17},{17,1},{2,18},{18,2},{3,19},{19,3},{4,20},{20... | collective-permute-start | bytes 6291464 | tf_op jit(solution)/shard_map/ppermute | solution.py:718
  309.5 15.9 %collective-permute-start.28 = (bf16[512,2048]{1,0:T(8,128)(2,1)S(1)}, bf16[512,2048]{1,0:T(8,128)(2,1)S(1)}, u32[]{:S(2)}, u32[]{:S(2)}) collective-permute-start(bf16[512,2048]{1,0:T(8,128)(2,1)S(1)} %convolution_convert_fusion.1), channel_id=1, source_target_pairs={{0,16},{16,0},{1,17},{17,1},{2,18},{18,2},{3,19},{19,3},{4,20},{20... | collective-permute-start | bytes 6291464 | tf_op jit(solution)/shard_map/ppermute | solution.py:718
  339.1 16.0 %all-to-all-start.2 = ((bf16[8,512,128]{2,1,0:T(8,128)(2,1)}), bf16[8,512,128]{2,1,0:T(8,128)(2,1)}, u32[]{:S(2)}, u32[]{:S(2)}) async-start(bf16[8,512,128]{2,1,0:T(8,128)(2,1)} %bitcast.248), calls=%async_computation.2 | async-start | bytes 2097152 | tf_op jit(solution)/shard_map/all_to_all | solution.py:903
  343.3 114.7 %reduce-scatter.2.cloned.1.call-start = ((), (), s32[]{:S(2)}) async-start(), calls=%async_computation.7 | async-start | bytes 7372800 | tf_op jit(solution)/shard_map/reduce_scatter | solution.py:1150
  355.2 56.5 %collective-permute-start.36 = (bf16[512,1024]{1,0:T(8,128)(2,1)}, bf16[512,1024]{1,0:T(8,128)(2,1)S(1)}, u32[]{:S(2)}, u32[]{:S(2)}) collective-permute-start(bf16[512,1024]{1,0:T(8,128)(2,1)} %fusion.78), channel_id=1, source_target_pairs={{0,1},{1,0},{2,3},{3,2},{4,5},{5,4},{6,7},{7,6},{8,9},{9,8},{10,11... | collective-permute-start | bytes 3145736 | tf_op jit(solution)/shard_map/ppermute | solution.py:718
  358.5 53.2 %collective-permute-start.32 = (bf16[1024,256]{1,0:T(8,128)(2,1)S(1)}, bf16[1024,256]{1,0:T(8,128)(2,1)S(1)}, u32[]{:S(2)}, u32[]{:S(2)}) collective-permute-start(bf16[1024,256]{1,0:T(8,128)(2,1)S(1)} %get-tuple-element.282), channel_id=1, source_target_pairs={{0,0},{16,1},{1,2},{17,3},{2,16},{18,17},{3,18},{19,19},{4,4},{20,... | collective-permute-start | bytes 1572872 | tf_op jit(solution)/shard_map/ppermute | solution.py:777
  364.2 47.5 %collective-permute-start.33 = (bf16[1024,256]{1,0:T(8,128)(2,1)S(1)}, bf16[1024,256]{1,0:T(8,128)(2,1)S(1)}, u32[]{:S(2)}, u32[]{:S(2)}) collective-permute-start(bf16[1024,256]{1,0:T(8,128)(2,1)S(1)} %get-tuple-element.281), channel_id=1, source_target_pairs={{16,0},{0,1},{17,2},{1,3},{18,16},{2,17},{19,18},{3,19},{20,4},{4,... | collective-permute-start | bytes 1572872 | tf_op jit(solution)/shard_map/ppermute | solution.py:777
  364.3 47.4 %collective-permute-start.34 = (bf16[1024,256]{1,0:T(8,128)(2,1)S(1)}, bf16[1024,256]{1,0:T(8,128)(2,1)S(1)}, u32[]{:S(2)}, u32[]{:S(2)}) collective-permute-start(bf16[1024,256]{1,0:T(8,128)(2,1)S(1)} %get-tuple-element.280), channel_id=1, source_target_pairs={{1,0},{17,1},{0,2},{16,3},{3,16},{19,17},{2,18},{18,19},{5,4},{21,... | collective-permute-start | bytes 1572872 | tf_op jit(solution)/shard_map/ppermute | solution.py:777
  364.7 47.0 %collective-permute-start.35 = (bf16[1024,256]{1,0:T(8,128)(2,1)S(1)}, bf16[1024,256]{1,0:T(8,128)(2,1)S(1)}, u32[]{:S(2)}, u32[]{:S(2)}) collective-permute-start(bf16[1024,256]{1,0:T(8,128)(2,1)S(1)} %get-tuple-element.279), channel_id=1, source_target_pairs={{17,0},{1,1},{16,2},{0,3},{19,16},{3,17},{18,18},{2,19},{21,4},{5,... | collective-permute-start | bytes 1572872 | tf_op jit(solution)/shard_map/ppermute | solution.py:777
  412.2 21.3 %collective-permute-start.37 = (bf16[512,256]{1,0:T(8,128)(2,1)S(1)}, bf16[512,256]{1,0:T(8,128)(2,1)S(1)}, u32[]{:S(2)}, u32[]{:S(2)}) collective-permute-start(bf16[512,256]{1,0:T(8,128)(2,1)S(1)} %get-tuple-element.310), channel_id=1, source_target_pairs={{0,0},{16,1},{1,2},{17,3},{2,16},{18,17},{3,18},{19,19},{4,4},{20,... | collective-permute-start | bytes 786440 | tf_op jit(solution)/shard_map/ppermute | solution.py:777
  416.3 17.2 %collective-permute-start.38 = (bf16[512,256]{1,0:T(8,128)(2,1)S(1)}, bf16[512,256]{1,0:T(8,128)(2,1)S(1)}, u32[]{:S(2)}, u32[]{:S(2)}) collective-permute-start(bf16[512,256]{1,0:T(8,128)(2,1)S(1)} %get-tuple-element.309), channel_id=1, source_target_pairs={{16,0},{0,1},{17,2},{1,3},{18,16},{2,17},{19,18},{3,19},{20,4},{4,... | collective-permute-start | bytes 786440 | tf_op jit(solution)/shard_map/ppermute | solution.py:777
  437.3 31.3 %all-to-all-start.3 = ((bf16[8,512,256]{1,2,0:T(8,128)(2,1)}), bf16[8,512,256]{1,2,0:T(8,128)(2,1)}, u32[]{:S(2)}, u32[]{:S(2)}) async-start(bf16[8,512,256]{1,2,0:T(8,128)(2,1)} %copy.126), calls=%async_computation.4 | async-start | bytes 4194304 | tf_op jit(solution)/shard_map/all_to_all | solution.py:909
  446.2 15.1 %collective-permute-start.39 = (bf16[512,256]{1,0:T(8,128)(2,1)}, bf16[512,256]{1,0:T(8,128)(2,1)}, u32[]{:S(2)}, u32[]{:S(2)}) collective-permute-start(bf16[512,256]{1,0:T(8,128)(2,1)} %get-tuple-element.308), channel_id=1, source_target_pairs={{1,0},{17,1},{0,2},{16,3},{3,16},{19,17},{2,18},{18,19},{5,4},{21,... | collective-permute-start | bytes 786440 | tf_op jit(solution)/shard_map/ppermute | solution.py:777
  447.1 15.0 %collective-permute-start.40 = (bf16[512,256]{1,0:T(8,128)(2,1)S(1)}, bf16[512,256]{1,0:T(8,128)(2,1)}, u32[]{:S(2)}, u32[]{:S(2)}) collective-permute-start(bf16[512,256]{1,0:T(8,128)(2,1)S(1)} %get-tuple-element.307), channel_id=1, source_target_pairs={{17,0},{1,1},{16,2},{0,3},{19,16},{3,17},{18,18},{2,19},{21,4},{5,... | collective-permute-start | bytes 786440 | tf_op jit(solution)/shard_map/ppermute | solution.py:777
  459.4 28.3 %collective-permute-start.41 = (bf16[144,2048]{1,0:T(8,128)(2,1)S(1)}, bf16[144,2048]{1,0:T(8,128)(2,1)S(1)}, u32[]{:S(2)}, u32[]{:S(2)}) collective-permute-start(bf16[144,2048]{1,0:T(8,128)(2,1)S(1)} %pad_maximum_fusion.7), channel_id=1, source_target_pairs={{0,2},{1,3},{2,0},{3,1},{4,6},{5,7},{6,4},{7,5},{8,10},{9,11},{10,... | collective-permute-start | bytes 1769480 | tf_op jit(solution)/shard_map/ppermute | solution.py:718
  508.2 21.6 %collective-permute-start.42 = (bf16[512,256]{1,0:T(8,128)(2,1)S(1)}, bf16[512,256]{1,0:T(8,128)(2,1)S(1)}, u32[]{:S(2)}, u32[]{:S(2)}) collective-permute-start(bf16[512,256]{1,0:T(8,128)(2,1)S(1)} %get-tuple-element.306), channel_id=1, source_target_pairs={{0,0},{16,1},{1,2},{17,3},{2,16},{18,17},{3,18},{19,19},{4,4},{20,... | collective-permute-start | bytes 786440 | tf_op jit(solution)/shard_map/ppermute | solution.py:777
  511.1 26.7 %collective-permute-start.43 = (bf16[512,256]{1,0:T(8,128)(2,1)S(1)}, bf16[512,256]{1,0:T(8,128)(2,1)S(1)}, u32[]{:S(2)}, u32[]{:S(2)}) collective-permute-start(bf16[512,256]{1,0:T(8,128)(2,1)S(1)} %get-tuple-element.305), channel_id=1, source_target_pairs={{16,0},{0,1},{17,2},{1,3},{18,16},{2,17},{19,18},{3,19},{20,4},{4,... | collective-permute-start | bytes 786440 | tf_op jit(solution)/shard_map/ppermute | solution.py:777
  511.3 36.7 %collective-permute-start.46 = (bf16[128,2048]{1,0:T(8,128)(2,1)S(1)}, bf16[128,2048]{1,0:T(8,128)(2,1)S(1)}, u32[]{:S(2)}, u32[]{:S(2)}) collective-permute-start(bf16[128,2048]{1,0:T(8,128)(2,1)S(1)} %add_convert_fusion.6.refs_0_), channel_id=1, source_target_pairs={{0,4},{4,0},{8,12},{12,8},{1,5},{5,1},{9,13},{13,9},{2,6},{6,2},{1... | collective-permute-start | bytes 1572872 | tf_op jit(solution)/shard_map/ppermute | solution.py:718
  513.4 34.7 %collective-permute-start.47 = (bf16[128,2048]{1,0:T(8,128)(2,1)S(1)}, bf16[128,2048]{1,0:T(8,128)(2,1)S(1)}, u32[]{:S(2)}, u32[]{:S(2)}) collective-permute-start(bf16[128,2048]{1,0:T(8,128)(2,1)S(1)} %add_convert_fusion.6.refs_0_), channel_id=1, source_target_pairs={{0,8},{4,12},{8,0},{12,4},{1,9},{5,13},{9,1},{13,5},{2,10},{6,14},... | collective-permute-start | bytes 1572872 | tf_op jit(solution)/shard_map/ppermute | solution.py:718
  516.0 32.1 %collective-permute-start.48 = (bf16[128,2048]{1,0:T(8,128)(2,1)S(1)}, bf16[128,2048]{1,0:T(8,128)(2,1)S(1)}, u32[]{:S(2)}, u32[]{:S(2)}) collective-permute-start(bf16[128,2048]{1,0:T(8,128)(2,1)S(1)} %add_convert_fusion.6.refs_0_), channel_id=1, source_target_pairs={{0,12},{4,8},{8,4},{12,0},{1,13},{5,9},{9,5},{13,1},{2,14},{6,10},... | collective-permute-start | bytes 1572872 | tf_op jit(solution)/shard_map/ppermute | solution.py:718
  551.9 20.8 %collective-permute-start.56 = (bf16[1,400,256]{2,1,0:T(8,128)(2,1)S(1)}, bf16[1,400,256]{2,1,0:T(8,128)(2,1)}, u32[]{:S(2)}, u32[]{:S(2)}) collective-permute-start(bf16[1,400,256]{2,1,0:T(8,128)(2,1)S(1)} %maximum_bitcast_fusion), channel_id=1, source_target_pairs={{0,4},{4,0},{8,12},{12,8},{1,5},{5,1},{9,13},{13,9},{2,6},{6,2},{1... | collective-permute-start | bytes 614408 | tf_op jit(solution)/shard_map/ppermute | solution.py:718
  (89 other events, 656.0 us)
Sparse Core Ops, SparseCore 0:
  133.0 65.1 all-gather.2
  246.7 54.5 all-gather.4
  355.3 68.1 reduce-scatter.1

commit v5 on v4

--- a/solution.py
+++ b/solution.py
@@ -1040,11 +1040,12 @@
         quarter_of(item, ctx) for item in (expand_weight, shrink_weight.T, output_weight.T)
     )
     quarters = lax.axis_size("ctx")
-    pair_pieces, (normed, attn_scaled, attn_inverse), labels = lax.optimization_barrier(
+    pair_pieces, (normed, attn_scaled, attn_inverse), labels, stacked = lax.optimization_barrier(
         (
             [swap(pair_wide, "ctx", j) for j in range(1, quarters)],
             norm_rows(second_rows.astype(f32), attention_gain, attention_shift),
             plane_labels(*after((segment_ids, bucket_ids, positions), second_rows)),
+            jnp.stack([first_half, second_cotangent]),
         )
     )
     places, segments, buckets = labels
@@ -1077,7 +1078,7 @@
     query_sorted, value_sorted = sorted_pair[:, :DH], sorted_pair[:, DH:]
     bounds = with_bound(bounds, query_sorted)
     (first_rows, second_grad_rows), (mix, logs) = rows_in(
-        after(jnp.stack([first_half, second_cotangent]), landed),
+        after(stacked, landed),
         attend(bounds, query_sorted, value_sorted, hot),
     )
     far_grad_rows = swap(after(second_grad_rows, mix), "tp", 1)
@@ -1159,7 +1160,8 @@
     second_out = (own_branch + far_branch.astype(f32)).astype(bf16)
     def with_far(pair_grad_heads):
         sums = after(early_mine, pair_grad_heads)
-        far = jnp.concatenate([sums[:, units : 2 * units], sums[:, 3 * units : 4 * units]], 1)
+        held = sums[: split // quarters]
+        far = jnp.concatenate([held[:, units : 2 * units], held[:, 3 * units : 4 * units]], 1)
         pair_sums = lax.dot_general(
             normed_all, pair_grad_heads, (((0,), (0,)), ((), ())), preferred_element_type=f32
         ).astype(bf16)
@@ -1173,7 +1175,8 @@
         out_of_places(places, jnp.concatenate(parts, 1)),
         with_far,
     )
-    near_sums = jnp.concatenate([early_mine[:, :units], early_mine[:, 2 * units : 3 * units]], 1)
+    held = early_mine[: split // quarters]
+    near_sums = jnp.concatenate([held[:, :units], held[:, 2 * units : 3 * units]], 1)
 
     grad_mine, grad_other = dot(pair_grad, pair_mine, NT), dot(pair_grad, pair_other, NT)
     normed_grad = jnp.concatenate(
@@ -1189,7 +1192,6 @@
     second_grad = (second_grad_rows.astype(f32) + attn_back).astype(bf16)
 
     early_own = (near_sums.astype(f32) + far_sums.astype(f32)).astype(bf16)
-    early_own = early_own[: split // quarters]
     pieces = [swap(plane_part(late, k), "tp", k) for k in range(1, planes)]
     late = sum((piece.astype(f32) for piece in pieces), plane_part(late, 0).astype(f32)).astype(bf16)
     split_at = width

time: 601 us -> 600 us (level)
  waiting for transfers between devices: 143 us -> 127 us
  starting transfers between devices: 122 us -> 129 us
    ppermute x39, waiting for transfers between devices: 57.9 us -> 51.2 us  [swap(): return lax.ppermute(vectors, axis, [(at, at ^ bits) for at in range(size)])]
    unnamed x148 -> x142, local copies, waits for them, and re-layouts: 29.1 us -> 28.7 us
  transfers between devices with their start and end apart: 71 -> 71, of which waited for: 21 -> 19; matrix products, arithmetic and copies ran while one was open for 39% -> 39% of each run, Pallas kernels for 8% -> 8%
where the time goes in v5:
time: 600 us; the launch traced here: 589 us
  matrix products  149 us (25%)
  starting transfers between devices  129 us (22%)
  waiting for transfers between devices  127 us (21%)
  local copies, waits for them, and re-layouts  76.5 us (13%)
  Pallas kernels  48.6 us (8%)
  other arithmetic  41.6 us (7%)
  between operations  17.2 us (3%)
    dot_general x16, matrix products, dot(): lax.dot_general(left, right, dims, preferred_element_type=jnp.float32)  83.9 us
    ppermute x39, waiting for transfers between devices, swap(): return lax.ppermute(vectors, axis, [(at, at ^ bits) for at in range(size)])  51.2 us
    ppermute x39, starting transfers between devices, swap(): return lax.ppermute(vectors, axis, [(at, at ^ bits) for at in range(size)])  46.9 us
    dot_general x3, matrix products, into_places(): jnp.einsum('pa,ad->pd', place_matrix(places), vectors, preferred_element_...  40.9 us
    ppermute x12, waiting for transfers between devices, rows_in(): lax.ppermute(chunk, ('shard', 'tp'), plane_pairs(step, False))  40.6 us
    ppermute x12, starting transfers between devices, rows_in(): lax.ppermute(chunk, ('shard', 'tp'), plane_pairs(step, False))  30.6 us
    ppermute x12, starting transfers between devices, send(): return lax.ppermute(piece, ('shard', 'tp'), plane_pairs(step, True))  29.7 us
    pallas_call x1, Pallas kernels, attend_back(): pl.pallas_call(attend_back_kernel, name='attend_back', out_shape=(jax.Sha...  29.5 us
  transfers between devices with their start and end apart: 71, of which 19 were waited for; matrix products, arithmetic and copies ran while one was open for 39% of the time, Pallas kernels for 8%

profile of v5, /device:TPU:1, one launch (start us, length us, event | category | flops | bytes accessed | tf_op | source)
XLA Modules:
  0.0 588.5 jit_solution(4147485836237251927)
XLA Ops:
  13.2 5.7 collective-permute-start.1
  23.5 4.4 pad_maximum_fusion.1
  27.9 8.3 %collective-permute-done.2 = bf16[784,256]{1,0:T(8,128)(2,1)} collective-permute-done((bf16[784,256]{1,0:T(8,128)(2,1)}, bf16[784,256]{1,0:T(8,128)(2,1)}, u32[]{:S(2)}, u32[]{:S(2)}) %collective-permute-start.2) | collective-permute-done | bytes 401440 | tf_op jit(solution)/shard_map/ppermute | solution.py:751
  36.2 7.2 %collective-permute-done.3 = bf16[784,256]{1,0:T(8,128)(2,1)} collective-permute-done((bf16[784,256]{1,0:T(8,128)(2,1)}, bf16[784,256]{1,0:T(8,128)(2,1)}, u32[]{:S(2)}, u32[]{:S(2)}) %collective-permute-start.3) | collective-permute-done | bytes 401440 | tf_op jit(solution)/shard_map/ppermute | solution.py:751
  43.4 11.9 %collective-permute-done.4 = bf16[784,256]{1,0:T(8,128)(2,1)} collective-permute-done((bf16[784,256]{1,0:T(8,128)(2,1)}, bf16[784,256]{1,0:T(8,128)(2,1)}, u32[]{:S(2)}, u32[]{:S(2)}) %collective-permute-start.4) | collective-permute-done | bytes 401440 | tf_op jit(solution)/shard_map/ppermute | solution.py:751
  74.9 7.0 %collective-permute-done.9 = s32[48,128]{1,0:T(8,128)S(1)} collective-permute-done((s32[48,128]{1,0:T(8,128)S(1)}, s32[48,128]{1,0:T(8,128)S(1)}, u32[]{:S(2)}, u32[]{:S(2)}) %collective-permute-start.9) | collective-permute-done | bytes 24608 | tf_op jit(solution)/shard_map/ppermute | solution.py:718
  106.0 4.8 all-to-all-start
  111.0 15.6 %fusion.12.hot_ref = bf16[4096,256]{1,0:T(8,128)(2,1)} fusion(pred[4096,256]{0,1:T(32,128)(4,1)} %bitcast_compare_fusion, s32[4096]{0:T(1024)S(1)} %bitcast.288), kind=kOutput, calls=%fused_computation.19 | convolution fusion | flops 8607760384 | bytes 3162112 | tf_op jit(solution)/shard_map/pa,ad->pd/dot_general | solution.py:308
  126.8 7.1 %all-to-all-done = bf16[8,512,256]{2,1,0:T(8,128)(2,1)S(1)} async-done(((bf16[8,512,256]{2,1,0:T(8,128)(2,1)}), bf16[8,512,256]{2,1,0:T(8,128)(2,1)S(1)}, u32[]{:S(2)}, u32[]{:S(2)}) %all-to-all-start) | async-done | bytes 2097184 | tf_op jit(solution)/shard_map/all_to_all | solution.py:903
  139.1 8.0 %collective-permute-start.17 = (bf16[1024,256]{1,0:T(8,128)(2,1)}, bf16[1024,256]{1,0:T(8,128)(2,1)S(1)}, u32[]{:S(2)}, u32[]{:S(2)}) collective-permute-start(bf16[1024,256]{1,0:T(8,128)(2,1)} %get-tuple-element.291), channel_id=1, source_target_pairs={{0,0},{1,16},{2,1},{3,17},{16,2},{17,18},{18,3},{19,19},{4,4},{5,2... | collective-permute-start | bytes 1572872 | tf_op jit(solution)/shard_map/ppermute | solution.py:751
  151.4 12.2 %fusion.13 = bf16[4096,256]{1,0:T(8,128)(2,1)S(1)} fusion(bf16[4096,256]{1,0:T(8,128)(2,1)S(1)} %bitcast.257, s32[4096]{0:T(1024)S(1)} %bitcast.289), kind=kOutput, calls=%fused_computation.20 | convolution fusion | flops 8607760384 | bytes 4210688 | tf_op jit(solution)/shard_map/pa,ad->pd/dot_general | solution.py:308
  167.3 17.5 %attend.1 = (f32[128,4096]{1,0:T(8,128)S(1)}, f32[8,512]{1,0:T(8,128)S(1)}) custom-call(s32[4]{0:T(128)S(1)} %pad_add_fusion.bounds_ref, bf16[4096,128]{1,0:T(8,128)(2,1)S(1)} %get-tuple-element.287.q_ref, bf16[4096,128]{1,0:T(8,128)(2,1)S(1)} %get-tuple-element.286.v_ref, bf16[4096,256]{1,0:T(8,128)(2,1)S(1)} %copy-done.4), custom_call_target="tpu_custom_call" | custom-call | flops 524288 | bytes 524288 | tf_op jit(solution)/shard_map/attend/pallas_call | solution.py:150
  184.8 8.5 %collective-permute-done.20 = bf16[1024,256]{1,0:T(8,128)(2,1)} collective-permute-done((bf16[1024,256]{1,0:T(8,128)(2,1)}, bf16[1024,256]{1,0:T(8,128)(2,1)}, u32[]{:S(2)}, u32[]{:S(2)}) %collective-permute-start.20) | collective-permute-done | bytes 524320 | tf_op jit(solution)/shard_map/ppermute | solution.py:751
  193.3 12.2 %fusion.16 = bf16[4096,128]{1,0:T(8,128)(2,1)S(1)} fusion(s32[4096]{0:T(1024)S(1)} %bitcast.290, f32[128,4096]{1,0:T(8,128)S(1)} %get-tuple-element.137.out_ref), kind=kOutput, calls=%fused_computation.23 | convolution fusion | flops 4312793088 | bytes 3162112 | tf_op jit(solution)/shard_map/dot_general | solution.py:30
  206.8 3.7 all-to-all-start.1
  223.4 4.0 convert_reduce_fusion.3
  229.3 15.6 %collective-permute-done.21 = bf16[512,1024]{1,0:T(8,128)(2,1)} collective-permute-done((bf16[512,1024]{1,0:T(8,128)(2,1)}, bf16[512,1024]{1,0:T(8,128)(2,1)}, u32[]{:S(2)}, u32[]{:S(2)}) %collective-permute-start.21) | collective-permute-done | bytes 1048608 | tf_op jit(solution)/shard_map/ppermute | solution.py:718
  245.1 6.5 %multiply_convert_fusion.1 = (bf16[512,2048]{1,0:T(8,128)(2,1)}, f32[512,2048]{1,0:T(8,128)}) fusion(f32[2048]{0:T(1024)S(1)} %pad_maximum_fusion.14, bf16[512,1024]{1,0:T(8,128)(2,1)} %fusion.53, bf16[1024,5120]{1,0:T(8,128)(2,1)} %all-gather.3.cloned.1.call-done), kind=kOutput, calls=%fused_computation.41 | convolution fusion | flops 2153775104 | bytes 11542528 | tf_op jit(solution)/shard_map/dot_general | solution.py:30
  253.9 6.8 %fusion.22 = bf16[512,2048]{1,0:T(8,128)(2,1)S(1)} fusion(f32[512,2048]{1,0:T(8,128)} %get-tuple-element.341, bf16[1024,5120]{1,0:T(8,128)(2,1)} %all-gather.3.cloned.1.call-done, f32[2048]{0:T(1024)S(1)} %pad_maximum_fusion.14, bf16[1024,1024]{1,0:T(8,128)(2,1)} %constant_dynamic-update-slice_fusion.8), kind=kOutput, calls=%fused_computation.29 | convolution fusion | flops 2159017984 | bytes 11542528 | tf_op jit(solution)/shard_map/dot_general | solution.py:30
  260.7 8.4 %collective-permute-done.22 = bf16[512,1024]{1,0:T(8,128)(2,1)} collective-permute-done((bf16[512,1024]{1,0:T(8,128)(2,1)}, bf16[512,1024]{1,0:T(8,128)(2,1)}, u32[]{:S(2)}, u32[]{:S(2)}) %collective-permute-start.22) | collective-permute-done | bytes 1048608 | tf_op jit(solution)/shard_map/ppermute | solution.py:718
  279.2 4.1 multiply_convert_fusion
  283.3 3.7 fusion.62
  287.0 5.4 fusion.28
  293.0 4.7 collective-permute-done.26
  297.8 4.7 fusion.75
  309.6 5.5 fusion.78
  315.1 4.6 fusion.35
  319.6 4.3 add_convert_fusion
  323.9 3.9 add_convert_fusion.1
  337.7 4.2 all-to-all-start.2
  346.8 4.4 fusion.11
  357.0 5.7 collective-permute-start.32
  363.3 4.4 collective-permute-start.35
  367.7 13.1 %fusion.15.grad_ref = bf16[4096,128]{1,0:T(8,128)(2,1)S(1)} fusion(bf16[4096,128]{1,0:T(8,128)(2,1)} %bitcast.63, s32[4096]{0:T(1024)S(1)} %bitcast.291), kind=kOutput, calls=%fused_computation.22 | convolution fusion | flops 4312268800 | bytes 2113536 | tf_op jit(solution)/shard_map/pa,ad->pd/dot_general | solution.py:308
  380.8 29.5 %attend_back.1 = (bf16[4096,128]{1,0:T(8,128)(2,1)S(1)}, bf16[4096,128]{1,0:T(8,128)(2,1)S(1)}) custom-call(s32[4]{0:T(128)S(1)} %pad_add_fusion.bounds_ref, bf16[4096,128]{1,0:T(8,128)(2,1)S(1)} %get-tuple-element.287.q_ref, bf16[4096,128]{1,0:T(8,128)(2,1)S(1)} %get-tuple-element.286.v_ref, bf16[4096,256]{1,0:T(8,128)(2,1)} %fusion.12.hot_ref, ...), custom_call_target="tpu_custom_call" | custom-call | flops 524288 | bytes 524288 | tf_op jit(solution)/shard_map/attend_back/pallas_call | solution.py:273
  410.8 4.1 collective-permute-start.37
  415.5 12.3 %fusion.14 = bf16[4096,256]{1,0:T(8,128)(2,1)S(1)} fusion(s32[4096]{0:T(1024)S(1)} %bitcast.292, bf16[4096,128]{1,0:T(8,128)(2,1)S(1)} %get-tuple-element.176, bf16[4096,128]{1,0:T(8,128)(2,1)S(1)} %get-tuple-element.175), kind=kOutput, calls=%fused_computation.21 | convolution fusion | flops 8611954688 | bytes 4210688 | tf_op jit(solution)/shard_map/dot_general | solution.py:30
  435.9 8.1 %all-to-all-start.3 = ((bf16[8,512,256]{1,2,0:T(8,128)(2,1)}), bf16[8,512,256]{1,2,0:T(8,128)(2,1)}, u32[]{:S(2)}, u32[]{:S(2)}) async-start(bf16[8,512,256]{1,2,0:T(8,128)(2,1)} %copy.126), calls=%async_computation.4 | async-start | bytes 4194304 | tf_op jit(solution)/shard_map/all_to_all | solution.py:909
  445.7 4.4 collective-permute-start.40
  450.1 6.6 %convolution_convert_fusion.3 = bf16[1024,256]{1,0:T(8,128)(2,1)} fusion(bf16[4096,1024]{1,0:T(8,128)(2,1)} %all-gather.5.cloned.1.call-done, bf16[4096,256]{1,0:T(8,128)(2,1)S(1)} %fusion.14), kind=kOutput, calls=%fused_computation.117 | convolution fusion | flops 2147745792 | bytes 11010048 | tf_op jit(solution)/shard_map/dot_general | solution.py:1165
  460.7 6.5 %all-to-all-done.3 = bf16[8,512,256]{1,2,0:T(8,128)(2,1)} async-done(((bf16[8,512,256]{1,2,0:T(8,128)(2,1)}), bf16[8,512,256]{1,2,0:T(8,128)(2,1)}, u32[]{:S(2)}, u32[]{:S(2)}) %all-to-all-start.3) | async-done | bytes 2097184 | tf_op jit(solution)/shard_map/all_to_all | solution.py:909
  467.2 16.1 %collective-permute-done.41 = bf16[128,2048]{1,0:T(8,128)(2,1)S(1)} collective-permute-done((bf16[128,2048]{1,0:T(8,128)(2,1)S(1)}, bf16[128,2048]{1,0:T(8,128)(2,1)S(1)}, u32[]{:S(2)}, u32[]{:S(2)}) %collective-permute-start.41) | collective-permute-done | bytes 524320 | tf_op jit(solution)/shard_map/ppermute | solution.py:718
  484.1 3.7 fusion.126
  503.8 3.4 collective-permute-start.42
  513.8 11.9 %collective-permute-done.42 = bf16[512,256]{1,0:T(8,128)(2,1)S(1)} collective-permute-done((bf16[512,256]{1,0:T(8,128)(2,1)S(1)}, bf16[512,256]{1,0:T(8,128)(2,1)S(1)}, u32[]{:S(2)}, u32[]{:S(2)}) %collective-permute-start.42) | collective-permute-done | bytes 262176 | tf_op jit(solution)/shard_map/ppermute | solution.py:777
  526.7 3.9 collective-permute-done.43
  530.6 6.0 %collective-permute-start.45 = (bf16[512,256]{1,0:T(8,128)(2,1)S(1)}, bf16[512,256]{1,0:T(8,128)(2,1)S(1)}, u32[]{:S(2)}, u32[]{:S(2)}) collective-permute-start(bf16[512,256]{1,0:T(8,128)(2,1)S(1)} %get-tuple-element.304), channel_id=1, source_target_pairs={{17,0},{1,1},{16,2},{0,3},{19,16},{3,17},{18,18},{2,19},{21,4},{5,... | collective-permute-start | bytes 786440 | tf_op jit(solution)/shard_map/ppermute | solution.py:777
  547.2 9.9 %collective-permute-start.56 = (bf16[1,400,256]{2,1,0:T(8,128)(2,1)S(1)}, bf16[1,400,256]{2,1,0:T(8,128)(2,1)}, u32[]{:S(2)}, u32[]{:S(2)}) collective-permute-start(bf16[1,400,256]{2,1,0:T(8,128)(2,1)S(1)} %maximum_bitcast_fusion), channel_id=1, source_target_pairs={{0,4},{4,0},{8,12},{12,8},{1,5},{5,1},{9,13},{13,9},{2,6},{6,2},{1... | collective-permute-start | bytes 614408 | tf_op jit(solution)/shard_map/ppermute | solution.py:718
  (454 shorter events, 196.9 us)
Async XLA Ops:
  13.2 14.7 %collective-permute-start.1 = (bf16[784,256]{1,0:T(8,128)(2,1)}, bf16[784,256]{1,0:T(8,128)(2,1)S(1)}, u32[]{:S(2)}, u32[]{:S(2)}) collective-permute-start(bf16[784,256]{1,0:T(8,128)(2,1)} %get-tuple-element.295), channel_id=1, source_target_pairs={{0,0},{1,16},{2,1},{3,17},{16,2},{17,18},{18,3},{19,19},{4,4},{5,2... | collective-permute-start | bytes 1204232 | tf_op jit(solution)/shard_map/ppermute | solution.py:751
  18.9 17.3 %collective-permute-start.2 = (bf16[784,256]{1,0:T(8,128)(2,1)}, bf16[784,256]{1,0:T(8,128)(2,1)}, u32[]{:S(2)}, u32[]{:S(2)}) collective-permute-start(bf16[784,256]{1,0:T(8,128)(2,1)} %get-tuple-element.294), channel_id=1, source_target_pairs={{0,16},{1,0},{2,17},{3,1},{16,18},{17,2},{18,19},{19,3},{4,20},{5,... | collective-permute-start | bytes 1204232 | tf_op jit(solution)/shard_map/ppermute | solution.py:751
  20.3 23.1 %collective-permute-start.3 = (bf16[784,256]{1,0:T(8,128)(2,1)}, bf16[784,256]{1,0:T(8,128)(2,1)}, u32[]{:S(2)}, u32[]{:S(2)}) collective-permute-start(bf16[784,256]{1,0:T(8,128)(2,1)} %get-tuple-element.293), channel_id=1, source_target_pairs={{0,1},{1,17},{2,0},{3,16},{16,3},{17,19},{18,2},{19,18},{4,5},{5,2... | collective-permute-start | bytes 1204232 | tf_op jit(solution)/shard_map/ppermute | solution.py:751
  20.5 34.8 %collective-permute-start.4 = (bf16[784,256]{1,0:T(8,128)(2,1)}, bf16[784,256]{1,0:T(8,128)(2,1)}, u32[]{:S(2)}, u32[]{:S(2)}) collective-permute-start(bf16[784,256]{1,0:T(8,128)(2,1)} %get-tuple-element.292), channel_id=1, source_target_pairs={{0,17},{1,1},{2,16},{3,0},{16,19},{17,3},{18,18},{19,2},{4,21},{5,... | collective-permute-start | bytes 1204232 | tf_op jit(solution)/shard_map/ppermute | solution.py:751
  59.3 26.3 %collective-permute-start.5 = (bf16[128,2048]{1,0:T(8,128)(2,1)S(1)}, bf16[128,2048]{1,0:T(8,128)(2,1)S(1)}, u32[]{:S(2)}, u32[]{:S(2)}) collective-permute-start(bf16[128,2048]{1,0:T(8,128)(2,1)S(1)} %bitcast.230), channel_id=1, source_target_pairs={{0,4},{4,0},{8,12},{12,8},{1,5},{5,1},{9,13},{13,9},{2,6},{6,2},{1... | collective-permute-start | bytes 1572872 | tf_op jit(solution)/shard_map/ppermute | solution.py:718
  60.5 25.9 %collective-permute-start.6 = (bf16[128,2048]{1,0:T(8,128)(2,1)S(1)}, bf16[128,2048]{1,0:T(8,128)(2,1)S(1)}, u32[]{:S(2)}, u32[]{:S(2)}) collective-permute-start(bf16[128,2048]{1,0:T(8,128)(2,1)S(1)} %bitcast.231), channel_id=1, source_target_pairs={{0,8},{4,12},{8,0},{12,4},{1,9},{5,13},{9,1},{13,5},{2,10},{6,14},... | collective-permute-start | bytes 1572872 | tf_op jit(solution)/shard_map/ppermute | solution.py:718
  61.8 25.4 %collective-permute-start.7 = (bf16[128,2048]{1,0:T(8,128)(2,1)S(1)}, bf16[128,2048]{1,0:T(8,128)(2,1)S(1)}, u32[]{:S(2)}, u32[]{:S(2)}) collective-permute-start(bf16[128,2048]{1,0:T(8,128)(2,1)S(1)} %bitcast.232), channel_id=1, source_target_pairs={{0,12},{4,8},{8,4},{12,0},{1,13},{5,9},{9,5},{13,1},{2,14},{6,10},... | collective-permute-start | bytes 1572872 | tf_op jit(solution)/shard_map/ppermute | solution.py:718
  94.9 31.8 %collective-permute-start.14 = (bf16[128,256]{1,0:T(8,128)(2,1)S(1)}, bf16[128,256]{1,0:T(8,128)(2,1)S(1)}, u32[]{:S(2)}, u32[]{:S(2)}) collective-permute-start(bf16[128,256]{1,0:T(8,128)(2,1)S(1)} %bitcast.234), channel_id=1, source_target_pairs={{0,1},{1,0},{2,3},{3,2},{4,5},{5,4},{6,7},{7,6},{8,9},{9,8},{10,11... | collective-permute-start | bytes 196616 | tf_op jit(solution)/shard_map/ppermute | solution.py:718
  95.0 31.8 %collective-permute-start.15 = (bf16[128,256]{1,0:T(8,128)(2,1)S(1)}, bf16[128,256]{1,0:T(8,128)(2,1)S(1)}, u32[]{:S(2)}, u32[]{:S(2)}) collective-permute-start(bf16[128,256]{1,0:T(8,128)(2,1)S(1)} %bitcast.235), channel_id=1, source_target_pairs={{0,2},{1,3},{2,0},{3,1},{4,6},{5,7},{6,4},{7,5},{8,10},{9,11},{10,... | collective-permute-start | bytes 196616 | tf_op jit(solution)/shard_map/ppermute | solution.py:718
  97.5 29.3 %collective-permute-start.16 = (bf16[128,256]{1,0:T(8,128)(2,1)S(1)}, bf16[128,256]{1,0:T(8,128)(2,1)S(1)}, u32[]{:S(2)}, u32[]{:S(2)}) collective-permute-start(bf16[128,256]{1,0:T(8,128)(2,1)S(1)} %bitcast.236), channel_id=1, source_target_pairs={{0,3},{1,2},{2,1},{3,0},{4,7},{5,6},{6,5},{7,4},{8,11},{9,10},{10,... | collective-permute-start | bytes 196616 | tf_op jit(solution)/shard_map/ppermute | solution.py:718
  98.6 28.2 %collective-permute-start.13 = (bf16[128,2048]{1,0:T(8,128)(2,1)S(1)}, bf16[128,2048]{1,0:T(8,128)(2,1)S(1)}, u32[]{:S(2)}, u32[]{:S(2)}) collective-permute-start(bf16[128,2048]{1,0:T(8,128)(2,1)S(1)} %pad_maximum_fusion.8.near_ref), channel_id=1, source_target_pairs={{0,2},{1,3},{2,0},{3,1},{4,6},{5,7},{6,4},{7,5},{8,10},{9,11},{10,... | collective-permute-start | bytes 1572872 | tf_op jit(solution)/shard_map/ppermute | solution.py:718
  106.0 28.0 %all-to-all-start = ((bf16[8,512,256]{2,1,0:T(8,128)(2,1)}), bf16[8,512,256]{2,1,0:T(8,128)(2,1)S(1)}, u32[]{:S(2)}, u32[]{:S(2)}) async-start(bf16[8,512,256]{2,1,0:T(8,128)(2,1)} %bitcast.224), calls=%async_computation | async-start | bytes 4194304 | tf_op jit(solution)/shard_map/all_to_all | solution.py:903
  110.8 111.7 %all-gather.3.cloned.1.call-start = ((), (), s32[]{:S(2)}) async-start(), calls=%async_computation.5 | async-start | bytes 11796480 | tf_op jit(solution)/shard_map/all_gather | solution.py:1070
  139.1 45.7 %collective-permute-start.17 = (bf16[1024,256]{1,0:T(8,128)(2,1)}, bf16[1024,256]{1,0:T(8,128)(2,1)S(1)}, u32[]{:S(2)}, u32[]{:S(2)}) collective-permute-start(bf16[1024,256]{1,0:T(8,128)(2,1)} %get-tuple-element.291), channel_id=1, source_target_pairs={{0,0},{1,16},{2,1},{3,17},{16,2},{17,18},{18,3},{19,19},{4,4},{5,2... | collective-permute-start | bytes 1572872 | tf_op jit(solution)/shard_map/ppermute | solution.py:751
  147.1 37.7 %collective-permute-start.18 = (bf16[1024,256]{1,0:T(8,128)(2,1)}, bf16[1024,256]{1,0:T(8,128)(2,1)S(1)}, u32[]{:S(2)}, u32[]{:S(2)}) collective-permute-start(bf16[1024,256]{1,0:T(8,128)(2,1)} %get-tuple-element.290), channel_id=1, source_target_pairs={{0,16},{1,0},{2,17},{3,1},{16,18},{17,2},{18,19},{19,3},{4,20},{5,... | collective-permute-start | bytes 1572872 | tf_op jit(solution)/shard_map/ppermute | solution.py:751
  147.2 37.6 %collective-permute-start.19 = (bf16[1024,256]{1,0:T(8,128)(2,1)}, bf16[1024,256]{1,0:T(8,128)(2,1)}, u32[]{:S(2)}, u32[]{:S(2)}) collective-permute-start(bf16[1024,256]{1,0:T(8,128)(2,1)} %get-tuple-element.289), channel_id=1, source_target_pairs={{0,1},{1,17},{2,0},{3,16},{16,3},{17,19},{18,2},{19,18},{4,5},{5,2... | collective-permute-start | bytes 1572872 | tf_op jit(solution)/shard_map/ppermute | solution.py:751
  149.5 43.8 %collective-permute-start.20 = (bf16[1024,256]{1,0:T(8,128)(2,1)}, bf16[1024,256]{1,0:T(8,128)(2,1)}, u32[]{:S(2)}, u32[]{:S(2)}) collective-permute-start(bf16[1024,256]{1,0:T(8,128)(2,1)} %get-tuple-element.288), channel_id=1, source_target_pairs={{0,17},{1,1},{2,16},{3,0},{16,19},{17,3},{18,18},{19,2},{4,21},{5,... | collective-permute-start | bytes 1572872 | tf_op jit(solution)/shard_map/ppermute | solution.py:751
  206.8 15.6 %all-to-all-start.1 = ((bf16[8,512,128]{1,2,0:T(8,128)(2,1)}), bf16[8,512,128]{1,2,0:T(8,128)(2,1)S(1)}, u32[]{:S(2)}, u32[]{:S(2)}) async-start(bf16[8,512,128]{1,2,0:T(8,128)(2,1)} %copy.121), calls=%async_computation.1 | async-start | bytes 2097152 | tf_op jit(solution)/shard_map/all_to_all | solution.py:909
  210.5 143.3 %all-gather.5.cloned.1.call-start = ((), (), s32[]{:S(2)}) async-start(), calls=%async_computation.6 | async-start | bytes 9437184 | tf_op jit(solution)/shard_map/all_gather | solution.py:1098
  219.9 25.0 %collective-permute-start.21 = (bf16[512,1024]{1,0:T(8,128)(2,1)}, bf16[512,1024]{1,0:T(8,128)(2,1)}, u32[]{:S(2)}, u32[]{:S(2)}) collective-permute-start(bf16[512,1024]{1,0:T(8,128)(2,1)} %unstack.11), channel_id=1, source_target_pairs={{0,1},{1,0},{2,3},{3,2},{4,5},{5,4},{6,7},{7,6},{8,9},{9,8},{10,11... | collective-permute-start | bytes 3145736 | tf_op jit(solution)/shard_map/ppermute | solution.py:718
  244.9 24.1 %collective-permute-start.22 = (bf16[512,1024]{1,0:T(8,128)(2,1)}, bf16[512,1024]{1,0:T(8,128)(2,1)}, u32[]{:S(2)}, u32[]{:S(2)}) collective-permute-start(bf16[512,1024]{1,0:T(8,128)(2,1)} %fusion.53), channel_id=1, source_target_pairs={{0,1},{1,0},{2,3},{3,2},{4,5},{5,4},{6,7},{7,6},{8,9},{9,8},{10,11... | collective-permute-start | bytes 3145736 | tf_op jit(solution)/shard_map/ppermute | solution.py:718
  269.3 23.7 %collective-permute-start.23 = (bf16[512,256]{1,0:T(8,128)(2,1)S(1)}, bf16[512,256]{1,0:T(8,128)(2,1)S(1)}, u32[]{:S(2)}, u32[]{:S(2)}) collective-permute-start(bf16[512,256]{1,0:T(8,128)(2,1)S(1)} %get-tuple-element.315), channel_id=1, source_target_pairs={{0,0},{1,16},{2,1},{3,17},{16,2},{17,18},{18,3},{19,19},{4,4},{5,2... | collective-permute-start | bytes 786440 | tf_op jit(solution)/shard_map/ppermute | solution.py:751
  272.7 20.3 %collective-permute-start.24 = (bf16[512,256]{1,0:T(8,128)(2,1)S(1)}, bf16[512,256]{1,0:T(8,128)(2,1)S(1)}, u32[]{:S(2)}, u32[]{:S(2)}) collective-permute-start(bf16[512,256]{1,0:T(8,128)(2,1)S(1)} %get-tuple-element.314), channel_id=1, source_target_pairs={{0,16},{1,0},{2,17},{3,1},{16,18},{17,2},{18,19},{19,3},{4,20},{5,... | collective-permute-start | bytes 786440 | tf_op jit(solution)/shard_map/ppermute | solution.py:751
  274.0 19.0 %collective-permute-start.25 = (bf16[512,256]{1,0:T(8,128)(2,1)S(1)}, bf16[512,256]{1,0:T(8,128)(2,1)S(1)}, u32[]{:S(2)}, u32[]{:S(2)}) collective-permute-start(bf16[512,256]{1,0:T(8,128)(2,1)S(1)} %get-tuple-element.313), channel_id=1, source_target_pairs={{0,1},{1,17},{2,0},{3,16},{16,3},{17,19},{18,2},{19,18},{4,5},{5,2... | collective-permute-start | bytes 786440 | tf_op jit(solution)/shard_map/ppermute | solution.py:751
  275.5 22.3 %collective-permute-start.26 = (bf16[512,256]{1,0:T(8,128)(2,1)S(1)}, bf16[512,256]{1,0:T(8,128)(2,1)S(1)}, u32[]{:S(2)}, u32[]{:S(2)}) collective-permute-start(bf16[512,256]{1,0:T(8,128)(2,1)S(1)} %get-tuple-element.312), channel_id=1, source_target_pairs={{0,17},{1,1},{2,16},{3,0},{16,19},{17,3},{18,18},{19,2},{4,21},{5,... | collective-permute-start | bytes 786440 | tf_op jit(solution)/shard_map/ppermute | solution.py:751
  302.4 25.4 %collective-permute-start.27 = (bf16[512,1024]{1,0:T(8,128)(2,1)S(1)}, bf16[512,1024]{1,0:T(8,128)(2,1)S(1)}, u32[]{:S(2)}, u32[]{:S(2)}) collective-permute-start(bf16[512,1024]{1,0:T(8,128)(2,1)S(1)} %fusion.75), channel_id=1, source_target_pairs={{0,1},{1,0},{2,3},{3,2},{4,5},{5,4},{6,7},{7,6},{8,9},{9,8},{10,11... | collective-permute-start | bytes 3145736 | tf_op jit(solution)/shard_map/ppermute | solution.py:718
  305.2 14.4 %collective-permute-start.29 = (bf16[512,2048]{1,0:T(8,128)(2,1)S(1)}, bf16[512,2048]{1,0:T(8,128)(2,1)S(1)}, u32[]{:S(2)}, u32[]{:S(2)}) collective-permute-start(bf16[512,2048]{1,0:T(8,128)(2,1)S(1)} %convolution_convert_fusion), channel_id=1, source_target_pairs={{0,16},{16,0},{1,17},{17,1},{2,18},{18,2},{3,19},{19,3},{4,20},{20... | collective-permute-start | bytes 6291464 | tf_op jit(solution)/shard_map/ppermute | solution.py:718
  308.0 15.9 %collective-permute-start.28 = (bf16[512,2048]{1,0:T(8,128)(2,1)S(1)}, bf16[512,2048]{1,0:T(8,128)(2,1)S(1)}, u32[]{:S(2)}, u32[]{:S(2)}) collective-permute-start(bf16[512,2048]{1,0:T(8,128)(2,1)S(1)} %convolution_convert_fusion.1), channel_id=1, source_target_pairs={{0,16},{16,0},{1,17},{17,1},{2,18},{18,2},{3,19},{19,3},{4,20},{20... | collective-permute-start | bytes 6291464 | tf_op jit(solution)/shard_map/ppermute | solution.py:718
  337.7 16.0 %all-to-all-start.2 = ((bf16[8,512,128]{2,1,0:T(8,128)(2,1)}), bf16[8,512,128]{2,1,0:T(8,128)(2,1)}, u32[]{:S(2)}, u32[]{:S(2)}) async-start(bf16[8,512,128]{2,1,0:T(8,128)(2,1)} %bitcast.248), calls=%async_computation.2 | async-start | bytes 2097152 | tf_op jit(solution)/shard_map/all_to_all | solution.py:903
  341.9 114.8 %reduce-scatter.2.cloned.1.call-start = ((), (), s32[]{:S(2)}) async-start(), calls=%async_computation.7 | async-start | bytes 7372800 | tf_op jit(solution)/shard_map/reduce_scatter | solution.py:1151
  353.8 56.5 %collective-permute-start.36 = (bf16[512,1024]{1,0:T(8,128)(2,1)}, bf16[512,1024]{1,0:T(8,128)(2,1)S(1)}, u32[]{:S(2)}, u32[]{:S(2)}) collective-permute-start(bf16[512,1024]{1,0:T(8,128)(2,1)} %fusion.78), channel_id=1, source_target_pairs={{0,1},{1,0},{2,3},{3,2},{4,5},{5,4},{6,7},{7,6},{8,9},{9,8},{10,11... | collective-permute-start | bytes 3145736 | tf_op jit(solution)/shard_map/ppermute | solution.py:718
  357.0 53.2 %collective-permute-start.32 = (bf16[1024,256]{1,0:T(8,128)(2,1)S(1)}, bf16[1024,256]{1,0:T(8,128)(2,1)S(1)}, u32[]{:S(2)}, u32[]{:S(2)}) collective-permute-start(bf16[1024,256]{1,0:T(8,128)(2,1)S(1)} %get-tuple-element.284), channel_id=1, source_target_pairs={{0,0},{16,1},{1,2},{17,3},{2,16},{18,17},{3,18},{19,19},{4,4},{20,... | collective-permute-start | bytes 1572872 | tf_op jit(solution)/shard_map/ppermute | solution.py:777
  362.8 47.5 %collective-permute-start.33 = (bf16[1024,256]{1,0:T(8,128)(2,1)S(1)}, bf16[1024,256]{1,0:T(8,128)(2,1)S(1)}, u32[]{:S(2)}, u32[]{:S(2)}) collective-permute-start(bf16[1024,256]{1,0:T(8,128)(2,1)S(1)} %get-tuple-element.283), channel_id=1, source_target_pairs={{16,0},{0,1},{17,2},{1,3},{18,16},{2,17},{19,18},{3,19},{20,4},{4,... | collective-permute-start | bytes 1572872 | tf_op jit(solution)/shard_map/ppermute | solution.py:777
  362.8 47.5 %collective-permute-start.34 = (bf16[1024,256]{1,0:T(8,128)(2,1)S(1)}, bf16[1024,256]{1,0:T(8,128)(2,1)S(1)}, u32[]{:S(2)}, u32[]{:S(2)}) collective-permute-start(bf16[1024,256]{1,0:T(8,128)(2,1)S(1)} %get-tuple-element.282), channel_id=1, source_target_pairs={{1,0},{17,1},{0,2},{16,3},{3,16},{19,17},{2,18},{18,19},{5,4},{21,... | collective-permute-start | bytes 1572872 | tf_op jit(solution)/shard_map/ppermute | solution.py:777
  363.3 47.0 %collective-permute-start.35 = (bf16[1024,256]{1,0:T(8,128)(2,1)S(1)}, bf16[1024,256]{1,0:T(8,128)(2,1)S(1)}, u32[]{:S(2)}, u32[]{:S(2)}) collective-permute-start(bf16[1024,256]{1,0:T(8,128)(2,1)S(1)} %get-tuple-element.281), channel_id=1, source_target_pairs={{17,0},{1,1},{16,2},{0,3},{19,16},{3,17},{18,18},{2,19},{21,4},{5,... | collective-permute-start | bytes 1572872 | tf_op jit(solution)/shard_map/ppermute | solution.py:777
  410.8 21.3 %collective-permute-start.37 = (bf16[512,256]{1,0:T(8,128)(2,1)S(1)}, bf16[512,256]{1,0:T(8,128)(2,1)S(1)}, u32[]{:S(2)}, u32[]{:S(2)}) collective-permute-start(bf16[512,256]{1,0:T(8,128)(2,1)S(1)} %get-tuple-element.311), channel_id=1, source_target_pairs={{0,0},{16,1},{1,2},{17,3},{2,16},{18,17},{3,18},{19,19},{4,4},{20,... | collective-permute-start | bytes 786440 | tf_op jit(solution)/shard_map/ppermute | solution.py:777
  414.9 17.2 %collective-permute-start.38 = (bf16[512,256]{1,0:T(8,128)(2,1)S(1)}, bf16[512,256]{1,0:T(8,128)(2,1)S(1)}, u32[]{:S(2)}, u32[]{:S(2)}) collective-permute-start(bf16[512,256]{1,0:T(8,128)(2,1)S(1)} %get-tuple-element.310), channel_id=1, source_target_pairs={{16,0},{0,1},{17,2},{1,3},{18,16},{2,17},{19,18},{3,19},{20,4},{4,... | collective-permute-start | bytes 786440 | tf_op jit(solution)/shard_map/ppermute | solution.py:777
  435.9 31.3 %all-to-all-start.3 = ((bf16[8,512,256]{1,2,0:T(8,128)(2,1)}), bf16[8,512,256]{1,2,0:T(8,128)(2,1)}, u32[]{:S(2)}, u32[]{:S(2)}) async-start(bf16[8,512,256]{1,2,0:T(8,128)(2,1)} %copy.126), calls=%async_computation.4 | async-start | bytes 4194304 | tf_op jit(solution)/shard_map/all_to_all | solution.py:909
  444.9 15.5 %collective-permute-start.39 = (bf16[512,256]{1,0:T(8,128)(2,1)}, bf16[512,256]{1,0:T(8,128)(2,1)}, u32[]{:S(2)}, u32[]{:S(2)}) collective-permute-start(bf16[512,256]{1,0:T(8,128)(2,1)} %get-tuple-element.309), channel_id=1, source_target_pairs={{1,0},{17,1},{0,2},{16,3},{3,16},{19,17},{2,18},{18,19},{5,4},{21,... | collective-permute-start | bytes 786440 | tf_op jit(solution)/shard_map/ppermute | solution.py:777
  445.7 15.0 %collective-permute-start.40 = (bf16[512,256]{1,0:T(8,128)(2,1)}, bf16[512,256]{1,0:T(8,128)(2,1)}, u32[]{:S(2)}, u32[]{:S(2)}) collective-permute-start(bf16[512,256]{1,0:T(8,128)(2,1)} %get-tuple-element.308), channel_id=1, source_target_pairs={{17,0},{1,1},{16,2},{0,3},{19,16},{3,17},{18,18},{2,19},{21,4},{5,... | collective-permute-start | bytes 786440 | tf_op jit(solution)/shard_map/ppermute | solution.py:777
  457.8 25.5 %collective-permute-start.41 = (bf16[128,2048]{1,0:T(8,128)(2,1)S(1)}, bf16[128,2048]{1,0:T(8,128)(2,1)S(1)}, u32[]{:S(2)}, u32[]{:S(2)}) collective-permute-start(bf16[128,2048]{1,0:T(8,128)(2,1)S(1)} %pad_maximum_fusion.9), channel_id=1, source_target_pairs={{0,2},{1,3},{2,0},{3,1},{4,6},{5,7},{6,4},{7,5},{8,10},{9,11},{10,... | collective-permute-start | bytes 1572872 | tf_op jit(solution)/shard_map/ppermute | solution.py:718
  503.8 21.9 %collective-permute-start.42 = (bf16[512,256]{1,0:T(8,128)(2,1)S(1)}, bf16[512,256]{1,0:T(8,128)(2,1)S(1)}, u32[]{:S(2)}, u32[]{:S(2)}) collective-permute-start(bf16[512,256]{1,0:T(8,128)(2,1)S(1)} %get-tuple-element.307), channel_id=1, source_target_pairs={{0,0},{16,1},{1,2},{17,3},{2,16},{18,17},{3,18},{19,19},{4,4},{20,... | collective-permute-start | bytes 786440 | tf_op jit(solution)/shard_map/ppermute | solution.py:777
  507.3 23.4 %collective-permute-start.43 = (bf16[512,256]{1,0:T(8,128)(2,1)S(1)}, bf16[512,256]{1,0:T(8,128)(2,1)S(1)}, u32[]{:S(2)}, u32[]{:S(2)}) collective-permute-start(bf16[512,256]{1,0:T(8,128)(2,1)S(1)} %get-tuple-element.306), channel_id=1, source_target_pairs={{16,0},{0,1},{17,2},{1,3},{18,16},{2,17},{19,18},{3,19},{20,4},{4,... | collective-permute-start | bytes 786440 | tf_op jit(solution)/shard_map/ppermute | solution.py:777
  507.5 34.3 %collective-permute-start.46 = (bf16[128,2048]{1,0:T(8,128)(2,1)S(1)}, bf16[128,2048]{1,0:T(8,128)(2,1)S(1)}, u32[]{:S(2)}, u32[]{:S(2)}) collective-permute-start(bf16[128,2048]{1,0:T(8,128)(2,1)S(1)} %add_convert_fusion.6.refs_0_), channel_id=1, source_target_pairs={{0,4},{4,0},{8,12},{12,8},{1,5},{5,1},{9,13},{13,9},{2,6},{6,2},{1... | collective-permute-start | bytes 1572872 | tf_op jit(solution)/shard_map/ppermute | solution.py:718
  509.8 31.9 %collective-permute-start.47 = (bf16[128,2048]{1,0:T(8,128)(2,1)S(1)}, bf16[128,2048]{1,0:T(8,128)(2,1)S(1)}, u32[]{:S(2)}, u32[]{:S(2)}) collective-permute-start(bf16[128,2048]{1,0:T(8,128)(2,1)S(1)} %add_convert_fusion.6.refs_0_), channel_id=1, source_target_pairs={{0,8},{4,12},{8,0},{12,4},{1,9},{5,13},{9,1},{13,5},{2,10},{6,14},... | collective-permute-start | bytes 1572872 | tf_op jit(solution)/shard_map/ppermute | solution.py:718
  511.2 30.6 %collective-permute-start.48 = (bf16[128,2048]{1,0:T(8,128)(2,1)S(1)}, bf16[128,2048]{1,0:T(8,128)(2,1)S(1)}, u32[]{:S(2)}, u32[]{:S(2)}) collective-permute-start(bf16[128,2048]{1,0:T(8,128)(2,1)S(1)} %add_convert_fusion.6.refs_0_), channel_id=1, source_target_pairs={{0,12},{4,8},{8,4},{12,0},{1,13},{5,9},{9,5},{13,1},{2,14},{6,10},... | collective-permute-start | bytes 1572872 | tf_op jit(solution)/shard_map/ppermute | solution.py:718
  541.8 15.3 %collective-permute-start.60 = (f32[512]{0:T(512)S(1)}, f32[512]{0:T(512)S(1)}, u32[]{:S(2)}, u32[]{:S(2)}) collective-permute-start(f32[512]{0:T(512)S(1)} %add_add_fusion.1), channel_id=1, source_target_pairs={{0,16},{16,0},{1,17},{17,1},{2,18},{18,2},{3,19},{19,3},{4,20},{20... | collective-permute-start | bytes 6152 | tf_op jit(solution)/shard_map/ppermute | solution.py:718
  547.2 21.2 %collective-permute-start.56 = (bf16[1,400,256]{2,1,0:T(8,128)(2,1)S(1)}, bf16[1,400,256]{2,1,0:T(8,128)(2,1)}, u32[]{:S(2)}, u32[]{:S(2)}) collective-permute-start(bf16[1,400,256]{2,1,0:T(8,128)(2,1)S(1)} %maximum_bitcast_fusion), channel_id=1, source_target_pairs={{0,4},{4,0},{8,12},{12,8},{1,5},{5,1},{9,13},{13,9},{2,6},{6,2},{1... | collective-permute-start | bytes 614408 | tf_op jit(solution)/shard_map/ppermute | solution.py:718
  (87 other events, 654.0 us)
Sparse Core Ops, SparseCore 0:
  136.7 65.1 all-gather.2
  245.3 54.5 all-gather.4
  353.9 68.1 reduce-scatter.1

commit v6 on v5

--- a/solution.py
+++ b/solution.py
@@ -1076,7 +1076,7 @@
 
     sorted_pair = into_places(places, landed)
     query_sorted, value_sorted = sorted_pair[:, :DH], sorted_pair[:, DH:]
-    bounds = with_bound(bounds, query_sorted)
+    bounds = with_bound(bounds, landed[:, :DH])
     (first_rows, second_grad_rows), (mix, logs) = rows_in(
         after(stacked, landed),
         attend(bounds, query_sorted, value_sorted, hot),

time: 600 us -> 600 us (level)
  no operation moved by 1% of the time
where the time goes in v6:
time: 600 us; the launch traced here: 589 us
  matrix products  149 us (25%)
  starting transfers between devices  129 us (22%)
  waiting for transfers between devices  127 us (21%)
  local copies, waits for them, and re-layouts  76.5 us (13%)
  Pallas kernels  48.6 us (8%)
  other arithmetic  41.6 us (7%)
  between operations  17.2 us (3%)
    dot_general x16, matrix products, dot(): lax.dot_general(left, right, dims, preferred_element_type=jnp.float32)  83.9 us
    ppermute x39, waiting for transfers between devices, swap(): return lax.ppermute(vectors, axis, [(at, at ^ bits) for at in range(size)])  51.2 us
    ppermute x39, starting transfers between devices, swap(): return lax.ppermute(vectors, axis, [(at, at ^ bits) for at in range(size)])  46.9 us
    dot_general x3, matrix products, into_places(): jnp.einsum('pa,ad->pd', place_matrix(places), vectors, preferred_element_...  40.9 us
    ppermute x12, waiting for transfers between devices, rows_in(): lax.ppermute(chunk, ('shard', 'tp'), plane_pairs(step, False))  40.6 us
    ppermute x12, starting transfers between devices, rows_in(): lax.ppermute(chunk, ('shard', 'tp'), plane_pairs(step, False))  30.6 us
    ppermute x12, starting transfers between devices, send(): return lax.ppermute(piece, ('shard', 'tp'), plane_pairs(step, True))  29.7 us
    pallas_call x1, Pallas kernels, attend_back(): pl.pallas_call(attend_back_kernel, name='attend_back', out_shape=(jax.Sha...  29.5 us
  transfers between devices with their start and end apart: 71, of which 19 were waited for; matrix products, arithmetic and copies ran while one was open for 39% of the time, Pallas kernels for 8%

profile of v6, /device:TPU:1, one launch (start us, length us, event | category | flops | bytes accessed | tf_op | source)
XLA Modules:
  0.0 588.5 jit_solution(9648250339076867659)
XLA Ops:
  13.2 5.7 collective-permute-start.1
  23.5 4.4 pad_maximum_fusion.1
  27.9 8.3 %collective-permute-done.2 = bf16[784,256]{1,0:T(8,128)(2,1)} collective-permute-done((bf16[784,256]{1,0:T(8,128)(2,1)}, bf16[784,256]{1,0:T(8,128)(2,1)}, u32[]{:S(2)}, u32[]{:S(2)}) %collective-permute-start.2) | collective-permute-done | bytes 401440 | tf_op jit(solution)/shard_map/ppermute | solution.py:751
  36.2 7.2 %collective-permute-done.3 = bf16[784,256]{1,0:T(8,128)(2,1)} collective-permute-done((bf16[784,256]{1,0:T(8,128)(2,1)}, bf16[784,256]{1,0:T(8,128)(2,1)}, u32[]{:S(2)}, u32[]{:S(2)}) %collective-permute-start.3) | collective-permute-done | bytes 401440 | tf_op jit(solution)/shard_map/ppermute | solution.py:751
  43.4 11.9 %collective-permute-done.4 = bf16[784,256]{1,0:T(8,128)(2,1)} collective-permute-done((bf16[784,256]{1,0:T(8,128)(2,1)}, bf16[784,256]{1,0:T(8,128)(2,1)}, u32[]{:S(2)}, u32[]{:S(2)}) %collective-permute-start.4) | collective-permute-done | bytes 401440 | tf_op jit(solution)/shard_map/ppermute | solution.py:751
  74.9 7.0 %collective-permute-done.9 = s32[48,128]{1,0:T(8,128)S(1)} collective-permute-done((s32[48,128]{1,0:T(8,128)S(1)}, s32[48,128]{1,0:T(8,128)S(1)}, u32[]{:S(2)}, u32[]{:S(2)}) %collective-permute-start.9) | collective-permute-done | bytes 24608 | tf_op jit(solution)/shard_map/ppermute | solution.py:718
  106.0 4.8 all-to-all-start
  111.0 15.6 %fusion.12.hot_ref = bf16[4096,256]{1,0:T(8,128)(2,1)} fusion(pred[4096,256]{0,1:T(32,128)(4,1)} %bitcast_compare_fusion, s32[4096]{0:T(1024)S(1)} %bitcast.289), kind=kOutput, calls=%fused_computation.19 | convolution fusion | flops 8607760384 | bytes 3162112 | tf_op jit(solution)/shard_map/pa,ad->pd/dot_general | solution.py:308
  126.8 7.1 %all-to-all-done = bf16[8,512,256]{2,1,0:T(8,128)(2,1)S(1)} async-done(((bf16[8,512,256]{2,1,0:T(8,128)(2,1)}), bf16[8,512,256]{2,1,0:T(8,128)(2,1)S(1)}, u32[]{:S(2)}, u32[]{:S(2)}) %all-to-all-start) | async-done | bytes 2097184 | tf_op jit(solution)/shard_map/all_to_all | solution.py:903
  139.1 8.0 %collective-permute-start.17 = (bf16[1024,256]{1,0:T(8,128)(2,1)}, bf16[1024,256]{1,0:T(8,128)(2,1)S(1)}, u32[]{:S(2)}, u32[]{:S(2)}) collective-permute-start(bf16[1024,256]{1,0:T(8,128)(2,1)} %get-tuple-element.291), channel_id=1, source_target_pairs={{0,0},{1,16},{2,1},{3,17},{16,2},{17,18},{18,3},{19,19},{4,4},{5,2... | collective-permute-start | bytes 1572872 | tf_op jit(solution)/shard_map/ppermute | solution.py:751
  151.4 12.2 %fusion.13 = bf16[4096,256]{1,0:T(8,128)(2,1)S(1)} fusion(bf16[4096,256]{1,0:T(8,128)(2,1)S(1)} %bitcast.247, s32[4096]{0:T(1024)S(1)} %bitcast.290), kind=kOutput, calls=%fused_computation.20 | convolution fusion | flops 8607760384 | bytes 4210688 | tf_op jit(solution)/shard_map/pa,ad->pd/dot_general | solution.py:308
  167.3 17.5 %attend.1 = (f32[128,4096]{1,0:T(8,128)S(1)}, f32[8,512]{1,0:T(8,128)S(1)}) custom-call(s32[4]{0:T(128)S(1)} %pad_add_fusion.bounds_ref, bf16[4096,128]{1,0:T(8,128)(2,1)S(1)} %get-tuple-element.287.q_ref, bf16[4096,128]{1,0:T(8,128)(2,1)S(1)} %get-tuple-element.286.v_ref, bf16[4096,256]{1,0:T(8,128)(2,1)S(1)} %copy-done.4), custom_call_target="tpu_custom_call" | custom-call | flops 524288 | bytes 524288 | tf_op jit(solution)/shard_map/attend/pallas_call | solution.py:150
  184.8 8.5 %collective-permute-done.20 = bf16[1024,256]{1,0:T(8,128)(2,1)} collective-permute-done((bf16[1024,256]{1,0:T(8,128)(2,1)}, bf16[1024,256]{1,0:T(8,128)(2,1)}, u32[]{:S(2)}, u32[]{:S(2)}) %collective-permute-start.20) | collective-permute-done | bytes 524320 | tf_op jit(solution)/shard_map/ppermute | solution.py:751
  193.3 12.2 %fusion.16 = bf16[4096,128]{1,0:T(8,128)(2,1)S(1)} fusion(s32[4096]{0:T(1024)S(1)} %bitcast.291, f32[128,4096]{1,0:T(8,128)S(1)} %get-tuple-element.137.out_ref), kind=kOutput, calls=%fused_computation.23 | convolution fusion | flops 4312793088 | bytes 3162112 | tf_op jit(solution)/shard_map/dot_general | solution.py:30
  206.8 3.7 all-to-all-start.1
  223.4 4.0 convert_reduce_fusion.3
  229.3 15.6 %collective-permute-done.21 = bf16[512,1024]{1,0:T(8,128)(2,1)} collective-permute-done((bf16[512,1024]{1,0:T(8,128)(2,1)}, bf16[512,1024]{1,0:T(8,128)(2,1)}, u32[]{:S(2)}, u32[]{:S(2)}) %collective-permute-start.21) | collective-permute-done | bytes 1048608 | tf_op jit(solution)/shard_map/ppermute | solution.py:718
  245.1 6.5 %multiply_convert_fusion.1 = (bf16[512,2048]{1,0:T(8,128)(2,1)}, f32[512,2048]{1,0:T(8,128)}) fusion(f32[2048]{0:T(1024)S(1)} %pad_maximum_fusion.14, bf16[512,1024]{1,0:T(8,128)(2,1)} %fusion.53, bf16[1024,5120]{1,0:T(8,128)(2,1)} %all-gather.3.cloned.1.call-done), kind=kOutput, calls=%fused_computation.41 | convolution fusion | flops 2153775104 | bytes 11542528 | tf_op jit(solution)/shard_map/dot_general | solution.py:30
  253.9 6.8 %fusion.22 = bf16[512,2048]{1,0:T(8,128)(2,1)S(1)} fusion(f32[512,2048]{1,0:T(8,128)} %get-tuple-element.341, bf16[1024,5120]{1,0:T(8,128)(2,1)} %all-gather.3.cloned.1.call-done, f32[2048]{0:T(1024)S(1)} %pad_maximum_fusion.14, bf16[1024,1024]{1,0:T(8,128)(2,1)} %constant_dynamic-update-slice_fusion.8), kind=kOutput, calls=%fused_computation.29 | convolution fusion | flops 2159017984 | bytes 11542528 | tf_op jit(solution)/shard_map/dot_general | solution.py:30
  260.7 8.4 %collective-permute-done.22 = bf16[512,1024]{1,0:T(8,128)(2,1)} collective-permute-done((bf16[512,1024]{1,0:T(8,128)(2,1)}, bf16[512,1024]{1,0:T(8,128)(2,1)}, u32[]{:S(2)}, u32[]{:S(2)}) %collective-permute-start.22) | collective-permute-done | bytes 1048608 | tf_op jit(solution)/shard_map/ppermute | solution.py:718
  279.2 4.1 multiply_convert_fusion
  283.3 3.7 fusion.62
  287.0 5.4 fusion.28
  293.0 4.7 collective-permute-done.26
  297.8 4.7 fusion.75
  309.6 5.5 fusion.78
  315.1 4.6 fusion.35
  319.6 4.3 add_convert_fusion
  323.9 3.9 add_convert_fusion.1
  337.7 4.2 all-to-all-start.2
  346.8 4.4 fusion.11
  357.0 5.7 collective-permute-start.32
  363.3 4.4 collective-permute-start.35
  367.7 13.1 %fusion.15.grad_ref = bf16[4096,128]{1,0:T(8,128)(2,1)S(1)} fusion(bf16[4096,128]{1,0:T(8,128)(2,1)} %bitcast.63, s32[4096]{0:T(1024)S(1)} %bitcast.292), kind=kOutput, calls=%fused_computation.22 | convolution fusion | flops 4312268800 | bytes 2113536 | tf_op jit(solution)/shard_map/pa,ad->pd/dot_general | solution.py:308
  380.8 29.5 %attend_back.1 = (bf16[4096,128]{1,0:T(8,128)(2,1)S(1)}, bf16[4096,128]{1,0:T(8,128)(2,1)S(1)}) custom-call(s32[4]{0:T(128)S(1)} %pad_add_fusion.bounds_ref, bf16[4096,128]{1,0:T(8,128)(2,1)S(1)} %get-tuple-element.287.q_ref, bf16[4096,128]{1,0:T(8,128)(2,1)S(1)} %get-tuple-element.286.v_ref, bf16[4096,256]{1,0:T(8,128)(2,1)} %fusion.12.hot_ref, ...), custom_call_target="tpu_custom_call" | custom-call | flops 524288 | bytes 524288 | tf_op jit(solution)/shard_map/attend_back/pallas_call | solution.py:273
  410.8 4.1 collective-permute-start.37
  415.5 12.3 %fusion.14 = bf16[4096,256]{1,0:T(8,128)(2,1)S(1)} fusion(s32[4096]{0:T(1024)S(1)} %bitcast.293, bf16[4096,128]{1,0:T(8,128)(2,1)S(1)} %get-tuple-element.176, bf16[4096,128]{1,0:T(8,128)(2,1)S(1)} %get-tuple-element.175), kind=kOutput, calls=%fused_computation.21 | convolution fusion | flops 8611954688 | bytes 4210688 | tf_op jit(solution)/shard_map/dot_general | solution.py:30
  435.9 8.1 %all-to-all-start.3 = ((bf16[8,512,256]{1,2,0:T(8,128)(2,1)}), bf16[8,512,256]{1,2,0:T(8,128)(2,1)}, u32[]{:S(2)}, u32[]{:S(2)}) async-start(bf16[8,512,256]{1,2,0:T(8,128)(2,1)} %copy.122), calls=%async_computation.4 | async-start | bytes 4194304 | tf_op jit(solution)/shard_map/all_to_all | solution.py:909
  445.7 4.4 collective-permute-start.40
  450.1 6.6 %convolution_convert_fusion.3 = bf16[1024,256]{1,0:T(8,128)(2,1)} fusion(bf16[4096,1024]{1,0:T(8,128)(2,1)} %all-gather.5.cloned.1.call-done, bf16[4096,256]{1,0:T(8,128)(2,1)S(1)} %fusion.14), kind=kOutput, calls=%fused_computation.117 | convolution fusion | flops 2147745792 | bytes 11010048 | tf_op jit(solution)/shard_map/dot_general | solution.py:1165
  460.7 6.5 %all-to-all-done.3 = bf16[8,512,256]{1,2,0:T(8,128)(2,1)} async-done(((bf16[8,512,256]{1,2,0:T(8,128)(2,1)}), bf16[8,512,256]{1,2,0:T(8,128)(2,1)}, u32[]{:S(2)}, u32[]{:S(2)}) %all-to-all-start.3) | async-done | bytes 2097184 | tf_op jit(solution)/shard_map/all_to_all | solution.py:909
  467.2 16.1 %collective-permute-done.41 = bf16[128,2048]{1,0:T(8,128)(2,1)S(1)} collective-permute-done((bf16[128,2048]{1,0:T(8,128)(2,1)S(1)}, bf16[128,2048]{1,0:T(8,128)(2,1)S(1)}, u32[]{:S(2)}, u32[]{:S(2)}) %collective-permute-start.41) | collective-permute-done | bytes 524320 | tf_op jit(solution)/shard_map/ppermute | solution.py:718
  484.1 3.7 fusion.126
  503.8 3.4 collective-permute-start.42
  513.8 11.9 %collective-permute-done.42 = bf16[512,256]{1,0:T(8,128)(2,1)S(1)} collective-permute-done((bf16[512,256]{1,0:T(8,128)(2,1)S(1)}, bf16[512,256]{1,0:T(8,128)(2,1)S(1)}, u32[]{:S(2)}, u32[]{:S(2)}) %collective-permute-start.42) | collective-permute-done | bytes 262176 | tf_op jit(solution)/shard_map/ppermute | solution.py:777
  526.7 3.9 collective-permute-done.43
  530.6 6.0 %collective-permute-start.45 = (bf16[512,256]{1,0:T(8,128)(2,1)S(1)}, bf16[512,256]{1,0:T(8,128)(2,1)S(1)}, u32[]{:S(2)}, u32[]{:S(2)}) collective-permute-start(bf16[512,256]{1,0:T(8,128)(2,1)S(1)} %get-tuple-element.304), channel_id=1, source_target_pairs={{17,0},{1,1},{16,2},{0,3},{19,16},{3,17},{18,18},{2,19},{21,4},{5,... | collective-permute-start | bytes 786440 | tf_op jit(solution)/shard_map/ppermute | solution.py:777
  547.2 9.9 %collective-permute-start.56 = (bf16[1,400,256]{2,1,0:T(8,128)(2,1)S(1)}, bf16[1,400,256]{2,1,0:T(8,128)(2,1)}, u32[]{:S(2)}, u32[]{:S(2)}) collective-permute-start(bf16[1,400,256]{2,1,0:T(8,128)(2,1)S(1)} %maximum_bitcast_fusion), channel_id=1, source_target_pairs={{0,4},{4,0},{8,12},{12,8},{1,5},{5,1},{9,13},{13,9},{2,6},{6,2},{1... | collective-permute-start | bytes 614408 | tf_op jit(solution)/shard_map/ppermute | solution.py:718
  (454 shorter events, 196.9 us)
Async XLA Ops:
  13.2 14.7 %collective-permute-start.1 = (bf16[784,256]{1,0:T(8,128)(2,1)}, bf16[784,256]{1,0:T(8,128)(2,1)S(1)}, u32[]{:S(2)}, u32[]{:S(2)}) collective-permute-start(bf16[784,256]{1,0:T(8,128)(2,1)} %get-tuple-element.295), channel_id=1, source_target_pairs={{0,0},{1,16},{2,1},{3,17},{16,2},{17,18},{18,3},{19,19},{4,4},{5,2... | collective-permute-start | bytes 1204232 | tf_op jit(solution)/shard_map/ppermute | solution.py:751
  18.9 17.3 %collective-permute-start.2 = (bf16[784,256]{1,0:T(8,128)(2,1)}, bf16[784,256]{1,0:T(8,128)(2,1)}, u32[]{:S(2)}, u32[]{:S(2)}) collective-permute-start(bf16[784,256]{1,0:T(8,128)(2,1)} %get-tuple-element.294), channel_id=1, source_target_pairs={{0,16},{1,0},{2,17},{3,1},{16,18},{17,2},{18,19},{19,3},{4,20},{5,... | collective-permute-start | bytes 1204232 | tf_op jit(solution)/shard_map/ppermute | solution.py:751
  20.3 23.1 %collective-permute-start.3 = (bf16[784,256]{1,0:T(8,128)(2,1)}, bf16[784,256]{1,0:T(8,128)(2,1)}, u32[]{:S(2)}, u32[]{:S(2)}) collective-permute-start(bf16[784,256]{1,0:T(8,128)(2,1)} %get-tuple-element.293), channel_id=1, source_target_pairs={{0,1},{1,17},{2,0},{3,16},{16,3},{17,19},{18,2},{19,18},{4,5},{5,2... | collective-permute-start | bytes 1204232 | tf_op jit(solution)/shard_map/ppermute | solution.py:751
  20.5 34.8 %collective-permute-start.4 = (bf16[784,256]{1,0:T(8,128)(2,1)}, bf16[784,256]{1,0:T(8,128)(2,1)}, u32[]{:S(2)}, u32[]{:S(2)}) collective-permute-start(bf16[784,256]{1,0:T(8,128)(2,1)} %get-tuple-element.292), channel_id=1, source_target_pairs={{0,17},{1,1},{2,16},{3,0},{16,19},{17,3},{18,18},{19,2},{4,21},{5,... | collective-permute-start | bytes 1204232 | tf_op jit(solution)/shard_map/ppermute | solution.py:751
  59.3 26.3 %collective-permute-start.5 = (bf16[128,2048]{1,0:T(8,128)(2,1)S(1)}, bf16[128,2048]{1,0:T(8,128)(2,1)S(1)}, u32[]{:S(2)}, u32[]{:S(2)}) collective-permute-start(bf16[128,2048]{1,0:T(8,128)(2,1)S(1)} %bitcast.230), channel_id=1, source_target_pairs={{0,4},{4,0},{8,12},{12,8},{1,5},{5,1},{9,13},{13,9},{2,6},{6,2},{1... | collective-permute-start | bytes 1572872 | tf_op jit(solution)/shard_map/ppermute | solution.py:718
  60.5 25.9 %collective-permute-start.6 = (bf16[128,2048]{1,0:T(8,128)(2,1)S(1)}, bf16[128,2048]{1,0:T(8,128)(2,1)S(1)}, u32[]{:S(2)}, u32[]{:S(2)}) collective-permute-start(bf16[128,2048]{1,0:T(8,128)(2,1)S(1)} %bitcast.231), channel_id=1, source_target_pairs={{0,8},{4,12},{8,0},{12,4},{1,9},{5,13},{9,1},{13,5},{2,10},{6,14},... | collective-permute-start | bytes 1572872 | tf_op jit(solution)/shard_map/ppermute | solution.py:718
  61.8 25.4 %collective-permute-start.7 = (bf16[128,2048]{1,0:T(8,128)(2,1)S(1)}, bf16[128,2048]{1,0:T(8,128)(2,1)S(1)}, u32[]{:S(2)}, u32[]{:S(2)}) collective-permute-start(bf16[128,2048]{1,0:T(8,128)(2,1)S(1)} %bitcast.232), channel_id=1, source_target_pairs={{0,12},{4,8},{8,4},{12,0},{1,13},{5,9},{9,5},{13,1},{2,14},{6,10},... | collective-permute-start | bytes 1572872 | tf_op jit(solution)/shard_map/ppermute | solution.py:718
  94.9 31.8 %collective-permute-start.14 = (bf16[128,256]{1,0:T(8,128)(2,1)S(1)}, bf16[128,256]{1,0:T(8,128)(2,1)S(1)}, u32[]{:S(2)}, u32[]{:S(2)}) collective-permute-start(bf16[128,256]{1,0:T(8,128)(2,1)S(1)} %bitcast.234), channel_id=1, source_target_pairs={{0,1},{1,0},{2,3},{3,2},{4,5},{5,4},{6,7},{7,6},{8,9},{9,8},{10,11... | collective-permute-start | bytes 196616 | tf_op jit(solution)/shard_map/ppermute | solution.py:718
  95.0 31.8 %collective-permute-start.15 = (bf16[128,256]{1,0:T(8,128)(2,1)S(1)}, bf16[128,256]{1,0:T(8,128)(2,1)S(1)}, u32[]{:S(2)}, u32[]{:S(2)}) collective-permute-start(bf16[128,256]{1,0:T(8,128)(2,1)S(1)} %bitcast.235), channel_id=1, source_target_pairs={{0,2},{1,3},{2,0},{3,1},{4,6},{5,7},{6,4},{7,5},{8,10},{9,11},{10,... | collective-permute-start | bytes 196616 | tf_op jit(solution)/shard_map/ppermute | solution.py:718
  97.5 29.3 %collective-permute-start.16 = (bf16[128,256]{1,0:T(8,128)(2,1)S(1)}, bf16[128,256]{1,0:T(8,128)(2,1)S(1)}, u32[]{:S(2)}, u32[]{:S(2)}) collective-permute-start(bf16[128,256]{1,0:T(8,128)(2,1)S(1)} %bitcast.236), channel_id=1, source_target_pairs={{0,3},{1,2},{2,1},{3,0},{4,7},{5,6},{6,5},{7,4},{8,11},{9,10},{10,... | collective-permute-start | bytes 196616 | tf_op jit(solution)/shard_map/ppermute | solution.py:718
  98.6 28.2 %collective-permute-start.13 = (bf16[128,2048]{1,0:T(8,128)(2,1)S(1)}, bf16[128,2048]{1,0:T(8,128)(2,1)S(1)}, u32[]{:S(2)}, u32[]{:S(2)}) collective-permute-start(bf16[128,2048]{1,0:T(8,128)(2,1)S(1)} %pad_maximum_fusion.8.near_ref), channel_id=1, source_target_pairs={{0,2},{1,3},{2,0},{3,1},{4,6},{5,7},{6,4},{7,5},{8,10},{9,11},{10,... | collective-permute-start | bytes 1572872 | tf_op jit(solution)/shard_map/ppermute | solution.py:718
  106.0 28.0 %all-to-all-start = ((bf16[8,512,256]{2,1,0:T(8,128)(2,1)}), bf16[8,512,256]{2,1,0:T(8,128)(2,1)S(1)}, u32[]{:S(2)}, u32[]{:S(2)}) async-start(bf16[8,512,256]{2,1,0:T(8,128)(2,1)} %bitcast.224), calls=%async_computation | async-start | bytes 4194304 | tf_op jit(solution)/shard_map/all_to_all | solution.py:903
  110.8 111.7 %all-gather.3.cloned.1.call-start = ((), (), s32[]{:S(2)}) async-start(), calls=%async_computation.5 | async-start | bytes 11796480 | tf_op jit(solution)/shard_map/all_gather | solution.py:1070
  139.1 45.7 %collective-permute-start.17 = (bf16[1024,256]{1,0:T(8,128)(2,1)}, bf16[1024,256]{1,0:T(8,128)(2,1)S(1)}, u32[]{:S(2)}, u32[]{:S(2)}) collective-permute-start(bf16[1024,256]{1,0:T(8,128)(2,1)} %get-tuple-element.291), channel_id=1, source_target_pairs={{0,0},{1,16},{2,1},{3,17},{16,2},{17,18},{18,3},{19,19},{4,4},{5,2... | collective-permute-start | bytes 1572872 | tf_op jit(solution)/shard_map/ppermute | solution.py:751
  147.1 37.7 %collective-permute-start.18 = (bf16[1024,256]{1,0:T(8,128)(2,1)}, bf16[1024,256]{1,0:T(8,128)(2,1)S(1)}, u32[]{:S(2)}, u32[]{:S(2)}) collective-permute-start(bf16[1024,256]{1,0:T(8,128)(2,1)} %get-tuple-element.290), channel_id=1, source_target_pairs={{0,16},{1,0},{2,17},{3,1},{16,18},{17,2},{18,19},{19,3},{4,20},{5,... | collective-permute-start | bytes 1572872 | tf_op jit(solution)/shard_map/ppermute | solution.py:751
  147.2 37.6 %collective-permute-start.19 = (bf16[1024,256]{1,0:T(8,128)(2,1)}, bf16[1024,256]{1,0:T(8,128)(2,1)}, u32[]{:S(2)}, u32[]{:S(2)}) collective-permute-start(bf16[1024,256]{1,0:T(8,128)(2,1)} %get-tuple-element.289), channel_id=1, source_target_pairs={{0,1},{1,17},{2,0},{3,16},{16,3},{17,19},{18,2},{19,18},{4,5},{5,2... | collective-permute-start | bytes 1572872 | tf_op jit(solution)/shard_map/ppermute | solution.py:751
  149.5 43.8 %collective-permute-start.20 = (bf16[1024,256]{1,0:T(8,128)(2,1)}, bf16[1024,256]{1,0:T(8,128)(2,1)}, u32[]{:S(2)}, u32[]{:S(2)}) collective-permute-start(bf16[1024,256]{1,0:T(8,128)(2,1)} %get-tuple-element.288), channel_id=1, source_target_pairs={{0,17},{1,1},{2,16},{3,0},{16,19},{17,3},{18,18},{19,2},{4,21},{5,... | collective-permute-start | bytes 1572872 | tf_op jit(solution)/shard_map/ppermute | solution.py:751
  206.8 15.6 %all-to-all-start.1 = ((bf16[8,512,128]{1,2,0:T(8,128)(2,1)}), bf16[8,512,128]{1,2,0:T(8,128)(2,1)S(1)}, u32[]{:S(2)}, u32[]{:S(2)}) async-start(bf16[8,512,128]{1,2,0:T(8,128)(2,1)} %copy.117), calls=%async_computation.1 | async-start | bytes 2097152 | tf_op jit(solution)/shard_map/all_to_all | solution.py:909
  210.5 143.3 %all-gather.5.cloned.1.call-start = ((), (), s32[]{:S(2)}) async-start(), calls=%async_computation.6 | async-start | bytes 9437184 | tf_op jit(solution)/shard_map/all_gather | solution.py:1098
  219.9 25.0 %collective-permute-start.21 = (bf16[512,1024]{1,0:T(8,128)(2,1)}, bf16[512,1024]{1,0:T(8,128)(2,1)}, u32[]{:S(2)}, u32[]{:S(2)}) collective-permute-start(bf16[512,1024]{1,0:T(8,128)(2,1)} %unstack.11), channel_id=1, source_target_pairs={{0,1},{1,0},{2,3},{3,2},{4,5},{5,4},{6,7},{7,6},{8,9},{9,8},{10,11... | collective-permute-start | bytes 3145736 | tf_op jit(solution)/shard_map/ppermute | solution.py:718
  244.9 24.1 %collective-permute-start.22 = (bf16[512,1024]{1,0:T(8,128)(2,1)}, bf16[512,1024]{1,0:T(8,128)(2,1)}, u32[]{:S(2)}, u32[]{:S(2)}) collective-permute-start(bf16[512,1024]{1,0:T(8,128)(2,1)} %fusion.53), channel_id=1, source_target_pairs={{0,1},{1,0},{2,3},{3,2},{4,5},{5,4},{6,7},{7,6},{8,9},{9,8},{10,11... | collective-permute-start | bytes 3145736 | tf_op jit(solution)/shard_map/ppermute | solution.py:718
  269.3 23.7 %collective-permute-start.23 = (bf16[512,256]{1,0:T(8,128)(2,1)S(1)}, bf16[512,256]{1,0:T(8,128)(2,1)S(1)}, u32[]{:S(2)}, u32[]{:S(2)}) collective-permute-start(bf16[512,256]{1,0:T(8,128)(2,1)S(1)} %get-tuple-element.315), channel_id=1, source_target_pairs={{0,0},{1,16},{2,1},{3,17},{16,2},{17,18},{18,3},{19,19},{4,4},{5,2... | collective-permute-start | bytes 786440 | tf_op jit(solution)/shard_map/ppermute | solution.py:751
  272.7 20.3 %collective-permute-start.24 = (bf16[512,256]{1,0:T(8,128)(2,1)S(1)}, bf16[512,256]{1,0:T(8,128)(2,1)S(1)}, u32[]{:S(2)}, u32[]{:S(2)}) collective-permute-start(bf16[512,256]{1,0:T(8,128)(2,1)S(1)} %get-tuple-element.314), channel_id=1, source_target_pairs={{0,16},{1,0},{2,17},{3,1},{16,18},{17,2},{18,19},{19,3},{4,20},{5,... | collective-permute-start | bytes 786440 | tf_op jit(solution)/shard_map/ppermute | solution.py:751
  274.0 19.0 %collective-permute-start.25 = (bf16[512,256]{1,0:T(8,128)(2,1)S(1)}, bf16[512,256]{1,0:T(8,128)(2,1)S(1)}, u32[]{:S(2)}, u32[]{:S(2)}) collective-permute-start(bf16[512,256]{1,0:T(8,128)(2,1)S(1)} %get-tuple-element.313), channel_id=1, source_target_pairs={{0,1},{1,17},{2,0},{3,16},{16,3},{17,19},{18,2},{19,18},{4,5},{5,2... | collective-permute-start | bytes 786440 | tf_op jit(solution)/shard_map/ppermute | solution.py:751
  275.5 22.3 %collective-permute-start.26 = (bf16[512,256]{1,0:T(8,128)(2,1)S(1)}, bf16[512,256]{1,0:T(8,128)(2,1)S(1)}, u32[]{:S(2)}, u32[]{:S(2)}) collective-permute-start(bf16[512,256]{1,0:T(8,128)(2,1)S(1)} %get-tuple-element.312), channel_id=1, source_target_pairs={{0,17},{1,1},{2,16},{3,0},{16,19},{17,3},{18,18},{19,2},{4,21},{5,... | collective-permute-start | bytes 786440 | tf_op jit(solution)/shard_map/ppermute | solution.py:751
  302.4 25.4 %collective-permute-start.27 = (bf16[512,1024]{1,0:T(8,128)(2,1)S(1)}, bf16[512,1024]{1,0:T(8,128)(2,1)S(1)}, u32[]{:S(2)}, u32[]{:S(2)}) collective-permute-start(bf16[512,1024]{1,0:T(8,128)(2,1)S(1)} %fusion.75), channel_id=1, source_target_pairs={{0,1},{1,0},{2,3},{3,2},{4,5},{5,4},{6,7},{7,6},{8,9},{9,8},{10,11... | collective-permute-start | bytes 3145736 | tf_op jit(solution)/shard_map/ppermute | solution.py:718
  305.2 14.4 %collective-permute-start.29 = (bf16[512,2048]{1,0:T(8,128)(2,1)S(1)}, bf16[512,2048]{1,0:T(8,128)(2,1)S(1)}, u32[]{:S(2)}, u32[]{:S(2)}) collective-permute-start(bf16[512,2048]{1,0:T(8,128)(2,1)S(1)} %convolution_convert_fusion), channel_id=1, source_target_pairs={{0,16},{16,0},{1,17},{17,1},{2,18},{18,2},{3,19},{19,3},{4,20},{20... | collective-permute-start | bytes 6291464 | tf_op jit(solution)/shard_map/ppermute | solution.py:718
  308.0 15.9 %collective-permute-start.28 = (bf16[512,2048]{1,0:T(8,128)(2,1)S(1)}, bf16[512,2048]{1,0:T(8,128)(2,1)S(1)}, u32[]{:S(2)}, u32[]{:S(2)}) collective-permute-start(bf16[512,2048]{1,0:T(8,128)(2,1)S(1)} %convolution_convert_fusion.1), channel_id=1, source_target_pairs={{0,16},{16,0},{1,17},{17,1},{2,18},{18,2},{3,19},{19,3},{4,20},{20... | collective-permute-start | bytes 6291464 | tf_op jit(solution)/shard_map/ppermute | solution.py:718
  337.7 16.0 %all-to-all-start.2 = ((bf16[8,512,128]{2,1,0:T(8,128)(2,1)}), bf16[8,512,128]{2,1,0:T(8,128)(2,1)}, u32[]{:S(2)}, u32[]{:S(2)}) async-start(bf16[8,512,128]{2,1,0:T(8,128)(2,1)} %bitcast.250), calls=%async_computation.2 | async-start | bytes 2097152 | tf_op jit(solution)/shard_map/all_to_all | solution.py:903
  341.9 114.8 %reduce-scatter.2.cloned.1.call-start = ((), (), s32[]{:S(2)}) async-start(), calls=%async_computation.7 | async-start | bytes 7372800 | tf_op jit(solution)/shard_map/reduce_scatter | solution.py:1151
  353.8 56.5 %collective-permute-start.36 = (bf16[512,1024]{1,0:T(8,128)(2,1)}, bf16[512,1024]{1,0:T(8,128)(2,1)S(1)}, u32[]{:S(2)}, u32[]{:S(2)}) collective-permute-start(bf16[512,1024]{1,0:T(8,128)(2,1)} %fusion.78), channel_id=1, source_target_pairs={{0,1},{1,0},{2,3},{3,2},{4,5},{5,4},{6,7},{7,6},{8,9},{9,8},{10,11... | collective-permute-start | bytes 3145736 | tf_op jit(solution)/shard_map/ppermute | solution.py:718
  357.0 53.2 %collective-permute-start.32 = (bf16[1024,256]{1,0:T(8,128)(2,1)S(1)}, bf16[1024,256]{1,0:T(8,128)(2,1)S(1)}, u32[]{:S(2)}, u32[]{:S(2)}) collective-permute-start(bf16[1024,256]{1,0:T(8,128)(2,1)S(1)} %get-tuple-element.284), channel_id=1, source_target_pairs={{0,0},{16,1},{1,2},{17,3},{2,16},{18,17},{3,18},{19,19},{4,4},{20,... | collective-permute-start | bytes 1572872 | tf_op jit(solution)/shard_map/ppermute | solution.py:777
  362.8 47.5 %collective-permute-start.33 = (bf16[1024,256]{1,0:T(8,128)(2,1)S(1)}, bf16[1024,256]{1,0:T(8,128)(2,1)S(1)}, u32[]{:S(2)}, u32[]{:S(2)}) collective-permute-start(bf16[1024,256]{1,0:T(8,128)(2,1)S(1)} %get-tuple-element.283), channel_id=1, source_target_pairs={{16,0},{0,1},{17,2},{1,3},{18,16},{2,17},{19,18},{3,19},{20,4},{4,... | collective-permute-start | bytes 1572872 | tf_op jit(solution)/shard_map/ppermute | solution.py:777
  362.8 47.5 %collective-permute-start.34 = (bf16[1024,256]{1,0:T(8,128)(2,1)S(1)}, bf16[1024,256]{1,0:T(8,128)(2,1)S(1)}, u32[]{:S(2)}, u32[]{:S(2)}) collective-permute-start(bf16[1024,256]{1,0:T(8,128)(2,1)S(1)} %get-tuple-element.282), channel_id=1, source_target_pairs={{1,0},{17,1},{0,2},{16,3},{3,16},{19,17},{2,18},{18,19},{5,4},{21,... | collective-permute-start | bytes 1572872 | tf_op jit(solution)/shard_map/ppermute | solution.py:777
  363.3 47.0 %collective-permute-start.35 = (bf16[1024,256]{1,0:T(8,128)(2,1)S(1)}, bf16[1024,256]{1,0:T(8,128)(2,1)S(1)}, u32[]{:S(2)}, u32[]{:S(2)}) collective-permute-start(bf16[1024,256]{1,0:T(8,128)(2,1)S(1)} %get-tuple-element.281), channel_id=1, source_target_pairs={{17,0},{1,1},{16,2},{0,3},{19,16},{3,17},{18,18},{2,19},{21,4},{5,... | collective-permute-start | bytes 1572872 | tf_op jit(solution)/shard_map/ppermute | solution.py:777
  410.8 21.3 %collective-permute-start.37 = (bf16[512,256]{1,0:T(8,128)(2,1)S(1)}, bf16[512,256]{1,0:T(8,128)(2,1)S(1)}, u32[]{:S(2)}, u32[]{:S(2)}) collective-permute-start(bf16[512,256]{1,0:T(8,128)(2,1)S(1)} %get-tuple-element.311), channel_id=1, source_target_pairs={{0,0},{16,1},{1,2},{17,3},{2,16},{18,17},{3,18},{19,19},{4,4},{20,... | collective-permute-start | bytes 786440 | tf_op jit(solution)/shard_map/ppermute | solution.py:777
  414.9 17.2 %collective-permute-start.38 = (bf16[512,256]{1,0:T(8,128)(2,1)S(1)}, bf16[512,256]{1,0:T(8,128)(2,1)S(1)}, u32[]{:S(2)}, u32[]{:S(2)}) collective-permute-start(bf16[512,256]{1,0:T(8,128)(2,1)S(1)} %get-tuple-element.310), channel_id=1, source_target_pairs={{16,0},{0,1},{17,2},{1,3},{18,16},{2,17},{19,18},{3,19},{20,4},{4,... | collective-permute-start | bytes 786440 | tf_op jit(solution)/shard_map/ppermute | solution.py:777
  435.9 31.3 %all-to-all-start.3 = ((bf16[8,512,256]{1,2,0:T(8,128)(2,1)}), bf16[8,512,256]{1,2,0:T(8,128)(2,1)}, u32[]{:S(2)}, u32[]{:S(2)}) async-start(bf16[8,512,256]{1,2,0:T(8,128)(2,1)} %copy.122), calls=%async_computation.4 | async-start | bytes 4194304 | tf_op jit(solution)/shard_map/all_to_all | solution.py:909
  444.9 15.5 %collective-permute-start.39 = (bf16[512,256]{1,0:T(8,128)(2,1)}, bf16[512,256]{1,0:T(8,128)(2,1)}, u32[]{:S(2)}, u32[]{:S(2)}) collective-permute-start(bf16[512,256]{1,0:T(8,128)(2,1)} %get-tuple-element.309), channel_id=1, source_target_pairs={{1,0},{17,1},{0,2},{16,3},{3,16},{19,17},{2,18},{18,19},{5,4},{21,... | collective-permute-start | bytes 786440 | tf_op jit(solution)/shard_map/ppermute | solution.py:777
  445.7 15.0 %collective-permute-start.40 = (bf16[512,256]{1,0:T(8,128)(2,1)}, bf16[512,256]{1,0:T(8,128)(2,1)}, u32[]{:S(2)}, u32[]{:S(2)}) collective-permute-start(bf16[512,256]{1,0:T(8,128)(2,1)} %get-tuple-element.308), channel_id=1, source_target_pairs={{17,0},{1,1},{16,2},{0,3},{19,16},{3,17},{18,18},{2,19},{21,4},{5,... | collective-permute-start | bytes 786440 | tf_op jit(solution)/shard_map/ppermute | solution.py:777
  457.8 25.5 %collective-permute-start.41 = (bf16[128,2048]{1,0:T(8,128)(2,1)S(1)}, bf16[128,2048]{1,0:T(8,128)(2,1)S(1)}, u32[]{:S(2)}, u32[]{:S(2)}) collective-permute-start(bf16[128,2048]{1,0:T(8,128)(2,1)S(1)} %pad_maximum_fusion.9), channel_id=1, source_target_pairs={{0,2},{1,3},{2,0},{3,1},{4,6},{5,7},{6,4},{7,5},{8,10},{9,11},{10,... | collective-permute-start | bytes 1572872 | tf_op jit(solution)/shard_map/ppermute | solution.py:718
  503.8 21.9 %collective-permute-start.42 = (bf16[512,256]{1,0:T(8,128)(2,1)S(1)}, bf16[512,256]{1,0:T(8,128)(2,1)S(1)}, u32[]{:S(2)}, u32[]{:S(2)}) collective-permute-start(bf16[512,256]{1,0:T(8,128)(2,1)S(1)} %get-tuple-element.307), channel_id=1, source_target_pairs={{0,0},{16,1},{1,2},{17,3},{2,16},{18,17},{3,18},{19,19},{4,4},{20,... | collective-permute-start | bytes 786440 | tf_op jit(solution)/shard_map/ppermute | solution.py:777
  507.3 23.4 %collective-permute-start.43 = (bf16[512,256]{1,0:T(8,128)(2,1)S(1)}, bf16[512,256]{1,0:T(8,128)(2,1)S(1)}, u32[]{:S(2)}, u32[]{:S(2)}) collective-permute-start(bf16[512,256]{1,0:T(8,128)(2,1)S(1)} %get-tuple-element.306), channel_id=1, source_target_pairs={{16,0},{0,1},{17,2},{1,3},{18,16},{2,17},{19,18},{3,19},{20,4},{4,... | collective-permute-start | bytes 786440 | tf_op jit(solution)/shard_map/ppermute | solution.py:777
  507.5 34.3 %collective-permute-start.46 = (bf16[128,2048]{1,0:T(8,128)(2,1)S(1)}, bf16[128,2048]{1,0:T(8,128)(2,1)S(1)}, u32[]{:S(2)}, u32[]{:S(2)}) collective-permute-start(bf16[128,2048]{1,0:T(8,128)(2,1)S(1)} %add_convert_fusion.6.refs_0_), channel_id=1, source_target_pairs={{0,4},{4,0},{8,12},{12,8},{1,5},{5,1},{9,13},{13,9},{2,6},{6,2},{1... | collective-permute-start | bytes 1572872 | tf_op jit(solution)/shard_map/ppermute | solution.py:718
  509.8 31.9 %collective-permute-start.47 = (bf16[128,2048]{1,0:T(8,128)(2,1)S(1)}, bf16[128,2048]{1,0:T(8,128)(2,1)S(1)}, u32[]{:S(2)}, u32[]{:S(2)}) collective-permute-start(bf16[128,2048]{1,0:T(8,128)(2,1)S(1)} %add_convert_fusion.6.refs_0_), channel_id=1, source_target_pairs={{0,8},{4,12},{8,0},{12,4},{1,9},{5,13},{9,1},{13,5},{2,10},{6,14},... | collective-permute-start | bytes 1572872 | tf_op jit(solution)/shard_map/ppermute | solution.py:718
  511.2 30.6 %collective-permute-start.48 = (bf16[128,2048]{1,0:T(8,128)(2,1)S(1)}, bf16[128,2048]{1,0:T(8,128)(2,1)S(1)}, u32[]{:S(2)}, u32[]{:S(2)}) collective-permute-start(bf16[128,2048]{1,0:T(8,128)(2,1)S(1)} %add_convert_fusion.6.refs_0_), channel_id=1, source_target_pairs={{0,12},{4,8},{8,4},{12,0},{1,13},{5,9},{9,5},{13,1},{2,14},{6,10},... | collective-permute-start | bytes 1572872 | tf_op jit(solution)/shard_map/ppermute | solution.py:718
  541.8 15.3 %collective-permute-start.60 = (f32[512]{0:T(512)S(1)}, f32[512]{0:T(512)S(1)}, u32[]{:S(2)}, u32[]{:S(2)}) collective-permute-start(f32[512]{0:T(512)S(1)} %add_add_fusion.1), channel_id=1, source_target_pairs={{0,16},{16,0},{1,17},{17,1},{2,18},{18,2},{3,19},{19,3},{4,20},{20... | collective-permute-start | bytes 6152 | tf_op jit(solution)/shard_map/ppermute | solution.py:718
  547.2 21.2 %collective-permute-start.56 = (bf16[1,400,256]{2,1,0:T(8,128)(2,1)S(1)}, bf16[1,400,256]{2,1,0:T(8,128)(2,1)}, u32[]{:S(2)}, u32[]{:S(2)}) collective-permute-start(bf16[1,400,256]{2,1,0:T(8,128)(2,1)S(1)} %maximum_bitcast_fusion), channel_id=1, source_target_pairs={{0,4},{4,0},{8,12},{12,8},{1,5},{5,1},{9,13},{13,9},{2,6},{6,2},{1... | collective-permute-start | bytes 614408 | tf_op jit(solution)/shard_map/ppermute | solution.py:718
  (87 other events, 654.0 us)
Sparse Core Ops, SparseCore 0:
  136.7 65.1 all-gather.2
  245.3 54.5 all-gather.4
  353.9 68.1 reduce-scatter.1
